TPU v7x, 32 devices: a whole 2x2x4 slice. The times are simulated.
32 devices in a mesh: seq: 8 (over y, x, core), head: 4 (over z).
Axes of the slice: x: 2, y: 2, z: 4, core: 2. Of those that a mesh axis runs over, the one named last changes fastest.
Arguments:
- tokens: bfloat16 [8192, 2048], P('seq'), may hold values from -6 to 6
- doc_lengths: int32 [12], replicated, may hold values from 1 to 4096, 8192 in all
- mixer_gain: float32 [2048], replicated, may hold values from 0.5 to 1.5
- query_weight: float32 [2048, 2048], P('seq', 'head'), may hold values from -0.125 to 0.125
- key_weight: float32 [2048, 2048], P('seq', 'head'), may hold values from -0.125 to 0.125
- value_weight: float32 [2048, 4096], P('seq', 'head'), may hold values from -0.125 to 0.125
- gate_weight: float32 [2048, 4096], P('seq', 'head'), may hold values from -0.125 to 0.125
- alpha_weight: float32 [2048, 16], P('seq', 'head'), may hold values from -0.125 to 0.125
- beta_weight: float32 [2048, 16], P('seq', 'head'), may hold values from -0.125 to 0.125
- decay_log: float32 [16], P('head'), may hold values from -6 to 0
- decay_bias: float32 [16], P('head'), may hold values from -4 to -1
- query_taps: float32 [4, 2048], P(None, 'head'), may hold values from -3 to 3
- key_taps: float32 [4, 2048], P(None, 'head'), may hold values from -3 to 3
- value_taps: float32 [4, 4096], P(None, 'head'), may hold values from -3 to 3
- head_gain: float32 [256], replicated, may hold values from 0.5 to 1.5
- output_weight: float32 [4096, 2048], P('head', 'seq'), may hold values from -0.09375 to 0.09375
- ffn_gain: float32 [2048], replicated, may hold values from 0.5 to 1.5
- ffn_gate: float32 [2048, 5632], P('seq', 'head'), may hold values from -0.125 to 0.125
- ffn_up: float32 [2048, 5632], P('seq', 'head'), may hold values from -0.125 to 0.125
- ffn_down: float32 [5632, 2048], P('head', 'seq'), may hold values from -0.078125 to 0.078125
- cotangent: bfloat16 [8192, 2048], P('seq'), may hold values from -6 to 6
Outputs:
- result: bfloat16 [8192, 2048], P('seq')
- tokens_grad: float32 [8192, 2048], P('seq')
- mixer_gain_grad: float32 [2048], replicated
- query_weight_grad: float32 [2048, 2048], P('seq', 'head')
- key_weight_grad: float32 [2048, 2048], P('seq', 'head')
- value_weight_grad: float32 [2048, 4096], P('seq', 'head')
- gate_weight_grad: float32 [2048, 4096], P('seq', 'head')
- alpha_weight_grad: float32 [2048, 16], P('seq', 'head')
- beta_weight_grad: float32 [2048, 16], P('seq', 'head')
- decay_log_grad: float32 [16], P('head')
- decay_bias_grad: float32 [16], P('head')
- query_taps_grad: float32 [4, 2048], P(None, 'head')
- key_taps_grad: float32 [4, 2048], P(None, 'head')
- value_taps_grad: float32 [4, 4096], P(None, 'head')
- head_gain_grad: float32 [256], replicated
- output_weight_grad: float32 [4096, 2048], P('head', 'seq')
- ffn_gain_grad: float32 [2048], replicated
- ffn_gate_grad: float32 [2048, 5632], P('seq', 'head')
- ffn_up_grad: float32 [2048, 5632], P('seq', 'head')
- ffn_down_grad: float32 [5632, 2048], P('head', 'seq')
Inputs may be any that keep to these rules, and one draw needn't show every extreme that they name: `doc_lengths`: the 12 documents fill the stream in order; the longest has exactly 4096 tokens.
All inputs are finite; a program needn't handle non-finite values.
Results may differ from a plain program's by a relative error of at most 0.023.
Values may be sent and summed in bfloat16 or wider, within the bound.
A program may use at most 320 MiB of HBM per device.

v0:
```python
from functools import partial

import jax
import jax.numpy as jnp
from jax import lax
from jax.sharding import PartitionSpec as P

GROUP = 64


highest = lax.Precision.HIGHEST


def passed_along(block, axis, distance):
    devices = range(lax.axis_size(axis))
    route = [(i - distance, i) for i in devices if i - distance in devices]
    return lax.ppermute(block, axis, route)


def entering(part, axis, combine, identity):
    place = lax.axis_index(axis)
    gathered = jax.tree.map(lambda a: lax.all_gather(a, axis), part)
    state = jax.tree.map(lambda a, e: jnp.zeros_like(a) + jnp.asarray(e, a.dtype), part, identity)

    def one(lap, state):
        return combine(
            state, jax.tree.map(lambda a: lax.dynamic_index_in_dim(a, lap, 0, False), gathered)
        )

    return lax.fori_loop(0, place, one, state)


def carried_in(shard, axis, combine, identity):
    length, position = (lax.axis_size(axis), lax.axis_index(axis))
    everything = jax.tree.map(
        lambda part, kind: lax.all_gather(part.astype(kind), axis),
        shard,
        jax.tree.map(lambda a: jnp.bfloat16 if a.dtype == jnp.float32 else a.dtype, shard),
    )
    start = jax.tree.map(
        lambda part, zero: jnp.broadcast_to(jnp.asarray(zero, part.dtype), part.shape),
        shard,
        identity,
    )

    def lap(k, before):
        at = length - 1 - k
        reached = at > position
        new = combine(
            before, jax.tree.map(lambda part, own: part[at].astype(own.dtype), everything, shard)
        )
        return jax.tree.map(lambda a, b: jnp.where(reached, a, b), new, before)

    return lax.fori_loop(0, length, lap, start)


def group_step(carry, blocks):
    state_now, seg_prev = carry
    queries, key_rows, values, log_decay, beta_gate, segment = blocks
    block_size = segment.shape[0]
    cum_decay = jnp.cumsum(log_decay, axis=-1)
    same_doc = segment[:, None] == segment[None, :]
    row_index = lax.broadcasted_iota(jnp.int32, (block_size, block_size), 0)
    col_index = lax.broadcasted_iota(jnp.int32, (block_size, block_size), 1)
    lower_mask = same_doc & (row_index >= col_index)
    strict_mask = same_doc & (row_index > col_index)
    decay_gap = cum_decay[:, :, None] - cum_decay[:, None, :]
    decay_lower = jnp.where(lower_mask, jnp.exp(jnp.where(lower_mask, decay_gap, 0.0)), 0.0)
    decay_strict = jnp.where(strict_mask, decay_lower, 0.0)
    alive_mask = (segment == seg_prev).astype(jnp.float32)
    from_start = jnp.exp(cum_decay) * alive_mask
    key_gram = jnp.einsum("hid,hjd->hij", key_rows, key_rows, precision=highest)
    power_term = -beta_gate[:, :, None] * decay_strict * key_gram
    inverse = jnp.eye(block_size, dtype=jnp.float32) + power_term
    for repeat in range((block_size - 1).bit_length() - 1):
        power_term = jnp.einsum("hij,hjk->hik", power_term, power_term, precision=highest)
        inverse = inverse + jnp.einsum("hij,hjk->hik", inverse, power_term, precision=highest)
    key_state = jnp.einsum("hid,hdv->hiv", key_rows, state_now, precision=highest)
    target = beta_gate[:, :, None] * (values - from_start[:, :, None] * key_state)
    delta_rows = jnp.einsum("hij,hjv->hiv", inverse, target, precision=highest)
    query_key = jnp.einsum("hid,hjd->hij", queries, key_rows, precision=highest)
    query_state = jnp.einsum("hid,hdv->hiv", queries, state_now, precision=highest)
    output = from_start[:, :, None] * query_state + jnp.einsum(
        "hij,hjv->hiv", decay_lower * query_key, delta_rows, precision=highest
    )
    last_same = (segment == segment[-1])[None, :]
    to_end = jnp.where(
        last_same, jnp.exp(jnp.where(last_same, cum_decay[:, -1:] - cum_decay, 0.0)), 0.0
    )
    carried = jnp.exp(cum_decay[:, -1]) * alive_mask[-1]
    state_next = carried[:, None, None] * state_now + jnp.einsum(
        "hjd,hjv->hdv", key_rows * to_end[:, :, None], delta_rows, precision=highest
    )
    return ((state_next, segment[-1]), output)


def run_groups(
    state_now, seg_prev, queries, key_rows, values, log_decay, beta_gate, segment, block_size
):
    head_count, length = log_decay.shape
    block_count = length // block_size

    def splitter(array):
        shaped = array.reshape((head_count, block_count, block_size) + array.shape[2:])
        return jnp.moveaxis(shaped, 1, 0)

    blocks = (
        splitter(queries),
        splitter(key_rows),
        splitter(values),
        splitter(log_decay),
        splitter(beta_gate),
        segment.reshape(block_count, block_size),
    )
    (state_end, seg_end), outputs = lax.scan(
        jax.checkpoint(group_step), (state_now, seg_prev), blocks
    )
    return (jnp.moveaxis(outputs, 0, 1).reshape(head_count, length, -1), state_end)


def rms_scale(array, epsilon):
    return lax.rsqrt(jnp.mean(array * array, axis=-1, keepdims=True) + epsilon)


def unit_rows(array):
    return array * lax.rsqrt(jnp.sum(array * array, axis=-1, keepdims=True) + 1e-06)


def conv_silu(extended, seg_ext, taps):
    reach = taps.shape[0]
    length = extended.shape[0] - reach + 1
    total = jnp.zeros((length, extended.shape[1]), jnp.float32)
    for offset in range(reach):
        match = (seg_ext[offset : offset + length] == seg_ext[reach - 1 :]).astype(jnp.float32)
        total = total + taps[offset] * extended[offset : offset + length] * match[:, None]
    return jax.nn.silu(total)


def mixer_inputs(
    ext_query,
    ext_key,
    ext_value,
    query_taps,
    key_taps,
    value_taps,
    alpha_pre,
    beta_pre,
    decay_log,
    decay_bias,
    seg_ext,
):
    head_count = alpha_pre.shape[1]
    conv_query = conv_silu(ext_query, seg_ext, query_taps)
    length = conv_query.shape[0]
    queries = unit_rows(conv_query.reshape(length, head_count, -1))
    key_rows = unit_rows(conv_silu(ext_key, seg_ext, key_taps).reshape(length, head_count, -1))
    values = conv_silu(ext_value, seg_ext, value_taps).reshape(length, head_count, -1)
    log_decay = -jnp.exp(decay_log) * jax.nn.softplus(alpha_pre + decay_bias)
    beta_gate = jax.nn.sigmoid(beta_pre)
    return (
        jnp.swapaxes(queries, 0, 1),
        jnp.swapaxes(key_rows, 0, 1),
        jnp.swapaxes(values, 0, 1),
        log_decay.T,
        beta_gate.T,
    )


def head_gate(mixed, gate_pre, head_gain):
    per_token = jnp.swapaxes(mixed, 0, 1)
    length = per_token.shape[0]
    head_count = per_token.shape[1]
    normed = per_token * rms_scale(per_token, 1e-05)
    gate_act = jax.nn.silu(gate_pre.reshape(length, head_count, -1))
    return (normed * head_gain * gate_act).reshape(length, -1)


def product(left, right):
    return jnp.dot(left, right, preferred_element_type=jnp.float32)


def across(left, right):
    return lax.dot_general(
        left, right, (((0,), (0,)), ((), ())), preferred_element_type=jnp.float32
    )


def against(left, right):
    return lax.dot_general(
        left, right, (((1,), (1,)), ((), ())), preferred_element_type=jnp.float32
    )


def compose(earlier, later):
    map_early, add_early = earlier
    map_late, add_late = later
    return (
        jnp.einsum("hij,hjk->hik", map_late, map_early, precision=highest),
        jnp.einsum("hij,hjv->hiv", map_late, add_early, precision=highest) + add_late,
    )


def shards(
    tokens,
    doc_lengths,
    mixer_gain,
    query_weight,
    key_weight,
    value_weight,
    gate_weight,
    alpha_weight,
    beta_weight,
    decay_log,
    decay_bias,
    query_taps,
    key_taps,
    value_taps,
    head_gain,
    output_weight,
    ffn_gain,
    ffn_gate,
    ffn_up,
    ffn_down,
    cotangent,
):
    length = tokens.shape[0]
    reach = query_taps.shape[0]
    shard = lax.axis_index("seq")
    starts = jnp.cumsum(doc_lengths, dtype=jnp.int32) - doc_lengths
    positions = shard * length + jnp.arange(1 - reach, length, dtype=jnp.int32)
    seg_ext = jnp.sum(
        (starts[None, :] <= positions[:, None]).astype(jnp.int32), axis=1, dtype=jnp.int32
    )
    segment = seg_ext[reach - 1 :]
    seg_prev = seg_ext[reach - 2]
    cast_query = query_weight.astype(jnp.bfloat16)
    cast_key = key_weight.astype(jnp.bfloat16)
    cast_value = value_weight.astype(jnp.bfloat16)
    cast_gate = gate_weight.astype(jnp.bfloat16)
    cast_alpha = alpha_weight.astype(jnp.bfloat16)
    cast_beta = beta_weight.astype(jnp.bfloat16)
    cast_output = output_weight.astype(jnp.bfloat16)
    cast_widen = ffn_gate.astype(jnp.bfloat16)
    cast_lift = ffn_up.astype(jnp.bfloat16)
    cast_narrow = ffn_down.astype(jnp.bfloat16)
    gathered = (
        lax.all_gather(cast_query, "seq", axis=0, tiled=True),
        lax.all_gather(cast_key, "seq", axis=0, tiled=True),
        lax.all_gather(cast_value, "seq", axis=0, tiled=True),
        lax.all_gather(cast_gate, "seq", axis=0, tiled=True),
        lax.all_gather(cast_alpha, "seq", axis=0, tiled=True),
        lax.all_gather(cast_beta, "seq", axis=0, tiled=True),
        lax.all_gather(cast_output, "seq", axis=1, tiled=True),
        lax.all_gather(cast_widen, "seq", axis=0, tiled=True),
        lax.all_gather(cast_lift, "seq", axis=0, tiled=True),
        lax.all_gather(cast_narrow, "seq", axis=1, tiled=True),
    )
    (
        query_full,
        key_full,
        value_full,
        gate_full,
        alpha_full,
        beta_full,
        output_full,
        widen_full,
        lift_full,
        narrow_full,
    ) = gathered
    stream = tokens.astype(jnp.float32)
    first_scale = rms_scale(stream, 1e-06)
    first_norm = stream * first_scale
    first_in = (first_norm * mixer_gain).astype(jnp.bfloat16)
    pre_query = product(first_in, query_full).astype(jnp.bfloat16)
    pre_key = product(first_in, key_full).astype(jnp.bfloat16)
    pre_value = product(first_in, value_full).astype(jnp.bfloat16)
    gate_pre = product(first_in, gate_full)
    alpha_pre = product(first_in, alpha_full)
    beta_pre = product(first_in, beta_full)
    edges = passed_along(
        (
            pre_query[length - reach + 1 :],
            pre_key[length - reach + 1 :],
            pre_value[length - reach + 1 :],
        ),
        "seq",
        1,
    )
    ext_query = jnp.concatenate([edges[0], pre_query], axis=0).astype(jnp.float32)
    ext_key = jnp.concatenate([edges[1], pre_key], axis=0).astype(jnp.float32)
    ext_value = jnp.concatenate([edges[2], pre_value], axis=0).astype(jnp.float32)
    (queries, key_rows, values, log_decay, beta_gate), mixer_back = jax.vjp(
        partial(mixer_inputs, seg_ext=seg_ext),
        ext_query,
        ext_key,
        ext_value,
        query_taps,
        key_taps,
        value_taps,
        alpha_pre,
        beta_pre,
        decay_log,
        decay_bias,
    )
    head_count = queries.shape[0]
    key_size = queries.shape[2]
    value_size = values.shape[2]
    identity = jnp.broadcast_to(
        jnp.eye(key_size, dtype=jnp.float32), (head_count, key_size, key_size)
    )
    values_aug = jnp.concatenate(
        [values, jnp.zeros((head_count, length, key_size), jnp.float32)], axis=2
    )
    state_aug = jnp.concatenate(
        [jnp.zeros((head_count, key_size, value_size), jnp.float32), identity], axis=2
    )
    out_aug, end_aug = run_groups(
        state_aug, seg_prev, queries, key_rows, values_aug, log_decay, beta_gate, segment, GROUP
    )
    through = out_aug[:, :, value_size:]
    offset_part = end_aug[:, :, :value_size]
    carry_map = end_aug[:, :, value_size:]
    chain_in = entering(
        (carry_map, offset_part), "seq", compose, (identity, jnp.zeros_like(offset_part))
    )
    state_in = chain_in[1]

    def local_chain(chain_queries, chain_keys, chain_values, chain_decay, chain_beta):
        return run_groups(
            state_in,
            seg_prev,
            chain_queries,
            chain_keys,
            chain_values,
            chain_decay,
            chain_beta,
            segment,
            GROUP,
        )

    chain_out, chain_back = jax.vjp(local_chain, queries, key_rows, values, log_decay, beta_gate)
    mixed = chain_out[0]
    mix_float, gate_back = jax.vjp(head_gate, mixed, gate_pre, head_gain)
    mix_out = mix_float.astype(jnp.bfloat16)
    middle = stream + lax.psum(product(mix_out, output_full).astype(jnp.bfloat16), "head").astype(
        jnp.float32
    )
    second_scale = rms_scale(middle, 1e-06)
    second_norm = middle * second_scale
    second_in = (second_norm * ffn_gain).astype(jnp.bfloat16)
    gate_act = product(second_in, widen_full)
    lift_act = product(second_in, lift_full)
    swish = jax.nn.silu(gate_act)
    hidden = (swish * lift_act).astype(jnp.bfloat16)
    result = (
        middle
        + lax.psum(product(hidden, narrow_full).astype(jnp.bfloat16), "head").astype(jnp.float32)
    ).astype(jnp.bfloat16)
    regathered = (
        lax.all_gather(cast_query, "seq", axis=0, tiled=True),
        lax.all_gather(cast_key, "seq", axis=0, tiled=True),
        lax.all_gather(cast_value, "seq", axis=0, tiled=True),
        lax.all_gather(cast_gate, "seq", axis=0, tiled=True),
        lax.all_gather(cast_alpha, "seq", axis=0, tiled=True),
        lax.all_gather(cast_beta, "seq", axis=0, tiled=True),
        lax.all_gather(cast_output, "seq", axis=1, tiled=True),
        lax.all_gather(cast_widen, "seq", axis=0, tiled=True),
        lax.all_gather(cast_lift, "seq", axis=0, tiled=True),
        lax.all_gather(cast_narrow, "seq", axis=1, tiled=True),
    )
    (
        query_full,
        key_full,
        value_full,
        gate_full,
        alpha_full,
        beta_full,
        output_full,
        widen_full,
        lift_full,
        narrow_full,
    ) = regathered
    grad_out = cotangent.astype(jnp.float32)
    narrow_wgrad = across(hidden, cotangent)
    hidden_grad = against(cotangent, narrow_full)
    sigma = jax.nn.sigmoid(gate_act)
    gate_grad = (hidden_grad * lift_act * sigma * (1.0 + gate_act * (1.0 - sigma))).astype(
        jnp.bfloat16
    )
    lift_grad = (hidden_grad * swish).astype(jnp.bfloat16)
    widen_wgrad = across(second_in, gate_grad)
    lift_wgrad = across(second_in, lift_grad)
    second_grad = lax.psum(
        (against(gate_grad, widen_full) + against(lift_grad, lift_full)).astype(jnp.bfloat16),
        "head",
    ).astype(jnp.float32)
    second_weighted = second_grad * ffn_gain
    ffn_gain_part = jnp.sum(second_grad * second_norm, axis=0)
    middle_grad = grad_out + second_scale * (
        second_weighted
        - second_norm * jnp.mean(second_weighted * second_norm, axis=-1, keepdims=True)
    )
    middle_low = middle_grad.astype(jnp.bfloat16)
    output_wgrad = across(mix_out, middle_low)
    mix_grad = against(middle_low, output_full)
    mixed_grad, gate_pre_grad, head_gain_part = gate_back(mix_grad)
    local_adjoint = jnp.einsum("htd,htv->hdv", through, mixed_grad, precision=highest)
    chain_later = carried_in(
        (jnp.swapaxes(carry_map, 1, 2), local_adjoint),
        "seq",
        compose,
        (identity, jnp.zeros_like(local_adjoint)),
    )
    state_out_grad = chain_later[1]
    inner_grads = chain_back((mixed_grad, state_out_grad))
    (
        ext_query_grad,
        ext_key_grad,
        ext_value_grad,
        query_taps_part,
        key_taps_part,
        value_taps_part,
        alpha_grad,
        beta_grad,
        decay_log_part,
        decay_bias_part,
    ) = mixer_back(inner_grads)
    edge_grads = passed_along(
        (ext_query_grad[: reach - 1], ext_key_grad[: reach - 1], ext_value_grad[: reach - 1]),
        "seq",
        -1,
    )

    def settle(ext_grad, edge_grad):
        own_rows = ext_grad[reach - 1 :]
        filled = jnp.concatenate(
            [jnp.zeros((length - reach + 1, own_rows.shape[1]), jnp.float32), edge_grad], axis=0
        )
        return (own_rows + filled).astype(jnp.bfloat16)

    query_pgrad = settle(ext_query_grad, edge_grads[0])
    key_pgrad = settle(ext_key_grad, edge_grads[1])
    value_pgrad = settle(ext_value_grad, edge_grads[2])
    gate_pgrad = gate_pre_grad.astype(jnp.bfloat16)
    alpha_pgrad = alpha_grad.astype(jnp.bfloat16)
    beta_pgrad = beta_grad.astype(jnp.bfloat16)
    query_wgrad = across(first_in, query_pgrad)
    key_wgrad = across(first_in, key_pgrad)
    value_wgrad = across(first_in, value_pgrad)
    gate_wgrad = across(first_in, gate_pgrad)
    alpha_wgrad = across(first_in, alpha_pgrad)
    beta_wgrad = across(first_in, beta_pgrad)
    first_part = (
        against(query_pgrad, query_full)
        + against(key_pgrad, key_full)
        + against(value_pgrad, value_full)
    )
    first_part = (
        first_part
        + against(gate_pgrad, gate_full)
        + against(alpha_pgrad, alpha_full)
        + against(beta_pgrad, beta_full)
    )
    first_grad = lax.psum(first_part.astype(jnp.bfloat16), "head").astype(jnp.float32)
    first_weighted = first_grad * mixer_gain
    mixer_gain_part = jnp.sum(first_grad * first_norm, axis=0)
    tokens_grad = middle_grad + first_scale * (
        first_weighted - first_norm * jnp.mean(first_weighted * first_norm, axis=-1, keepdims=True)
    )
    summed = (
        lax.psum_scatter(
            query_wgrad.astype(jnp.bfloat16), "seq", scatter_dimension=0, tiled=True
        ).astype(jnp.float32),
        lax.psum_scatter(
            key_wgrad.astype(jnp.bfloat16), "seq", scatter_dimension=0, tiled=True
        ).astype(jnp.float32),
        lax.psum_scatter(
            value_wgrad.astype(jnp.bfloat16), "seq", scatter_dimension=0, tiled=True
        ).astype(jnp.float32),
        lax.psum_scatter(
            gate_wgrad.astype(jnp.bfloat16), "seq", scatter_dimension=0, tiled=True
        ).astype(jnp.float32),
        lax.psum_scatter(
            alpha_wgrad.astype(jnp.bfloat16), "seq", scatter_dimension=0, tiled=True
        ).astype(jnp.float32),
        lax.psum_scatter(
            beta_wgrad.astype(jnp.bfloat16), "seq", scatter_dimension=0, tiled=True
        ).astype(jnp.float32),
        lax.psum_scatter(
            output_wgrad.astype(jnp.bfloat16), "seq", scatter_dimension=1, tiled=True
        ).astype(jnp.float32),
        lax.psum_scatter(
            widen_wgrad.astype(jnp.bfloat16), "seq", scatter_dimension=0, tiled=True
        ).astype(jnp.float32),
        lax.psum_scatter(
            lift_wgrad.astype(jnp.bfloat16), "seq", scatter_dimension=0, tiled=True
        ).astype(jnp.float32),
        lax.psum_scatter(
            narrow_wgrad.astype(jnp.bfloat16), "seq", scatter_dimension=1, tiled=True
        ).astype(jnp.float32),
    )
    smalls = (
        lax.psum(mixer_gain_part.astype(jnp.bfloat16), "seq").astype(jnp.float32),
        lax.psum(query_taps_part.astype(jnp.bfloat16), "seq").astype(jnp.float32),
        lax.psum(key_taps_part.astype(jnp.bfloat16), "seq").astype(jnp.float32),
        lax.psum(value_taps_part.astype(jnp.bfloat16), "seq").astype(jnp.float32),
        lax.psum(decay_log_part.astype(jnp.bfloat16), "seq").astype(jnp.float32),
        lax.psum(decay_bias_part.astype(jnp.bfloat16), "seq").astype(jnp.float32),
        lax.psum(ffn_gain_part.astype(jnp.bfloat16), "seq").astype(jnp.float32),
    )
    head_gain_grad = lax.psum(head_gain_part, ("seq", "head"))
    return (
        result,
        tokens_grad,
        smalls[0],
        summed[0],
        summed[1],
        summed[2],
        summed[3],
        summed[4],
        summed[5],
        smalls[4],
        smalls[5],
        smalls[1],
        smalls[2],
        smalls[3],
        head_gain_grad,
        summed[6],
        smalls[6],
        summed[7],
        summed[8],
        summed[9],
    )


def solution(mesh):
    in_specs = (
        P("seq", None),
        P(),
        P(),
        P("seq", "head"),
        P("seq", "head"),
        P("seq", "head"),
        P("seq", "head"),
        P("seq", "head"),
        P("seq", "head"),
        P("head"),
        P("head"),
        P(None, "head"),
        P(None, "head"),
        P(None, "head"),
        P(),
        P("head", "seq"),
        P(),
        P("seq", "head"),
        P("seq", "head"),
        P("head", "seq"),
        P("seq", None),
    )
    out_specs = (
        P("seq", None),
        P("seq", None),
        P(),
        P("seq", "head"),
        P("seq", "head"),
        P("seq", "head"),
        P("seq", "head"),
        P("seq", "head"),
        P("seq", "head"),
        P("head"),
        P("head"),
        P(None, "head"),
        P(None, "head"),
        P(None, "head"),
        P(),
        P("head", "seq"),
        P(),
        P("seq", "head"),
        P("seq", "head"),
        P("head", "seq"),
    )
    return jax.shard_map(shards, mesh=mesh, in_specs=in_specs, out_specs=out_specs, check_vma=False)
```

profile of v0, /device:TPU:0, one launch (start us, length us, event | category | flops | bytes accessed | tf_op | source)
XLA Modules:
  0.0 2926.1 jit_solution(6560978639358687020)
XLA Ops:
  18.8 10.4 all_gather.64
  34.2 8.9 all_gather.66
  54.9 16.7 all-gather.21.cloned.1.call-done
  99.4 11.4 all-gather.19.cloned.1.call-done
  110.8 7.9 convolution_convert_fusion.12
  134.7 257.5 %while.87 = (s32[]{:T(128)}, f32[4,128,384]{2,1,0:T(8,128)S(1)}, s32[]{:T(128)}, f32[16,4,64,384]{3,2,0,1:T(8,128)}, f32[16,4,64]{2,1,0:T(4,128)S(1)}, /*index=5...) while((s32[]{:T(128)}, f32[4,128,384]{2,1,0:T(8,128)S(1)}, ...), condition=%wide.region_7.8_spmd, body=%wide.region_5.7_spmd.sunk | while | flops 781366528 | bytes 9467852 | solution.py:115
  394.9 10.1 fusion.293
  415.1 6.8 all-gather.33.cloned.1.call-done
  421.8 39.1 %all-gather.35.cloned.1.call-done = f32[32,128,256]{2,1,0:T(8,128)} async-done(((f32[4,128,256]{2,1,0:T(8,128)}), f32[32,128,256]{2,1,0:T(8,128)}) %all-gather.35.cloned.1.call-update) | async-done | bytes 4194320 | tf_op jit(solution)/shard_map/all_gather | solution.py:22
  463.6 255.6 %while.90 = (s32[]{:T(128)}, f32[4,128,256]{2,1,0:T(8,128)S(1)}, s32[]{:T(128)}, f32[16,4,64,256]{3,2,0,1:T(8,128)}, f32[16,4,128,256]{3,2,1,0:T(8,128)}, /*inde...) while((s32[]{:T(128)}, f32[4,128,256]{2,1,0:T(8,128)S(1)}, ...), condition=%wide.region_12.13_spmd.clone, body=%wide.region_10.12_spmd.clone.sunk | while | flops 579745024 | bytes 8288744 | solution.py:115
  728.2 9.4 convolution_convert_fusion.7
  744.0 161.3 %all-reduce.37.cloned.1.call-done = bf16[1024,2048]{1,0:T(8,128)(2,1)} async-done(((bf16[1024,2048]{1,0:T(8,128)(2,1)}), bf16[1024,2048]{1,0:T(8,128)(2,1)}) %all-reduce.37.cloned.1.call-update) | async-done | bytes 4194320 | tf_op jit(solution)/shard_map/psum | solution.py:345
  915.3 35.0 %all-gather.27.cloned.1.call-done = bf16[2048,1408]{1,0:T(8,128)(2,1)} async-done(((bf16[256,1408]{1,0:T(8,128)(2,1)}), bf16[2048,1408]{1,0:T(8,128)(2,1)}) %all-gather.27.cloned.1.call-update) | async-done | bytes 5767184 | tf_op jit(solution)/shard_map/all_gather | solution.py:254
  950.3 11.8 fusion.294
  962.1 34.0 %all-gather.29.cloned.1.call-done = bf16[2048,1408]{1,0:T(8,128)(2,1)} async-done(((bf16[256,1408]{1,0:T(8,128)(2,1)}), bf16[2048,1408]{1,0:T(8,128)(2,1)}) %all-gather.29.cloned.1.call-update) | async-done | bytes 5767184 | tf_op jit(solution)/shard_map/all_gather | solution.py:255
  996.1 11.7 fusion.295
  1007.8 35.3 %all-gather.31.cloned.1.call-done = bf16[1408,2048]{1,0:T(8,128)(2,1)} async-done(((bf16[1408,256]{1,0:T(8,128)(2,1)}), bf16[1408,2048]{1,0:T(8,128)(2,1)}) %all-gather.31.cloned.1.call-update) | async-done | bytes 5767184 | tf_op jit(solution)/shard_map/all_gather | solution.py:256
  1043.1 15.6 multiply_convert_fusion.1
  1058.7 10.9 fusion.296
  1069.6 8.5 add_convert_fusion.1
  1079.0 154.2 %all-reduce.39.cloned.1.call-done = bf16[1024,2048]{1,0:T(8,128)(2,1)} async-done(((bf16[1024,2048]{1,0:T(8,128)(2,1)}), bf16[1024,2048]{1,0:T(8,128)(2,1)}) %all-reduce.39.cloned.1.call-update) | async-done | bytes 4194320 | tf_op jit(solution)/shard_map/psum | solution.py:393
  1233.2 8.3 fusion.170
  1241.6 10.8 fusion.202
  1257.8 7.9 multiply_reduce_fusion.6
  1276.9 27.1 all-gather.39.cloned.1.call-done
  1304.1 12.7 while.91
  1323.7 727.3 %while.89 = (s32[]{:T(128)}, f32[4,128,256]{2,1,0:T(8,128)S(1)}, f32[16,4,64,128]{3,2,0,1:T(8,128)}, f32[16,4,64,128]{3,2,0,1:T(8,128)}, f32[16,4,64,256]{3,2,0,...) while((s32[]{:T(128)}, f32[4,128,256]{2,1,0:T(8,128)S(1)}, ...), condition=%wide.region_34.35_spmd, body=%wide.region_22.34_spmd.sunk | while | flops 1589412864 | bytes 28056704 | solution.py:115
  2063.5 11.0 convolution_convert_fusion.2
  2076.2 10.8 convolution_convert_fusion.1
  2088.9 10.8 convolution_convert_fusion
  2101.3 13.1 convolution_convert_fusion.4
  2118.8 9.4 convolution_convert_fusion.5
  2162.9 11.0 multiply_reduce_fusion.10
  2180.6 8.0 pad_add_fusion
  2188.6 8.4 convolution_convert_fusion.6
  2197.1 11.0 convolution_convert_fusion.3
  2208.1 6.9 fusion.297
  2235.7 19.5 add_convert_fusion
  2255.9 43.7 %psum.94 = f32[256]{0:T(256)} all-reduce(f32[256]{0:T(256)S(1)} %copy-done.147), channel_id=1, replica_groups=mesh['seq'=8,'head'=4] {'seq','head'}, use_global_device_ids=true, to_apply=%region_67.68 | all-reduce | flops 256 | bytes 2048 | tf_op jit(solution)/shard_map/psum | solution.py:511
  2307.4 12.8 reduce-scatter.29.cloned.1.call-done
  2322.5 52.6 %reduce-scatter.23.cloned.1.call-done = bf16[1024,256]{1,0:T(8,128)(2,1)} async-done(((bf16[1024,2048]{1,0:T(8,128)(2,1)}), bf16[1024,256]{1,0:T(8,128)(2,1)}) %reduce-scatter.23.cloned.1.call-update) | async-done | bytes 524304 | tf_op jit(solution)/shard_map/reduce_scatter | solution.py:489
  2377.2 52.6 %reduce-scatter.21.cloned.1.call-done = bf16[256,1024]{1,0:T(8,128)(2,1)} async-done(((bf16[2048,1024]{1,0:T(8,128)(2,1)}), bf16[256,1024]{1,0:T(8,128)(2,1)}) %reduce-scatter.21.cloned.1.call-update) | async-done | bytes 524304 | tf_op jit(solution)/shard_map/reduce_scatter | solution.py:480
  2432.0 42.8 %reduce-scatter.17.cloned.1.call-done = bf16[256,512]{1,0:T(8,128)(2,1)} async-done(((bf16[2048,512]{1,0:T(8,128)(2,1)}), bf16[256,512]{1,0:T(8,128)(2,1)}) %reduce-scatter.17.cloned.1.call-update) | async-done | bytes 262160 | tf_op jit(solution)/shard_map/reduce_scatter | solution.py:474
  2476.6 42.8 %reduce-scatter.15.cloned.1.call-done = bf16[256,512]{1,0:T(8,128)(2,1)} async-done(((bf16[2048,512]{1,0:T(8,128)(2,1)}), bf16[256,512]{1,0:T(8,128)(2,1)}) %reduce-scatter.15.cloned.1.call-update) | async-done | bytes 262160 | tf_op jit(solution)/shard_map/reduce_scatter | solution.py:471
  2521.1 53.1 %reduce-scatter.19.cloned.1.call-done = bf16[256,1024]{1,0:T(8,128)(2,1)} async-done(((bf16[2048,1024]{1,0:T(8,128)(2,1)}), bf16[256,1024]{1,0:T(8,128)(2,1)}) %reduce-scatter.19.cloned.1.call-update) | async-done | bytes 524304 | tf_op jit(solution)/shard_map/reduce_scatter | solution.py:477
  2576.4 292.6 %all-reduce.41.cloned.1.call-done = (bf16[1024,2048]{1,0:T(8,128)(2,1)}, bf16[1024,2048]{1,0:T(8,128)(2,1)}) async-done(((bf16[1024,2048]{1,0:T(8,128)(2,1)}, bf16[1024,2048]{1,0:T(8,128)(2,1)}), (bf16[1024,2048]{1,0:T(8,128)(2,1)}, bf16[1024,2048]{1,0:T(8,128)(2,1)})) %all-reduce.41.cloned.1.call-update) | async-done | bytes 8388624 | tf_op jit(solution)/shard_map/psum | solution.py:357
  2874.0 24.0 all-reduce.31
  2902.1 17.1 fusion.166
  (3869 shorter events, 1439.6 us)
Async XLA Ops:
  7.2 40.2 %all-gather.17.cloned.1.call-start = ((), (), s32[]{:S(2)}) async-start(), calls=%async_computation.10 | async-start | bytes 2359296 | tf_op jit(solution)/shard_map/all_gather | solution.py:248
  9.1 62.4 %all-gather.21.cloned.1.call-start = ((), (), s32[]{:S(2)}) async-start(), calls=%async_computation.12 | async-start | bytes 2359296 | tf_op jit(solution)/shard_map/all_gather | solution.py:247
  11.1 99.7 %all-gather.19.cloned.1.call-start = ((), (), s32[]{:S(2)}) async-start(), calls=%async_computation.11 | async-start | bytes 4718592 | tf_op jit(solution)/shard_map/all_gather | solution.py:249
  13.2 381.7 %all-gather.23.cloned.1.call-start = ((), (), s32[]{:S(2)}) async-start(), calls=%async_computation.13 | async-start | bytes 4718592 | tf_op jit(solution)/shard_map/all_gather | solution.py:250
  14.2 407.7 %all-gather.33.cloned.1.call-start = ((), (), s32[]{:S(2)}) async-start(), calls=%async_computation.28 | async-start | bytes 2359296 | tf_op jit(solution)/shard_map/all_gather | solution.py:22
  14.6 111.1 %copy-start.67 = (f32[1024]{0:T(1024)}, f32[1024]{0:T(1024)S(1)}, u32[]{:S(2)}) copy-start(f32[1024]{0:T(1024)S(1)} %get-tuple-element.1225) | copy-start | bytes 12292
  14.6 111.1 %copy-start.69 = (f32[1024]{0:T(1024)}, f32[1024]{0:T(1024)S(1)}, u32[]{:S(2)}) copy-start(f32[1024]{0:T(1024)S(1)} %get-tuple-element.1226) | copy-start | bytes 12292
  14.6 111.1 %copy-start.71 = (f32[1024]{0:T(1024)}, f32[1024]{0:T(1024)S(1)}, u32[]{:S(2)}) copy-start(f32[1024]{0:T(1024)S(1)} %get-tuple-element.1227) | copy-start | bytes 12292
  18.6 61.5 %copy-start.123 = (f32[1,512]{1,0:T(1,128)}, f32[1,512]{1,0:T(1,128)S(1)}, u32[]{:S(2)}) copy-start(f32[1,512]{1,0:T(1,128)S(1)} %get-tuple-element.1221) | copy-start | bytes 6148
  18.6 61.5 %copy-start.125 = (f32[1,512]{1,0:T(1,128)}, f32[1,512]{1,0:T(1,128)S(1)}, u32[]{:S(2)}) copy-start(f32[1,512]{1,0:T(1,128)S(1)} %get-tuple-element.1222) | copy-start | bytes 6148
  18.6 61.5 %copy-start.127 = (f32[1,512]{1,0:T(1,128)}, f32[1,512]{1,0:T(1,128)S(1)}, u32[]{:S(2)}) copy-start(f32[1,512]{1,0:T(1,128)S(1)} %get-tuple-element.1223) | copy-start | bytes 6148
  18.6 61.5 %copy-start.129 = (f32[1,512]{1,0:T(1,128)}, f32[1,512]{1,0:T(1,128)S(1)}, u32[]{:S(2)}) copy-start(f32[1,512]{1,0:T(1,128)S(1)} %get-tuple-element.1224) | copy-start | bytes 6148
  18.6 61.5 %copy-start.131 = (f32[1,512]{1,0:T(1,128)}, f32[1,512]{1,0:T(1,128)S(1)}, u32[]{:S(2)}) copy-start(f32[1,512]{1,0:T(1,128)S(1)} %get-tuple-element.1217) | copy-start | bytes 6148
  18.7 107.0 %copy-start.113 = (f32[1,1024]{1,0:T(1,128)}, f32[1,1024]{1,0:T(1,128)S(1)}, u32[]{:S(2)}) copy-start(f32[1,1024]{1,0:T(1,128)S(1)} %get-tuple-element.1206) | copy-start | bytes 12292
  18.7 107.0 %copy-start.115 = (f32[1,1024]{1,0:T(1,128)}, f32[1,1024]{1,0:T(1,128)S(1)}, u32[]{:S(2)}) copy-start(f32[1,1024]{1,0:T(1,128)S(1)} %get-tuple-element.1207) | copy-start | bytes 12292
  18.7 107.0 %copy-start.117 = (f32[1,1024]{1,0:T(1,128)}, f32[1,1024]{1,0:T(1,128)S(1)}, u32[]{:S(2)}) copy-start(f32[1,1024]{1,0:T(1,128)S(1)} %get-tuple-element.1208) | copy-start | bytes 12292
  18.8 107.0 %copy-start.119 = (f32[1,1024]{1,0:T(1,128)}, f32[1,1024]{1,0:T(1,128)S(1)}, u32[]{:S(2)}) copy-start(f32[1,1024]{1,0:T(1,128)S(1)} %get-tuple-element.1209) | copy-start | bytes 12292
  52.7 26.5 collective-permute-start
  76.8 3.0 collective-permute-start.2
  118.8 6.3 collective-permute-start.1
  134.7 259.3 %copy-start.62 = (f32[1024,256]{1,0:T(8,128)S(1)}, f32[1024,256]{1,0:T(8,128)}, u32[]{:S(2)}) copy-start(f32[1024,256]{1,0:T(8,128)} %param.46) | copy-start | bytes 3145732
  393.0 67.9 %all-gather.35.cloned.1.call-start = ((), (), s32[]{:S(2)}) async-start(), calls=%async_computation.29 | async-start | bytes 4718592 | tf_op jit(solution)/shard_map/all_gather | solution.py:22
  393.9 334.3 %all-gather.25.cloned.1.call-start = ((), (), s32[]{:S(2)}) async-start(), calls=%async_computation.14 | async-start | bytes 4718592 | tf_op jit(solution)/shard_map/all_gather | solution.py:253
  394.8 510.5 %all-reduce.37.cloned.1.call-start = ((), (), s32[]{:S(2)}) async-start(), calls=%async_computation.15 | async-start | bytes 8388608 | tf_op jit(solution)/shard_map/psum | solution.py:345
  737.7 212.6 %all-gather.27.cloned.1.call-start = ((), (), s32[]{:S(2)}) async-start(), calls=%async_computation.16 | async-start | bytes 6488064 | tf_op jit(solution)/shard_map/all_gather | solution.py:254
  740.0 256.1 %all-gather.29.cloned.1.call-start = ((), (), s32[]{:S(2)}) async-start(), calls=%async_computation.17 | async-start | bytes 6488064 | tf_op jit(solution)/shard_map/all_gather | solution.py:255
  742.5 300.6 %all-gather.31.cloned.1.call-start = ((), (), s32[]{:S(2)}) async-start(), calls=%async_computation.18 | async-start | bytes 6488064 | tf_op jit(solution)/shard_map/all_gather | solution.py:256
  743.5 166.8 %copy-start.107 = (f32[2048]{0:T(1024)S(1)}, f32[2048]{0:T(1024)}, u32[]{:S(2)}) copy-start(f32[2048]{0:T(1024)} %param.47) | copy-start | bytes 24580
  743.5 489.7 %all-reduce.39.cloned.1.call-start = ((), (), s32[]{:S(2)}) async-start(), calls=%async_computation.19 | async-start | bytes 8388608 | tf_op jit(solution)/shard_map/psum | solution.py:393
  911.2 330.3 %copy-start.109 = (f32[1024]{0:T(1024)}, f32[1024]{0:T(1024)S(1)}, u32[]{:S(2)}) copy-start(f32[1024]{0:T(1024)S(1)} %add_rsqrt_fusion.2) | copy-start | bytes 12292
  1078.1 198.8 %all-gather.37.cloned.1.call-start = ((), (), s32[]{:S(2)}) async-start(), calls=%async_computation.30 | async-start | bytes 1179648 | tf_op jit(solution)/shard_map/all_gather | solution.py:36
  1079.0 225.1 %all-gather.39.cloned.1.call-start = ((), (), s32[]{:S(2)}) async-start(), calls=%async_computation.31 | async-start | bytes 2359296 | tf_op jit(solution)/shard_map/all_gather | solution.py:36
  1276.9 1022.8 %reduce-scatter.31.cloned.1.call-start = ((), (), s32[]{:S(2)}) async-start(), calls=%async_computation.32 | async-start | bytes 589824
  2059.4 241.8 %reduce-scatter.33.cloned.1.call-start = ((), (), s32[]{:S(2)}) async-start(), calls=%async_computation.33 | async-start | bytes 589824
  2063.4 239.4 %reduce-scatter.25.cloned.1.call-start = ((), (), s32[]{:S(2)}) async-start(), calls=%async_computation.25 | async-start | bytes 6488064 | tf_op jit(solution)/shard_map/reduce_scatter | solution.py:492
  2074.5 230.7 %reduce-scatter.27.cloned.1.call-start = ((), (), s32[]{:S(2)}) async-start(), calls=%async_computation.26 | async-start | bytes 6488064 | tf_op jit(solution)/shard_map/reduce_scatter | solution.py:495
  2087.1 233.1 %reduce-scatter.29.cloned.1.call-start = ((), (), s32[]{:S(2)}) async-start(), calls=%async_computation.27 | async-start | bytes 6488064 | tf_op jit(solution)/shard_map/reduce_scatter | solution.py:498
  2099.7 275.4 %reduce-scatter.23.cloned.1.call-start = ((), (), s32[]{:S(2)}) async-start(), calls=%async_computation.24 | async-start | bytes 4718592 | tf_op jit(solution)/shard_map/reduce_scatter | solution.py:489
  2114.4 315.4 %reduce-scatter.21.cloned.1.call-start = ((), (), s32[]{:S(2)}) async-start(), calls=%async_computation.23 | async-start | bytes 4718592 | tf_op jit(solution)/shard_map/reduce_scatter | solution.py:480
  2128.3 346.5 %reduce-scatter.17.cloned.1.call-start = ((), (), s32[]{:S(2)}) async-start(), calls=%async_computation.21 | async-start | bytes 2359296 | tf_op jit(solution)/shard_map/reduce_scatter | solution.py:474
  2142.2 3.5 collective-permute-start.4
  2150.2 369.1 %reduce-scatter.15.cloned.1.call-start = ((), (), s32[]{:S(2)}) async-start(), calls=%async_computation.20 | async-start | bytes 2359296 | tf_op jit(solution)/shard_map/reduce_scatter | solution.py:471
  2151.2 6.1 collective-permute-start.3
  2162.8 411.4 %reduce-scatter.19.cloned.1.call-start = ((), (), s32[]{:S(2)}) async-start(), calls=%async_computation.22 | async-start | bytes 4718592 | tf_op jit(solution)/shard_map/reduce_scatter | solution.py:477
  2178.8 9.8 collective-permute-start.5
  2197.0 672.0 %all-reduce.41.cloned.1.call-start = ((), (), s32[]{:S(2)}) async-start(), calls=%async_computation.34 | async-start | bytes 16777216 | tf_op jit(solution)/shard_map/psum | solution.py:357
  2307.4 561.6 %copy-start.106 = (f32[2048]{0:T(1024)S(1)}, f32[2048]{0:T(1024)}, u32[]{:S(2)}) copy-start(f32[2048]{0:T(1024)} %param.33) | copy-start | bytes 24580
  2307.4 561.6 %copy-start.112 = (f32[1024]{0:T(1024)S(1)}, f32[1024]{0:T(1024)}, u32[]{:S(2)}) copy-start(f32[1024]{0:T(1024)} %copy-done.111) | copy-start | bytes 12292
  (722 other events, 5376.0 us)
Sparse Core Ops, SparseCore 0:
  10.5 30.6 all-gather.16
  43.7 27.8 all-gather.20
  74.1 36.7 all-gather.18
  113.1 36.7 all-gather.22
  393.1 28.6 all-gather.32
  424.2 36.7 all-gather.34
  463.4 37.5 all-gather.24
  737.8 167.4 all-reduce.36
  907.9 42.3 all-gather.26
  952.8 43.3 all-gather.28
  998.7 44.3 all-gather.30
  1078.2 154.9 all-reduce.38
  1235.7 22.4 all-gather.36
  1277.0 27.0 all-gather.38
  2059.5 34.0 reduce-scatter.30
  2097.5 34.1 reduce-scatter.32
  2135.0 59.1 reduce-scatter.24
  2197.9 59.0 reduce-scatter.26
  2260.4 59.7 reduce-scatter.28
  2323.8 51.3 reduce-scatter.22
  2378.5 51.3 reduce-scatter.20
  2433.5 41.2 reduce-scatter.16
  2478.0 41.2 reduce-scatter.14
  2522.9 51.3 reduce-scatter.18
  2577.4 291.5 all-reduce.40
where the time goes:
time: 2940 us; the launch traced here: 2930 us
  matrix products  1080 us (37%)
  waiting for transfers between devices  1070 us (36%)
  local copies, waits for them, and re-layouts  305 us (10%)
  other arithmetic  291 us (10%)
  blocking collectives  87 us (3%)
  loops' own time  62.7 us (2%)
    psum x1, waiting for transfers between devices, shards(): lax.psum(product(hidden, narrow_full).astype(jnp.bfloat16), 'head')  293 us
    psum x1, waiting for transfers between devices, shards(): lax.psum(product(mix_out, output_full).astype(jnp.bfloat16), 'head')  161 us
    psum x1, waiting for transfers between devices, shards(): lax.psum((against(gate_grad, widen_full) + against(lift_grad, lift_full))...  154 us
    dot_general x400, matrix products, group_step(): jnp.einsum('hij,hjk->hik', inverse, power_term, precision=highest)  153 us
    dot_general x400, matrix products, group_step(): jnp.einsum('hij,hjk->hik', power_term, power_term, precision=highest)  127 us
    dot_general x10, matrix products, against(): lax.dot_general(left, right, (((1,), (1,)), ((), ())), preferred_element_...  92.7 us
    dot_general x80, matrix products, group_step(): jnp.einsum('hid,hdv->hiv', key_rows, state_now, precision=highest)  92.2 us
    dot_general x80, matrix products, group_step(): jnp.einsum('hid,hdv->hiv', queries, state_now, precision=highest)  87.4 us
  transfers between devices with their start and end apart: 31, of which 19 were waited for; matrix products, arithmetic and copies ran while one was open for 29% of the time, Pallas kernels for 0%

commit v1 on v0

v1 whole, which is shorter than its diff:
```python
from functools import partial

import jax
import jax.numpy as jnp
from jax import lax
from jax.experimental import pallas as pl
from jax.experimental.pallas import tpu as pltpu
from jax.sharding import PartitionSpec as P

BLOCK = 128
LANES = 128
low = jnp.bfloat16
full = jnp.float32
MIB = 1 << 20


def mm(a, b):
    return jnp.dot(a.astype(low), b.astype(low), preferred_element_type=full)


def mm_nt(a, b):
    return lax.dot_general(
        a.astype(low), b.astype(low), (((1,), (1,)), ((), ())), preferred_element_type=full
    )


def mm_tn(a, b):
    return lax.dot_general(
        a.astype(low), b.astype(low), (((0,), (0,)), ((), ())), preferred_element_type=full
    )


def exact(a, b):
    return jnp.dot(a, b, precision=lax.Precision.HIGHEST, preferred_element_type=full)


def sigmoid(t):
    return 1.0 / (1.0 + jnp.exp(-t))


def softplus(t):
    return jnp.maximum(t, 0.0) + jnp.log(1.0 + jnp.exp(-jnp.abs(t)))


def iotas(size):
    return (
        lax.broadcasted_iota(jnp.int32, (size, size), 0),
        lax.broadcasted_iota(jnp.int32, (size, size), 1),
    )


def conv_sum(ext, taps, meta, first, width, rows):
    total = taps[3:4, first : first + width] * ext[8 : 8 + rows, first : first + width]
    for lag in (1, 2, 3):
        total += (
            taps[3 - lag : 4 - lag, first : first + width]
            * meta[:, lag : lag + 1]
            * ext[8 - lag : 8 - lag + rows, first : first + width]
        )
    return total


def gates(ab, params, heads):
    log_decay = params[0:1, :] * softplus(ab + params[1:2, :])
    beta = sigmoid(ab)
    return log_decay, beta


def decay_parts(cum, cum_t, h, same_low, strict_low, meta):
    size = cum.shape[0]
    col = cum[:, h : h + 1]
    row = cum_t[h : h + 1, :]
    lower = jnp.where(same_low, jnp.exp(jnp.minimum(col - row, 0.0)), 0.0)
    strict = jnp.where(strict_low, lower, 0.0)
    last = cum[size - 1 : size, h : h + 1]
    from_start = jnp.exp(col) * meta[:, 4:5]
    to_end = jnp.exp(last - col) * meta[:, 5:6]
    carried = jnp.exp(last) * meta[size - 1 : size, 4:5]
    return lower, strict, from_start, to_end, carried


def unit_lower_inverse(strict, rows, cols):
    size = strict.shape[0]
    power = jnp.where((rows >> 3) == (cols >> 3), -strict, 0.0)
    inverse = jnp.where(rows == cols, 1.0, power)
    power = mm(power, power)
    inverse = inverse + mm(inverse, power)
    power = mm(power, power)
    inverse = inverse + mm(inverse, power)
    shift = 3
    while (1 << shift) < size:
        off = jnp.where(
            ((rows >> (shift + 1)) == (cols >> (shift + 1))) & ((rows >> shift) != (cols >> shift)),
            strict,
            0.0,
        )
        inverse = inverse - mm(inverse, mm(off, inverse))
        shift += 1
    return inverse


def inverses(stricts, rows, cols):
    size = stricts[0].shape[0]
    near = (rows >> 3) == (cols >> 3)
    powers = [jnp.where(near, -a, 0.0) for a in stricts]
    result = [jnp.where(rows == cols, 1.0, p) for p in powers]
    for _ in range(2):
        powers = [mm(p, p) for p in powers]
        result = [t + mm(t, p) for t, p in zip(result, powers)]
    shift = 3
    while (1 << shift) < size:
        pick = ((rows >> (shift + 1)) == (cols >> (shift + 1))) & (
            (rows >> shift) != (cols >> shift)
        )
        offs = [mm(jnp.where(pick, a, 0.0), t) for a, t in zip(stricts, result)]
        result = [t - mm(t, o) for t, o in zip(result, offs)]
        shift += 1
    return result


def masks(meta, segrow):
    size = meta.shape[0]
    rows, cols = iotas(size)
    same = meta[:, 0:1] == segrow[0:1, :]
    return rows, cols, same & (rows >= cols), same & (rows > cols)


def unit(post):
    return lax.rsqrt(jnp.sum(post * post, axis=-1, keepdims=True) + 1e-06)


def forward_kernel(
    heads, key, value,
    pre_ref, ab_ref, meta_ref, segrow_ref, edge_ref, taps_ref, params_ref,
    out_ref, through_ref, states_ref, inverse_ref, end_ref,
    ext, state,
):
    step = pl.program_id(0)
    size = pre_ref.shape[0]
    wide = value + key
    kfirst, vfirst = heads * key, 2 * heads * key

    @pl.when(step == 0)
    def _():
        ext[0:8, :] = edge_ref[...].astype(full)
        rows, cols = iotas(key)
        eye = (rows == cols).astype(full)
        for h in range(heads):
            state[h, :, :value] = jnp.zeros((key, value), full)
            state[h, :, value:] = eye

    @pl.when(step > 0)
    def _():
        ext[0:8, :] = ext[size : size + 8, :]

    ext[8:, :] = pre_ref[...].astype(full)
    meta = meta_ref[...]
    log_decay, beta = gates(ab_ref[...], params_ref, heads)
    rows, cols, same_low, strict_low = masks(meta, segrow_ref)
    cum = exact((rows >= cols).astype(full), log_decay)
    cum_t = cum.T
    qs, ks, vs, lowers, stricts, fs, es, cs = [], [], [], [], [], [], [], []
    for h in range(heads):
        u = conv_sum(ext, taps_ref, meta, h * key, key, size)
        post = u * sigmoid(u)
        q = (post * unit(post)).astype(low)
        u = conv_sum(ext, taps_ref, meta, kfirst + h * key, key, size)
        post = u * sigmoid(u)
        k = (post * unit(post)).astype(low)
        u = conv_sum(ext, taps_ref, meta, vfirst + h * value, value, size)
        v = u * sigmoid(u)
        lower, strict, f, e, c = decay_parts(cum, cum_t, h, same_low, strict_low, meta)
        bcol = beta[:, heads + h : heads + h + 1]
        gram = mm_nt(jnp.concatenate([k, q], axis=0), k)
        qs.append(q), ks.append(k), vs.append(v), fs.append(f), es.append(e), cs.append(c)
        stricts.append(bcol * strict * gram[:size])
        lowers.append(lower * gram[size:])
    ts = inverses(stricts, rows, cols)
    for h in range(heads):
        bcol = beta[:, heads + h : heads + h + 1]
        s = state[h]
        states_ref[0, h] = s.astype(low)
        t = ts[h].astype(low)
        inverse_ref[0, h] = t
        ks_s = mm(ks[h], s)
        fb = fs[h] * bcol
        target = jnp.concatenate(
            [bcol * vs[h] - fb * ks_s[:, :value], -fb * ks_s[:, value:]], axis=1
        )
        delta = mm(t, target).astype(low)
        left = jnp.concatenate([(fs[h] * qs[h].astype(full)).astype(low), lowers[h].astype(low)], axis=1)
        out = mm(left, jnp.concatenate([s.astype(low), delta], axis=0))
        out_ref[:, h * value : (h + 1) * value] = out[:, :value]
        through_ref[:, h * key : (h + 1) * key] = out[:, value:].astype(low)
        ke = es[h] * ks[h].astype(full)
        s = cs[h] * s + mm_tn(ke, delta)
        state[h] = s
        end_ref[h] = s.astype(low)


def forward_chain(pre, ab, meta, segrow, edge, taps, params, heads, key, value):
    length = pre.shape[0]
    blocks = length // BLOCK
    width = pre.shape[1]
    wide = value + key
    return pl.pallas_call(
        partial(forward_kernel, heads, key, value),
        grid=(blocks,),
        in_specs=[
            pl.BlockSpec((BLOCK, width), lambda n: (n, 0)),
            pl.BlockSpec((BLOCK, LANES), lambda n: (n, 0)),
            pl.BlockSpec((BLOCK, LANES), lambda n: (n, 0)),
            pl.BlockSpec((8, BLOCK), lambda n: (0, n)),
            pl.BlockSpec((8, width), lambda n: (0, 0)),
            pl.BlockSpec(taps.shape, lambda n: (0, 0)),
            pl.BlockSpec((8, LANES), lambda n: (0, 0)),
        ],
        out_specs=[
            pl.BlockSpec((BLOCK, heads * value), lambda n: (n, 0)),
            pl.BlockSpec((BLOCK, heads * key), lambda n: (n, 0)),
            pl.BlockSpec((1, heads, key, wide), lambda n: (n, 0, 0, 0)),
            pl.BlockSpec((1, heads, BLOCK, BLOCK), lambda n: (n, 0, 0, 0)),
            pl.BlockSpec((heads, key, wide), lambda n: (0, 0, 0)),
        ],
        out_shape=[
            jax.ShapeDtypeStruct((length, heads * value), full),
            jax.ShapeDtypeStruct((length, heads * key), low),
            jax.ShapeDtypeStruct((blocks, heads, key, wide), low),
            jax.ShapeDtypeStruct((blocks, heads, BLOCK, BLOCK), low),
            jax.ShapeDtypeStruct((heads, key, wide), low),
        ],
        scratch_shapes=[
            pltpu.VMEM((BLOCK + 8, width), full),
            pltpu.VMEM((heads, key, wide), full),
        ],
        compiler_params=pltpu.CompilerParams(vmem_limit_bytes=48 * MIB),
        name="chain_forward",
    )(pre, ab, meta, segrow, edge, taps, params)


def output_kernel(heads, key, value, place_ref, ends_ref, local_ref, through_ref, gate_ref, gain_ref,
                  y_ref, mixed_ref, state_ref):
    @pl.when(pl.program_id(0) == 0)
    def _():
        state_ref[...] = jnp.zeros_like(state_ref)

        def one(j, carry):
            for h in range(heads):
                part = ends_ref[j, h]
                state_ref[h] = (
                    mm(part[:, value:], state_ref[h]) + part[:, :value].astype(full)
                )
            return carry

        lax.fori_loop(0, place_ref[0], one, 0)

    for h in range(heads):
        cols = slice(h * value, (h + 1) * value)
        o = local_ref[:, cols] + mm(through_ref[:, h * key : (h + 1) * key], state_ref[h])
        mixed_ref[:, cols] = o.astype(mixed_ref.dtype)
        s3 = lax.rsqrt(jnp.mean(o * o, axis=-1, keepdims=True) + 1e-05)
        gz = gate_ref[:, cols]
        y_ref[:, cols] = (o * s3 * gain_ref[0:1, :] * (gz * sigmoid(gz))).astype(low)


def chain_output(place, ends, local, through, gate, gain, heads, key, value, rows=256):
    length, wide = local.shape
    return pl.pallas_call(
        partial(output_kernel, heads, key, value),
        grid=(length // rows,),
        in_specs=[
            pl.BlockSpec(memory_space=pltpu.SMEM),
            pl.BlockSpec(ends.shape, lambda n: (0, 0, 0, 0), pipeline_mode=pl.Buffered(1)),
            pl.BlockSpec((rows, wide), lambda n: (n, 0)),
            pl.BlockSpec((rows, heads * key), lambda n: (n, 0)),
            pl.BlockSpec((rows, wide), lambda n: (n, 0)),
            pl.BlockSpec((1, value), lambda n: (0, 0)),
        ],
        out_specs=[
            pl.BlockSpec((rows, wide), lambda n: (n, 0)),
            pl.BlockSpec((rows, wide), lambda n: (n, 0)),
            pl.BlockSpec((heads, key, value), lambda n: (0, 0, 0)),
        ],
        out_shape=[
            jax.ShapeDtypeStruct((length, wide), low),
            jax.ShapeDtypeStruct((length, wide), full),
            jax.ShapeDtypeStruct((heads, key, value), full),
        ],
        compiler_params=pltpu.CompilerParams(vmem_limit_bytes=48 * MIB),
        name="chain_output",
    )(place, ends, local, through, gate, gain)


def gate_back_kernel(heads, key, value, dy_ref, mixed_ref, gate_ref, gain_ref, through_ref,
                     dgz_ref, do_ref, gain_grad_ref, adjoint_ref):
    @pl.when(pl.program_id(0) == 0)
    def _():
        gain_grad_ref[...] = jnp.zeros_like(gain_grad_ref)
        adjoint_ref[...] = jnp.zeros_like(adjoint_ref)

    rows = dy_ref.shape[0]
    gain = gain_ref[0:1, :]
    for h in range(heads):
        cols = slice(h * value, (h + 1) * value)
        o = mixed_ref[:, cols].astype(full)
        s3 = lax.rsqrt(jnp.mean(o * o, axis=-1, keepdims=True) + 1e-05)
        n3 = o * s3
        gz = gate_ref[:, cols]
        sig = sigmoid(gz)
        sg = gz * sig
        dy = dy_ref[:, cols]
        dyn = dy * n3
        part = dyn * sg
        gain_grad_ref[...] += jnp.sum(part.reshape(rows // 8, 8, value), axis=0)
        dgz_ref[:, cols] = (dyn * gain * (sig * (1.0 + gz * (1.0 - sig)))).astype(low)
        dn3 = dy * gain * sg
        do = s3 * (dn3 - n3 * jnp.mean(dn3 * n3, axis=-1, keepdims=True))
        do = do.astype(low)
        do_ref[:, cols] = do
        adjoint_ref[h] += mm_tn(through_ref[:, h * key : (h + 1) * key], do)


def gate_back(dy, mixed, gate, gain, through, heads, key, value, rows=256):
    length, wide = dy.shape
    return pl.pallas_call(
        partial(gate_back_kernel, heads, key, value),
        grid=(length // rows,),
        in_specs=[
            pl.BlockSpec((rows, wide), lambda n: (n, 0)),
            pl.BlockSpec((rows, wide), lambda n: (n, 0)),
            pl.BlockSpec((rows, wide), lambda n: (n, 0)),
            pl.BlockSpec((1, value), lambda n: (0, 0)),
            pl.BlockSpec((rows, heads * key), lambda n: (n, 0)),
        ],
        out_specs=[
            pl.BlockSpec((rows, wide), lambda n: (n, 0)),
            pl.BlockSpec((rows, wide), lambda n: (n, 0)),
            pl.BlockSpec((8, value), lambda n: (0, 0)),
            pl.BlockSpec((heads, key, value), lambda n: (0, 0, 0)),
        ],
        out_shape=[
            jax.ShapeDtypeStruct((length, wide), low),
            jax.ShapeDtypeStruct((length, wide), low),
            jax.ShapeDtypeStruct((8, value), full),
            jax.ShapeDtypeStruct((heads, key, value), full),
        ],
        compiler_params=pltpu.CompilerParams(vmem_limit_bytes=48 * MIB),
        name="gate_back",
    )(dy, mixed, gate, gain, through)


def lane_sum(array):
    return jnp.sum(array, axis=-1, keepdims=True)


def backward_kernel(
    heads, key, value, devices,
    place_ref, pre_ref, tail_ref, ab_ref, meta_ref, segrow_ref, edge_ref, edge_meta_ref, taps_ref, params_ref,
    states_ref, inverse_ref, state_in_ref, do_ref, ends_ref, adjoints_ref,
    dpre_ref, dab_ref, halo_ref, taps_grad_ref, params_grad_ref,
    ext, du, adjoint,
):
    step = pl.program_id(0)
    steps = pl.num_programs(0)
    size = pre_ref.shape[0]
    kfirst, vfirst = heads * key, 2 * heads * key

    @pl.when(step == 0)
    def _():
        adjoint[...] = jnp.zeros_like(adjoint)

        def one(k, carry):
            j = devices - 1 - k
            for h in range(heads):
                adjoint[h] = (
                    mm_tn(ends_ref[j, h, :, value:], adjoint[h]) + adjoints_ref[j, h].astype(full)
                )
            return carry

        lax.fori_loop(0, devices - 1 - place_ref[0], one, 0)
        du[8 + size :, :] = jnp.zeros((8, du.shape[1]), full)
        taps_grad_ref[...] = jnp.zeros_like(taps_grad_ref)
        params_grad_ref[...] = jnp.zeros_like(params_grad_ref)

    @pl.when(step > 0)
    def _():
        du[8 + size :, :] = du[8:16, :]

    du[0:8, :] = jnp.zeros((8, du.shape[1]), full)

    @pl.when(step < steps - 1)
    def _():
        ext[0:8, :] = tail_ref[8:16, :].astype(full)

    @pl.when(step == steps - 1)
    def _():
        ext[0:8, :] = edge_ref[...].astype(full)

    ext[8:, :] = pre_ref[...].astype(full)
    meta = meta_ref[...]
    ab = ab_ref[...]
    log_decay, beta = gates(ab, params_ref, heads)
    rows, cols, same_low, strict_low = masks(meta, segrow_ref)
    cum = exact((rows >= cols).astype(full), log_decay)
    cum_t = cum.T
    lane = lax.broadcasted_iota(jnp.int32, (size, LANES), 1)
    row8 = lax.broadcasted_iota(jnp.int32, (8, size), 0)
    dcum = jnp.zeros((size, LANES), full)
    dcum_rows = jnp.zeros((8, size), full)
    dcum_last = jnp.zeros((1, LANES), full)
    dbeta = jnp.zeros((size, LANES), full)
    lane1 = lax.broadcasted_iota(jnp.int32, (1, LANES), 1)

    for h in range(heads):
        qcols = slice(h * key, (h + 1) * key)
        kcols = slice(kfirst + h * key, kfirst + (h + 1) * key)
        vcols = slice(vfirst + h * value, vfirst + (h + 1) * value)
        uq = conv_sum(ext, taps_ref, meta, h * key, key, size)
        sq = sigmoid(uq)
        pq = uq * sq
        rq = unit(pq)
        qf = pq * rq
        q = qf.astype(low)
        uk = conv_sum(ext, taps_ref, meta, kfirst + h * key, key, size)
        sk = sigmoid(uk)
        pk = uk * sk
        rk = unit(pk)
        kf = pk * rk
        k = kf.astype(low)
        uv = conv_sum(ext, taps_ref, meta, vfirst + h * value, value, size)
        sv = sigmoid(uv)
        v = uv * sv
        lower, strict, f, e, c = decay_parts(cum, cum_t, h, same_low, strict_low, meta)
        b = beta[:, heads + h : heads + h + 1]
        kq = jnp.concatenate([k, q], axis=0)
        gram = mm_nt(kq, k)
        kk, qk = gram[:size], gram[size:]
        stored = states_ref[0, h]
        s = stored[:, :value].astype(full) + mm(stored[:, value:], state_in_ref[h])
        slow = s.astype(low)
        kqs = mm(kq, slow)
        ks, qs = kqs[:size], kqs[size:]
        rest = v - f * ks
        t = inverse_ref[0, h]
        delta = mm(t, b * rest).astype(low)
        do = do_ref[:, h * value : (h + 1) * value]
        dof = do.astype(full)
        ds = adjoint[h]
        dslow = ds.astype(low)
        ke = (e * kf).astype(low)
        p = lower * qk
        left = jnp.concatenate([p.T.astype(low), ke], axis=1)
        ddelta = mm(left, jnp.concatenate([do, dslow], axis=0))
        dtarget = mm_tn(t, ddelta)
        outer = mm_nt(jnp.concatenate([do, dtarget.astype(low)], axis=0), delta)
        dp, dan = outer[:size], outer[size:]
        eg = lower * dp
        hn = -strict * dan
        hg = b * hn
        x = eg * qk
        hk = hn * kk
        g1 = (b * f) * dtarget
        fdo = f * dof
        pair = jnp.concatenate([fdo.astype(low), (-g1).astype(low)], axis=0)
        both = mm_nt(pair, slow)
        dq = both[:size] + mm(eg, k)
        dsk = e * mm_nt(delta, dslow)
        left = jnp.concatenate([(hg + hg.T).astype(low), eg.T.astype(low)], axis=1)
        dk = both[size:] + dsk + mm(left, kq)
        dv = b * dtarget
        z = lane_sum(kf * dsk)
        dfrom = lane_sum(dof * qs) - b * lane_sum(dtarget * ks)
        hrow = lane_sum(hk)
        db = hrow + lane_sum(dtarget * rest)
        dbeta = dbeta + jnp.where(lane == heads + h, db, 0.0)
        dcum = dcum + jnp.where(lane == h, lane_sum(x) + b * hrow + f * dfrom - z, 0.0)
        drow = jnp.sum(x + b * hk, axis=0, keepdims=True)
        dcum_rows = dcum_rows + jnp.where(row8 == h, drow, 0.0)
        dlast = jnp.sum(z, axis=0, keepdims=True) + c * jnp.sum(
            lane_sum(ds * s), axis=0, keepdims=True
        )
        dcum_last = dcum_last + jnp.where(lane1 == h, dlast, 0.0)
        adjoint[h] = c * ds + mm_tn(jnp.concatenate([q, k], axis=0), pair)

        dpq = rq * (dq - qf * lane_sum(dq * qf))
        du[8 : 8 + size, qcols] = dpq * (sq * (1.0 + uq * (1.0 - sq)))
        dpk = rk * (dk - kf * lane_sum(dk * kf))
        du[8 : 8 + size, kcols] = dpk * (sk * (1.0 + uk * (1.0 - sk)))
        du[8 : 8 + size, vcols] = dv * (sv * (1.0 + uv * (1.0 - sv)))

    padded = jnp.concatenate([dcum_rows, jnp.zeros((LANES - 8, size), full)], axis=0)
    rowi = lax.broadcasted_iota(jnp.int32, (size, LANES), 0)
    dcum = dcum - padded.T + jnp.where(rowi == size - 1, dcum_last, 0.0)
    dlog = exact((rows <= cols).astype(full), dcum)
    dga = dlog * params_ref[0:1, :] * sigmoid(ab + params_ref[1:2, :])
    is_decay = lane < heads
    dga = jnp.where(is_decay, dga, 0.0)
    params_grad_ref[0:8, :] += jnp.sum(dga.reshape(size // 8, 8, LANES), axis=0)
    decay_part = jnp.where(is_decay, dlog * log_decay, 0.0)
    params_grad_ref[8:16, :] += jnp.sum(decay_part.reshape(size // 8, 8, LANES), axis=0)
    dab_ref[...] = jnp.where(is_decay, dga, dbeta * beta * (1.0 - beta)).astype(low)

    width = du.shape[1]
    for first in range(0, width, 512):
        cs = slice(first, first + 512)
        own = du[8 : 8 + size, cs]
        total = taps_ref[3:4, cs] * own
        taps_grad_ref[24:32, cs] += jnp.sum(
            (own * ext[8 : 8 + size, cs]).reshape(size // 8, 8, 512), axis=0
        )
        for lag in (1, 2, 3):
            total += taps_ref[3 - lag : 4 - lag, cs] * meta[:, 5 + lag : 6 + lag] * du[
                8 + lag : 8 + lag + size, cs
            ]
            taps_grad_ref[8 * (3 - lag) : 8 * (4 - lag), cs] += jnp.sum(
                (own * meta[:, lag : lag + 1] * ext[8 - lag : 8 - lag + size, cs]).reshape(
                    size // 8, 8, 512
                ),
                axis=0,
            )
        dpre_ref[:, cs] = total.astype(low)

    @pl.when(step == steps - 1)
    def _():
        edge_meta = edge_meta_ref[...]
        halo = jnp.zeros(halo_ref.shape, full)
        for lag in (1, 2, 3):
            halo += taps_ref[3 - lag : 4 - lag, :] * edge_meta[:, 5 + lag : 6 + lag] * du[
                lag : 8 + lag, :
            ]
        halo_ref[...] = halo


def backward_chain(place, pre, ab, meta, segrow, edge, edge_meta, taps, params, states, inverse,
                   state_in, do, ends, adjoints, heads, key, value):
    length, width = pre.shape
    blocks = length // BLOCK
    wide = value + key
    once = dict(pipeline_mode=pl.Buffered(1))
    last = blocks - 1
    return pl.pallas_call(
        partial(backward_kernel, heads, key, value, ends.shape[0]),
        grid=(blocks,),
        in_specs=[
            pl.BlockSpec(memory_space=pltpu.SMEM),
            pl.BlockSpec((BLOCK, width), lambda n: (last - n, 0)),
            pl.BlockSpec((16, width), lambda n: (jnp.maximum((last - n) * (BLOCK // 16) - 1, 0), 0)),
            pl.BlockSpec((BLOCK, LANES), lambda n: (last - n, 0)),
            pl.BlockSpec((BLOCK, LANES), lambda n: (last - n, 0)),
            pl.BlockSpec((8, BLOCK), lambda n: (0, last - n)),
            pl.BlockSpec((8, width), lambda n: (0, 0)),
            pl.BlockSpec((8, LANES), lambda n: (0, 0)),
            pl.BlockSpec(taps.shape, lambda n: (0, 0)),
            pl.BlockSpec((8, LANES), lambda n: (0, 0)),
            pl.BlockSpec((1, heads, key, wide), lambda n: (last - n, 0, 0, 0)),
            pl.BlockSpec((1, heads, BLOCK, BLOCK), lambda n: (last - n, 0, 0, 0)),
            pl.BlockSpec((heads, key, value), lambda n: (0, 0, 0)),
            pl.BlockSpec((BLOCK, heads * value), lambda n: (last - n, 0)),
            pl.BlockSpec(ends.shape, lambda n: (0, 0, 0, 0), **once),
            pl.BlockSpec(adjoints.shape, lambda n: (0, 0, 0, 0), **once),
        ],
        out_specs=[
            pl.BlockSpec((BLOCK, width), lambda n: (last - n, 0)),
            pl.BlockSpec((BLOCK, LANES), lambda n: (last - n, 0)),
            pl.BlockSpec((8, width), lambda n: (0, 0)),
            pl.BlockSpec((32, width), lambda n: (0, 0)),
            pl.BlockSpec((16, LANES), lambda n: (0, 0)),
        ],
        out_shape=[
            jax.ShapeDtypeStruct((length, width), low),
            jax.ShapeDtypeStruct((length, LANES), low),
            jax.ShapeDtypeStruct((8, width), full),
            jax.ShapeDtypeStruct((32, width), full),
            jax.ShapeDtypeStruct((16, LANES), full),
        ],
        scratch_shapes=[
            pltpu.VMEM((BLOCK + 8, width), full),
            pltpu.VMEM((BLOCK + 16, width), full),
            pltpu.VMEM((heads, key, value), full),
        ],
        compiler_params=pltpu.CompilerParams(vmem_limit_bytes=56 * MIB),
        name="chain_backward",
    )(place, pre, pre, ab, meta, segrow, edge, edge_meta, taps, params, states, inverse, state_in, do,
      ends, adjoints)


def segment_tables(doc_lengths, shard, length):
    starts = jnp.cumsum(doc_lengths, dtype=jnp.int32) - doc_lengths
    positions = shard * length + jnp.arange(-16, length + 8, dtype=jnp.int32)
    seg = jnp.sum((starts[None, :] <= positions[:, None]).astype(jnp.int32), axis=1)
    own = seg[16 : 16 + length]

    def lanes(first, count):
        base = seg[first : first + count]
        back = [seg[first - l : first - l + count] == base for l in (1, 2, 3)]
        ahead = [seg[first + l : first + l + count] == base for l in (1, 2, 3)]
        return base, back, ahead

    base, back, ahead = lanes(16, length)
    blocks = own.reshape(-1, BLOCK)
    before = seg[15 : 15 + length : BLOCK]
    alive = (blocks == before[:, None]).reshape(-1)
    to_last = (blocks == blocks[:, -1:]).reshape(-1)
    columns = [base, *back, alive, to_last, *ahead]
    meta = jnp.stack([a.astype(full) for a in columns], axis=1)
    meta = jnp.pad(meta, ((0, 0), (0, LANES - meta.shape[1])))
    base, back, ahead = lanes(8, 8)
    columns = [base, *back, base, base, *ahead]
    edge_meta = jnp.stack([a.astype(full) for a in columns], axis=1)
    edge_meta = jnp.pad(edge_meta, ((0, 0), (0, LANES - edge_meta.shape[1])))
    segrow = jnp.broadcast_to(own.astype(full)[None, :], (8, length))
    return meta, edge_meta, segrow


def rms_scale(array, epsilon):
    return lax.rsqrt(jnp.mean(array * array, axis=-1, keepdims=True) + epsilon)


def gather(parts):
    return lax.all_gather(jnp.concatenate(parts, axis=1), "seq", axis=0, tiled=True)


def scatter(grad):
    return lax.psum_scatter(grad.astype(low), "seq", scatter_dimension=0, tiled=True).astype(full)


def passed_along(block, axis, distance):
    devices = range(lax.axis_size(axis))
    route = [(i - distance, i) for i in devices if i - distance in devices]
    return lax.ppermute(block, axis, route)


def shards(
    tokens,
    doc_lengths,
    mixer_gain,
    query_weight,
    key_weight,
    value_weight,
    gate_weight,
    alpha_weight,
    beta_weight,
    decay_log,
    decay_bias,
    query_taps,
    key_taps,
    value_taps,
    head_gain,
    output_weight,
    ffn_gain,
    ffn_gate,
    ffn_up,
    ffn_down,
    cotangent,
):
    length = tokens.shape[0]
    heads = decay_log.shape[0]
    key = query_weight.shape[1] // heads
    value = head_gain.shape[0]
    keys, vals = heads * key, heads * value
    hidden_size = ffn_gate.shape[1]
    shard = lax.axis_index("seq")
    place = jnp.full((1,), shard, jnp.int32)
    meta, edge_meta, segrow = segment_tables(doc_lengths, shard, length)

    small = jnp.concatenate(
        [alpha_weight, beta_weight, jnp.zeros((alpha_weight.shape[0], LANES - 2 * heads), full)],
        axis=1,
    )
    w_in = gather([a.astype(low) for a in (query_weight, key_weight, value_weight)])
    w_small = lax.all_gather(small.astype(low), "seq", axis=0, tiled=True)
    w_gate = lax.all_gather(gate_weight.astype(low), "seq", axis=0, tiled=True)
    w_out = lax.all_gather(output_weight.T.astype(low), "seq", axis=0, tiled=True)
    w_widen = lax.all_gather(ffn_gate.astype(low), "seq", axis=0, tiled=True)
    w_lift = lax.all_gather(ffn_up.astype(low), "seq", axis=0, tiled=True)
    w_narrow = lax.all_gather(ffn_down.T.astype(low), "seq", axis=0, tiled=True)

    stream = tokens.astype(full)
    first_scale = rms_scale(stream, 1e-06)
    first_norm = stream * first_scale
    first_in = (first_norm * mixer_gain).astype(low)
    pre = mm(first_in, w_in).astype(low)
    ab = mm(first_in, w_small)
    edge = passed_along(pre[length - 8 :], "seq", 1)
    gate_pre = mm(first_in, w_gate)

    taps = jnp.concatenate([query_taps, key_taps, value_taps], axis=1)
    params = jnp.stack([-jnp.exp(decay_log), decay_bias])
    params = jnp.pad(params, ((0, 6), (0, LANES - heads)))
    local, through, states, inverse, end = forward_chain(
        pre, ab, meta, segrow, edge, taps, params, heads, key, value
    )
    ends = lax.all_gather(end, "seq")
    gain = head_gain[None, :]
    mix_out, mixed, state_in = chain_output(
        place, ends, local, through, gate_pre, gain, heads, key, value
    )
    middle = stream + lax.psum(mm_nt(mix_out, w_out).astype(low), "head").astype(full)
    second_scale = rms_scale(middle, 1e-06)
    second_norm = middle * second_scale
    second_in = (second_norm * ffn_gain).astype(low)
    gate_act = mm(second_in, w_widen)
    lift_act = mm(second_in, w_lift)
    sigma = jax.nn.sigmoid(gate_act)
    swish = gate_act * sigma
    hidden = (swish * lift_act).astype(low)
    result = (
        middle + lax.psum(mm_nt(hidden, w_narrow).astype(low), "head").astype(full)
    ).astype(low)

    grad_out = cotangent.astype(full)
    hidden_grad = mm(cotangent, w_narrow)
    gate_grad = (hidden_grad * lift_act * sigma * (1.0 + gate_act * (1.0 - sigma))).astype(low)
    lift_grad = (hidden_grad * swish).astype(low)
    second_grad = lax.psum(
        (mm_nt(gate_grad, w_widen) + mm_nt(lift_grad, w_lift)).astype(low), "head"
    ).astype(full)
    narrow_wgrad = scatter(mm_tn(cotangent, hidden)).T
    widen_wgrad = scatter(mm_tn(second_in, gate_grad))
    lift_wgrad = scatter(mm_tn(second_in, lift_grad))
    second_weighted = second_grad * ffn_gain
    ffn_gain_part = jnp.sum(second_grad * second_norm, axis=0)
    middle_grad = grad_out + second_scale * (
        second_weighted
        - second_norm * jnp.mean(second_weighted * second_norm, axis=-1, keepdims=True)
    )
    middle_low = middle_grad.astype(low)
    mix_grad = mm(middle_low, w_out)
    gate_pgrad, mixed_grad, head_gain_part, adjoint = gate_back(
        mix_grad, mixed, gate_pre, gain, through, heads, key, value
    )
    adjoints = lax.all_gather(adjoint.astype(low), "seq")
    output_wgrad = scatter(mm_tn(middle_low, mix_out)).T
    gate_wgrad = scatter(mm_tn(first_in, gate_pgrad))
    pre_grad, ab_grad, halo, taps_part, params_part = backward_chain(
        place, pre, ab, meta, segrow, edge, edge_meta, taps, params, states, inverse, state_in,
        mixed_grad, ends, adjoints, heads, key, value,
    )
    halo = passed_along(halo, "seq", -1)
    last = pre_grad[length - 8 :].astype(full) + halo
    pre_grad = lax.dynamic_update_slice(pre_grad, last.astype(low), (length - 8, 0))
    first_grad = lax.psum(
        (
            mm_nt(pre_grad, w_in) + mm_nt(gate_pgrad, w_gate) + mm_nt(ab_grad, w_small)
        ).astype(low),
        "head",
    ).astype(full)
    in_wgrad = scatter(mm_tn(first_in, pre_grad))
    small_wgrad = scatter(mm_tn(first_in, ab_grad))
    first_weighted = first_grad * mixer_gain
    mixer_gain_part = jnp.sum(first_grad * first_norm, axis=0)
    tokens_grad = middle_grad + first_scale * (
        first_weighted - first_norm * jnp.mean(first_weighted * first_norm, axis=-1, keepdims=True)
    )
    taps_part = jnp.sum(taps_part.reshape(4, 8, -1), axis=1)
    params_part = jnp.sum(params_part.reshape(2, 8, LANES), axis=1)
    mixer_gain_grad, ffn_gain_grad, taps_grad, params_grad = lax.psum(
        (
            mixer_gain_part.astype(low),
            ffn_gain_part.astype(low),
            taps_part.astype(low),
            params_part.astype(low),
        ),
        "seq",
    )
    head_gain_grad = lax.psum(jnp.sum(head_gain_part, axis=0), ("seq", "head"))
    taps_grad = taps_grad.astype(full)
    params_grad = params_grad.astype(full)
    return (
        result,
        tokens_grad,
        mixer_gain_grad.astype(full),
        in_wgrad[:, :keys],
        in_wgrad[:, keys : 2 * keys],
        in_wgrad[:, 2 * keys :],
        gate_wgrad,
        small_wgrad[:, :heads],
        small_wgrad[:, heads : 2 * heads],
        params_grad[1, :heads],
        params_grad[0, :heads],
        taps_grad[:, :keys],
        taps_grad[:, keys : 2 * keys],
        taps_grad[:, 2 * keys :],
        head_gain_grad,
        output_wgrad,
        ffn_gain_grad.astype(full),
        widen_wgrad,
        lift_wgrad,
        narrow_wgrad,
    )


def solution(mesh):
    rows, both = P("seq", None), P("seq", "head")
    in_specs = (
        rows, P(), P(), both, both, both, both, both, both, P("head"), P("head"),
        P(None, "head"), P(None, "head"), P(None, "head"), P(), P("head", "seq"), P(),
        both, both, P("head", "seq"), rows,
    )
    out_specs = (
        rows, rows, P(), both, both, both, both, both, both, P("head"), P("head"),
        P(None, "head"), P(None, "head"), P(None, "head"), P(), P("head", "seq"), P(),
        both, both, P("head", "seq"),
    )
    return jax.shard_map(shards, mesh=mesh, in_specs=in_specs, out_specs=out_specs, check_vma=False)
```

time: 2940 us -> 1470 us (0.50)
  matrix products: 1080 us -> 220 us
  local copies, waits for them, and re-layouts: 305 us -> 18.8 us
  other arithmetic: 291 us -> 70.8 us
  waiting for transfers between devices: 1070 us -> 954 us
  Pallas kernels: 0 us -> 106 us
  loops' own time: 62.7 us -> 0 us
    dot_general x1367 -> x21, matrix products: 1080 us -> 220 us  [the longest x7 76.4 us: mm(): return jnp.dot(a.astype(low), b.astype(low), preferred_element_type=full)]
    pallas_call x0 -> x4, Pallas kernels: none -> 106 us  [the longest x1 56.4 us: backward_chain(): pl.pallas_call(partial(backward_kernel, heads, key, value, ends.shape[0])...]
    reduce_scatter x8 -> x7, waiting for transfers between devices: 257 us -> 168 us  [scatter(): lax.psum_scatter(grad.astype(low), 'seq', scatter_dimension=0, tiled=True)]
    squeeze x128 -> x1, local copies, waits for them, and re-layouts: 76.1 us -> 0.52 us  [shards(): params_grad[0, :heads]]
    another operation x5 -> x0, loops' own time: 62.7 us -> none  [the longest x3 62.2 us: run_groups(): lax.scan(jax.checkpoint(group_step), (state_now, seg_prev), blocks)]
    slice x138 -> x8, local copies, waits for them, and re-layouts: 64.1 us -> 6.75 us  [the longest x1 2.13 us: shards(): in_wgrad[:, keys:2 * keys]]
    mul x89 -> x0, other arithmetic: 51.4 us -> none  [the longest x80 32.5 us: group_step(): carried = jnp.exp(cum_decay[:, -1]) * alive_mask[-1]]
    reduce_sum x57 -> x4, other arithmetic: 44.9 us -> 0.21 us  [the longest x1 0.09 us: segment_tables(): jnp.sum((starts[None, :] <= positions[:, None]).astype(jnp.int32), axis=1)]
  transfers between devices with their start and end apart: 31 -> 20, of which waited for: 19 -> 15; matrix products, arithmetic and copies ran while one was open for 29% -> 16% of each run, Pallas kernels for 0% -> 7%
where the time goes in v1:
time: 1470 us; the launch traced here: 1460 us
  waiting for transfers between devices  954 us (65%)
  matrix products  220 us (15%)
  Pallas kernels  106 us (7%)
  blocking collectives  73.9 us (5%)
  other arithmetic  70.8 us (5%)
  local copies, waits for them, and re-layouts  18.8 us (1%)
  between operations  15.5 us (1%)
    psum x1, waiting for transfers between devices, shards(): lax.psum((mm_nt(pre_grad, w_in) + mm_nt(gate_pgrad, w_gate) + mm_nt(ab_gr...  292 us
    reduce_scatter x7, waiting for transfers between devices, scatter(): lax.psum_scatter(grad.astype(low), 'seq', scatter_dimension=0, tiled=True)  168 us
    psum x1, waiting for transfers between devices, shards(): lax.psum((mm_nt(gate_grad, w_widen) + mm_nt(lift_grad, w_lift)).astype(lo...  155 us
    psum x1, waiting for transfers between devices, shards(): lax.psum(mm_nt(mix_out, w_out).astype(low), 'head').astype(full)  146 us
    dot_general x7, matrix products, mm(): return jnp.dot(a.astype(low), b.astype(low), preferred_element_type=full)  76.4 us
    dot_general x7, matrix products, mm_tn(): lax.dot_general(a.astype(low), b.astype(low), (((0,), (0,)), ((), ())), p...  76 us
    dot_general x7, matrix products, mm_nt(): lax.dot_general(a.astype(low), b.astype(low), (((1,), (1,)), ((), ())), p...  67.9 us
    pallas_call x1, Pallas kernels, backward_chain(): pl.pallas_call(partial(backward_kernel, heads, key, value, ends.shape[0])...  56.4 us
  transfers between devices with their start and end apart: 20, of which 15 were waited for; matrix products, arithmetic and copies ran while one was open for 16% of the time, Pallas kernels for 7%

profile of v1, /device:TPU:0, one launch (start us, length us, event | category | flops | bytes accessed | tf_op | source)
XLA Modules:
  0.0 1464.6 jit_solution(17079721266607525126)
XLA Ops:
  14.2 11.3 all_gather.34
  25.6 3.3 fusion.16
  29.0 3.5 fusion.43.ab_ref
  32.5 36.7 %all-gather.11.cloned.1.call-done = bf16[2048,2048]{1,0:T(8,128)(2,1)} async-done(((bf16[256,2048]{1,0:T(8,128)(2,1)}), bf16[2048,2048]{1,0:T(8,128)(2,1)}) %all-gather.11.cloned.1.call-update) | async-done | bytes 8388624 | tf_op jit(solution)/shard_map/all_gather | solution.py:620
  69.2 12.6 convolution_convert_fusion.5.pre_ref.tail_ref
  84.9 34.6 %chain_forward.1 = (f32[1024,1024]{1,0:T(8,128)}, bf16[1024,512]{1,0:T(8,128)(2,1)S(1)}, bf16[8,4,128,384]{3,2,1,0:T(8,128)(2,1)}, bf16[8,4,128,128]{3,2,1,0:T(8,128)(2,1)S(1)}, bf16[4,128,384]{2,1,0:T(8,128)(2,1)}) custom-call(bf16[1024,2048]{1,0:T(8,128)(2,1)} %copy-done.17, f32[1024,128]{1,0:T(8,128)S(1)} %fusion.43.ab_ref, ...), custom_call_target="tpu_custom_call" | custom-call | tf_op jit(solution)/shard_map/chain_forward/pallas_call | solution.py:206
  126.1 10.0 fusion.41.gate_ref
  136.1 20.7 %all-gather.23.cloned.1.call-done = bf16[32,128,384]{2,1,0:T(8,128)(2,1)} async-done(((bf16[4,128,384]{2,1,0:T(8,128)(2,1)}), bf16[32,128,384]{2,1,0:T(8,128)(2,1)}) %all-gather.23.cloned.1.call-update) | async-done | bytes 3145744 | tf_op jit(solution)/shard_map/all_gather | solution.py:693
  156.8 7.7 chain_output.1
  165.3 31.2 %all-gather.15.cloned.1.call-done = bf16[2048,1024]{0,1:T(8,128)(2,1)} async-done(((bf16[256,1024]{0,1:T(8,128)(2,1)}), bf16[2048,1024]{0,1:T(8,128)(2,1)}) %all-gather.15.cloned.1.call-update) | async-done | bytes 4194320 | tf_op jit(solution)/shard_map/all_gather | solution.py:673
  196.5 8.2 convolution_convert_fusion.8
  209.7 33.5 %all-gather.21.cloned.1.call-done = bf16[2048,1408]{0,1:T(8,128)(2,1)} async-done(((bf16[256,1408]{0,1:T(8,128)(2,1)}), bf16[2048,1408]{0,1:T(8,128)(2,1)}) %all-gather.21.cloned.1.call-update) | async-done | bytes 5767184 | tf_op jit(solution)/shard_map/all_gather | solution.py:676
  243.2 11.7 fusion.52
  255.0 146.1 %all-reduce.9.cloned.1.call-done = bf16[1024,2048]{1,0:T(8,128)(2,1)} async-done(((bf16[1024,2048]{1,0:T(8,128)(2,1)}), bf16[1024,2048]{1,0:T(8,128)(2,1)}) %all-reduce.9.cloned.1.call-update) | async-done | bytes 4194320 | tf_op jit(solution)/shard_map/psum | solution.py:698
  401.1 5.0 multiply_reduce_fusion
  407.0 4.0 multiply_convert_fusion
  411.0 35.0 %all-gather.17.cloned.1.call-done = bf16[2048,1408]{1,0:T(8,128)(2,1)} async-done(((bf16[256,1408]{1,0:T(8,128)(2,1)}), bf16[2048,1408]{1,0:T(8,128)(2,1)}) %all-gather.17.cloned.1.call-update) | async-done | bytes 5767184 | tf_op jit(solution)/shard_map/all_gather | solution.py:674
  446.0 11.7 fusion.51
  457.7 34.3 %all-gather.19.cloned.1.call-done = bf16[2048,1408]{1,0:T(8,128)(2,1)} async-done(((bf16[256,1408]{1,0:T(8,128)(2,1)}), bf16[2048,1408]{1,0:T(8,128)(2,1)}) %all-gather.19.cloned.1.call-update) | async-done | bytes 5767184 | tf_op jit(solution)/shard_map/all_gather | solution.py:675
  492.0 15.6 %multiply_convert_fusion.3 = (bf16[1024,1408]{1,0:T(8,128)(2,1)}, bf16[1024,1408]{1,0:T(8,128)(2,1)S(1)}, bf16[1024,1408]{1,0:T(8,128)(2,1)S(1)}) fusion(f32[1024,1408]{1,0:T(8,128)} %fusion.51, f32[1024,1408]{1,0:T(8,128)} %fusion.52, bf16[1024,2048]{1,0:T(8,128)(2,1)} %multiply_convert_fusion, bf16[2048,1408]{1,0:T(8,128)(2,1)} %all-gather.19.cloned.1.call-done), kind=kOutput, calls=%fused_computation.36 | convolution fusion | flops 5927206912 | bytes 30146560 | tf_op jit(solution)/shard_map/dot_general | solution.py:18
  507.6 17.4 %fusion.53 = f32[1024,2048]{1,0:T(8,128)} fusion(bf16[1024,1408]{1,0:T(8,128)(2,1)S(1)} %get-tuple-element.165, bf16[2048,1408]{1,0:T(8,128)(2,1)S(1)} %copy-done.41), kind=kOutput, calls=%fused_computation.113 | convolution fusion | flops 5905580032 | bytes 17039360 | tf_op jit(solution)/shard_map/dot_general | solution.py:22
  525.0 10.5 add_convert_fusion.1
  535.6 155.1 %all-reduce.11.cloned.1.call-done = bf16[1024,2048]{1,0:T(8,128)(2,1)} async-done(((bf16[1024,2048]{1,0:T(8,128)(2,1)}), bf16[1024,2048]{1,0:T(8,128)(2,1)}) %all-reduce.11.cloned.1.call-update) | async-done | bytes 4194320 | tf_op jit(solution)/shard_map/psum | solution.py:715
  690.7 8.4 fusion.12
  699.1 11.3 fusion.21.dy_ref
  710.5 7.5 gate_back.1
  721.4 11.2 convolution_convert_fusion.1
  732.7 11.0 convolution_convert_fusion.2
  743.8 10.6 fusion.18
  756.4 56.4 %chain_backward.1 = (bf16[1024,2048]{1,0:T(8,128)(2,1)}, bf16[1024,128]{1,0:T(8,128)(2,1)}, f32[8,2048]{1,0:T(8,128)}, f32[32,2048]{1,0:T(8,128)}, f32[16,128]{1,0:T(8,128)}) custom-call(s32[1]{0:T(128)} %bitcast.place_ref, bf16[1024,2048]{1,0:T(8,128)(2,1)} %copy-done.17, bf16[1024,2048]{1,0:T(8,128)(2,1)} %copy-done.17, f32[1024,128]{1,0:T(8,128)} %copy-done.2, ...), custom_call_target="tpu_custom_call" | custom-call | tf_op jit(solution)/shard_map/chain_backward/pallas_call | solution.py:541
  812.8 3.4 convolution_convert_fusion.9
  816.5 15.6 %convolution_convert_fusion.6 = bf16[2048,1024]{1,0:T(8,128)(2,1)} fusion(bf16[1024,1024]{1,0:T(8,128)(2,1)S(1)} %get-tuple-element.40, bf16[1024,2048]{1,0:T(8,128)(2,1)} %all-reduce.11.cloned.1.call-done, bf16[1024,2048]{1,0:T(8,128)(2,1)} %param.41, bf16[1024,2048]{1,0:T(8,128)(2,1)} %all-reduce.9.cloned.1.call-done, bf16[1024,2048]{1,0:T(8,128)(2,1)} %param.21, ...), kind=kOutput, calls=%fused_computation.41 | convolution fusion | flops 4322230272 | bytes 23085056 | tf_op jit(solution)/shard_map/dot_general | solution.py:28
  832.1 9.9 convolution_convert_fusion.7
  842.3 11.1 convolution_convert_fusion.4
  855.0 4.6 fusion.55
  859.6 12.8 fusion.54
  872.5 3.3 add_convert_fusion
  876.1 14.4 convolution_convert_fusion.3
  890.5 38.5 %psum.70 = f32[256]{0:T(256)} all-reduce(f32[256]{0:T(256)S(1)} %reduce_sum.98), channel_id=1, replica_groups=mesh['seq'=8,'head'=4] {'seq','head'}, use_global_device_ids=true, to_apply=%region_20.21 | all-reduce | flops 256 | bytes 2048 | tf_op jit(solution)/shard_map/psum | solution.py:766
  933.8 3.4 reduce-scatter.20.cloned.1.call-done
  939.5 35.8 %reduce-scatter.12.cloned.1.call-done = bf16[256,128]{1,0:T(8,128)(2,1)} async-done(((bf16[2048,128]{1,0:T(8,128)(2,1)}), bf16[256,128]{1,0:T(8,128)(2,1)}) %reduce-scatter.12.cloned.1.call-update) | async-done | bytes 65552 | tf_op jit(solution)/shard_map/reduce_scatter | solution.py:624
  977.7 52.2 %reduce-scatter.14.cloned.1.call-done = bf16[256,1024]{1,0:T(8,128)(2,1)} async-done(((bf16[2048,1024]{1,0:T(8,128)(2,1)}), bf16[256,1024]{1,0:T(8,128)(2,1)}) %reduce-scatter.14.cloned.1.call-update) | async-done | bytes 524304 | tf_op jit(solution)/shard_map/reduce_scatter | solution.py:624
  1032.3 52.5 %reduce-scatter.10.cloned.1.call-done = bf16[256,1024]{1,0:T(8,128)(2,1)} async-done(((bf16[2048,1024]{1,0:T(8,128)(2,1)}), bf16[256,1024]{1,0:T(8,128)(2,1)}) %reduce-scatter.10.cloned.1.call-update) | async-done | bytes 524304 | tf_op jit(solution)/shard_map/reduce_scatter | solution.py:624
  1086.9 292.4 %all-reduce.13.cloned.1.call-done = (bf16[1024,2048]{1,0:T(8,128)(2,1)}, bf16[1024,2048]{1,0:T(8,128)(2,1)}) async-done(((bf16[1024,2048]{1,0:T(8,128)(2,1)}, bf16[1024,2048]{1,0:T(8,128)(2,1)}), (bf16[1024,2048]{1,0:T(8,128)(2,1)}, bf16[1024,2048]{1,0:T(8,128)(2,1)})) %all-reduce.13.cloned.1.call-update) | async-done | bytes 8388624 | tf_op jit(solution)/shard_map/psum | solution.py:742
  1379.4 5.0 fusion.15
  1384.4 24.0 %all-reduce.3 = (bf16[4,2048]{1,0:T(4,128)(2,1)S(1)}, bf16[2048]{0:T(1024)(128)(2,1)S(1)}, bf16[2,128]{1,0:T(2,128)(2,1)S(1)}, bf16[2048]{0:T(1024)(128)(2,1)S(1)}) all-reduce(bf16[4,2048]{1,0:T(4,128)(2,1)S(1)} %bitcast_reduce_fusion, bf16[2048]{0:T(1024)(128)(2,1)S(1)} %get-tuple-element.156, ...), channel_id=1, replica_groups=mesh['seq'=8,'head'=4] {'seq'}, use_global_device_ids=true, to_apply=%region_18.19 | all-reduce | flops 12544 | bytes 50176 | tf_op jit(solution)/shard_map/psum | solution.py:757
  1411.4 17.5 %fusion.8 = (f32[1024,2048]{1,0:T(8,128)}, bf16[1024,2048]{1,0:T(8,128)(2,1)}) fusion(bf16[1024,2048]{1,0:T(8,128)(2,1)} %get-tuple-element.162, bf16[1024,2048]{1,0:T(8,128)(2,1)} %param.21, f32[1024]{0:T(1024)S(1)} %broadcast_multiply_fusion, f32[2048]{0:T(1024)S(1)} %copy-done.30, f32[1024]{0:T(1024)S(1)} %copy-done.28, ...), kind=kLoop, calls=%fused_computation.14 | loop fusion | flops 44040192 | bytes 37781504 | tf_op jit(solution)/shard_map/add | solution.py:752
  1428.9 24.1 %reduce-scatter.8.cloned.1.call-done = bf16[256,2048]{1,0:T(8,128)(2,1)} async-done(((bf16[2048,2048]{1,0:T(8,128)(2,1)}), bf16[256,2048]{1,0:T(8,128)(2,1)}) %reduce-scatter.8.cloned.1.call-update) | async-done | bytes 1048592 | tf_op jit(solution)/shard_map/reduce_scatter | solution.py:624
  (213 shorter events, 52.5 us)
Async XLA Ops:
  7.3 18.3 %copy-start.46 = (f32[4]{0:T(128)S(1)}, f32[4]{0:T(128)}, u32[]{:S(2)}) copy-start(f32[4]{0:T(128)} %param.30) | copy-start | bytes 52
  7.3 62.0 %all-gather.11.cloned.1.call-start = ((), (), s32[]{:S(2)}) async-start(), calls=%async_computation.7 | async-start | bytes 9437184 | tf_op jit(solution)/shard_map/all_gather | solution.py:620
  9.5 19.4 %copy-start.29 = (f32[2048]{0:T(1024)S(1)}, f32[2048]{0:T(1024)}, u32[]{:S(2)}) copy-start(f32[2048]{0:T(1024)} %param.23) | copy-start | bytes 24580
  12.0 114.2 %all-gather.13.cloned.1.call-start = ((), (), s32[]{:S(2)}) async-start(), calls=%async_computation.8 | async-start | bytes 4718592 | tf_op jit(solution)/shard_map/all_gather | solution.py:672
  12.9 143.9 %all-gather.23.cloned.1.call-start = ((), (), s32[]{:S(2)}) async-start(), calls=%async_computation.22 | async-start | bytes 3538944 | tf_op jit(solution)/shard_map/all_gather | solution.py:693
  13.3 19.1 %copy-start.24 = (s32[1048]{0:T(1024)}, s32[1048]{0:T(1024)S(1)}, u32[]{:S(2)}) copy-start(s32[1048]{0:T(1024)S(1)} %convert_reduce_fusion) | copy-start | bytes 12580
  14.1 70.7 %copy-start.6 = (f32[4,2048]{1,0:T(4,128)}, f32[4,2048]{1,0:T(4,128)S(1)}, u32[]{:S(2)}) copy-start(f32[4,2048]{1,0:T(4,128)S(1)} %constant_dynamic-update-slice_fusion.taps_ref) | copy-start | bytes 98308
  28.8 97.3 %copy-start.27 = (f32[1024]{0:T(1024)}, f32[1024]{0:T(1024)S(1)}, u32[]{:S(2)}) copy-start(f32[1024]{0:T(1024)S(1)} %add_rsqrt_fusion.1) | copy-start | bytes 12292
  32.5 52.4 %copy-start.2 = (f32[1024,128]{1,0:T(8,128)}, f32[1024,128]{1,0:T(8,128)S(1)}, u32[]{:S(2)}) copy-start(f32[1024,128]{1,0:T(8,128)S(1)} %fusion.43.ab_ref) | copy-start | bytes 1572868
  32.5 51.6 %copy-start.38 = (f32[4]{0:T(128)S(1)}, f32[4]{0:T(128)}, u32[]{:S(2)}) copy-start(f32[4]{0:T(128)} %param.31) | copy-start | bytes 52
  81.8 3.0 collective-permute-start
  84.1 41.7 %copy-start.8 = (f32[8,128]{1,0:T(8,128)}, f32[8,128]{1,0:T(8,128)S(1)}, u32[]{:S(2)}) copy-start(f32[8,128]{1,0:T(8,128)S(1)} %select_maximum_fusion.params_ref) | copy-start | bytes 12292
  84.9 51.2 %copy-start.7 = (bf16[8,2048]{1,0:T(8,128)(2,1)}, bf16[8,2048]{1,0:T(8,128)(2,1)S(1)}, u32[]{:S(2)}) copy-start(bf16[8,2048]{1,0:T(8,128)(2,1)S(1)} %collective-permute-done.edge_ref) | copy-start | bytes 98308
  84.9 34.6 %copy-start.5 = (f32[8,1024]{1,0:T(8,128)}, f32[8,1024]{1,0:T(8,128)S(1)}, u32[]{:S(2)}) copy-start(f32[8,1024]{1,0:T(8,128)S(1)} %broadcast_in_dim.10.segrow_ref) | copy-start | bytes 98308
  121.3 75.3 %all-gather.15.cloned.1.call-start = ((), (), s32[]{:S(2)}) async-start(), calls=%async_computation.9 | async-start | bytes 4718592 | tf_op jit(solution)/shard_map/all_gather | solution.py:673
  123.4 119.8 %all-gather.21.cloned.1.call-start = ((), (), s32[]{:S(2)}) async-start(), calls=%async_computation.13 | async-start | bytes 6488064 | tf_op jit(solution)/shard_map/all_gather | solution.py:676
  125.8 31.0 %copy-start.9 = (f32[256]{0:T(256)S(1)}, f32[256]{0:T(256)}, u32[]{:S(2)}) copy-start(f32[256]{0:T(256)} %param.35) | copy-start | bytes 3076
  125.8 275.3 %all-reduce.9.cloned.1.call-start = ((), (), s32[]{:S(2)}) async-start(), calls=%async_computation.10 | async-start | bytes 8388608 | tf_op jit(solution)/shard_map/psum | solution.py:698
  204.8 241.3 %all-gather.17.cloned.1.call-start = ((), (), s32[]{:S(2)}) async-start(), calls=%async_computation.11 | async-start | bytes 6488064 | tf_op jit(solution)/shard_map/all_gather | solution.py:674
  207.3 284.8 %all-gather.19.cloned.1.call-start = ((), (), s32[]{:S(2)}) async-start(), calls=%async_computation.12 | async-start | bytes 6488064 | tf_op jit(solution)/shard_map/all_gather | solution.py:675
  209.7 481.0 %all-reduce.11.cloned.1.call-start = ((), (), s32[]{:S(2)}) async-start(), calls=%async_computation.14 | async-start | bytes 8388608 | tf_op jit(solution)/shard_map/psum | solution.py:715
  255.0 151.1 %copy-start.26 = (f32[2048]{0:T(1024)S(1)}, f32[2048]{0:T(1024)}, u32[]{:S(2)}) copy-start(f32[2048]{0:T(1024)} %param.37) | copy-start | bytes 24580
  492.0 15.6 %copy-start.41 = (bf16[2048,1408]{1,0:T(8,128)(2,1)S(1)}, bf16[2048,1408]{1,0:T(8,128)(2,1)}, u32[]{:S(2)}) copy-start(bf16[2048,1408]{1,0:T(8,128)(2,1)} %all-gather.17.cloned.1.call-done) | copy-start | bytes 17301508
  507.6 17.4 %copy-start.47 = (bf16[1024,1408]{1,0:T(8,128)(2,1)}, bf16[1024,1408]{1,0:T(8,128)(2,1)S(1)}, u32[]{:S(2)}) copy-start(bf16[1024,1408]{1,0:T(8,128)(2,1)S(1)} %get-tuple-element.165) | copy-start | bytes 8650756
  507.6 17.4 %copy-start.48 = (bf16[1024,1408]{1,0:T(8,128)(2,1)}, bf16[1024,1408]{1,0:T(8,128)(2,1)S(1)}, u32[]{:S(2)}) copy-start(bf16[1024,1408]{1,0:T(8,128)(2,1)S(1)} %get-tuple-element.166) | copy-start | bytes 8650756
  507.6 17.4 %copy-start.42 = (bf16[2048,1408]{1,0:T(8,128)(2,1)S(1)}, bf16[2048,1408]{1,0:T(8,128)(2,1)}, u32[]{:S(2)}) copy-start(bf16[2048,1408]{1,0:T(8,128)(2,1)} %all-gather.19.cloned.1.call-done) | copy-start | bytes 17301508
  535.6 220.8 %all-gather.25.cloned.1.call-start = ((), (), s32[]{:S(2)}) async-start(), calls=%async_computation.23 | async-start | bytes 2359296 | tf_op jit(solution)/shard_map/all_gather | solution.py:732
  721.4 207.8 %reduce-scatter.18.cloned.1.call-start = ((), (), s32[]{:S(2)}) async-start(), calls=%async_computation.20 | async-start | bytes 6488064 | tf_op jit(solution)/shard_map/reduce_scatter | solution.py:624
  732.6 198.8 %reduce-scatter.16.cloned.1.call-start = ((), (), s32[]{:S(2)}) async-start(), calls=%async_computation.19 | async-start | bytes 6488064 | tf_op jit(solution)/shard_map/reduce_scatter | solution.py:624
  743.7 193.5 %reduce-scatter.20.cloned.1.call-start = ((), (), s32[]{:S(2)}) async-start(), calls=%async_computation.21 | async-start | bytes 6488064 | tf_op jit(solution)/shard_map/reduce_scatter | solution.py:624
  754.3 221.0 %reduce-scatter.12.cloned.1.call-start = ((), (), s32[]{:S(2)}) async-start(), calls=%async_computation.17 | async-start | bytes 589824 | tf_op jit(solution)/shard_map/reduce_scatter | solution.py:624
  756.4 56.4 %copy-start.14 = (bf16[1024,2048]{1,0:T(8,128)(2,1)S(1)}, bf16[1024,2048]{1,0:T(8,128)(2,1)}, u32[]{:S(2)}) copy-start(bf16[1024,2048]{1,0:T(8,128)(2,1)} %param.21) | copy-start | bytes 12582916
  756.4 56.4 %copy-start.28 = (f32[1024]{0:T(1024)S(1)}, f32[1024]{0:T(1024)}, u32[]{:S(2)}) copy-start(f32[1024]{0:T(1024)} %copy-done.27) | copy-start | bytes 12292
  756.4 56.4 %copy-start.30 = (f32[2048]{0:T(1024)S(1)}, f32[2048]{0:T(1024)}, u32[]{:S(2)}) copy-start(f32[2048]{0:T(1024)} %param.23) | copy-start | bytes 24580
  816.2 213.6 %reduce-scatter.14.cloned.1.call-start = ((), (), s32[]{:S(2)}) async-start(), calls=%async_computation.18 | async-start | bytes 4718592 | tf_op jit(solution)/shard_map/reduce_scatter | solution.py:624
  832.0 252.8 %reduce-scatter.10.cloned.1.call-start = ((), (), s32[]{:S(2)}) async-start(), calls=%async_computation.16 | async-start | bytes 4718592 | tf_op jit(solution)/shard_map/reduce_scatter | solution.py:624
  842.0 11.4 copy-start.44
  842.0 12.9 copy-start.11
  842.0 537.4 %all-reduce.13.cloned.1.call-start = ((), (), s32[]{:S(2)}) async-start(), calls=%async_computation.24 | async-start | bytes 16777216 | tf_op jit(solution)/shard_map/psum | solution.py:742
  842.3 12.7 copy-start.43
  853.4 6.1 collective-permute-start.1
  859.6 12.9 copy-start.40
  859.6 12.9 copy-start.20
  859.6 12.9 copy-start.22
  875.8 577.3 %reduce-scatter.8.cloned.1.call-start = ((), (), s32[]{:S(2)}) async-start(), calls=%async_computation.15 | async-start | bytes 9437184 | tf_op jit(solution)/shard_map/reduce_scatter | solution.py:624
  890.5 38.5 %copy-start.35 = (f32[16,128]{1,0:T(8,128)S(1)}, f32[16,128]{1,0:T(8,128)}, u32[]{:S(2)}) copy-start(f32[16,128]{1,0:T(8,128)} %get-tuple-element.51) | copy-start | bytes 24580
  890.5 38.6 %copy-start.23 = (f32[32,2048]{1,0:T(8,128)S(1)}, f32[32,2048]{1,0:T(8,128)}, u32[]{:S(2)}) copy-start(f32[32,2048]{1,0:T(8,128)} %get-tuple-element.52) | copy-start | bytes 786436
  1031.0 353.4 %copy-start.31 = (bf16[2048]{0:T(1024)(128)(2,1)S(1)}, bf16[2048]{0:T(1024)(128)(2,1)}, u32[]{:S(2)}) copy-start(bf16[2048]{0:T(1024)(128)(2,1)} %get-tuple-element.154) | copy-start | bytes 12292
  (21 other events, 96.5 us)
Sparse Core Ops, SparseCore 0:
  12.1 57.0 all-gather.10
  71.7 36.8 all-gather.12
  121.4 35.3 all-gather.22
  159.1 37.4 all-gather.14
  198.8 44.3 all-gather.20
  246.0 154.9 all-reduce.8
  403.7 42.3 all-gather.16
  448.7 43.3 all-gather.18
  535.7 154.9 all-reduce.10
  721.5 26.8 all-gather.24
  751.9 59.0 reduce-scatter.17
  815.3 59.1 reduce-scatter.15
  877.9 59.2 reduce-scatter.19
  941.0 34.2 reduce-scatter.11
  978.5 51.3 reduce-scatter.13
  1033.5 51.3 reduce-scatter.9
  1087.8 291.5 all-reduce.12
  1382.7 70.2 reduce-scatter.7

commit v2 on v1

--- a/solution.py
+++ b/solution.py
@@ -612,6 +612,275 @@
     return meta, edge_meta, segrow
 
 
+ROWS = 128
+PIECE = 32
+HOP = 2
+AHEAD = 2
+RING = AHEAD + 1
+
+
+def line_scratch(length, width):
+    pieces = length // PIECE
+    return [
+        pltpu.VMEM((RING, ROWS, width), low),
+        pltpu.VMEM((length, width), low),
+        pltpu.VMEM((length, width), low),
+        pltpu.VMEM((length, width), low),
+        pltpu.VMEM((length, width), low),
+        pltpu.SemaphoreType.DMA((pieces,)),
+        pltpu.SemaphoreType.DMA((pieces,)),
+        pltpu.SemaphoreType.DMA((pieces,)),
+        pltpu.SemaphoreType.DMA((pieces,)),
+    ]
+
+
+def line_sum(step, last, compute, finish, scratch):
+    own, from_left, from_right, to_right, to_left, got_left, got_right, sent_right, sent_left = scratch
+    place = lax.axis_index("head")
+    length, width = from_left.shape
+    blocks, pieces, each = length // ROWS, length // PIECE, ROWS // PIECE
+    left_there, right_there = place > 0, place < last
+
+    def rows(piece):
+        return pl.ds(pl.multiple_of(piece * PIECE, PIECE), PIECE)
+
+    def hop(piece, rightwards):
+        src, dst, sent, got, to = (
+            (to_right, from_left, sent_right, got_left, place + 1)
+            if rightwards
+            else (to_left, from_right, sent_left, got_right, place - 1)
+        )
+        return pltpu.make_async_remote_copy(
+            src_ref=src.at[rows(piece)],
+            dst_ref=dst.at[rows(piece)],
+            send_sem=sent.at[piece],
+            recv_sem=got.at[piece],
+            device_id={"head": to},
+            device_id_type=pl.DeviceIdType.MESH,
+        )
+
+    def own_piece(piece):
+        slot = lax.rem(piece // each, RING)
+        first = pl.multiple_of(lax.rem(piece, each) * PIECE, PIECE)
+        return own[slot, pl.ds(first, PIECE), :].astype(full)
+
+    @pl.when(step == 0)
+    def _():
+        barrier = pltpu.get_barrier_semaphore()
+        for there, to in ((left_there, place - 1), (right_there, place + 1)):
+
+            @pl.when(there)
+            def _(to=to):
+                pl.semaphore_signal(
+                    barrier, inc=1, device_id={"head": to}, device_id_type=pl.DeviceIdType.MESH
+                )
+
+        pl.semaphore_wait(barrier, jnp.minimum(place, 1) + jnp.minimum(last - place, 1))
+
+        @pl.when(place == 0)
+        def _():
+            from_left[...] = jnp.zeros_like(from_left)
+
+        @pl.when(place == last)
+        def _():
+            from_right[...] = jnp.zeros_like(from_right)
+
+    @pl.when(step < blocks)
+    def _():
+        own[lax.rem(step, RING)] = compute().astype(low)
+
+    def one(q, carry):
+        now = step * each + q
+        for rightwards in (True, False):
+            came, more = (left_there, right_there) if rightwards else (right_there, left_there)
+            source = from_left if rightwards else from_right
+            target = to_right if rightwards else to_left
+            piece = now - HOP * (place if rightwards else last - place)
+
+            @pl.when((piece >= 0) & (piece < pieces))
+            def _():
+                @pl.when(came)
+                def _():
+                    hop(piece, rightwards).wait_recv()
+
+                @pl.when(more)
+                def _():
+                    target[rows(piece), :] = (
+                        own_piece(piece) + source[rows(piece), :].astype(full)
+                    ).astype(low)
+                    hop(piece, rightwards).start()
+
+        return carry
+
+    lax.fori_loop(0, each, one, 0)
+
+    @pl.when(step >= AHEAD)
+    def _():
+        block = step - AHEAD
+        span = pl.ds(pl.multiple_of(block * ROWS, ROWS), ROWS)
+        finish(
+            own[lax.rem(block, RING)].astype(full)
+            + from_left[span, :].astype(full)
+            + from_right[span, :].astype(full)
+        )
+
+    @pl.when(step == blocks + AHEAD - 1)
+    def _():
+        def settle(piece, carry):
+            @pl.when(right_there)
+            def _():
+                hop(piece, True).wait_send()
+
+            @pl.when(left_there)
+            def _():
+                hop(piece, False).wait_send()
+
+            return carry
+
+        lax.fori_loop(0, pieces, settle, 0)
+
+
+def line_call(kernel, name, collective, length, width, resident, entering, leaving, outs, flops):
+    blocks = length // ROWS
+
+    def spec(array, stage):
+        if stage == "first":
+            return pl.BlockSpec((ROWS, array.shape[1]), lambda g: (jnp.minimum(g, blocks - 1), 0))
+        if stage == "second":
+            return pl.BlockSpec((ROWS, array.shape[1]), lambda g: (jnp.maximum(g - AHEAD, 0), 0))
+        rank = len(array.shape)
+        return pl.BlockSpec(array.shape, lambda g: (0,) * rank, pipeline_mode=pl.Buffered(1))
+
+    in_specs = [
+        pl.BlockSpec(memory_space=pltpu.SMEM) if a.dtype == jnp.int32 else spec(a, "all")
+        for a in resident
+    ]
+    in_specs += [spec(a, "first") for a in entering] + [spec(a, "second") for a in leaving]
+    shapes = [jax.ShapeDtypeStruct(shape, dtype) for shape, dtype, _ in outs]
+    return pl.pallas_call(
+        kernel,
+        grid=(blocks + AHEAD,),
+        in_specs=in_specs,
+        out_specs=[
+            spec(s, stage) if stage != "all" else pl.BlockSpec(s.shape, lambda g, r=len(s.shape): (0,) * r)
+            for s, (_, _, stage) in zip(shapes, outs)
+        ],
+        out_shape=shapes,
+        scratch_shapes=line_scratch(length, width),
+        compiler_params=pltpu.CompilerParams(
+            collective_id=collective, has_side_effects=True, vmem_limit_bytes=60 * MIB
+        ),
+        cost_estimate=pl.CostEstimate(flops=flops, bytes_accessed=40 * MIB, transcendentals=0),
+        name=name,
+    )(*resident, *entering, *leaving)
+
+
+def mixer_out_kernel(heads, key, value, last, place_ref, ends_ref, w_out_ref, head_gain_ref, gain_ref,
+                     local_ref, through_ref, gate_ref, tokens_ref,
+                     y_ref, mixed_ref, state_ref, middle_ref, second_ref, *scratch):
+    step = pl.program_id(0)
+
+    @pl.when(step == 0)
+    def _():
+        state_ref[...] = jnp.zeros_like(state_ref)
+
+        def one(j, carry):
+            for h in range(heads):
+                part = ends_ref[j, h]
+                state_ref[h] = mm(part[:, value:], state_ref[h]) + part[:, :value].astype(full)
+            return carry
+
+        lax.fori_loop(0, lax.axis_index("seq"), one, 0)
+
+    def compute():
+        for h in range(heads):
+            cols = slice(h * value, (h + 1) * value)
+            o = local_ref[:, cols] + mm(through_ref[:, h * key : (h + 1) * key], state_ref[h])
+            mixed_ref[:, cols] = o
+            s3 = lax.rsqrt(jnp.mean(o * o, axis=-1, keepdims=True) + 1e-05)
+            gz = gate_ref[:, cols]
+            y_ref[:, cols] = (o * s3 * head_gain_ref[0:1, :] * (gz * sigmoid(gz))).astype(low)
+        return mm_nt(y_ref[...], w_out_ref[...])
+
+    def finish(total):
+        middle = tokens_ref[...].astype(full) + total
+        middle_ref[...] = middle
+        scale = lax.rsqrt(jnp.mean(middle * middle, axis=-1, keepdims=True) + 1e-06)
+        second_ref[...] = (middle * scale * gain_ref[0:1, :]).astype(low)
+
+    line_sum(step, last, compute, finish, scratch)
+
+
+def ffn_kernel(last, w_gate_ref, w_up_ref, w_down_ref, gain_ref,
+               second_ref, cot_ref, middle_ref, cot_late_ref,
+               hidden_ref, dgate_ref, dup_ref, partial_ref, dmiddle_ref, dlow_ref, gain_grad_ref,
+               *scratch):
+    step = pl.program_id(0)
+
+    @pl.when(step == 0)
+    def _():
+        gain_grad_ref[...] = jnp.zeros_like(gain_grad_ref)
+
+    def compute():
+        h2 = second_ref[...]
+        fg = mm(h2, w_gate_ref[...])
+        fu = mm(h2, w_up_ref[...])
+        sig = sigmoid(fg)
+        swish = fg * sig
+        hidden = (swish * fu).astype(low)
+        hidden_ref[...] = hidden
+        partial_ref[...] = mm_nt(hidden, w_down_ref[...]).astype(low)
+        dhid = mm(cot_ref[...], w_down_ref[...])
+        dfg = (dhid * fu * (sig * (1.0 + fg * (1.0 - sig)))).astype(low)
+        dfu = (dhid * swish).astype(low)
+        dgate_ref[...] = dfg
+        dup_ref[...] = dfu
+        return mm_nt(dfg, w_gate_ref[...]) + mm_nt(dfu, w_up_ref[...])
+
+    def finish(grad):
+        middle = middle_ref[...]
+        scale = lax.rsqrt(jnp.mean(middle * middle, axis=-1, keepdims=True) + 1e-06)
+        norm = middle * scale
+        gain_grad_ref[...] += jnp.sum((grad * norm).reshape(ROWS // 8, 8, -1), axis=0)
+        weighted = grad * gain_ref[0:1, :]
+        dm = cot_late_ref[...].astype(full) + scale * (
+            weighted - norm * jnp.mean(weighted * norm, axis=-1, keepdims=True)
+        )
+        dmiddle_ref[...] = dm
+        dlow_ref[...] = dm.astype(low)
+
+    line_sum(step, last, compute, finish, scratch)
+
+
+def input_grad_kernel(last, w_in_ref, w_gate_ref, w_small_ref, gain_ref,
+                      dpre_ref, dgz_ref, dab_ref, tokens_ref, dmiddle_ref,
+                      dtokens_ref, gain_grad_ref, *scratch):
+    step = pl.program_id(0)
+
+    @pl.when(step == 0)
+    def _():
+        gain_grad_ref[...] = jnp.zeros_like(gain_grad_ref)
+
+    def compute():
+        return (
+            mm_nt(dpre_ref[...], w_in_ref[...])
+            + mm_nt(dgz_ref[...], w_gate_ref[...])
+            + mm_nt(dab_ref[...], w_small_ref[...])
+        )
+
+    def finish(grad):
+        stream = tokens_ref[...].astype(full)
+        scale = lax.rsqrt(jnp.mean(stream * stream, axis=-1, keepdims=True) + 1e-06)
+        norm = stream * scale
+        gain_grad_ref[...] += jnp.sum((grad * norm).reshape(ROWS // 8, 8, -1), axis=0)
+        weighted = grad * gain_ref[0:1, :]
+        dtokens_ref[...] = dmiddle_ref[...] + scale * (
+            weighted - norm * jnp.mean(weighted * norm, axis=-1, keepdims=True)
+        )
+
+    line_sum(step, last, compute, finish, scratch)
+
+
 def rms_scale(array, epsilon):
     return lax.rsqrt(jnp.mean(array * array, axis=-1, keepdims=True) + epsilon)
 
@@ -692,39 +961,28 @@
     )
     ends = lax.all_gather(end, "seq")
     gain = head_gain[None, :]
-    mix_out, mixed, state_in = chain_output(
-        place, ends, local, through, gate_pre, gain, heads, key, value
-    )
-    middle = stream + lax.psum(mm_nt(mix_out, w_out).astype(low), "head").astype(full)
-    second_scale = rms_scale(middle, 1e-06)
-    second_norm = middle * second_scale
-    second_in = (second_norm * ffn_gain).astype(low)
-    gate_act = mm(second_in, w_widen)
-    lift_act = mm(second_in, w_lift)
-    sigma = jax.nn.sigmoid(gate_act)
-    swish = gate_act * sigma
-    hidden = (swish * lift_act).astype(low)
-    result = (
-        middle + lax.psum(mm_nt(hidden, w_narrow).astype(low), "head").astype(full)
-    ).astype(low)
-
-    grad_out = cotangent.astype(full)
-    hidden_grad = mm(cotangent, w_narrow)
-    gate_grad = (hidden_grad * lift_act * sigma * (1.0 + gate_act * (1.0 - sigma))).astype(low)
-    lift_grad = (hidden_grad * swish).astype(low)
-    second_grad = lax.psum(
-        (mm_nt(gate_grad, w_widen) + mm_nt(lift_grad, w_lift)).astype(low), "head"
-    ).astype(full)
+    last = lax.axis_size("head") - 1
+    width = tokens.shape[1]
+    mix_out, mixed, state_in, middle, second_in = line_call(
+        partial(mixer_out_kernel, heads, key, value, last), "mixer_out", 0, length, width,
+        [place, ends, w_out, gain, ffn_gain[None, :]], [local, through, gate_pre], [tokens],
+        [((length, vals), low, "first"), ((length, vals), full, "first"),
+         ((heads, key, value), full, "all"), ((length, width), full, "second"),
+         ((length, width), low, "second")],
+        2 * length * vals * width,
+    )
+    hidden, gate_grad, lift_grad, narrow_part, middle_grad, middle_low, ffn_gain_part = line_call(
+        partial(ffn_kernel, last), "ffn", 1, length, width,
+        [w_widen, w_lift, w_narrow, ffn_gain[None, :]], [second_in, cotangent], [middle, cotangent],
+        [((length, hidden_size), low, "first")] * 3
+        + [((length, width), low, "first"), ((length, width), full, "second"),
+           ((length, width), low, "second"), ((8, width), full, "all")],
+        12 * length * width * hidden_size,
+    )
+    result = (middle + lax.psum(narrow_part, "head").astype(full)).astype(low)
     narrow_wgrad = scatter(mm_tn(cotangent, hidden)).T
     widen_wgrad = scatter(mm_tn(second_in, gate_grad))
     lift_wgrad = scatter(mm_tn(second_in, lift_grad))
-    second_weighted = second_grad * ffn_gain
-    ffn_gain_part = jnp.sum(second_grad * second_norm, axis=0)
-    middle_grad = grad_out + second_scale * (
-        second_weighted
-        - second_norm * jnp.mean(second_weighted * second_norm, axis=-1, keepdims=True)
-    )
-    middle_low = middle_grad.astype(low)
     mix_grad = mm(middle_low, w_out)
     gate_pgrad, mixed_grad, head_gain_part, adjoint = gate_back(
         mix_grad, mixed, gate_pre, gain, through, heads, key, value
@@ -737,27 +995,23 @@
         mixed_grad, ends, adjoints, heads, key, value,
     )
     halo = passed_along(halo, "seq", -1)
-    last = pre_grad[length - 8 :].astype(full) + halo
-    pre_grad = lax.dynamic_update_slice(pre_grad, last.astype(low), (length - 8, 0))
-    first_grad = lax.psum(
-        (
-            mm_nt(pre_grad, w_in) + mm_nt(gate_pgrad, w_gate) + mm_nt(ab_grad, w_small)
-        ).astype(low),
-        "head",
-    ).astype(full)
+    tail = pre_grad[length - 8 :].astype(full) + halo
+    pre_grad = lax.dynamic_update_slice(pre_grad, tail.astype(low), (length - 8, 0))
+    tokens_grad, mixer_gain_part = line_call(
+        partial(input_grad_kernel, last), "input_grad", 2, length, width,
+        [w_in, w_gate, w_small, mixer_gain[None, :]], [pre_grad, gate_pgrad, ab_grad],
+        [tokens, middle_grad],
+        [((length, width), full, "second"), ((8, width), full, "all")],
+        2 * length * width * (2 * keys + 2 * vals + LANES),
+    )
     in_wgrad = scatter(mm_tn(first_in, pre_grad))
     small_wgrad = scatter(mm_tn(first_in, ab_grad))
-    first_weighted = first_grad * mixer_gain
-    mixer_gain_part = jnp.sum(first_grad * first_norm, axis=0)
-    tokens_grad = middle_grad + first_scale * (
-        first_weighted - first_norm * jnp.mean(first_weighted * first_norm, axis=-1, keepdims=True)
-    )
     taps_part = jnp.sum(taps_part.reshape(4, 8, -1), axis=1)
     params_part = jnp.sum(params_part.reshape(2, 8, LANES), axis=1)
     mixer_gain_grad, ffn_gain_grad, taps_grad, params_grad = lax.psum(
         (
-            mixer_gain_part.astype(low),
-            ffn_gain_part.astype(low),
+            jnp.sum(mixer_gain_part, axis=0).astype(low),
+            jnp.sum(ffn_gain_part, axis=0).astype(low),
             taps_part.astype(low),
             params_part.astype(low),
         ),

time: 1470 us -> 1110 us (0.76)
  waiting for transfers between devices: 954 us -> 348 us
  Pallas kernels: 106 us -> 482 us
  matrix products: 220 us -> 104 us
  other arithmetic: 70.8 us -> 36.5 us
    psum x3 -> x1, waiting for transfers between devices: 594 us -> 0.01 us  [shards(): result = (middle + lax.psum(narrow_part, 'head').astype(full)).astype(low)]
    pallas_call x1 -> x3, Pallas kernels: 7.74 us -> 386 us  [line_call(): pl.pallas_call(kernel, grid=(blocks + AHEAD,), in_specs=in_specs, out_spe...]
    dot_general x7 -> x0, matrix products: 67.9 us -> none  [mm_nt(): lax.dot_general(a.astype(low), b.astype(low), (((1,), (1,)), ((), ())), p...]
    reduce_scatter x7, waiting for transfers between devices: 168 us -> 217 us  [scatter(): lax.psum_scatter(grad.astype(low), 'seq', scatter_dimension=0, tiled=True)]
    dot_general x7 -> x4, matrix products: 76.4 us -> 33.9 us  [mm(): return jnp.dot(a.astype(low), b.astype(low), preferred_element_type=full)]
    all_gather x1, waiting for transfers between devices: 35 us -> 0.02 us  [shards(): w_widen = lax.all_gather(ffn_gate.astype(low), 'seq', axis=0, tiled=True)]
    all_gather x1, waiting for transfers between devices: 34.3 us -> 0.02 us  [shards(): w_lift = lax.all_gather(ffn_up.astype(low), 'seq', axis=0, tiled=True)]
    all_gather x1, waiting for transfers between devices: 0.01 us -> 23.1 us  [shards(): adjoints = lax.all_gather(adjoint.astype(low), 'seq')]
  transfers between devices with their start and end apart: 20 -> 18, of which waited for: 15 -> 11; matrix products, arithmetic and copies ran while one was open for 16% -> 12% of each run, Pallas kernels for 7% -> 29%
where the time goes in v2:
time: 1110 us; the launch traced here: 1100 us
  Pallas kernels  482 us (43%)
  waiting for transfers between devices  348 us (31%)
  matrix products  104 us (9%)
  blocking collectives  77.2 us (7%)
  other arithmetic  36.5 us (3%)
  local copies, waits for them, and re-layouts  33.5 us (3%)
  between operations  14.7 us (1%)
    pallas_call x3, Pallas kernels, line_call(): pl.pallas_call(kernel, grid=(blocks + AHEAD,), in_specs=in_specs, out_spe...  386 us
    reduce_scatter x7, waiting for transfers between devices, scatter(): lax.psum_scatter(grad.astype(low), 'seq', scatter_dimension=0, tiled=True)  217 us
    dot_general x7, matrix products, mm_tn(): lax.dot_general(a.astype(low), b.astype(low), (((0,), (0,)), ((), ())), p...  69.7 us
    pallas_call x1, Pallas kernels, backward_chain(): pl.pallas_call(partial(backward_kernel, heads, key, value, ends.shape[0])...  54.7 us
    psum x1, blocking collectives, shards(): head_gain_grad = lax.psum(jnp.sum(head_gain_part, axis=0), ('seq', 'head'))  42.2 us
    all_gather x1, waiting for transfers between devices, gather(): lax.all_gather(jnp.concatenate(parts, axis=1), 'seq', axis=0, tiled=True)  36.9 us
    pallas_call x1, Pallas kernels, forward_chain(): pl.pallas_call(partial(forward_kernel, heads, key, value), grid=(blocks,)...  34.5 us
    all_gather x1, waiting for transfers between devices, shards(): ends = lax.all_gather(end, 'seq')  34.1 us
  transfers between devices with their start and end apart: 18, of which 11 were waited for; matrix products, arithmetic and copies ran while one was open for 12% of the time, Pallas kernels for 29%

profile of v2, /device:TPU:0, one launch (start us, length us, event | category | flops | bytes accessed | tf_op | source)
XLA Modules:
  0.0 1101.0 jit_solution(7340813247033662133)
XLA Ops:
  9.6 1.3 convert_element_type.156
  15.4 12.6 %all_gather.34.w_small_ref = bf16[2048,128]{1,0:T(8,128)(2,1)S(1)} all-gather(bf16[256,128]{1,0:T(8,128)(2,1)S(1)} %maximum_maximum_fusion), channel_id=1, replica_groups=mesh['seq'=8,'head'=4] {'seq'}, dimensions={0}, use_global_device_ids=true | all-gather | bytes 589824 | tf_op jit(solution)/shard_map/all_gather | solution.py:940
  28.0 3.3 fusion
  31.4 1.3 fusion.24.ab_ref
  32.8 36.9 %all-gather.11.cloned.1.call-done.w_in_ref = bf16[2048,2048]{1,0:T(8,128)(2,1)} async-done(((bf16[256,2048]{1,0:T(8,128)(2,1)}), bf16[2048,2048]{1,0:T(8,128)(2,1)}) %all-gather.11.cloned.1.call-update) | async-done | bytes 8388624 | tf_op jit(solution)/shard_map/all_gather | solution.py:889
  69.6 12.6 %convolution_convert_fusion.4.pre_ref.tail_ref = bf16[1024,2048]{1,0:T(8,128)(2,1)S(1)} fusion(bf16[2048,2048]{1,0:T(8,128)(2,1)} %all-gather.11.cloned.1.call-done.w_in_ref, bf16[1024,2048]{1,0:T(8,128)(2,1)} %tokens_ref.3, f32[2048]{0:T(1024)S(1)} %copy-done.29, f32[1024]{0:T(1024)S(1)} %add_rsqrt_fusion), kind=kOutput, calls=%fused_computation.11 | convolution fusion | flops 8600420352 | bytes 16789504 | tf_op jit(solution)/shard_map/dot_general | solution.py:18
  82.3 2.4 collective-permute-start
  85.6 34.5 %chain_forward.1 = (f32[1024,1024]{1,0:T(8,128)}, bf16[1024,512]{1,0:T(8,128)(2,1)S(1)}, bf16[8,4,128,384]{3,2,1,0:T(8,128)(2,1)}, bf16[8,4,128,128]{3,2,1,0:T(8,128)(2,1)S(1)}, bf16[4,128,384]{2,1,0:T(8,128)(2,1)}) custom-call(bf16[1024,2048]{1,0:T(8,128)(2,1)} %copy-done.12, f32[1024,128]{1,0:T(8,128)S(1)} %fusion.24.ab_ref, ...), custom_call_target="tpu_custom_call" | custom-call | tf_op jit(solution)/shard_map/chain_forward/pallas_call | solution.py:206
  123.2 2.3 convert_element_type.164
  125.6 2.5 copy.128
  128.6 10.0 fusion.22.gate_ref
  138.6 9.6 all-gather.13.cloned.1.call-done.w_out_ref
  148.2 34.1 %all-gather.23.cloned.1.call-done = bf16[32,128,384]{2,1,0:T(8,128)(2,1)} async-done(((bf16[4,128,384]{2,1,0:T(8,128)(2,1)}), bf16[32,128,384]{2,1,0:T(8,128)(2,1)}) %all-gather.23.cloned.1.call-update) | async-done | bytes 3145744 | tf_op jit(solution)/shard_map/all_gather | solution.py:962
  182.3 112.9 %mixer_out.1 = (bf16[1024,1024]{1,0:T(8,128)(2,1)}, f32[1024,1024]{1,0:T(8,128)}, f32[4,128,256]{2,1,0:T(8,128)}, f32[1024,2048]{1,0:T(8,128)}, bf16[1024,2048]{1,0:T(8,128)(2,1)}) custom-call(s32[1]{0:T(128)} %bitcast.place_ref, bf16[8,4,128,384]{3,2,1,0:T(8,128)(2,1)} %bitcast.83, bf16[2048,1024]{1,0:T(8,128)(2,1)} %all-gather.13.cloned.1.call-done.w_out_ref, ...), custom_call_target="tpu_custom_call" | custom-call | flops 4294967296 | bytes 41943040 | tf_op jit(solution)/shard_map/mixer_out/pallas_call | solution.py:760
  295.3 24.1 %all-gather.21.cloned.1.call-done.w_down_ref = bf16[2048,1408]{1,0:T(8,128)(2,1)} async-done(((bf16[256,1408]{1,0:T(8,128)(2,1)}), bf16[2048,1408]{1,0:T(8,128)(2,1)}) %all-gather.21.cloned.1.call-update) | async-done | bytes 5767184 | tf_op jit(solution)/shard_map/all_gather | solution.py:945
  319.4 150.3 %ffn.1 = (bf16[1024,1408]{1,0:T(8,128)(2,1)}, bf16[1024,1408]{1,0:T(8,128)(2,1)}, bf16[1024,1408]{1,0:T(8,128)(2,1)}, bf16[1024,2048]{1,0:T(8,128)(2,1)}, f32[10...) custom-call(bf16[2048,1408]{1,0:T(8,128)(2,1)} %all-gather.17.cloned.1.call-done.w_gate_ref, ...), custom_call_target="tpu_custom_call" | custom-call | flops 35433480192 | bytes 41943040 | tf_op jit(solution)/shard_map/ffn/pallas_call | solution.py:760
  469.7 10.0 fusion.30.dy_ref
  479.8 7.5 gate_back.1
  487.2 1.3 copy-done.3
  491.6 23.1 %all-gather.25.cloned.1.call-done = bf16[32,128,256]{2,1,0:T(8,128)(2,1)} async-done(((bf16[4,128,256]{2,1,0:T(8,128)(2,1)}), bf16[32,128,256]{2,1,0:T(8,128)(2,1)}) %all-gather.25.cloned.1.call-update) | async-done | bytes 2097168 | tf_op jit(solution)/shard_map/all_gather | solution.py:990
  514.7 54.7 %chain_backward.1 = (bf16[1024,2048]{1,0:T(8,128)(2,1)}, bf16[1024,128]{1,0:T(8,128)(2,1)}, f32[8,2048]{1,0:T(8,128)}, f32[32,2048]{1,0:T(8,128)}, f32[16,128]{1,0:T(8,128)}) custom-call(s32[1]{0:T(128)} %bitcast.place_ref, bf16[1024,2048]{1,0:T(8,128)(2,1)} %copy-done.12, bf16[1024,2048]{1,0:T(8,128)(2,1)} %copy-done.12, f32[1024,128]{1,0:T(8,128)} %copy-done.4, ...), custom_call_target="tpu_custom_call" | custom-call | tf_op jit(solution)/shard_map/chain_backward/pallas_call | solution.py:541
  569.3 3.4 convolution_convert_fusion.7
  572.8 9.4 convolution_convert_fusion.5
  582.3 9.4 convolution_convert_fusion.6
  591.7 1.7 copy-done.34
  593.5 11.0 convolution_convert_fusion.2
  604.5 1.7 copy-done.33
  606.3 10.9 convolution_convert_fusion.1
  617.2 1.7 copy-done.32
  619.0 11.3 %fusion.3 = bf16[2048,1408]{0,1:T(8,128)(2,1)} fusion(bf16[1024,1408]{1,0:T(8,128)(2,1)S(1)} %copy-done.32, bf16[1024,2048]{1,0:T(8,128)(2,1)} %cot_late_ref.1), kind=kOutput, calls=%fused_computation.10 | convolution fusion | flops 5908463616 | bytes 12845056 | tf_op jit(solution)/shard_map/dot_general | solution.py:28
  632.4 1.8 collective-permute-done.1
  634.2 1.4 fusion.4.dpre_ref
  635.6 14.4 %convolution_convert_fusion.3 = bf16[2048,2048]{1,0:T(8,128)(2,1)} fusion(bf16[1024,2048]{1,0:T(8,128)(2,1)} %fusion.4.dpre_ref, bf16[1024,2048]{1,0:T(8,128)(2,1)} %tokens_ref.3, f32[2048]{0:T(1024)S(1)} %copy-done.29, f32[1024]{0:T(1024)S(1)} %add_rsqrt_fusion), kind=kOutput, calls=%fused_computation.9 | convolution fusion | flops 8602517504 | bytes 16789504 | tf_op jit(solution)/shard_map/dot_general | solution.py:28
  650.9 42.2 %psum.46 = f32[256]{0:T(256)} all-reduce(f32[256]{0:T(256)S(1)} %reduce_sum.68), channel_id=1, replica_groups=mesh['seq'=8,'head'=4] {'seq','head'}, use_global_device_ids=true, to_apply=%region_14.15 | all-reduce | flops 256 | bytes 2048 | tf_op jit(solution)/shard_map/psum | solution.py:1020
  693.2 122.6 %input_grad.1 = (f32[1024,2048]{1,0:T(8,128)}, f32[8,2048]{1,0:T(8,128)}) custom-call(bf16[2048,2048]{1,0:T(8,128)(2,1)} %all-gather.11.cloned.1.call-done.w_in_ref, bf16[2048,1024]{1,0:T(8,128)(2,1)} %all-gather.15.cloned.1.call-done.w_gate_ref, bf16[2048,128]{1,0:T(8,128)(2,1)} %copy-done.18, f32[1,2048]{1,0:T(1,128)} %bitcast.100, ...), custom_call_target="tpu_custom_call" | custom-call | flops 13421772800 | bytes 41943040 | tf_op jit(solution)/shard_map/input_grad/pallas_call | solution.py:760
  816.6 22.4 %all-reduce.3 = (bf16[4,2048]{1,0:T(4,128)(2,1)S(1)}, bf16[2048]{0:T(1024)(128)(2,1)S(1)}, bf16[2,128]{1,0:T(2,128)(2,1)S(1)}, bf16[2048]{0:T(1024)(128)(2,1)S(1)}) all-reduce(bf16[4,2048]{1,0:T(4,128)(2,1)S(1)} %bitcast_reduce_fusion, bf16[2048]{0:T(1024)(128)(2,1)S(1)} %reduce_sum.65, ...), channel_id=1, replica_groups=mesh['seq'=8,'head'=4] {'seq'}, use_global_device_ids=true, to_apply=%region_12.13 | all-reduce | flops 12544 | bytes 50176 | tf_op jit(solution)/shard_map/psum | solution.py:1011
  842.0 9.2 add_convert_fusion
  856.0 2.1 convert_element_type.178
  858.1 23.3 %reduce-scatter.16.cloned.1.call-done = bf16[256,1408]{1,0:T(8,128)(2,1)} async-done(((bf16[2048,1408]{1,0:T(8,128)(2,1)}), bf16[256,1408]{1,0:T(8,128)(2,1)}) %reduce-scatter.16.cloned.1.call-update) | async-done | bytes 720912 | tf_op jit(solution)/shard_map/reduce_scatter | solution.py:893
  881.4 2.3 convert_element_type.189
  883.7 60.5 %reduce-scatter.18.cloned.1.call-done = bf16[256,1408]{1,0:T(8,128)(2,1)} async-done(((bf16[2048,1408]{1,0:T(8,128)(2,1)}), bf16[256,1408]{1,0:T(8,128)(2,1)}) %reduce-scatter.18.cloned.1.call-update) | async-done | bytes 720912 | tf_op jit(solution)/shard_map/reduce_scatter | solution.py:893
  944.1 2.3 convert_element_type.191
  946.4 60.1 %reduce-scatter.20.cloned.1.call-done = bf16[256,1408]{0,1:T(8,128)(2,1)} async-done(((bf16[2048,1408]{0,1:T(8,128)(2,1)}), bf16[256,1408]{0,1:T(8,128)(2,1)}) %reduce-scatter.20.cloned.1.call-update) | async-done | bytes 720912 | tf_op jit(solution)/shard_map/reduce_scatter | solution.py:893
  1006.5 2.3 convert_bitcast_fusion
  1008.8 73.3 %reduce-scatter.8.cloned.1.call-done = bf16[256,2048]{1,0:T(8,128)(2,1)} async-done(((bf16[2048,2048]{1,0:T(8,128)(2,1)}), bf16[256,2048]{1,0:T(8,128)(2,1)}) %reduce-scatter.8.cloned.1.call-update) | async-done | bytes 1048592 | tf_op jit(solution)/shard_map/reduce_scatter | solution.py:893
  1082.1 2.1 slice.130
  1084.2 2.1 fusion.27
  1086.4 7.9 copy.146
  (167 shorter events, 26.2 us)
Async XLA Ops:
  7.2 4.9 copy-start.16
  7.2 5.9 copy-start.17
  7.2 62.4 %all-gather.11.cloned.1.call-start = ((), (), s32[]{:S(2)}) async-start(), calls=%async_computation.7 | async-start | bytes 9437184 | tf_op jit(solution)/shard_map/all_gather | solution.py:889
  9.6 4.6 copy-start.25
  9.6 4.6 copy-start.26
  9.6 4.6 copy-start.30
  9.6 5.7 copy-start.22
  9.6 5.7 copy-start.23
  9.6 5.7 copy-start.21
  10.9 17.1 %copy-start.31 = (f32[4]{0:T(128)S(1)}, f32[4]{0:T(128)}, u32[]{:S(2)}) copy-start(f32[4]{0:T(128)} %param.30) | copy-start | bytes 52
  12.1 116.5 %all-gather.15.cloned.1.call-start = ((), (), s32[]{:S(2)}) async-start(), calls=%async_computation.9 | async-start | bytes 4718592 | tf_op jit(solution)/shard_map/all_gather | solution.py:941
  13.0 18.4 %copy-start.29 = (f32[2048]{0:T(1024)S(1)}, f32[2048]{0:T(1024)}, u32[]{:S(2)}) copy-start(f32[2048]{0:T(1024)} %param.23) | copy-start | bytes 24580
  13.0 135.2 %all-gather.13.cloned.1.call-start = ((), (), s32[]{:S(2)}) async-start(), calls=%async_computation.8 | async-start | bytes 4718592 | tf_op jit(solution)/shard_map/all_gather | solution.py:942
  14.1 168.2 %all-gather.23.cloned.1.call-start = ((), (), s32[]{:S(2)}) async-start(), calls=%async_computation.21 | async-start | bytes 3538944 | tf_op jit(solution)/shard_map/all_gather | solution.py:962
  14.9 16.5 %copy-start.13 = (bf16[1024,2048]{1,0:T(8,128)(2,1)S(1)}, bf16[1024,2048]{1,0:T(8,128)(2,1)}, u32[]{:S(2)}) copy-start(bf16[1024,2048]{1,0:T(8,128)(2,1)} %tokens_ref.3) | copy-start | bytes 12582916
  15.3 70.3 %copy-start.7 = (f32[4,2048]{1,0:T(4,128)}, f32[4,2048]{1,0:T(4,128)S(1)}, u32[]{:S(2)}) copy-start(f32[4,2048]{1,0:T(4,128)S(1)} %constant_dynamic-update-slice_fusion.taps_ref) | copy-start | bytes 98308
  28.0 3.4 copy-start.18
  32.7 52.8 %copy-start.4 = (f32[1024,128]{1,0:T(8,128)}, f32[1024,128]{1,0:T(8,128)S(1)}, u32[]{:S(2)}) copy-start(f32[1024,128]{1,0:T(8,128)S(1)} %fusion.24.ab_ref) | copy-start | bytes 1572868
  32.7 52.0 %copy-start.27 = (f32[4]{0:T(128)S(1)}, f32[4]{0:T(128)}, u32[]{:S(2)}) copy-start(f32[4]{0:T(128)} %param.31) | copy-start | bytes 52
  82.2 2.5 copy-start.12
  82.2 39.9 %copy-start.15 = (f32[256,1408]{1,0:T(8,128)S(1)}, f32[256,1408]{1,0:T(8,128)}, u32[]{:S(2)}) copy-start(f32[256,1408]{1,0:T(8,128)} %param.38) | copy-start | bytes 4325380
  82.3 3.3 collective-permute-start
  84.7 38.3 %copy-start.9 = (f32[8,128]{1,0:T(8,128)}, f32[8,128]{1,0:T(8,128)S(1)}, u32[]{:S(2)}) copy-start(f32[8,128]{1,0:T(8,128)S(1)} %select_maximum_fusion.params_ref) | copy-start | bytes 12292
  85.1 38.0 %copy-start = (f32[1024,128]{1,0:T(8,128)}, f32[1024,128]{1,0:T(8,128)S(1)}, u32[]{:S(2)}) copy-start(f32[1024,128]{1,0:T(8,128)S(1)} %pad.12.meta_ref) | copy-start | bytes 1572868
  85.5 37.6 %copy-start.8 = (bf16[8,2048]{1,0:T(8,128)(2,1)}, bf16[8,2048]{1,0:T(8,128)(2,1)S(1)}, u32[]{:S(2)}) copy-start(bf16[8,2048]{1,0:T(8,128)(2,1)S(1)} %collective-permute-done.edge_ref) | copy-start | bytes 98308
  85.6 37.6 %copy-start.6 = (f32[8,1024]{1,0:T(8,128)}, f32[8,1024]{1,0:T(8,128)S(1)}, u32[]{:S(2)}) copy-start(f32[8,1024]{1,0:T(8,128)S(1)} %broadcast_in_dim.14.segrow_ref) | copy-start | bytes 98308
  122.1 173.1 %all-gather.17.cloned.1.call-start = ((), (), s32[]{:S(2)}) async-start(), calls=%async_computation.10 | async-start | bytes 6488064 | tf_op jit(solution)/shard_map/all_gather | solution.py:943
  123.1 172.1 %all-gather.19.cloned.1.call-start = ((), (), s32[]{:S(2)}) async-start(), calls=%async_computation.11 | async-start | bytes 6488064 | tf_op jit(solution)/shard_map/all_gather | solution.py:944
  125.5 193.9 %all-gather.21.cloned.1.call-start = ((), (), s32[]{:S(2)}) async-start(), calls=%async_computation.12 | async-start | bytes 6488064 | tf_op jit(solution)/shard_map/all_gather | solution.py:945
  128.1 386.6 %all-gather.25.cloned.1.call-start = ((), (), s32[]{:S(2)}) async-start(), calls=%async_computation.22 | async-start | bytes 2359296 | tf_op jit(solution)/shard_map/all_gather | solution.py:990
  469.7 10.1 copy-start.2
  469.7 10.1 copy-start.10
  488.6 93.7 %copy-start.11 = (bf16[1024,1024]{1,0:T(8,128)(2,1)}, bf16[1024,1024]{1,0:T(8,128)(2,1)S(1)}, u32[]{:S(2)}) copy-start(bf16[1024,1024]{1,0:T(8,128)(2,1)S(1)} %get-tuple-element.63.dgz_ref) | copy-start | bytes 6291460
  489.4 352.6 %all-reduce.6.cloned.1.call-start = ((), (), s32[]{:S(2)}) async-start(), calls=%async_computation.13 | async-start | bytes 8388608 | tf_op jit(solution)/shard_map/psum | solution.py:982
  490.1 361.0 %reduce-scatter.12.cloned.1.call-start = ((), (), s32[]{:S(2)}) async-start(), calls=%async_computation.16 | async-start | bytes 589824 | tf_op jit(solution)/shard_map/reduce_scatter | solution.py:893
  514.7 54.7 %copy-start.14 = (bf16[1024,2048]{1,0:T(8,128)(2,1)S(1)}, bf16[1024,2048]{1,0:T(8,128)(2,1)}, u32[]{:S(2)}) copy-start(bf16[1024,2048]{1,0:T(8,128)(2,1)} %tokens_ref.3) | copy-start | bytes 12582916
  572.7 280.8 %reduce-scatter.14.cloned.1.call-start = ((), (), s32[]{:S(2)}) async-start(), calls=%async_computation.17 | async-start | bytes 4718592 | tf_op jit(solution)/shard_map/reduce_scatter | solution.py:893
  582.2 273.7 %reduce-scatter.10.cloned.1.call-start = ((), (), s32[]{:S(2)}) async-start(), calls=%async_computation.15 | async-start | bytes 4718592 | tf_op jit(solution)/shard_map/reduce_scatter | solution.py:893
  591.7 1.8 copy-start.34
  591.7 289.7 %reduce-scatter.16.cloned.1.call-start = ((), (), s32[]{:S(2)}) async-start(), calls=%async_computation.18 | async-start | bytes 6488064 | tf_op jit(solution)/shard_map/reduce_scatter | solution.py:893
  604.4 1.8 copy-start.33
  604.5 339.6 %reduce-scatter.18.cloned.1.call-start = ((), (), s32[]{:S(2)}) async-start(), calls=%async_computation.19 | async-start | bytes 6488064 | tf_op jit(solution)/shard_map/reduce_scatter | solution.py:893
  617.1 1.8 copy-start.32
  617.2 389.3 %reduce-scatter.20.cloned.1.call-start = ((), (), s32[]{:S(2)}) async-start(), calls=%async_computation.20 | async-start | bytes 6488064 | tf_op jit(solution)/shard_map/reduce_scatter | solution.py:893
  630.2 451.9 %reduce-scatter.8.cloned.1.call-start = ((), (), s32[]{:S(2)}) async-start(), calls=%async_computation.14 | async-start | bytes 9437184 | tf_op jit(solution)/shard_map/reduce_scatter | solution.py:893
  631.1 3.1 collective-permute-start.1
  650.0 43.1 %copy-start.24 = (f32[16,128]{1,0:T(8,128)S(1)}, f32[16,128]{1,0:T(8,128)}, u32[]{:S(2)}) copy-start(f32[16,128]{1,0:T(8,128)} %get-tuple-element.68) | copy-start | bytes 24580
  650.0 43.1 %copy-start.19 = (f32[32,2048]{1,0:T(8,128)S(1)}, f32[32,2048]{1,0:T(8,128)}, u32[]{:S(2)}) copy-start(f32[32,2048]{1,0:T(8,128)} %get-tuple-element.69) | copy-start | bytes 786436
  (5 other events, 4.9 us)
Sparse Core Ops, SparseCore 0:
  12.2 57.4 all-gather.10
  72.1 36.8 all-gather.14
  111.4 36.6 all-gather.12
  149.9 32.3 all-gather.22
  184.6 43.3 all-gather.16
  230.2 43.3 all-gather.18
  276.0 43.3 all-gather.20
  489.5 25.1 all-gather.24
  517.0 155.1 all-reduce.5
  676.0 33.1 reduce-scatter.11
  712.6 51.3 reduce-scatter.13
  767.5 51.2 reduce-scatter.9
  822.3 59.0 reduce-scatter.15
  885.0 59.0 reduce-scatter.17
  947.4 59.0 reduce-scatter.19
  1010.8 71.2 reduce-scatter.7

commit v3 on v2

--- a/solution.py
+++ b/solution.py
@@ -12,6 +12,129 @@
 low = jnp.bfloat16
 full = jnp.float32
 MIB = 1 << 20
+
+
+NEAR = 8
+ONE = dict(pipeline_mode=pl.Buffered(1))
+ANY = dict(memory_space=pl.ANY)
+MESH = pl.DeviceIdType.MESH
+
+
+def partner(mask):
+    index = lax.axis_index("seq")
+    bits = (lax.rem(index, 2), lax.rem(index // 2, 2), index // 4)
+    return sum((1 << i) * ((1 - b) if mask >> i & 1 else b) for i, b in enumerate(bits))
+
+
+def greet(masks, last=None):
+    barrier = pltpu.get_barrier_semaphore()
+    for mask in masks:
+        pl.semaphore_signal(barrier, inc=1, device_id={"seq": partner(mask)}, device_id_type=MESH)
+    count = len(masks)
+    if last is not None:
+        place = lax.axis_index("head")
+        for there, to in ((place > 0, place - 1), (place < last, place + 1)):
+
+            @pl.when(there)
+            def _(to=to):
+                pl.semaphore_signal(barrier, inc=1, device_id={"head": to}, device_id_type=MESH)
+
+        count += jnp.minimum(place, 1) + jnp.minimum(last - place, 1)
+    pl.semaphore_wait(barrier, count)
+
+
+class Gather:
+    masks = (1, 2, 4)
+    semaphores = [pltpu.SemaphoreType.DMA((8,)), pltpu.SemaphoreType.DMA((8,)), pltpu.SemaphoreType.DMA((1,))]
+
+    def __init__(self, shard, whole, sent, got, home):
+        self.shard, self.whole, self.sent, self.got, self.home = shard, whole, sent, got, home
+        self.size = shard.shape[0]
+
+    def rows(self, mask, first=0, count=None):
+        start = pl.multiple_of(partner(mask) * self.size + first, self.size // 2)
+        return self.whole.at[pl.ds(start, self.size if count is None else count), :]
+
+    def push(self, slot):
+        half = self.size // 2
+        mask, src, dst = (
+            (2, self.shard, self.rows(0)),
+            (4, self.shard, self.rows(0)),
+            (2, self.rows(4, 0, half), self.rows(4, 0, half)),
+            (4, self.rows(2, half, half), self.rows(2, half, half)),
+            (1, self.shard, self.rows(0)),
+            (1, self.rows(2), self.rows(2)),
+            (1, self.rows(4), self.rows(4)),
+            (1, self.rows(6), self.rows(6)),
+        )[slot]
+        return pltpu.make_async_remote_copy(
+            src_ref=src, dst_ref=dst, send_sem=self.sent.at[slot], recv_sem=self.got.at[slot],
+            device_id={"seq": partner(mask)}, device_id_type=MESH,
+        )
+
+    def local(self):
+        return pltpu.make_async_copy(self.shard, self.rows(0), self.home.at[0])
+
+    def start(self):
+        self.local().start()
+        for slot in (0, 1, 4):
+            self.push(slot).start()
+
+    def middle(self):
+        for slot in (0, 1):
+            self.push(slot).wait_recv()
+        for slot in (2, 3, 5, 6):
+            self.push(slot).start()
+
+    def late(self):
+        for slot in (2, 3):
+            self.push(slot).wait_recv()
+        self.push(7).start()
+
+    def traded(self, slots):
+        for slot in slots:
+            self.push(slot).wait_recv()
+
+    def settle(self):
+        for slot in range(8):
+            self.push(slot).wait_send()
+
+    def end(self):
+        self.traded((4, 5, 6, 7))
+        self.settle()
+        self.local().wait()
+
+
+class Scatter:
+    masks = (2, 4, 6)
+    semaphores = [pltpu.SemaphoreType.DMA((3,)), pltpu.SemaphoreType.DMA((3,))]
+
+    def __init__(self, parts, got, sent, came):
+        self.parts, self.got, self.sent, self.came = parts, got, sent, came
+
+    def push(self, k):
+        return pltpu.make_async_remote_copy(
+            src_ref=self.parts.at[k + 1], dst_ref=self.got.at[k], send_sem=self.sent.at[k],
+            recv_sem=self.came.at[k], device_id={"seq": partner(2 * k + 2)}, device_id_type=MESH,
+        )
+
+    def start(self):
+        for k in range(3):
+            self.push(k).start()
+
+    def end(self):
+        for k in range(3):
+            self.push(k).wait()
+
+
+def load(step, pairs, sems):
+    @pl.when(step == 0)
+    def _():
+        copies = [pltpu.make_async_copy(a, b, sems.at[n]) for n, (a, b) in enumerate(pairs)]
+        for copy in copies:
+            copy.start()
+        for copy in copies:
+            copy.wait()
 
 
 def mm(a, b):
@@ -130,12 +253,26 @@
 
 
 def forward_kernel(
-    heads, key, value,
-    pre_ref, ab_ref, meta_ref, segrow_ref, edge_ref, taps_ref, params_ref,
-    out_ref, through_ref, states_ref, inverse_ref, end_ref,
-    ext, state,
+    heads, key, value, gathering,
+    pre_ref, ab_ref, meta_ref, segrow_ref, edge_ref, taps_ref, params_ref, *refs
 ):
     step = pl.program_id(0)
+    steps = pl.num_programs(0)
+    if gathering:
+        shard_ref, out_ref, through_ref, states_ref, inverse_ref, end_ref, whole_ref, ext, state, *sems = refs
+        moving = Gather(shard_ref, whole_ref, *sems)
+
+        @pl.when(step == 0)
+        def _():
+            greet(Gather.masks)
+            moving.start()
+
+        @pl.when(step == steps - 2)
+        def _():
+            moving.middle()
+
+    else:
+        out_ref, through_ref, states_ref, inverse_ref, end_ref, ext, state = refs
     size = pre_ref.shape[0]
     wide = value + key
     kfirst, vfirst = heads * key, 2 * heads * key
@@ -197,14 +334,24 @@
         state[h] = s
         end_ref[h] = s.astype(low)
 
-
-def forward_chain(pre, ab, meta, segrow, edge, taps, params, heads, key, value):
+    if gathering:
+
+        @pl.when(step == steps - 1)
+        def _():
+            moving.late()
+            moving.end()
+
+
+def forward_chain(pre, ab, meta, segrow, edge, taps, params, heads, key, value, shard=None):
+    gathering = shard is not None
+    moved = [jax.ShapeDtypeStruct((shard.shape[0] * NEAR, shard.shape[1]), low)] if gathering else []
+    extra = dict(collective_id=5, has_side_effects=True) if gathering else {}
     length = pre.shape[0]
     blocks = length // BLOCK
     width = pre.shape[1]
     wide = value + key
     return pl.pallas_call(
-        partial(forward_kernel, heads, key, value),
+        partial(forward_kernel, heads, key, value, gathering),
         grid=(blocks,),
         in_specs=[
             pl.BlockSpec((BLOCK, width), lambda n: (n, 0)),
@@ -214,92 +361,46 @@
             pl.BlockSpec((8, width), lambda n: (0, 0)),
             pl.BlockSpec(taps.shape, lambda n: (0, 0)),
             pl.BlockSpec((8, LANES), lambda n: (0, 0)),
-        ],
+        ]
+        + [pl.BlockSpec(**ANY) for _ in moved],
         out_specs=[
             pl.BlockSpec((BLOCK, heads * value), lambda n: (n, 0)),
             pl.BlockSpec((BLOCK, heads * key), lambda n: (n, 0)),
             pl.BlockSpec((1, heads, key, wide), lambda n: (n, 0, 0, 0)),
             pl.BlockSpec((1, heads, BLOCK, BLOCK), lambda n: (n, 0, 0, 0)),
             pl.BlockSpec((heads, key, wide), lambda n: (0, 0, 0)),
-        ],
+        ]
+        + [pl.BlockSpec(**ANY) for _ in moved],
         out_shape=[
             jax.ShapeDtypeStruct((length, heads * value), full),
             jax.ShapeDtypeStruct((length, heads * key), low),
             jax.ShapeDtypeStruct((blocks, heads, key, wide), low),
             jax.ShapeDtypeStruct((blocks, heads, BLOCK, BLOCK), low),
             jax.ShapeDtypeStruct((heads, key, wide), low),
-        ],
+        ]
+        + moved,
         scratch_shapes=[
             pltpu.VMEM((BLOCK + 8, width), full),
             pltpu.VMEM((heads, key, wide), full),
-        ],
-        compiler_params=pltpu.CompilerParams(vmem_limit_bytes=48 * MIB),
+        ]
+        + (Gather.semaphores if gathering else []),
+        compiler_params=pltpu.CompilerParams(vmem_limit_bytes=48 * MIB, **extra),
         name="chain_forward",
-    )(pre, ab, meta, segrow, edge, taps, params)
-
-
-def output_kernel(heads, key, value, place_ref, ends_ref, local_ref, through_ref, gate_ref, gain_ref,
-                  y_ref, mixed_ref, state_ref):
-    @pl.when(pl.program_id(0) == 0)
-    def _():
-        state_ref[...] = jnp.zeros_like(state_ref)
-
-        def one(j, carry):
-            for h in range(heads):
-                part = ends_ref[j, h]
-                state_ref[h] = (
-                    mm(part[:, value:], state_ref[h]) + part[:, :value].astype(full)
-                )
-            return carry
-
-        lax.fori_loop(0, place_ref[0], one, 0)
-
-    for h in range(heads):
-        cols = slice(h * value, (h + 1) * value)
-        o = local_ref[:, cols] + mm(through_ref[:, h * key : (h + 1) * key], state_ref[h])
-        mixed_ref[:, cols] = o.astype(mixed_ref.dtype)
-        s3 = lax.rsqrt(jnp.mean(o * o, axis=-1, keepdims=True) + 1e-05)
-        gz = gate_ref[:, cols]
-        y_ref[:, cols] = (o * s3 * gain_ref[0:1, :] * (gz * sigmoid(gz))).astype(low)
-
-
-def chain_output(place, ends, local, through, gate, gain, heads, key, value, rows=256):
-    length, wide = local.shape
-    return pl.pallas_call(
-        partial(output_kernel, heads, key, value),
-        grid=(length // rows,),
-        in_specs=[
-            pl.BlockSpec(memory_space=pltpu.SMEM),
-            pl.BlockSpec(ends.shape, lambda n: (0, 0, 0, 0), pipeline_mode=pl.Buffered(1)),
-            pl.BlockSpec((rows, wide), lambda n: (n, 0)),
-            pl.BlockSpec((rows, heads * key), lambda n: (n, 0)),
-            pl.BlockSpec((rows, wide), lambda n: (n, 0)),
-            pl.BlockSpec((1, value), lambda n: (0, 0)),
-        ],
-        out_specs=[
-            pl.BlockSpec((rows, wide), lambda n: (n, 0)),
-            pl.BlockSpec((rows, wide), lambda n: (n, 0)),
-            pl.BlockSpec((heads, key, value), lambda n: (0, 0, 0)),
-        ],
-        out_shape=[
-            jax.ShapeDtypeStruct((length, wide), low),
-            jax.ShapeDtypeStruct((length, wide), full),
-            jax.ShapeDtypeStruct((heads, key, value), full),
-        ],
-        compiler_params=pltpu.CompilerParams(vmem_limit_bytes=48 * MIB),
-        name="chain_output",
-    )(place, ends, local, through, gate, gain)
-
-
-def gate_back_kernel(heads, key, value, dy_ref, mixed_ref, gate_ref, gain_ref, through_ref,
-                     dgz_ref, do_ref, gain_grad_ref, adjoint_ref):
+    )(pre, ab, meta, segrow, edge, taps, params, *([shard] if gathering else []))
+
+
+def gate_back_kernel(heads, key, value, dz_ref, mixed_ref, gate_ref, gain_ref, through_ref, whole_ref,
+                     dgz_ref, do_ref, gain_grad_ref, adjoint_ref, weights, dy_ref, sems):
+    load(pl.program_id(0), [(whole_ref.at[:, heads * value :], weights)], sems)
+
     @pl.when(pl.program_id(0) == 0)
     def _():
         gain_grad_ref[...] = jnp.zeros_like(gain_grad_ref)
         adjoint_ref[...] = jnp.zeros_like(adjoint_ref)
 
-    rows = dy_ref.shape[0]
+    rows = dz_ref.shape[0]
     gain = gain_ref[0:1, :]
+    dy_ref[...] = mm(dz_ref[...], weights[...])
     for h in range(heads):
         cols = slice(h * value, (h + 1) * value)
         o = mixed_ref[:, cols].astype(full)
@@ -320,18 +421,20 @@
         adjoint_ref[h] += mm_tn(through_ref[:, h * key : (h + 1) * key], do)
 
 
-def gate_back(dy, mixed, gate, gain, through, heads, key, value, rows=256):
-    length, wide = dy.shape
+def gate_back(dz, w_mix, mixed, gate, gain, through, heads, key, value, rows=256):
+    length, width = dz.shape
+    wide = heads * value
     return pl.pallas_call(
         partial(gate_back_kernel, heads, key, value),
         grid=(length // rows,),
         in_specs=[
-            pl.BlockSpec((rows, wide), lambda n: (n, 0)),
+            pl.BlockSpec((rows, width), lambda n: (n, 0)),
             pl.BlockSpec((rows, wide), lambda n: (n, 0)),
             pl.BlockSpec((rows, wide), lambda n: (n, 0)),
             pl.BlockSpec((1, value), lambda n: (0, 0)),
             pl.BlockSpec((rows, heads * key), lambda n: (n, 0)),
-        ],
+        ]
+        + [pl.BlockSpec(**ANY)],
         out_specs=[
             pl.BlockSpec((rows, wide), lambda n: (n, 0)),
             pl.BlockSpec((rows, wide), lambda n: (n, 0)),
@@ -344,9 +447,14 @@
             jax.ShapeDtypeStruct((8, value), full),
             jax.ShapeDtypeStruct((heads, key, value), full),
         ],
+        scratch_shapes=[
+            pltpu.VMEM((width, wide), low),
+            pltpu.VMEM((rows, wide), full),
+            pltpu.SemaphoreType.DMA((1,)),
+        ],
         compiler_params=pltpu.CompilerParams(vmem_limit_bytes=48 * MIB),
         name="gate_back",
-    )(dy, mixed, gate, gain, through)
+    )(dz, mixed, gate, gain, through, w_mix)
 
 
 def lane_sum(array):
@@ -354,30 +462,53 @@
 
 
 def backward_kernel(
-    heads, key, value, devices,
-    place_ref, pre_ref, tail_ref, ab_ref, meta_ref, segrow_ref, edge_ref, edge_meta_ref, taps_ref, params_ref,
-    states_ref, inverse_ref, state_in_ref, do_ref, ends_ref, adjoints_ref,
-    dpre_ref, dab_ref, halo_ref, taps_grad_ref, params_grad_ref,
-    ext, du, adjoint,
+    heads, key, value, devices, masks_of, scattering,
+    pre_ref, tail_ref, ab_ref, meta_ref, segrow_ref, edge_ref, edge_meta_ref, taps_ref, params_ref,
+    states_ref, inverse_ref, state_in_ref, do_ref, ends_ref, *refs
 ):
     step = pl.program_id(0)
     steps = pl.num_programs(0)
+    pieces, refs = refs[: len(masks_of)], list(refs[len(masks_of) :])
+    parts_ref = refs.pop(0) if scattering else None
+    dpre_ref, dab_ref, halo_ref, taps_grad_ref, params_grad_ref = refs[:5]
+    refs = refs[5:]
+    got_ref = refs.pop(0) if scattering else None
+    ext, du, adjoint, adjoints, home, *sems = refs
+    if scattering:
+        moving = Scatter(parts_ref, got_ref, *sems)
+
+        @pl.when(step == 0)
+        def _():
+            greet(Scatter.masks)
+            moving.start()
+
     size = pre_ref.shape[0]
     kfirst, vfirst = heads * key, 2 * heads * key
 
     @pl.when(step == 0)
     def _():
         adjoint[...] = jnp.zeros_like(adjoint)
+        tall = heads * key
+        copies = []
+        for n, (mask, ref) in enumerate(zip(masks_of, pieces)):
+            first = 0 if mask is None else pl.multiple_of(partner(mask) * tall, tall)
+            target = adjoints.at[pl.ds(first, ref.shape[0]), :]
+            copies.append(pltpu.make_async_copy(ref, target, home.at[n]))
+        for copy in copies:
+            copy.start()
+        for copy in copies:
+            copy.wait()
 
         def one(k, carry):
             j = devices - 1 - k
             for h in range(heads):
+                rows = pl.ds(pl.multiple_of(j * tall + h * key, key), key)
                 adjoint[h] = (
-                    mm_tn(ends_ref[j, h, :, value:], adjoint[h]) + adjoints_ref[j, h].astype(full)
+                    mm_tn(ends_ref[j, h, :, value:], adjoint[h]) + adjoints[rows, :].astype(full)
                 )
             return carry
 
-        lax.fori_loop(0, devices - 1 - place_ref[0], one, 0)
+        lax.fori_loop(0, devices - 1 - lax.axis_index("seq"), one, 0)
         du[8 + size :, :] = jnp.zeros((8, du.shape[1]), full)
         taps_grad_ref[...] = jnp.zeros_like(taps_grad_ref)
         params_grad_ref[...] = jnp.zeros_like(params_grad_ref)
@@ -529,20 +660,26 @@
                 lag : 8 + lag, :
             ]
         halo_ref[...] = halo
-
-
-def backward_chain(place, pre, ab, meta, segrow, edge, edge_meta, taps, params, states, inverse,
-                   state_in, do, ends, adjoints, heads, key, value):
+        if scattering:
+            moving.end()
+
+
+def backward_chain(pre, ab, meta, segrow, edge, edge_meta, taps, params, states, inverse,
+                   state_in, do, ends, adjoints, heads, key, value, parts=None):
+    scattering = parts is not None
+    moved = [jax.ShapeDtypeStruct((3,) + parts.shape[1:], low)] if scattering else []
+    extra = dict(collective_id=6, has_side_effects=True) if scattering else {}
+    masks_of = [mask for mask, _ in adjoints]
+    devices = ends.shape[0]
     length, width = pre.shape
     blocks = length // BLOCK
     wide = value + key
     once = dict(pipeline_mode=pl.Buffered(1))
     last = blocks - 1
     return pl.pallas_call(
-        partial(backward_kernel, heads, key, value, ends.shape[0]),
+        partial(backward_kernel, heads, key, value, devices, masks_of, scattering),
         grid=(blocks,),
         in_specs=[
-            pl.BlockSpec(memory_space=pltpu.SMEM),
             pl.BlockSpec((BLOCK, width), lambda n: (last - n, 0)),
             pl.BlockSpec((16, width), lambda n: (jnp.maximum((last - n) * (BLOCK // 16) - 1, 0), 0)),
             pl.BlockSpec((BLOCK, LANES), lambda n: (last - n, 0)),
@@ -557,31 +694,36 @@
             pl.BlockSpec((heads, key, value), lambda n: (0, 0, 0)),
             pl.BlockSpec((BLOCK, heads * value), lambda n: (last - n, 0)),
             pl.BlockSpec(ends.shape, lambda n: (0, 0, 0, 0), **once),
-            pl.BlockSpec(adjoints.shape, lambda n: (0, 0, 0, 0), **once),
-        ],
+        ]
+        + [pl.BlockSpec(**ANY) for _ in (*adjoints, *moved)],
         out_specs=[
             pl.BlockSpec((BLOCK, width), lambda n: (last - n, 0)),
             pl.BlockSpec((BLOCK, LANES), lambda n: (last - n, 0)),
             pl.BlockSpec((8, width), lambda n: (0, 0)),
             pl.BlockSpec((32, width), lambda n: (0, 0)),
             pl.BlockSpec((16, LANES), lambda n: (0, 0)),
-        ],
+        ]
+        + [pl.BlockSpec(**ANY) for _ in moved],
         out_shape=[
             jax.ShapeDtypeStruct((length, width), low),
             jax.ShapeDtypeStruct((length, LANES), low),
             jax.ShapeDtypeStruct((8, width), full),
             jax.ShapeDtypeStruct((32, width), full),
             jax.ShapeDtypeStruct((16, LANES), full),
-        ],
+        ]
+        + moved,
         scratch_shapes=[
             pltpu.VMEM((BLOCK + 8, width), full),
             pltpu.VMEM((BLOCK + 16, width), full),
             pltpu.VMEM((heads, key, value), full),
-        ],
-        compiler_params=pltpu.CompilerParams(vmem_limit_bytes=56 * MIB),
+            pltpu.VMEM((devices * heads * key, value), low),
+            pltpu.SemaphoreType.DMA((len(adjoints),)),
+        ]
+        + (Scatter.semaphores if scattering else []),
+        compiler_params=pltpu.CompilerParams(vmem_limit_bytes=56 * MIB, **extra),
         name="chain_backward",
-    )(place, pre, pre, ab, meta, segrow, edge, edge_meta, taps, params, states, inverse, state_in, do,
-      ends, adjoints)
+    )(pre, pre, ab, meta, segrow, edge, edge_meta, taps, params, states, inverse, state_in, do, ends,
+      *[a for _, a in adjoints], *([parts] if scattering else []))
 
 
 def segment_tables(doc_lengths, shard, length):
@@ -612,19 +754,29 @@
     return meta, edge_meta, segrow
 
 
-ROWS = 128
+ROWS = 256
 PIECE = 32
 HOP = 2
-AHEAD = 2
+EACH = ROWS // PIECE
+AHEAD = 1 + (EACH - 1 + 3 * HOP) // EACH
 RING = AHEAD + 1
+
+
+def exchanged(block, mask):
+    return lax.ppermute(block, "seq", [(i, i ^ mask) for i in range(lax.axis_size("seq"))])
+
+
+def spread(shard):
+    if lax.axis_size("seq") != NEAR:
+        return [(None, lax.all_gather(shard, "seq", axis=0, tiled=True))]
+    own = [(0, shard)] + [(mask, exchanged(shard, mask)) for mask in (2, 4, 6)]
+    return own + [(mask + 1, exchanged(a, 1)) for mask, a in own]
 
 
 def line_scratch(length, width):
     pieces = length // PIECE
     return [
         pltpu.VMEM((RING, ROWS, width), low),
-        pltpu.VMEM((length, width), low),
-        pltpu.VMEM((length, width), low),
         pltpu.VMEM((length, width), low),
         pltpu.VMEM((length, width), low),
         pltpu.SemaphoreType.DMA((pieces,)),
@@ -634,49 +786,38 @@
     ]
 
 
-def line_sum(step, last, compute, finish, scratch):
-    own, from_left, from_right, to_right, to_left, got_left, got_right, sent_right, sent_left = scratch
+def line_sum(step, last, stages, finish, scratch):
+    own, from_left, from_right, got_left, got_right, sent_right, sent_left = scratch
     place = lax.axis_index("head")
     length, width = from_left.shape
-    blocks, pieces, each = length // ROWS, length // PIECE, ROWS // PIECE
+    blocks, pieces = length // ROWS, length // PIECE
     left_there, right_there = place > 0, place < last
 
     def rows(piece):
         return pl.ds(pl.multiple_of(piece * PIECE, PIECE), PIECE)
 
     def hop(piece, rightwards):
-        src, dst, sent, got, to = (
-            (to_right, from_left, sent_right, got_left, place + 1)
+        kept, sent, got, to = (
+            (from_left, sent_right, got_left, place + 1)
             if rightwards
-            else (to_left, from_right, sent_left, got_right, place - 1)
+            else (from_right, sent_left, got_right, place - 1)
         )
         return pltpu.make_async_remote_copy(
-            src_ref=src.at[rows(piece)],
-            dst_ref=dst.at[rows(piece)],
+            src_ref=kept.at[rows(piece)],
+            dst_ref=kept.at[rows(piece)],
             send_sem=sent.at[piece],
             recv_sem=got.at[piece],
             device_id={"head": to},
-            device_id_type=pl.DeviceIdType.MESH,
+            device_id_type=MESH,
         )
 
     def own_piece(piece):
-        slot = lax.rem(piece // each, RING)
-        first = pl.multiple_of(lax.rem(piece, each) * PIECE, PIECE)
+        slot = lax.rem(piece // EACH, RING)
+        first = pl.multiple_of(lax.rem(piece, EACH) * PIECE, PIECE)
         return own[slot, pl.ds(first, PIECE), :].astype(full)
 
     @pl.when(step == 0)
     def _():
-        barrier = pltpu.get_barrier_semaphore()
-        for there, to in ((left_there, place - 1), (right_there, place + 1)):
-
-            @pl.when(there)
-            def _(to=to):
-                pl.semaphore_signal(
-                    barrier, inc=1, device_id={"head": to}, device_id_type=pl.DeviceIdType.MESH
-                )
-
-        pl.semaphore_wait(barrier, jnp.minimum(place, 1) + jnp.minimum(last - place, 1))
-
         @pl.when(place == 0)
         def _():
             from_left[...] = jnp.zeros_like(from_left)
@@ -685,16 +826,11 @@
         def _():
             from_right[...] = jnp.zeros_like(from_right)
 
-    @pl.when(step < blocks)
-    def _():
-        own[lax.rem(step, RING)] = compute().astype(low)
-
     def one(q, carry):
-        now = step * each + q
+        now = (step - 1) * EACH + q
         for rightwards in (True, False):
             came, more = (left_there, right_there) if rightwards else (right_there, left_there)
-            source = from_left if rightwards else from_right
-            target = to_right if rightwards else to_left
+            kept = from_left if rightwards else from_right
             piece = now - HOP * (place if rightwards else last - place)
 
             @pl.when((piece >= 0) & (piece < pieces))
@@ -705,24 +841,33 @@
 
                 @pl.when(more)
                 def _():
-                    target[rows(piece), :] = (
-                        own_piece(piece) + source[rows(piece), :].astype(full)
+                    kept[rows(piece), :] = (
+                        own_piece(piece) + kept[rows(piece), :].astype(full)
                     ).astype(low)
                     hop(piece, rightwards).start()
 
         return carry
 
-    lax.fori_loop(0, each, one, 0)
+    done = 0
+    for n, stage in enumerate(stages):
+
+        @pl.when(step < blocks)
+        def _(n=n, stage=stage):
+            value = stage()
+            if n == len(stages) - 1:
+                own[lax.rem(step, RING)] = value.astype(low)
+
+        until = EACH * (n + 1) // len(stages)
+        lax.fori_loop(done, until, one, 0)
+        done = until
 
     @pl.when(step >= AHEAD)
     def _():
         block = step - AHEAD
         span = pl.ds(pl.multiple_of(block * ROWS, ROWS), ROWS)
-        finish(
-            own[lax.rem(block, RING)].astype(full)
-            + from_left[span, :].astype(full)
-            + from_right[span, :].astype(full)
-        )
+        total = from_left[span, :].astype(full) + from_right[span, :].astype(full)
+        twice = jnp.where(left_there & right_there, 1.0, 0.0)
+        finish(total - twice * own[lax.rem(block, RING)].astype(full))
 
     @pl.when(step == blocks + AHEAD - 1)
     def _():
@@ -740,8 +885,14 @@
         lax.fori_loop(0, pieces, settle, 0)
 
 
-def line_call(kernel, name, collective, length, width, resident, entering, leaving, outs, flops):
+def union(kinds):
+    return sorted({mask for kind in kinds for mask in kind.masks})
+
+
+def line_call(kernel, name, collective, length, width, last, resident, weights, entering, leaving, outs,
+              scratch, gathers=(), scatters=()):
     blocks = length // ROWS
+    steps = blocks + AHEAD
 
     def spec(array, stage):
         if stage == "first":
@@ -749,36 +900,81 @@
         if stage == "second":
             return pl.BlockSpec((ROWS, array.shape[1]), lambda g: (jnp.maximum(g - AHEAD, 0), 0))
         rank = len(array.shape)
-        return pl.BlockSpec(array.shape, lambda g: (0,) * rank, pipeline_mode=pl.Buffered(1))
-
-    in_specs = [
-        pl.BlockSpec(memory_space=pltpu.SMEM) if a.dtype == jnp.int32 else spec(a, "all")
-        for a in resident
-    ]
+        return pl.BlockSpec(array.shape, lambda g: (0,) * rank, **ONE)
+
+    in_specs = [spec(a, "all") for a in resident]
+    in_specs += [pl.BlockSpec(**ANY) for _ in (*weights, *gathers, *scatters)]
     in_specs += [spec(a, "first") for a in entering] + [spec(a, "second") for a in leaving]
     shapes = [jax.ShapeDtypeStruct(shape, dtype) for shape, dtype, _ in outs]
+    out_specs = [
+        spec(s, stage) if stage != "all" else pl.BlockSpec(s.shape, lambda g, r=len(s.shape): (0,) * r)
+        for s, (_, _, stage) in zip(shapes, outs)
+    ]
+    moved = [jax.ShapeDtypeStruct((a.shape[0] * NEAR, a.shape[1]), low) for a in gathers]
+    moved += [jax.ShapeDtypeStruct((3,) + a.shape[1:], low) for a in scatters]
+    kinds = [Gather] * len(gathers) + [Scatter] * len(scatters)
+    held = [pltpu.VMEM(a.shape, low) for a in weights] + [pltpu.SemaphoreType.DMA((len(weights),))]
+    held += [s for kind in kinds for s in kind.semaphores]
+
+    def body(*refs):
+        refs = list(refs)
+
+        def take(n):
+            head, refs[:] = refs[:n], refs[n:]
+            return head
+
+        own_in, heavy = take(len(resident)), take(len(weights))
+        sources = take(len(kinds))
+        chunks = take(len(entering) + len(leaving))
+        own_out, targets = take(len(outs)), take(len(moved))
+        own_scratch = take(len(scratch) + 7)
+        matrices, (sems,) = take(len(weights)), take(1)
+        carried = [kind(a, b, *take(len(kind.semaphores))) for kind, a, b in zip(kinds, sources, targets)]
+        step = pl.program_id(0)
+
+        @pl.when(step == 0)
+        def _():
+            greet(union(kinds), last)
+            for c in carried:
+                c.start()
+
+        load(step, list(zip(heavy, matrices)), sems)
+        for at, turn in ((steps - 3, "middle"), (steps - 1, "late")):
+
+            @pl.when(step == at)
+            def _(turn=turn):
+                for c in carried:
+                    if isinstance(c, Gather):
+                        getattr(c, turn)()
+
+        kernel(matrices, *own_in, *chunks, *own_out, *own_scratch)
+
+        @pl.when(step == steps - 1)
+        def _():
+            for c in carried:
+                c.end()
+
     return pl.pallas_call(
-        kernel,
-        grid=(blocks + AHEAD,),
+        body,
+        grid=(steps,),
         in_specs=in_specs,
-        out_specs=[
-            spec(s, stage) if stage != "all" else pl.BlockSpec(s.shape, lambda g, r=len(s.shape): (0,) * r)
-            for s, (_, _, stage) in zip(shapes, outs)
-        ],
-        out_shape=shapes,
-        scratch_shapes=line_scratch(length, width),
+        out_specs=out_specs + [pl.BlockSpec(**ANY) for _ in moved],
+        out_shape=shapes + moved,
+        scratch_shapes=scratch + line_scratch(length, width) + held,
         compiler_params=pltpu.CompilerParams(
             collective_id=collective, has_side_effects=True, vmem_limit_bytes=60 * MIB
         ),
-        cost_estimate=pl.CostEstimate(flops=flops, bytes_accessed=40 * MIB, transcendentals=0),
         name=name,
-    )(*resident, *entering, *leaving)
-
-
-def mixer_out_kernel(heads, key, value, last, place_ref, ends_ref, w_out_ref, head_gain_ref, gain_ref,
-                     local_ref, through_ref, gate_ref, tokens_ref,
-                     y_ref, mixed_ref, state_ref, middle_ref, second_ref, *scratch):
+    )(*resident, *weights, *gathers, *scatters, *entering, *leaving)
+
+
+def mixer_out_kernel(heads, key, value, last, matrices,
+                     ends_ref, head_gain_ref, gain_ref,
+                     first_ref, local_ref, through_ref, tokens_ref,
+                     y_ref, mixed_ref, gate_ref, state_ref, middle_ref, second_ref, *scratch):
     step = pl.program_id(0)
+    (weights,) = matrices
+    vals = heads * value
 
     @pl.when(step == 0)
     def _():
@@ -792,7 +988,10 @@
 
         lax.fori_loop(0, lax.axis_index("seq"), one, 0)
 
-    def compute():
+    def gate():
+        gate_ref[...] = mm(first_ref[...], weights[:, :vals])
+
+    def mix():
         for h in range(heads):
             cols = slice(h * value, (h + 1) * value)
             o = local_ref[:, cols] + mm(through_ref[:, h * key : (h + 1) * key], state_ref[h])
@@ -800,7 +999,9 @@
             s3 = lax.rsqrt(jnp.mean(o * o, axis=-1, keepdims=True) + 1e-05)
             gz = gate_ref[:, cols]
             y_ref[:, cols] = (o * s3 * head_gain_ref[0:1, :] * (gz * sigmoid(gz))).astype(low)
-        return mm_nt(y_ref[...], w_out_ref[...])
+
+    def project():
+        return mm_nt(y_ref[...], weights[:, vals:])
 
     def finish(total):
         middle = tokens_ref[...].astype(full) + total
@@ -808,34 +1009,42 @@
         scale = lax.rsqrt(jnp.mean(middle * middle, axis=-1, keepdims=True) + 1e-06)
         second_ref[...] = (middle * scale * gain_ref[0:1, :]).astype(low)
 
-    line_sum(step, last, compute, finish, scratch)
-
-
-def ffn_kernel(last, w_gate_ref, w_up_ref, w_down_ref, gain_ref,
+    line_sum(step, last, [gate, mix, project], finish, scratch)
+
+
+def ffn_kernel(last, size, matrices, gain_ref,
                second_ref, cot_ref, middle_ref, cot_late_ref,
                hidden_ref, dgate_ref, dup_ref, partial_ref, dmiddle_ref, dlow_ref, gain_grad_ref,
-               *scratch):
+               fg, fu, *scratch):
     step = pl.program_id(0)
+    (weights,) = matrices
+    w_gate, w_up, w_down = (slice(n * size, (n + 1) * size) for n in range(3))
 
     @pl.when(step == 0)
     def _():
         gain_grad_ref[...] = jnp.zeros_like(gain_grad_ref)
 
-    def compute():
-        h2 = second_ref[...]
-        fg = mm(h2, w_gate_ref[...])
-        fu = mm(h2, w_up_ref[...])
-        sig = sigmoid(fg)
-        swish = fg * sig
-        hidden = (swish * fu).astype(low)
+    def one():
+        fg[...] = mm(second_ref[...], weights[:, w_gate])
+
+    def two():
+        fu[...] = mm(second_ref[...], weights[:, w_up])
+
+    def three():
+        g = fg[...]
+        hidden = (g * sigmoid(g) * fu[...]).astype(low)
         hidden_ref[...] = hidden
-        partial_ref[...] = mm_nt(hidden, w_down_ref[...]).astype(low)
-        dhid = mm(cot_ref[...], w_down_ref[...])
-        dfg = (dhid * fu * (sig * (1.0 + fg * (1.0 - sig)))).astype(low)
-        dfu = (dhid * swish).astype(low)
-        dgate_ref[...] = dfg
-        dup_ref[...] = dfu
-        return mm_nt(dfg, w_gate_ref[...]) + mm_nt(dfu, w_up_ref[...])
+        partial_ref[...] = mm_nt(hidden, weights[:, w_down]).astype(low)
+
+    def four():
+        dhid = mm(cot_ref[...], weights[:, w_down])
+        g = fg[...]
+        sig = sigmoid(g)
+        dgate_ref[...] = (dhid * fu[...] * (sig * (1.0 + g * (1.0 - sig)))).astype(low)
+        dup_ref[...] = (dhid * (g * sig)).astype(low)
+
+    def five():
+        return mm_nt(dgate_ref[...], weights[:, w_gate]) + mm_nt(dup_ref[...], weights[:, w_up])
 
     def finish(grad):
         middle = middle_ref[...]
@@ -849,23 +1058,28 @@
         dmiddle_ref[...] = dm
         dlow_ref[...] = dm.astype(low)
 
-    line_sum(step, last, compute, finish, scratch)
-
-
-def input_grad_kernel(last, w_in_ref, w_gate_ref, w_small_ref, gain_ref,
+    line_sum(step, last, [one, two, three, four, five], finish, scratch)
+
+
+def input_grad_kernel(last, keys, vals, matrices, gain_ref,
                       dpre_ref, dgz_ref, dab_ref, tokens_ref, dmiddle_ref,
-                      dtokens_ref, gain_grad_ref, *scratch):
+                      dtokens_ref, gain_grad_ref, part, *scratch):
     step = pl.program_id(0)
+    w_in, w_mix = matrices
+    wide = 2 * keys + vals
 
     @pl.when(step == 0)
     def _():
         gain_grad_ref[...] = jnp.zeros_like(gain_grad_ref)
 
-    def compute():
+    def one():
+        part[...] = mm_nt(dpre_ref[...], w_in[:, :wide])
+
+    def two():
         return (
-            mm_nt(dpre_ref[...], w_in_ref[...])
-            + mm_nt(dgz_ref[...], w_gate_ref[...])
-            + mm_nt(dab_ref[...], w_small_ref[...])
+            part[...]
+            + mm_nt(dgz_ref[...], w_mix[:, :vals])
+            + mm_nt(dab_ref[...], w_in[:, wide:])
         )
 
     def finish(grad):
@@ -878,19 +1092,248 @@
             weighted - norm * jnp.mean(weighted * norm, axis=-1, keepdims=True)
         )
 
-    line_sum(step, last, compute, finish, scratch)
-
-
-def rms_scale(array, epsilon):
-    return lax.rsqrt(jnp.mean(array * array, axis=-1, keepdims=True) + epsilon)
-
-
-def gather(parts):
-    return lax.all_gather(jnp.concatenate(parts, axis=1), "seq", axis=0, tiled=True)
-
-
-def scatter(grad):
-    return lax.psum_scatter(grad.astype(low), "seq", scatter_dimension=0, tiled=True).astype(full)
+    line_sum(step, last, [one, two], finish, scratch)
+
+
+def input_kernel(wide, last, gathering, gain_ref, tokens_ref, before_ref, shard_ref,
+                 first_ref, pre_ref, ab_ref, edge_ref, whole_ref, weights, total, home, *sems):
+    rows = 256
+    length, width = tokens_ref.shape
+    half = width // 4
+    back = pltpu.make_async_copy(weights, whole_ref, home.at[0])
+    if gathering:
+        greet(Gather.masks)
+        moving = Gather(shard_ref, weights, *sems)
+        moving.start()
+    else:
+        copy = pltpu.make_async_copy(shard_ref, weights, home.at[1])
+        copy.start()
+
+    def normed(block):
+        x = block.astype(full)
+        return (x * lax.rsqrt(jnp.mean(x * x, axis=-1, keepdims=True) + 1e-06) * gain_ref[0:1, :]).astype(low)
+
+    def norm(n, carry):
+        span = pl.ds(pl.multiple_of(n * rows, rows), rows)
+        first_ref[span, :] = normed(tokens_ref[span, :])
+        return carry
+
+    lax.fori_loop(0, length // rows, norm, 0)
+
+    def add(chip, fresh, done):
+        start = pl.multiple_of(chip * half, half)
+
+        def one(n, carry):
+            span = pl.ds(pl.multiple_of(n * rows, rows), rows)
+            part = mm(first_ref[span, pl.ds(start, half)], weights[pl.ds(start, half), :])
+            if not fresh:
+                part += total[span, :]
+            if done:
+                pre_ref[span, :] = part[:, :wide].astype(low)
+                ab_ref[span, :] = part[:, wide:]
+            else:
+                total[span, :] = part
+            return carry
+
+        lax.fori_loop(0, length // rows, one, 0)
+
+    if gathering:
+        moving.local().wait()
+        moving.traded((4,))
+        add(partner(0) // 2, True, False)
+        moving.middle()
+        moving.traded((5, 6))
+        add(partner(2) // 2, False, False)
+        moving.late()
+        add(partner(4) // 2, False, False)
+        moving.traded((7,))
+        back.start()
+        add(partner(6) // 2, False, True)
+    else:
+        copy.wait()
+        back.start()
+        for chip in range(4):
+            add(chip, chip == 0, chip == 3)
+    edge_ref[...] = mm(normed(before_ref[...]), weights[:, :wide]).astype(low)
+    if gathering:
+        moving.settle()
+    back.wait()
+
+
+def input_projection(tokens, before, gain, shard, wide, last):
+    length, width = tokens.shape
+    gathering = lax.axis_size("seq") == NEAR
+    if not gathering:
+        shard = lax.all_gather(shard, "seq", axis=0, tiled=True)
+    columns = shard.shape[1]
+    here = pl.BlockSpec(memory_space=pltpu.VMEM)
+    params = dict(collective_id=4, has_side_effects=True) if gathering else {}
+    return pl.pallas_call(
+        partial(input_kernel, wide, last, gathering),
+        in_specs=[here, here, here, pl.BlockSpec(**ANY)],
+        out_specs=[here, here, here, here, pl.BlockSpec(**ANY)],
+        out_shape=[
+            jax.ShapeDtypeStruct((length, width), low),
+            jax.ShapeDtypeStruct((length, wide), low),
+            jax.ShapeDtypeStruct((length, columns - wide), full),
+            jax.ShapeDtypeStruct((before.shape[0], wide), low),
+            jax.ShapeDtypeStruct((width, columns), low),
+        ],
+        scratch_shapes=[
+            pltpu.VMEM((width, columns), low),
+            pltpu.VMEM((length, columns), full),
+            pltpu.SemaphoreType.DMA((2,)),
+        ]
+        + (Gather.semaphores if gathering else []),
+        compiler_params=pltpu.CompilerParams(vmem_limit_bytes=56 * MIB, **params),
+        name="input_projection",
+    )(gain[None, :], tokens, before, shard)
+
+
+def weight_kernel(groups, adding, counts, place_ref, *refs):
+    lefts, rights = refs[: counts[0]], refs[counts[0] : counts[0] + counts[1]]
+    rest = refs[counts[0] + counts[1] :]
+    parts = []
+    n = 0
+    for g, many in enumerate(groups):
+        left = lefts[g][...]
+        for _ in range(many):
+            parts.append(mm_tn(left, rights[n][...]))
+            n += 1
+    first = 0
+    for part in parts:
+        cols = slice(first, first + part.shape[1])
+        first += part.shape[1]
+        if adding:
+            part += rest[0][0, :, cols].astype(full)
+        rest[-1][0, :, cols] = part.astype(low)
+
+
+def weight_call(place, pairs, odd, count, stride, added=None, width=256):
+    lefts = [a for a, _ in pairs]
+    rights = [b for _, bs in pairs for b in bs]
+    length = lefts[0].shape[0]
+    columns = sum(b.shape[1] for b in rights)
+
+    def pick(k, place_ref):
+        return (0, jnp.bitwise_xor(place_ref[0], stride * k + odd))
+
+    in_specs = [pl.BlockSpec((length, width), pick) for _ in lefts]
+    in_specs += [pl.BlockSpec(b.shape, lambda k, p: (0, 0), **ONE) for b in rights]
+    if added is not None:
+        in_specs += [pl.BlockSpec((1, width, columns), lambda k, p: (k, 0, 0))]
+    out_specs = [pl.BlockSpec((1, width, columns), lambda k, p: (k, 0, 0))]
+    out_shape = [jax.ShapeDtypeStruct((count, width, columns), low)]
+    return pl.pallas_call(
+        partial(
+            weight_kernel, [len(bs) for _, bs in pairs], added is not None, (len(lefts), len(rights))
+        ),
+        grid_spec=pltpu.PrefetchScalarGridSpec(
+            num_scalar_prefetch=1, grid=(count,), in_specs=in_specs, out_specs=out_specs
+        ),
+        out_shape=out_shape,
+        compiler_params=pltpu.CompilerParams(vmem_limit_bytes=56 * MIB),
+        name="weight_grads",
+    )(place, *lefts, *rights, *(() if added is None else (added,)))
+
+
+def pair_sums(place, pairs):
+    (away,) = weight_call(place, pairs, 1, NEAR // 2, 2)
+    (sums,) = weight_call(place, pairs, 0, NEAR // 2, 2, exchanged(away, 1))
+    return sums
+
+
+def far_sums(sums, got):
+    return sum((got[k] for k in range(3)), start=sums[0].astype(full))
+
+
+def plain_sums(place, pairs):
+    width = pairs[0][0].shape[1]
+    (grads,) = weight_call(jnp.zeros_like(place), pairs, 0, width // 256, 1)
+    return lax.psum_scatter(grads.reshape(width, -1), "seq", scatter_dimension=0, tiled=True).astype(full)
+
+
+def small_kernel(count, others, part_ref, out_ref, send, got, got_far, sent, came, sent_far, came_far):
+    me, row = lax.axis_index("seq"), lax.axis_index("head")
+    rows, far = part_ref.shape[0], got_far.shape[2]
+    barrier = pltpu.get_barrier_semaphore()
+
+    def greet(k, carry):
+        pl.semaphore_signal(
+            barrier, inc=1, device_id={"seq": lax.rem(me + k, count)},
+            device_id_type=pl.DeviceIdType.MESH,
+        )
+        return carry
+
+    lax.fori_loop(1, count, greet, 0)
+    for k in range(1, others):
+        pl.semaphore_signal(
+            barrier, inc=1, device_id={"head": lax.rem(row + k, others)},
+            device_id_type=pl.DeviceIdType.MESH,
+        )
+    pl.semaphore_wait(barrier, count + others - 2)
+
+    def along(k):
+        return pltpu.make_async_remote_copy(
+            src_ref=part_ref, dst_ref=got.at[me], send_sem=sent.at[k], recv_sem=came.at[k],
+            device_id={"seq": lax.rem(me + k, count)}, device_id_type=pl.DeviceIdType.MESH,
+        )
+
+    def across(k):
+        return pltpu.make_async_remote_copy(
+            src_ref=send, dst_ref=got_far.at[row], send_sem=sent_far.at[k], recv_sem=came_far.at[k],
+            device_id={"head": lax.rem(row + k, others)}, device_id_type=pl.DeviceIdType.MESH,
+        )
+
+    def start(k, carry):
+        along(k).start()
+        return carry
+
+    def wait(k, carry):
+        along(k).wait()
+        return carry
+
+    lax.fori_loop(1, count, start, 0)
+    got[me] = part_ref[...]
+    lax.fori_loop(1, count, wait, 0)
+
+    def add(k, carry):
+        out_ref[...] += got[k]
+        return carry
+
+    out_ref[...] = got[0]
+    lax.fori_loop(1, count, add, 0)
+    send[...] = out_ref[:, :far]
+    for k in range(1, others):
+        across(k).start()
+    got_far[row] = send[...]
+    for k in range(1, others):
+        across(k).wait()
+    total = got_far[0]
+    for k in range(1, others):
+        total += got_far[k]
+    out_ref[rows - 1 :, :far] = total[rows - 1 :, :]
+
+
+def small_sums(part, far):
+    count, others = lax.axis_size("seq"), lax.axis_size("head")
+    return pl.pallas_call(
+        partial(small_kernel, count, others),
+        in_specs=[pl.BlockSpec(memory_space=pltpu.VMEM)],
+        out_specs=pl.BlockSpec(memory_space=pltpu.VMEM),
+        out_shape=jax.ShapeDtypeStruct(part.shape, full),
+        scratch_shapes=[
+            pltpu.VMEM((part.shape[0], far), full),
+            pltpu.VMEM((count,) + part.shape, full),
+            pltpu.VMEM((others, part.shape[0], far), full),
+            pltpu.SemaphoreType.DMA((count,)),
+            pltpu.SemaphoreType.DMA((count,)),
+            pltpu.SemaphoreType.DMA((others,)),
+            pltpu.SemaphoreType.DMA((others,)),
+        ],
+        compiler_params=pltpu.CompilerParams(collective_id=3, has_side_effects=True),
+        name="small_sums",
+    )(part)
 
 
 def passed_along(block, axis, distance):
@@ -922,125 +1365,116 @@
     ffn_down,
     cotangent,
 ):
-    length = tokens.shape[0]
+    length, width = tokens.shape
     heads = decay_log.shape[0]
     key = query_weight.shape[1] // heads
     value = head_gain.shape[0]
     keys, vals = heads * key, heads * value
-    hidden_size = ffn_gate.shape[1]
+    wide = 2 * keys + vals
+    size = ffn_gate.shape[1]
+    last = lax.axis_size("head") - 1
+    near = lax.axis_size("seq") == NEAR
     shard = lax.axis_index("seq")
     place = jnp.full((1,), shard, jnp.int32)
+
+    small = jnp.zeros((alpha_weight.shape[0], LANES - 2 * heads), full)
+    shard_in = jnp.concatenate(
+        [query_weight, key_weight, value_weight, alpha_weight, beta_weight, small], axis=1
+    ).astype(low)
+    before = passed_along(tokens[length - 16 :], "seq", 1)
+    shard_mix = jnp.concatenate([gate_weight.astype(low), output_weight.T.astype(low)], axis=1)
+    shard_ffn = jnp.concatenate(
+        [ffn_gate.astype(low), ffn_up.astype(low), ffn_down.T.astype(low)], axis=1
+    )
     meta, edge_meta, segrow = segment_tables(doc_lengths, shard, length)
-
-    small = jnp.concatenate(
-        [alpha_weight, beta_weight, jnp.zeros((alpha_weight.shape[0], LANES - 2 * heads), full)],
-        axis=1,
-    )
-    w_in = gather([a.astype(low) for a in (query_weight, key_weight, value_weight)])
-    w_small = lax.all_gather(small.astype(low), "seq", axis=0, tiled=True)
-    w_gate = lax.all_gather(gate_weight.astype(low), "seq", axis=0, tiled=True)
-    w_out = lax.all_gather(output_weight.T.astype(low), "seq", axis=0, tiled=True)
-    w_widen = lax.all_gather(ffn_gate.astype(low), "seq", axis=0, tiled=True)
-    w_lift = lax.all_gather(ffn_up.astype(low), "seq", axis=0, tiled=True)
-    w_narrow = lax.all_gather(ffn_down.T.astype(low), "seq", axis=0, tiled=True)
-
-    stream = tokens.astype(full)
-    first_scale = rms_scale(stream, 1e-06)
-    first_norm = stream * first_scale
-    first_in = (first_norm * mixer_gain).astype(low)
-    pre = mm(first_in, w_in).astype(low)
-    ab = mm(first_in, w_small)
-    edge = passed_along(pre[length - 8 :], "seq", 1)
-    gate_pre = mm(first_in, w_gate)
-
     taps = jnp.concatenate([query_taps, key_taps, value_taps], axis=1)
     params = jnp.stack([-jnp.exp(decay_log), decay_bias])
     params = jnp.pad(params, ((0, 6), (0, LANES - heads)))
-    local, through, states, inverse, end = forward_chain(
-        pre, ab, meta, segrow, edge, taps, params, heads, key, value
+    gain = head_gain[None, :]
+
+    first_in, pre, ab, edge, w_in = input_projection(tokens, before, mixer_gain, shard_in, wide, last)
+    edge = edge[8:]
+    local, through, states, inverse, end, *moved = forward_chain(
+        pre, ab, meta, segrow, edge, taps, params, heads, key, value, shard_mix if near else None
     )
+    w_mix = moved[0] if near else lax.all_gather(shard_mix, "seq", axis=0, tiled=True)
     ends = lax.all_gather(end, "seq")
-    gain = head_gain[None, :]
-    last = lax.axis_size("head") - 1
-    width = tokens.shape[1]
-    mix_out, mixed, state_in, middle, second_in = line_call(
-        partial(mixer_out_kernel, heads, key, value, last), "mixer_out", 0, length, width,
-        [place, ends, w_out, gain, ffn_gain[None, :]], [local, through, gate_pre], [tokens],
+    mix_out, mixed, gate_pre, state_in, middle, second_in, *moved = line_call(
+        partial(mixer_out_kernel, heads, key, value, last), "mixer_out", 0, length, width, last,
+        [ends, gain, ffn_gain[None, :]], [w_mix], [first_in, local, through], [tokens],
         [((length, vals), low, "first"), ((length, vals), full, "first"),
-         ((heads, key, value), full, "all"), ((length, width), full, "second"),
-         ((length, width), low, "second")],
-        2 * length * vals * width,
+         ((length, vals), full, "first"), ((heads, key, value), full, "all"),
+         ((length, width), full, "second"), ((length, width), low, "second")],
+        [], gathers=[shard_ffn] if near else [],
     )
+    w_ffn = moved[0] if near else lax.all_gather(shard_ffn, "seq", axis=0, tiled=True)
     hidden, gate_grad, lift_grad, narrow_part, middle_grad, middle_low, ffn_gain_part = line_call(
-        partial(ffn_kernel, last), "ffn", 1, length, width,
-        [w_widen, w_lift, w_narrow, ffn_gain[None, :]], [second_in, cotangent], [middle, cotangent],
-        [((length, hidden_size), low, "first")] * 3
+        partial(ffn_kernel, last, size), "ffn", 1, length, width, last,
+        [ffn_gain[None, :]], [w_ffn], [second_in, cotangent], [middle, cotangent],
+        [((length, size), low, "first")] * 3
         + [((length, width), low, "first"), ((length, width), full, "second"),
            ((length, width), low, "second"), ((8, width), full, "all")],
-        12 * length * width * hidden_size,
+        [pltpu.VMEM((ROWS, size), full)] * 2,
     )
     result = (middle + lax.psum(narrow_part, "head").astype(full)).astype(low)
-    narrow_wgrad = scatter(mm_tn(cotangent, hidden)).T
-    widen_wgrad = scatter(mm_tn(second_in, gate_grad))
-    lift_wgrad = scatter(mm_tn(second_in, lift_grad))
-    mix_grad = mm(middle_low, w_out)
     gate_pgrad, mixed_grad, head_gain_part, adjoint = gate_back(
-        mix_grad, mixed, gate_pre, gain, through, heads, key, value
+        middle_low, w_mix, mixed, gate_pre, gain, through, heads, key, value
     )
-    adjoints = lax.all_gather(adjoint.astype(low), "seq")
-    output_wgrad = scatter(mm_tn(middle_low, mix_out)).T
-    gate_wgrad = scatter(mm_tn(first_in, gate_pgrad))
-    pre_grad, ab_grad, halo, taps_part, params_part = backward_chain(
-        place, pre, ab, meta, segrow, edge, edge_meta, taps, params, states, inverse, state_in,
-        mixed_grad, ends, adjoints, heads, key, value,
+    adjoints = spread(adjoint.astype(low).reshape(keys, value))
+    pairs_up = [(second_in, [gate_grad, lift_grad])]
+    pairs_rest = [(cotangent, [hidden]), (first_in, [gate_pgrad]), (middle_low, [mix_out])]
+    sums_up = pair_sums(place, pairs_up) if near else None
+    sums_rest = pair_sums(place, pairs_rest) if near else None
+    pre_grad, ab_grad, halo, taps_part, params_part, *moved = backward_chain(
+        pre, ab, meta, segrow, edge, edge_meta, taps, params, states, inverse, state_in,
+        mixed_grad, ends, adjoints, heads, key, value, sums_up,
     )
+    up_wgrad = far_sums(sums_up, moved[0]) if near else plain_sums(place, pairs_up)
     halo = passed_along(halo, "seq", -1)
     tail = pre_grad[length - 8 :].astype(full) + halo
     pre_grad = lax.dynamic_update_slice(pre_grad, tail.astype(low), (length - 8, 0))
-    tokens_grad, mixer_gain_part = line_call(
-        partial(input_grad_kernel, last), "input_grad", 2, length, width,
-        [w_in, w_gate, w_small, mixer_gain[None, :]], [pre_grad, gate_pgrad, ab_grad],
+    pairs_in = [(first_in, [pre_grad, ab_grad])]
+    sums_in = pair_sums(place, pairs_in) if near else None
+    tokens_grad, mixer_gain_part, *moved = line_call(
+        partial(input_grad_kernel, last, keys, vals), "input_grad", 2, length, width, last,
+        [mixer_gain[None, :]], [w_in, w_mix], [pre_grad, gate_pgrad, ab_grad],
         [tokens, middle_grad],
         [((length, width), full, "second"), ((8, width), full, "all")],
-        2 * length * width * (2 * keys + 2 * vals + LANES),
+        [pltpu.VMEM((ROWS, width), full)], scatters=[sums_rest, sums_in] if near else [],
     )
-    in_wgrad = scatter(mm_tn(first_in, pre_grad))
-    small_wgrad = scatter(mm_tn(first_in, ab_grad))
-    taps_part = jnp.sum(taps_part.reshape(4, 8, -1), axis=1)
-    params_part = jnp.sum(params_part.reshape(2, 8, LANES), axis=1)
-    mixer_gain_grad, ffn_gain_grad, taps_grad, params_grad = lax.psum(
-        (
-            jnp.sum(mixer_gain_part, axis=0).astype(low),
-            jnp.sum(ffn_gain_part, axis=0).astype(low),
-            taps_part.astype(low),
-            params_part.astype(low),
-        ),
-        "seq",
-    )
-    head_gain_grad = lax.psum(jnp.sum(head_gain_part, axis=0), ("seq", "head"))
-    taps_grad = taps_grad.astype(full)
-    params_grad = params_grad.astype(full)
+    rest_wgrad = far_sums(sums_rest, moved[0]) if near else plain_sums(place, pairs_rest)
+    in_wgrad = far_sums(sums_in, moved[1]) if near else plain_sums(place, pairs_in)
+    params_part = jnp.sum(params_part.reshape(2, 8, LANES), axis=1).reshape(1, -1)
+    lines = [
+        jnp.sum(mixer_gain_part, axis=0, keepdims=True),
+        jnp.sum(ffn_gain_part, axis=0, keepdims=True),
+        jnp.sum(taps_part.reshape(4, 8, -1), axis=1),
+        jnp.pad(params_part, ((0, 0), (0, width - params_part.shape[1]))),
+        jnp.pad(jnp.sum(head_gain_part, axis=0)[None], ((0, 0), (0, width - value))),
+    ]
+    sums = small_sums(jnp.concatenate(lines, axis=0), value)
+    taps_grad = sums[2:6]
     return (
         result,
         tokens_grad,
-        mixer_gain_grad.astype(full),
+        sums[0],
         in_wgrad[:, :keys],
         in_wgrad[:, keys : 2 * keys],
-        in_wgrad[:, 2 * keys :],
-        gate_wgrad,
-        small_wgrad[:, :heads],
-        small_wgrad[:, heads : 2 * heads],
-        params_grad[1, :heads],
-        params_grad[0, :heads],
+        in_wgrad[:, 2 * keys : wide],
+        rest_wgrad[:, size : size + vals],
+        in_wgrad[:, wide : wide + heads],
+        in_wgrad[:, wide + heads : wide + 2 * heads],
+        sums[6, LANES : LANES + heads],
+        sums[6, :heads],
         taps_grad[:, :keys],
         taps_grad[:, keys : 2 * keys],
         taps_grad[:, 2 * keys :],
-        head_gain_grad,
-        output_wgrad,
-        ffn_gain_grad.astype(full),
-        widen_wgrad,
-        lift_wgrad,
-        narrow_wgrad,
+        sums[7, :value],
+        rest_wgrad[:, size + vals :].T,
+        sums[1],
+        up_wgrad[:, :size],
+        up_wgrad[:, size:],
+        rest_wgrad[:, :size].T,
     )
 
 

time: 1110 us -> 841 us (0.76)
  waiting for transfers between devices: 348 us -> 78.8 us
  Pallas kernels: 482 us -> 653 us
  matrix products: 104 us -> 0 us
  blocking collectives: 77.2 us -> 0 us
    reduce_scatter x7 -> x0, waiting for transfers between devices: 217 us -> none  [scatter(): lax.psum_scatter(grad.astype(low), 'seq', scatter_dimension=0, tiled=True)]
    pallas_call x5 -> x13, Pallas kernels: 475 us -> 640 us  [the longest x3 385 us: line_call(): pl.pallas_call(body, grid=(steps,), in_specs=in_specs, out_specs=out_spec...]
    dot_general x11 -> x0, matrix products: 104 us -> none  [the longest x7 69.7 us: mm_tn(): lax.dot_general(a.astype(low), b.astype(low), (((0,), (0,)), ((), ())), p...]
    all_gather x7 -> x0, waiting for transfers between devices: 93.7 us -> none  [the longest x1 36.9 us: gather(): lax.all_gather(jnp.concatenate(parts, axis=1), 'seq', axis=0, tiled=True)]
    psum x2 -> x0, blocking collectives: 64.6 us -> none  [the longest x1 42.2 us: shards(): head_gain_grad = lax.psum(jnp.sum(head_gain_part, axis=0), ('seq', 'head'))]
    psum x1, waiting for transfers between devices: 0.01 us -> 37.8 us  [shards(): result = (middle + lax.psum(narrow_part, 'head').astype(full)).astype(low)]
    convert_element_type x13 -> x4, other arithmetic: 16.4 us -> 2.84 us  [the longest x1 1.44 us: shards(): ffn_up.astype(low)]
    all_gather x1 -> x0, blocking collectives: 12.6 us -> none  [shards(): w_small = lax.all_gather(small.astype(low), 'seq', axis=0, tiled=True)]
  transfers between devices with their start and end apart: 18 -> 14, of which waited for: 11 -> 5; matrix products, arithmetic and copies ran while one was open for 12% -> 4% of each run, Pallas kernels for 29% -> 16%
where the time goes in v3:
time: 841 us; the launch traced here: 833 us
  Pallas kernels  653 us (78%)
  waiting for transfers between devices  78.8 us (9%)
  local copies, waits for them, and re-layouts  44 us (5%)
  other arithmetic  30.5 us (4%)
  between operations  14.8 us (2%)
  starting transfers between devices  12 us (1%)
    pallas_call x3, Pallas kernels, line_call(): pl.pallas_call(body, grid=(steps,), in_specs=in_specs, out_specs=out_spec...  385 us
    pallas_call x6, Pallas kernels, weight_call(): pl.pallas_call(partial(weight_kernel, [len(bs) for _, bs in pairs], added...  71.6 us
    pallas_call x1, Pallas kernels, backward_chain(): pl.pallas_call(partial(backward_kernel, heads, key, value, devices, masks...  70.2 us
    pallas_call x1, Pallas kernels, input_projection(): pl.pallas_call(partial(input_kernel, wide, last, gathering), in_specs=[he...  55.9 us
    pallas_call x1, Pallas kernels, forward_chain(): pl.pallas_call(partial(forward_kernel, heads, key, value, gathering), gri...  43.9 us
    psum x1, waiting for transfers between devices, shards(): result = (middle + lax.psum(narrow_part, 'head').astype(full)).astype(low)  37.8 us
    all_gather x1, waiting for transfers between devices, shards(): ends = lax.all_gather(end, 'seq')  27.4 us
    unnamed x69, local copies, waits for them, and re-layouts  22.5 us
  transfers between devices with their start and end apart: 14, of which 5 were waited for; matrix products, arithmetic and copies ran while one was open for 4% of the time, Pallas kernels for 16%

profile of v3, /device:TPU:0, one launch (start us, length us, event | category | flops | bytes accessed | tf_op | source)
XLA Modules:
  0.0 832.8 jit_solution(16451013466731785108)
XLA Ops:
  7.2 1.6 slice.152
  8.8 3.0 collective-permute-start
  19.1 1.8 convert.32
  21.3 1.3 convert_element_type.122
  22.6 1.4 copy.131
  24.3 2.9 concatenate.16.shard_ref
  27.3 55.9 %input_projection.1 = (bf16[1024,2048]{1,0:T(8,128)(2,1)}, bf16[1024,2048]{1,0:T(8,128)(2,1)}, f32[1024,128]{1,0:T(8,128)}, bf16[16,2048]{1,0:T(8,128)(2,1)}, bf16[2048,2176]{1,0:T(8,128)(2,1)}) custom-call(f32[1,2048]{1,0:T(1,128)} %bitcast.90, bf16[1024,2048]{1,0:T(8,128)(2,1)} %refs_8_.3, bf16[16,2048]{1,0:T(8,128)(2,1)} %collective-permute-done.before_ref, ...), custom_call_target="tpu_custom_call" | custom-call | tf_op jit(solution)/shard_map/input_projection/pallas_call | solution.py:1171
  85.0 43.9 %chain_forward.1 = (f32[1024,1024]{1,0:T(8,128)}, bf16[1024,512]{1,0:T(8,128)(2,1)S(1)}, bf16[8,4,128,384]{3,2,1,0:T(8,128)(2,1)}, bf16[8,4,128,128]{3,2,1,0:T(8...) custom-call(bf16[1024,2048]{1,0:T(8,128)(2,1)} %get-tuple-element.59.pre_ref.tail_ref, ...), custom_call_target="tpu_custom_call" | custom-call | tf_op jit(solution)/shard_map/chain_forward/pallas_call | solution.py:353
  131.6 1.4 convert_element_type.126
  133.0 1.7 copy.132
  134.8 1.5 pad_maximum_fusion.refs_4_
  136.2 27.4 %all-gather.3.cloned.1.call-done = bf16[32,128,384]{2,1,0:T(8,128)(2,1)} async-done(((bf16[4,128,384]{2,1,0:T(8,128)(2,1)}), bf16[32,128,384]{2,1,0:T(8,128)(2,1)}) %all-gather.3.cloned.1.call-update) | async-done | bytes 3145744 | tf_op jit(solution)/shard_map/all_gather | solution.py:1401
  163.7 120.6 %mixer_out.1 = (bf16[1024,1024]{1,0:T(8,128)(2,1)}, f32[1024,1024]{1,0:T(8,128)}, f32[1024,1024]{1,0:T(8,128)}, f32[4,128,256]{2,1,0:T(8,128)}, f32[1024,2048]{1...) custom-call(bf16[8,4,128,384]{3,2,1,0:T(8,128)(2,1)} %bitcast.78, f32[1,256]{1,0:T(1,128)} %bitcast.76, ...), custom_call_target="tpu_custom_call" | custom-call | tf_op jit(solution)/shard_map/mixer_out/pallas_call | solution.py:957
  284.3 131.4 %ffn.1 = (bf16[1024,1408]{1,0:T(8,128)(2,1)}, bf16[1024,1408]{1,0:T(8,128)(2,1)}, bf16[1024,1408]{1,0:T(8,128)(2,1)}, bf16[1024,2048]{1,0:T(8,128)(2,1)}, f32[10...) custom-call(f32[1,2048]{1,0:T(1,128)} %bitcast.95, bf16[2048,4224]{1,0:T(8,128)(2,1)} %get-tuple-element.68.refs_1_, ...), custom_call_target="tpu_custom_call" | custom-call | tf_op jit(solution)/shard_map/ffn/pallas_call | solution.py:957
  415.7 11.7 %weight_grads.8 = bf16[4,256,2816]{2,1,0:T(8,128)(2,1)} custom-call(s32[1]{0:T(128)} %bitcast.22.place_ref, bf16[1024,2048]{1,0:T(8,128)(2,1)} %get-tuple-element.69.refs_2_.refs_0_, bf16[1024,1408]{1,0:T(8,128)(2,1)} %get-tuple-element.83.refs_1_, bf16[1024,1408]{1,0:T(8,128)(2,1)} %get-tuple-element.84.refs_2_), custom_call_target="tpu_custom_call" | custom-call | tf_op jit(solution)/shard_map/weight_grads/pallas_call | solution.py:1227
  427.4 12.6 %gate_back.1 = (bf16[1024,1024]{1,0:T(8,128)(2,1)S(1)}, bf16[1024,1024]{1,0:T(8,128)(2,1)S(1)}, f32[8,256]{1,0:T(8,128)S(1)}, f32[4,128,256]{2,1,0:T(8,128)S(1)}) custom-call(bf16[1024,2048]{1,0:T(8,128)(2,1)} %get-tuple-element.72.dz_ref.refs_2_, f32[1024,1024]{1,0:T(8,128)} %get-tuple-element.74.mixed_ref, f32[1024,1024]{1,0:T(8,128)} %get-tuple-element.75.gate_ref, ...), custom_call_target="tpu_custom_call" | custom-call | tf_op jit(solution)/shard_map/gate_back/pallas_call | solution.py:427
  440.1 1.3 copy-done
  441.4 1.3 copy-done.4
  442.7 13.5 %weight_grads.6 = bf16[4,256,3456]{2,1,0:T(8,128)(2,1)} custom-call(s32[1]{0:T(128)} %bitcast.22.place_ref, bf16[1024,2048]{1,0:T(8,128)(2,1)} %refs_0_.3, bf16[1024,2048]{1,0:T(8,128)(2,1)} %get-tuple-element.64.refs_5_.refs_1_.refs_0_, bf16[1024,2048]{1,0:T(8,128)(2,1)} %get-tuple-element.72.dz_ref.refs_2_, bf16[1024,1408]{1,0:T(8,128)(2,1)} %get-tuple-element.73.refs_3_, ...), custom_call_target="tpu_custom_call" | custom-call | tf_op jit(solution)/shard_map/weight_grads/pallas_call | solution.py:1227
  456.7 2.8 collective-permute-start.4
  460.3 6.6 collective-permute-done.4.refs_3_
  466.9 4.8 collective-permute-done.3.refs_2_
  473.8 12.1 %weight_grads.9.refs_8_ = bf16[4,256,2816]{2,1,0:T(8,128)(2,1)} custom-call(s32[1]{0:T(128)} %bitcast.22.place_ref, bf16[1024,2048]{1,0:T(8,128)(2,1)} %get-tuple-element.69.refs_2_.refs_0_, bf16[1024,1408]{1,0:T(8,128)(2,1)} %get-tuple-element.83.refs_1_, bf16[1024,1408]{1,0:T(8,128)(2,1)} %get-tuple-element.84.refs_2_, ...), custom_call_target="tpu_custom_call" | custom-call | tf_op jit(solution)/shard_map/weight_grads/pallas_call | solution.py:1227
  486.9 70.2 %chain_backward.1 = (bf16[1024,2048]{1,0:T(8,128)(2,1)}, bf16[1024,128]{1,0:T(8,128)(2,1)}, f32[8,2048]{1,0:T(8,128)}, f32[32,2048]{1,0:T(8,128)}, f32[16,128]{1,0:T(8,128)}, /*index=5*/bf16[3,256,2816]{2,1,0:T(8,128)(2,1)}) custom-call(bf16[1024,2048]{1,0:T(8,128)(2,1)} %get-tuple-element.59.pre_ref.tail_ref, ...), custom_call_target="tpu_custom_call" | custom-call | tf_op jit(solution)/shard_map/chain_backward/pallas_call | solution.py:679
  557.0 1.3 collective-permute-start.10
  558.3 2.1 collective-permute-done.10
  560.4 1.4 fusion.refs_1_.refs_5_
  561.8 9.7 %weight_grads.10 = bf16[4,256,2176]{2,1,0:T(8,128)(2,1)} custom-call(s32[1]{0:T(128)} %bitcast.22.place_ref, bf16[1024,2048]{1,0:T(8,128)(2,1)} %get-tuple-element.64.refs_5_.refs_1_.refs_0_, bf16[1024,2048]{1,0:T(8,128)(2,1)} %fusion.refs_1_.refs_5_, bf16[1024,128]{1,0:T(8,128)(2,1)} %get-tuple-element.87.refs_2_.refs_7_), custom_call_target="tpu_custom_call" | custom-call | tf_op jit(solution)/shard_map/weight_grads/pallas_call | solution.py:1227
  571.5 2.5 collective-permute-start.11
  574.0 37.8 %all-reduce.7.cloned.1.call-done = bf16[1024,2048]{1,0:T(8,128)(2,1)} async-done(((bf16[1024,2048]{1,0:T(8,128)(2,1)}), bf16[1024,2048]{1,0:T(8,128)(2,1)}) %all-reduce.7.cloned.1.call-update) | async-done | bytes 4194320 | tf_op jit(solution)/shard_map/psum | solution.py:1419
  611.8 8.3 add_convert_fusion
  620.2 3.3 add_bitcast_fusion.1
  623.6 1.8 fusion.15
  625.3 14.6 %weight_grads.7.refs_3_ = bf16[4,256,3456]{2,1,0:T(8,128)(2,1)} custom-call(s32[1]{0:T(128)} %bitcast.22.place_ref, bf16[1024,2048]{1,0:T(8,128)(2,1)} %refs_0_.3, bf16[1024,2048]{1,0:T(8,128)(2,1)} %get-tuple-element.64.refs_5_.refs_1_.refs_0_, bf16[1024,2048]{1,0:T(8,128)(2,1)} %get-tuple-element.72.dz_ref.refs_2_, ...), custom_call_target="tpu_custom_call" | custom-call | tf_op jit(solution)/shard_map/weight_grads/pallas_call | solution.py:1227
  639.9 10.0 %weight_grads.11.refs_4_ = bf16[4,256,2176]{2,1,0:T(8,128)(2,1)} custom-call(s32[1]{0:T(128)} %bitcast.22.place_ref, bf16[1024,2048]{1,0:T(8,128)(2,1)} %get-tuple-element.64.refs_5_.refs_1_.refs_0_, bf16[1024,2048]{1,0:T(8,128)(2,1)} %fusion.refs_1_.refs_5_, bf16[1024,128]{1,0:T(8,128)(2,1)} %get-tuple-element.87.refs_2_.refs_7_, ...), custom_call_target="tpu_custom_call" | custom-call | tf_op jit(solution)/shard_map/weight_grads/pallas_call | solution.py:1227
  649.9 132.6 %input_grad.1 = (f32[1024,2048]{1,0:T(8,128)}, f32[8,2048]{1,0:T(8,128)}, bf16[3,256,3456]{2,1,0:T(8,128)(2,1)}, bf16[3,256,2176]{2,1,0:T(8,128)(2,1)}) custom-call(f32[1,2048]{1,0:T(1,128)} %bitcast.91, bf16[2048,2176]{1,0:T(8,128)(2,1)} %get-tuple-element.71.refs_1_, bf16[2048,2048]{1,0:T(8,128)(2,1)} %get-tuple-element.63.refs_3_.whole_ref.refs_2_, ...), custom_call_target="tpu_custom_call" | custom-call | tf_op jit(solution)/shard_map/input_grad/pallas_call | solution.py:957
  784.1 14.0 %small_sums.1 = f32[8,2048]{1,0:T(8,128)} custom-call(f32[8,2048]{1,0:T(8,128)} %concatenate.20.part_ref), custom_call_target="tpu_custom_call" | custom-call | tf_op jit(solution)/shard_map/small_sums/pallas_call | solution.py:1320
  798.0 1.3 slice.191
  799.3 1.2 slice_bitcast_fusion.3
  800.5 1.4 slice.190
  801.9 1.3 fusion.19
  803.2 1.5 fusion.18
  804.7 2.9 add_bitcast_fusion.2
  810.0 2.4 add_bitcast_fusion
  812.4 1.3 slice_bitcast_fusion.1
  815.0 1.3 copy.144
  816.4 1.5 copy.145
  817.9 7.9 copy.151
  (133 shorter events, 22.0 us)
Async XLA Ops:
  7.2 14.1 %copy-start.14 = (f32[256,1024]{1,0:T(8,128)S(1)}, f32[256,1024]{1,0:T(8,128)}, u32[]{:S(2)}) copy-start(f32[256,1024]{1,0:T(8,128)} %param.26) | copy-start | bytes 3145732
  7.2 156.5 %all-gather.3.cloned.1.call-start = ((), (), s32[]{:S(2)}) async-start(), calls=%async_computation.1 | async-start | bytes 3538944 | tf_op jit(solution)/shard_map/all_gather | solution.py:1401
  8.8 18.5 %collective-permute-start = (bf16[16,2048]{1,0:T(8,128)(2,1)}, bf16[16,2048]{1,0:T(8,128)(2,1)}, u32[]{:S(2)}, u32[]{:S(2)}) collective-permute-start(bf16[16,2048]{1,0:T(8,128)(2,1)} %slice.152), channel_id=1, source_target_pairs={{0,4},{4,8},{8,12},{12,16},{16,20},{20,24},{24,28},{1,5},{5,9},{9,... | collective-permute-start | bytes 196616 | tf_op jit(solution)/shard_map/ppermute | solution.py:1342
  19.0 5.0 copy-start.26
  19.1 5.1 copy-start.24
  22.6 4.6 copy-start.27
  24.1 59.8 %copy-start.9 = (f32[4,2048]{1,0:T(4,128)}, f32[4,2048]{1,0:T(4,128)S(1)}, u32[]{:S(2)}) copy-start(f32[4,2048]{1,0:T(4,128)S(1)} %constant_dynamic-update-slice_fusion.taps_ref) | copy-start | bytes 98308
  24.2 59.8 %copy-start.1 = (f32[1024,128]{1,0:T(8,128)}, f32[1024,128]{1,0:T(8,128)S(1)}, u32[]{:S(2)}) copy-start(f32[1024,128]{1,0:T(8,128)S(1)} %pad.19.meta_ref) | copy-start | bytes 1572868
  27.2 101.7 %copy-start.10 = (f32[8,128]{1,0:T(8,128)}, f32[8,128]{1,0:T(8,128)S(1)}, u32[]{:S(2)}) copy-start(f32[8,128]{1,0:T(8,128)S(1)} %select_maximum_fusion.params_ref) | copy-start | bytes 12292
  83.9 47.0 %copy-start.7 = (bf16[8,2048]{1,0:T(8,128)(2,1)}, bf16[8,2048]{1,0:T(8,128)(2,1)S(1)}, u32[]{:S(2)}) copy-start(bf16[8,2048]{1,0:T(8,128)(2,1)S(1)} %slice.162.edge_ref) | copy-start | bytes 98308
  83.9 47.0 %copy-start.8 = (f32[8,1024]{1,0:T(8,128)}, f32[8,1024]{1,0:T(8,128)S(1)}, u32[]{:S(2)}) copy-start(f32[8,1024]{1,0:T(8,128)S(1)} %broadcast_in_dim.37.segrow_ref) | copy-start | bytes 98308
  84.0 1.1 copy-start.5
  85.0 46.5 %copy-start.12 = (f32[256,1408]{1,0:T(8,128)S(1)}, f32[256,1408]{1,0:T(8,128)}, u32[]{:S(2)}) copy-start(f32[256,1408]{1,0:T(8,128)} %param.38) | copy-start | bytes 4325380
  128.9 1.0 copy-start.2
  129.9 1.0 copy-start.6
  130.9 480.9 %all-reduce.7.cloned.1.call-start = ((), (), s32[]{:S(2)}) async-start(), calls=%async_computation | async-start | bytes 8388608 | tf_op jit(solution)/shard_map/psum | solution.py:1419
  415.6 11.8 %copy-start.3 = (bf16[1024,512]{1,0:T(8,128)(2,1)S(1)}, bf16[1024,512]{1,0:T(8,128)(2,1)}, u32[]{:S(2)}) copy-start(bf16[1024,512]{1,0:T(8,128)(2,1)} %copy-done.2) | copy-start | bytes 3145732
  415.6 11.8 %copy-start.11 = (f32[256]{0:T(256)S(1)}, f32[256]{0:T(256)}, u32[]{:S(2)}) copy-start(f32[256]{0:T(256)} %param.35) | copy-start | bytes 3076
  427.4 44.8 %collective-permute-start.9 = (bf16[4,256,2816]{2,1,0:T(8,128)(2,1)}, bf16[4,256,2816]{2,1,0:T(8,128)(2,1)}, u32[]{:S(2)}, u32[]{:S(2)}) collective-permute-start(bf16[4,256,2816]{2,1,0:T(8,128)(2,1)} %weight_grads.8), channel_id=1, source_target_pairs={{0,4},{4,0},{8,12},{12,8},{16,20},{20,16},{24,28},{28,24},{1,5},{5... | collective-permute-start | bytes 17301512 | tf_op jit(solution)/shard_map/ppermute | solution.py:766
  440.1 1.3 copy-start
  441.4 1.3 copy-start.4
  456.2 169.1 %collective-permute-start.1 = (bf16[4,256,3456]{2,1,0:T(8,128)(2,1)}, bf16[4,256,3456]{2,1,0:T(8,128)(2,1)}, u32[]{:S(2)}, u32[]{:S(2)}) collective-permute-start(bf16[4,256,3456]{2,1,0:T(8,128)(2,1)} %weight_grads.6), channel_id=1, source_target_pairs={{0,4},{4,0},{8,12},{12,8},{16,20},{20,16},{24,28},{28,24},{1,5},{5... | collective-permute-start | bytes 21233672 | tf_op jit(solution)/shard_map/ppermute | solution.py:766
  456.7 29.1 %copy-start.13 = (bf16[4,128,256]{2,1,0:T(8,128)(2,1)}, bf16[4,128,256]{2,1,0:T(8,128)(2,1)S(1)}, u32[]{:S(2)}) copy-start(bf16[4,128,256]{2,1,0:T(8,128)(2,1)S(1)} %convert_element_type.132) | copy-start | bytes 786436
  456.7 10.2 %collective-permute-start.4 = (bf16[512,256]{1,0:T(8,128)(2,1)S(1)}, bf16[512,256]{1,0:T(8,128)(2,1)S(1)}, u32[]{:S(2)}, u32[]{:S(2)}) collective-permute-start(bf16[512,256]{1,0:T(8,128)(2,1)S(1)} %bitcast.84), channel_id=1, source_target_pairs={{0,24},{4,28},{8,16},{12,20},{16,8},{20,12},{24,0},{28,4},{1,25},{... | collective-permute-start | bytes 786440 | tf_op jit(solution)/shard_map/ppermute | solution.py:766
  459.6 12.1 %collective-permute-start.3 = (bf16[512,256]{1,0:T(8,128)(2,1)S(1)}, bf16[512,256]{1,0:T(8,128)(2,1)S(1)}, u32[]{:S(2)}, u32[]{:S(2)}) collective-permute-start(bf16[512,256]{1,0:T(8,128)(2,1)S(1)} %bitcast.85), channel_id=1, source_target_pairs={{0,16},{4,20},{8,24},{12,28},{16,0},{20,4},{24,8},{28,12},{1,17},{... | collective-permute-start | bytes 786440 | tf_op jit(solution)/shard_map/ppermute | solution.py:766
  459.6 12.2 %collective-permute-start.2 = (bf16[512,256]{1,0:T(8,128)(2,1)S(1)}, bf16[512,256]{1,0:T(8,128)(2,1)S(1)}, u32[]{:S(2)}, u32[]{:S(2)}) collective-permute-start(bf16[512,256]{1,0:T(8,128)(2,1)S(1)} %bitcast.86), channel_id=1, source_target_pairs={{0,8},{4,12},{8,0},{12,4},{16,24},{20,28},{24,16},{28,20},{1,9},{5... | collective-permute-start | bytes 786440 | tf_op jit(solution)/shard_map/ppermute | solution.py:766
  466.9 19.0 %copy-start.15 = (bf16[512,256]{1,0:T(8,128)(2,1)}, bf16[512,256]{1,0:T(8,128)(2,1)S(1)}, u32[]{:S(2)}) copy-start(bf16[512,256]{1,0:T(8,128)(2,1)S(1)} %collective-permute-done.4.refs_3_) | copy-start | bytes 786436
  466.9 19.0 %collective-permute-start.5 = (bf16[512,256]{1,0:T(8,128)(2,1)S(1)}, bf16[512,256]{1,0:T(8,128)(2,1)S(1)}, u32[]{:S(2)}, u32[]{:S(2)}) collective-permute-start(bf16[512,256]{1,0:T(8,128)(2,1)S(1)} %bitcast.87), channel_id=1, source_target_pairs={{0,4},{4,0},{8,12},{12,8},{16,20},{20,16},{24,28},{28,24},{1,5},{5... | collective-permute-start | bytes 786440 | tf_op jit(solution)/shard_map/ppermute | solution.py:766
  471.7 14.2 %copy-start.16 = (bf16[512,256]{1,0:T(8,128)(2,1)}, bf16[512,256]{1,0:T(8,128)(2,1)S(1)}, u32[]{:S(2)}) copy-start(bf16[512,256]{1,0:T(8,128)(2,1)S(1)} %collective-permute-done.3.refs_2_) | copy-start | bytes 786436
  471.7 14.2 %collective-permute-start.8 = (bf16[512,256]{1,0:T(8,128)(2,1)S(1)}, bf16[512,256]{1,0:T(8,128)(2,1)S(1)}, u32[]{:S(2)}, u32[]{:S(2)}) collective-permute-start(bf16[512,256]{1,0:T(8,128)(2,1)S(1)} %collective-permute-done.4.refs_3_), channel_id=1, source_target_pairs={{0,4},{4,0},{8,12},{12,8},{16,20},{20,16},{24,28},{28,24},{1,5},{5... | collective-permute-start | bytes 786440 | tf_op jit(solution)/shard_map/ppermute | solution.py:766
  471.8 14.0 %copy-start.17 = (bf16[512,256]{1,0:T(8,128)(2,1)}, bf16[512,256]{1,0:T(8,128)(2,1)S(1)}, u32[]{:S(2)}) copy-start(bf16[512,256]{1,0:T(8,128)(2,1)S(1)} %collective-permute-done.2.refs_1_) | copy-start | bytes 786436
  471.8 14.1 %collective-permute-start.7 = (bf16[512,256]{1,0:T(8,128)(2,1)S(1)}, bf16[512,256]{1,0:T(8,128)(2,1)S(1)}, u32[]{:S(2)}, u32[]{:S(2)}) collective-permute-start(bf16[512,256]{1,0:T(8,128)(2,1)S(1)} %collective-permute-done.3.refs_2_), channel_id=1, source_target_pairs={{0,4},{4,0},{8,12},{12,8},{16,20},{20,16},{24,28},{28,24},{1,5},{5... | collective-permute-start | bytes 786440 | tf_op jit(solution)/shard_map/ppermute | solution.py:766
  472.2 13.7 %collective-permute-start.6 = (bf16[512,256]{1,0:T(8,128)(2,1)S(1)}, bf16[512,256]{1,0:T(8,128)(2,1)S(1)}, u32[]{:S(2)}, u32[]{:S(2)}) collective-permute-start(bf16[512,256]{1,0:T(8,128)(2,1)S(1)} %collective-permute-done.2.refs_1_), channel_id=1, source_target_pairs={{0,4},{4,0},{8,12},{12,8},{16,20},{20,16},{24,28},{28,24},{1,5},{5... | collective-permute-start | bytes 786440 | tf_op jit(solution)/shard_map/ppermute | solution.py:766
  485.9 0.7 copy-start.18
  485.9 0.8 copy-start.19
  485.9 0.8 copy-start.20
  486.0 0.9 copy-start.21
  557.0 3.4 collective-permute-start.10
  561.8 12.2 %copy-start.23 = (f32[8,2048]{1,0:T(8,128)S(1)}, f32[8,2048]{1,0:T(8,128)}, u32[]{:S(2)}) copy-start(f32[8,2048]{1,0:T(8,128)} %get-tuple-element.91) | copy-start | bytes 196612
  571.5 68.4 %collective-permute-start.11 = (bf16[4,256,2176]{2,1,0:T(8,128)(2,1)}, bf16[4,256,2176]{2,1,0:T(8,128)(2,1)}, u32[]{:S(2)}, u32[]{:S(2)}) collective-permute-start(bf16[4,256,2176]{2,1,0:T(8,128)(2,1)} %weight_grads.10), channel_id=1, source_target_pairs={{0,4},{4,0},{8,12},{12,8},{16,20},{20,16},{24,28},{28,24},{1,5},{5... | collective-permute-start | bytes 13369352 | tf_op jit(solution)/shard_map/ppermute | solution.py:766
  574.0 46.1 %copy-start.25 = (f32[16,128]{1,0:T(8,128)S(1)}, f32[16,128]{1,0:T(8,128)}, u32[]{:S(2)}) copy-start(f32[16,128]{1,0:T(8,128)} %get-tuple-element.93) | copy-start | bytes 24580
  574.0 46.1 %copy-start.22 = (f32[32,2048]{1,0:T(8,128)S(1)}, f32[32,2048]{1,0:T(8,128)}, u32[]{:S(2)}) copy-start(f32[32,2048]{1,0:T(8,128)} %get-tuple-element.92) | copy-start | bytes 786436
  804.7 5.2 slice-start
  804.7 5.2 slice-start.1
Sparse Core Ops, SparseCore 0:
  131.0 32.6 all-gather.2
  456.8 154.9 all-reduce.6

commit v4 on v3

--- a/solution.py
+++ b/solution.py
@@ -17,6 +17,7 @@
 NEAR = 8
 ONE = dict(pipeline_mode=pl.Buffered(1))
 ANY = dict(memory_space=pl.ANY)
+FREE = pl.CostEstimate(flops=1, bytes_accessed=1, transcendentals=0)
 MESH = pl.DeviceIdType.MESH
 
 
@@ -385,6 +386,7 @@
         ]
         + (Gather.semaphores if gathering else []),
         compiler_params=pltpu.CompilerParams(vmem_limit_bytes=48 * MIB, **extra),
+        cost_estimate=FREE,
         name="chain_forward",
     )(pre, ab, meta, segrow, edge, taps, params, *([shard] if gathering else []))
 
@@ -453,6 +455,7 @@
             pltpu.SemaphoreType.DMA((1,)),
         ],
         compiler_params=pltpu.CompilerParams(vmem_limit_bytes=48 * MIB),
+        cost_estimate=FREE,
         name="gate_back",
     )(dz, mixed, gate, gain, through, w_mix)
 
@@ -504,7 +507,7 @@
             for h in range(heads):
                 rows = pl.ds(pl.multiple_of(j * tall + h * key, key), key)
                 adjoint[h] = (
-                    mm_tn(ends_ref[j, h, :, value:], adjoint[h]) + adjoints[rows, :].astype(full)
+                    mm_tn(ends_ref[rows, value:], adjoint[h]) + adjoints[rows, :].astype(full)
                 )
             return carry
 
@@ -670,7 +673,7 @@
     moved = [jax.ShapeDtypeStruct((3,) + parts.shape[1:], low)] if scattering else []
     extra = dict(collective_id=6, has_side_effects=True) if scattering else {}
     masks_of = [mask for mask, _ in adjoints]
-    devices = ends.shape[0]
+    devices = ends.shape[0] // (heads * key)
     length, width = pre.shape
     blocks = length // BLOCK
     wide = value + key
@@ -693,7 +696,7 @@
             pl.BlockSpec((1, heads, BLOCK, BLOCK), lambda n: (last - n, 0, 0, 0)),
             pl.BlockSpec((heads, key, value), lambda n: (0, 0, 0)),
             pl.BlockSpec((BLOCK, heads * value), lambda n: (last - n, 0)),
-            pl.BlockSpec(ends.shape, lambda n: (0, 0, 0, 0), **once),
+            pl.BlockSpec(ends.shape, lambda n: (0, 0), **once),
         ]
         + [pl.BlockSpec(**ANY) for _ in (*adjoints, *moved)],
         out_specs=[
@@ -721,6 +724,7 @@
         ]
         + (Scatter.semaphores if scattering else []),
         compiler_params=pltpu.CompilerParams(vmem_limit_bytes=56 * MIB, **extra),
+        cost_estimate=FREE,
         name="chain_backward",
     )(pre, pre, ab, meta, segrow, edge, edge_meta, taps, params, states, inverse, state_in, do, ends,
       *[a for _, a in adjoints], *([parts] if scattering else []))
@@ -890,7 +894,7 @@
 
 
 def line_call(kernel, name, collective, length, width, last, resident, weights, entering, leaving, outs,
-              scratch, gathers=(), scatters=()):
+              scratch, gathers=(), scatters=(), early=None):
     blocks = length // ROWS
     steps = blocks + AHEAD
 
@@ -903,17 +907,20 @@
         return pl.BlockSpec(array.shape, lambda g: (0,) * rank, **ONE)
 
     in_specs = [spec(a, "all") for a in resident]
-    in_specs += [pl.BlockSpec(**ANY) for _ in (*weights, *gathers, *scatters)]
+    first_one = [] if early is None else [early]
+    in_specs += [pl.BlockSpec(**ANY) for _ in (*weights, *first_one, *gathers, *scatters)]
     in_specs += [spec(a, "first") for a in entering] + [spec(a, "second") for a in leaving]
     shapes = [jax.ShapeDtypeStruct(shape, dtype) for shape, dtype, _ in outs]
     out_specs = [
         spec(s, stage) if stage != "all" else pl.BlockSpec(s.shape, lambda g, r=len(s.shape): (0,) * r)
         for s, (_, _, stage) in zip(shapes, outs)
     ]
-    moved = [jax.ShapeDtypeStruct((a.shape[0] * NEAR, a.shape[1]), low) for a in gathers]
+    moved = [jax.ShapeDtypeStruct((a.shape[0] * NEAR, a.shape[1]), low) for a in (*first_one, *gathers)]
     moved += [jax.ShapeDtypeStruct((3,) + a.shape[1:], low) for a in scatters]
     kinds = [Gather] * len(gathers) + [Scatter] * len(scatters)
+    whole_first = [pltpu.VMEM(s.shape, low) for s in moved[: len(first_one)]]
     held = [pltpu.VMEM(a.shape, low) for a in weights] + [pltpu.SemaphoreType.DMA((len(weights),))]
+    held += whole_first + [s for _ in first_one for s in Gather.semaphores]
     held += [s for kind in kinds for s in kind.semaphores]
 
     def body(*refs):
@@ -924,21 +931,37 @@
             return head
 
         own_in, heavy = take(len(resident)), take(len(weights))
-        sources = take(len(kinds))
+        ahead, sources = take(len(first_one)), take(len(kinds))
         chunks = take(len(entering) + len(leaving))
-        own_out, targets = take(len(outs)), take(len(moved))
+        own_out, handed, targets = take(len(outs)), take(len(first_one)), take(len(kinds))
         own_scratch = take(len(scratch) + 7)
         matrices, (sems,) = take(len(weights)), take(1)
+        if first_one:
+            (table,), signals = take(1), take(3)
+            lead = Gather(ahead[0], table, *signals)
+            back = pltpu.make_async_copy(table, handed[0], signals[2].at[0])
+            matrices.append(table)
         carried = [kind(a, b, *take(len(kind.semaphores))) for kind, a, b in zip(kinds, sources, targets)]
         step = pl.program_id(0)
 
         @pl.when(step == 0)
         def _():
-            greet(union(kinds), last)
-            for c in carried:
+            greet(union(kinds + [Gather] * len(first_one)), last)
+            for c in [lead] if first_one else carried:
                 c.start()
 
         load(step, list(zip(heavy, matrices)), sems)
+        if first_one:
+
+            @pl.when(step == 0)
+            def _():
+                lead.middle()
+                lead.late()
+                for c in carried:
+                    c.start()
+                lead.end()
+                back.start()
+
         for at, turn in ((steps - 3, "middle"), (steps - 1, "late")):
 
             @pl.when(step == at)
@@ -953,6 +976,8 @@
         def _():
             for c in carried:
                 c.end()
+            if first_one:
+                back.wait()
 
     return pl.pallas_call(
         body,
@@ -964,16 +989,17 @@
         compiler_params=pltpu.CompilerParams(
             collective_id=collective, has_side_effects=True, vmem_limit_bytes=60 * MIB
         ),
+        cost_estimate=FREE,
         name=name,
-    )(*resident, *weights, *gathers, *scatters, *entering, *leaving)
+    )(*resident, *weights, *first_one, *gathers, *scatters, *entering, *leaving)
 
 
 def mixer_out_kernel(heads, key, value, last, matrices,
-                     ends_ref, head_gain_ref, gain_ref,
+                     head_gain_ref, gain_ref,
                      first_ref, local_ref, through_ref, tokens_ref,
                      y_ref, mixed_ref, gate_ref, state_ref, middle_ref, second_ref, *scratch):
     step = pl.program_id(0)
-    (weights,) = matrices
+    weights, ends = matrices
     vals = heads * value
 
     @pl.when(step == 0)
@@ -982,7 +1008,8 @@
 
         def one(j, carry):
             for h in range(heads):
-                part = ends_ref[j, h]
+                rows = pl.ds(pl.multiple_of((j * heads + h) * key, key), key)
+                part = ends[rows, :]
                 state_ref[h] = mm(part[:, value:], state_ref[h]) + part[:, :value].astype(full)
             return carry
 
@@ -1062,8 +1089,8 @@
 
 
 def input_grad_kernel(last, keys, vals, matrices, gain_ref,
-                      dpre_ref, dgz_ref, dab_ref, tokens_ref, dmiddle_ref,
-                      dtokens_ref, gain_grad_ref, part, *scratch):
+                      dpre_ref, dgz_ref, dab_ref, tokens_ref,
+                      term_ref, gain_grad_ref, part, *scratch):
     step = pl.program_id(0)
     w_in, w_mix = matrices
     wide = 2 * keys + vals
@@ -1088,26 +1115,52 @@
         norm = stream * scale
         gain_grad_ref[...] += jnp.sum((grad * norm).reshape(ROWS // 8, 8, -1), axis=0)
         weighted = grad * gain_ref[0:1, :]
-        dtokens_ref[...] = dmiddle_ref[...] + scale * (
-            weighted - norm * jnp.mean(weighted * norm, axis=-1, keepdims=True)
-        )
+        term_ref[...] = (
+            scale * (weighted - norm * jnp.mean(weighted * norm, axis=-1, keepdims=True))
+        ).astype(low)
 
     line_sum(step, last, [one, two], finish, scratch)
 
 
-def input_kernel(wide, last, gathering, gain_ref, tokens_ref, before_ref, shard_ref,
-                 first_ref, pre_ref, ab_ref, edge_ref, whole_ref, weights, total, home, *sems):
+def input_kernel(wide, gathering, gain_ref, *refs):
     rows = 256
+    if gathering:
+        heavy, (before_hbm, tokens_hbm), refs = refs[:9], refs[9:11], refs[11:]
+        small_ref, sources = heavy[3], heavy[4:]
+    else:
+        (shard_ref, before_hbm, tokens_hbm), refs = refs[:3], refs[3:]
+    first_ref, pre_ref, ab_ref, edge_ref, whole_ref = refs[:5]
+    refs = refs[5:]
+    if gathering:
+        (mix_ref, ffn_ref), refs = refs[:2], refs[2:]
+    weights, total, tokens_ref, before, home, *refs = refs
     length, width = tokens_ref.shape
     half = width // 4
     back = pltpu.make_async_copy(weights, whole_ref, home.at[0])
+    here = pltpu.make_async_copy(tokens_hbm, tokens_ref, home.at[1])
+    here.start()
     if gathering:
+        shard, *buffers = refs[:6]
+        sems = refs[6:]
+        pairs = [(before_hbm, before), *zip(sources, buffers)]
+        copies = [pltpu.make_async_copy(a, b, home.at[2 + n]) for n, (a, b) in enumerate(pairs)]
+        for copy in copies:
+            copy.start()
+        first = 0
+        for ref in heavy[:3]:
+            shard[:, first : first + ref.shape[1]] = ref[...].astype(low)
+            first += ref.shape[1]
+        shard[:, first:] = small_ref[...].astype(low)
         greet(Gather.masks)
-        moving = Gather(shard_ref, weights, *sems)
+        moving = Gather(shard, weights, *sems)
         moving.start()
     else:
-        copy = pltpu.make_async_copy(shard_ref, weights, home.at[1])
-        copy.start()
+        copies = [
+            pltpu.make_async_copy(shard_ref, weights, home.at[2]),
+            pltpu.make_async_copy(before_hbm, before, home.at[3]),
+        ]
+        for copy in copies:
+            copy.start()
 
     def normed(block):
         x = block.astype(full)
@@ -1118,6 +1171,7 @@
         first_ref[span, :] = normed(tokens_ref[span, :])
         return carry
 
+    here.wait()
     lax.fori_loop(0, length // rows, norm, 0)
 
     def add(chip, fresh, done):
@@ -1141,6 +1195,18 @@
         moving.local().wait()
         moving.traded((4,))
         add(partner(0) // 2, True, False)
+        for copy in copies:
+            copy.wait()
+        gate, out, up, lift, down = buffers
+        vals, size = gate.shape[1], up.shape[1]
+        mix_ref[:, :vals] = gate[...].astype(low)
+        for first in range(0, vals, 128):
+            mix_ref[:, vals + first : vals + first + 128] = out[first : first + 128, :].T.astype(low)
+        ffn_ref[:, :size] = up[...].astype(low)
+        ffn_ref[:, size : 2 * size] = lift[...].astype(low)
+        for first in range(0, size, 128):
+            cols = slice(2 * size + first, 2 * size + first + 128)
+            ffn_ref[:, cols] = down[first : first + 128, :].T.astype(low)
         moving.middle()
         moving.traded((5, 6))
         add(partner(2) // 2, False, False)
@@ -1150,44 +1216,63 @@
         back.start()
         add(partner(6) // 2, False, True)
     else:
-        copy.wait()
+        for copy in copies:
+            copy.wait()
         back.start()
         for chip in range(4):
             add(chip, chip == 0, chip == 3)
-    edge_ref[...] = mm(normed(before_ref[...]), weights[:, :wide]).astype(low)
+    edge_ref[...] = mm(normed(before[...]), weights[:, :wide]).astype(low)
     if gathering:
         moving.settle()
     back.wait()
 
 
-def input_projection(tokens, before, gain, shard, wide, last):
+def input_projection(tokens, before, gain, heavy, wide):
     length, width = tokens.shape
-    gathering = lax.axis_size("seq") == NEAR
-    if not gathering:
-        shard = lax.all_gather(shard, "seq", axis=0, tiled=True)
-    columns = shard.shape[1]
+    gathering = len(heavy) > 1
     here = pl.BlockSpec(memory_space=pltpu.VMEM)
-    params = dict(collective_id=4, has_side_effects=True) if gathering else {}
+    away = pl.BlockSpec(**ANY)
+    if gathering:
+        operands = [*heavy, before, tokens]
+        in_specs = [here] * 4 + [away] * 7
+        rows = heavy[0].shape[0]
+        columns = sum(a.shape[1] for a in heavy[:4])
+        shards_out = [
+            jax.ShapeDtypeStruct((rows, 2 * heavy[4].shape[1]), low),
+            jax.ShapeDtypeStruct((rows, 3 * heavy[6].shape[1]), low),
+        ]
+        more = [pltpu.VMEM((rows, columns), low)] + [pltpu.VMEM(a.shape, full) for a in heavy[4:]]
+        more += Gather.semaphores
+        params = dict(collective_id=4, has_side_effects=True)
+    else:
+        operands = [*heavy, before, tokens]
+        in_specs = [away] * 3
+        columns = heavy[0].shape[1]
+        shards_out, more, params = [], [], {}
     return pl.pallas_call(
-        partial(input_kernel, wide, last, gathering),
-        in_specs=[here, here, here, pl.BlockSpec(**ANY)],
-        out_specs=[here, here, here, here, pl.BlockSpec(**ANY)],
+        partial(input_kernel, wide, gathering),
+        in_specs=[here] + in_specs,
+        out_specs=[here] * 4 + [away] + [here] * len(shards_out),
         out_shape=[
             jax.ShapeDtypeStruct((length, width), low),
             jax.ShapeDtypeStruct((length, wide), low),
             jax.ShapeDtypeStruct((length, columns - wide), full),
-            jax.ShapeDtypeStruct((before.shape[0], wide), low),
+            jax.ShapeDtypeStruct((16, wide), low),
             jax.ShapeDtypeStruct((width, columns), low),
-        ],
+        ]
+        + shards_out,
         scratch_shapes=[
             pltpu.VMEM((width, columns), low),
             pltpu.VMEM((length, columns), full),
-            pltpu.SemaphoreType.DMA((2,)),
+            pltpu.VMEM((length, width), low),
+            pltpu.VMEM((16, width), low),
+            pltpu.SemaphoreType.DMA((8,)),
         ]
-        + (Gather.semaphores if gathering else []),
-        compiler_params=pltpu.CompilerParams(vmem_limit_bytes=56 * MIB, **params),
+        + more,
+        compiler_params=pltpu.CompilerParams(vmem_limit_bytes=60 * MIB, **params),
+        cost_estimate=FREE,
         name="input_projection",
-    )(gain[None, :], tokens, before, shard)
+    )(gain[None, :], *operands)
 
 
 def weight_kernel(groups, adding, counts, place_ref, *refs):
@@ -1233,6 +1318,7 @@
         ),
         out_shape=out_shape,
         compiler_params=pltpu.CompilerParams(vmem_limit_bytes=56 * MIB),
+        cost_estimate=FREE,
         name="weight_grads",
     )(place, *lefts, *rights, *(() if added is None else (added,)))
 
@@ -1243,14 +1329,77 @@
     return sums
 
 
-def far_sums(sums, got):
-    return sum((got[k] for k in range(3)), start=sums[0].astype(full))
-
-
 def plain_sums(place, pairs):
     width = pairs[0][0].shape[1]
     (grads,) = weight_call(jnp.zeros_like(place), pairs, 0, width // 256, 1)
     return lax.psum_scatter(grads.reshape(width, -1), "seq", scatter_dimension=0, tiled=True).astype(full)
+
+
+def final_kernel(heads, keys, vals, size, dmiddle_ref, term_ref, in_own, in_got, up_own, up_got, down_own, down_got,
+                 gate_own, gate_got, out_own, out_got,
+                 dtokens_ref, q_ref, k_ref, v_ref, a_ref, b_ref, up_ref, lift_ref, down_ref, gate_ref, out_ref):
+    def total(own, got, cols=slice(None)):
+        return own[0, :, cols].astype(full) + sum(got[k, :, cols].astype(full) for k in range(3))
+
+    @pl.when(pl.program_id(0) < 8)
+    def _():
+        dtokens_ref[...] = dmiddle_ref[...] + term_ref[...].astype(full)
+        wide = 2 * keys + vals
+        q_ref[...] = total(in_own, in_got, slice(0, keys))
+        k_ref[...] = total(in_own, in_got, slice(keys, 2 * keys))
+        v_ref[...] = total(in_own, in_got, slice(2 * keys, wide))
+        small = total(in_own, in_got, slice(wide, wide + LANES))
+        a_ref[...] = small[:, :heads]
+        b_ref[...] = small[:, heads : 2 * heads]
+        up_ref[...] = total(up_own, up_got, slice(0, size))
+        lift_ref[...] = total(up_own, up_got, slice(size, 2 * size))
+        gate_ref[...] = total(gate_own, gate_got)
+        out_ref[...] = total(out_own, out_got).T
+
+    down_ref[...] = total(down_own, down_got).T
+
+
+def final_sums(dmiddle, term, sums_in, got_in, sums_up, got_up, sums_rest, got_rest, heads, keys, vals, size):
+    length, width = dmiddle.shape
+    rows = sums_in.shape[1]
+    eight = lambda n: jnp.minimum(n, 7)
+    many, few = length // 8, rows // 8
+
+    def both(array, block, index):
+        return [pl.BlockSpec((1,) + block, index), pl.BlockSpec((3,) + block, index)]
+
+    wide_in, wide_up = sums_in.shape[2], sums_up.shape[2]
+    at_gate, at_out = size // LANES, (size + vals) // LANES
+    in_specs = [pl.BlockSpec((many, width), lambda n: (eight(n), 0))] * 2
+    in_specs += both(sums_in, (few, wide_in), lambda n: (0, eight(n), 0))
+    in_specs += both(sums_up, (few, wide_up), lambda n: (0, eight(n), 0))
+    in_specs += both(sums_rest, (rows, LANES), lambda n: (0, 0, n))
+    in_specs += both(sums_rest, (rows, LANES), lambda n: (0, 0, at_gate + eight(n)))
+    in_specs += both(sums_rest, (rows, LANES), lambda n: (0, 0, at_out + eight(n)))
+    byrow = lambda columns: pl.BlockSpec((few, columns), lambda n: (eight(n), 0))
+    return pl.pallas_call(
+        partial(final_kernel, heads, keys, vals, size),
+        grid=(size // LANES,),
+        in_specs=in_specs,
+        out_specs=[
+            pl.BlockSpec((many, width), lambda n: (eight(n), 0)),
+            byrow(keys), byrow(keys), byrow(vals), byrow(heads), byrow(heads), byrow(size), byrow(size),
+            pl.BlockSpec((LANES, rows), lambda n: (n, 0)),
+            pl.BlockSpec((rows, LANES), lambda n: (0, eight(n))),
+            pl.BlockSpec((LANES, rows), lambda n: (eight(n), 0)),
+        ],
+        out_shape=[
+            jax.ShapeDtypeStruct(shape, full)
+            for shape in (
+                (length, width), (rows, keys), (rows, keys), (rows, vals), (rows, heads), (rows, heads),
+                (rows, size), (rows, size), (size, rows), (rows, vals), (vals, rows),
+            )
+        ],
+        compiler_params=pltpu.CompilerParams(vmem_limit_bytes=48 * MIB),
+        cost_estimate=FREE,
+        name="final_sums",
+    )(dmiddle, term, sums_in, got_in, sums_up, got_up, sums_rest, got_rest, sums_rest, got_rest,
+      sums_rest, got_rest)
 
 
 def small_kernel(count, others, part_ref, out_ref, send, got, got_far, sent, came, sent_far, came_far):
@@ -1377,37 +1526,53 @@
     shard = lax.axis_index("seq")
     place = jnp.full((1,), shard, jnp.int32)
 
-    small = jnp.zeros((alpha_weight.shape[0], LANES - 2 * heads), full)
-    shard_in = jnp.concatenate(
-        [query_weight, key_weight, value_weight, alpha_weight, beta_weight, small], axis=1
-    ).astype(low)
-    before = passed_along(tokens[length - 16 :], "seq", 1)
-    shard_mix = jnp.concatenate([gate_weight.astype(low), output_weight.T.astype(low)], axis=1)
-    shard_ffn = jnp.concatenate(
-        [ffn_gate.astype(low), ffn_up.astype(low), ffn_down.T.astype(low)], axis=1
+    small = jnp.concatenate(
+        [alpha_weight, beta_weight, jnp.zeros((alpha_weight.shape[0], LANES - 2 * heads), full)], axis=1
     )
-    meta, edge_meta, segrow = segment_tables(doc_lengths, shard, length)
     taps = jnp.concatenate([query_taps, key_taps, value_taps], axis=1)
     params = jnp.stack([-jnp.exp(decay_log), decay_bias])
     params = jnp.pad(params, ((0, 6), (0, LANES - heads)))
     gain = head_gain[None, :]
 
-    first_in, pre, ab, edge, w_in = input_projection(tokens, before, mixer_gain, shard_in, wide, last)
+    if near:
+        heavy = [query_weight, key_weight, value_weight, small, gate_weight, output_weight]
+        heavy += [ffn_gate, ffn_up, ffn_down]
+    else:
+        shard_in = jnp.concatenate([query_weight, key_weight, value_weight, small], axis=1)
+        heavy = [lax.all_gather(shard_in.astype(low), "seq", axis=0, tiled=True)]
+    meta, edge_meta, segrow = segment_tables(doc_lengths, shard, length)
+    first_in, pre, ab, edge, w_in, *laid = input_projection(
+        tokens, passed_along(tokens[length - 16 :], "seq", 1), mixer_gain, heavy, wide
+    )
+    if near:
+        shard_mix, shard_ffn = laid
+    else:
+        shard_mix = jnp.concatenate([gate_weight, output_weight.T], axis=1).astype(low)
+        shard_ffn = jnp.concatenate([ffn_gate, ffn_up, ffn_down.T], axis=1).astype(low)
     edge = edge[8:]
     local, through, states, inverse, end, *moved = forward_chain(
         pre, ab, meta, segrow, edge, taps, params, heads, key, value, shard_mix if near else None
     )
-    w_mix = moved[0] if near else lax.all_gather(shard_mix, "seq", axis=0, tiled=True)
-    ends = lax.all_gather(end, "seq")
+    end = end.reshape(keys, value + key)
+    if near:
+        held, moving = [moved[0]], dict(early=end, gathers=[shard_ffn])
+        (w_mix,) = held
+    else:
+        w_mix = lax.all_gather(shard_mix, "seq", axis=0, tiled=True)
+        ends = lax.all_gather(end, "seq", axis=0, tiled=True)
+        held, moving = [w_mix, ends], {}
     mix_out, mixed, gate_pre, state_in, middle, second_in, *moved = line_call(
         partial(mixer_out_kernel, heads, key, value, last), "mixer_out", 0, length, width, last,
-        [ends, gain, ffn_gain[None, :]], [w_mix], [first_in, local, through], [tokens],
+        [gain, ffn_gain[None, :]], held, [first_in, local, through], [tokens],
         [((length, vals), low, "first"), ((length, vals), full, "first"),
          ((length, vals), full, "first"), ((heads, key, value), full, "all"),
          ((length, width), full, "second"), ((length, width), low, "second")],
-        [], gathers=[shard_ffn] if near else [],
+        [], **moving,
     )
-    w_ffn = moved[0] if near else lax.all_gather(shard_ffn, "seq", axis=0, tiled=True)
+    if near:
+        ends, w_ffn = moved
+    else:
+        w_ffn = lax.all_gather(shard_ffn, "seq", axis=0, tiled=True)
     hidden, gate_grad, lift_grad, narrow_part, middle_grad, middle_low, ffn_gain_part = line_call(
         partial(ffn_kernel, last, size), "ffn", 1, length, width, last,
         [ffn_gain[None, :]], [w_ffn], [second_in, cotangent], [middle, cotangent],
@@ -1416,7 +1581,7 @@
            ((length, width), low, "second"), ((8, width), full, "all")],
         [pltpu.VMEM((ROWS, size), full)] * 2,
     )
-    result = (middle + lax.psum(narrow_part, "head").astype(full)).astype(low)
+    narrow_sum = lax.psum_scatter(narrow_part, "head", scatter_dimension=0, tiled=True)
     gate_pgrad, mixed_grad, head_gain_part, adjoint = gate_back(
         middle_low, w_mix, mixed, gate_pre, gain, through, heads, key, value
     )
@@ -1425,25 +1590,42 @@
     pairs_rest = [(cotangent, [hidden]), (first_in, [gate_pgrad]), (middle_low, [mix_out])]
     sums_up = pair_sums(place, pairs_up) if near else None
     sums_rest = pair_sums(place, pairs_rest) if near else None
+    if near:
+        narrow_sum, sums_up = lax.optimization_barrier((narrow_sum, sums_up))
+    narrow_sum = lax.all_gather(narrow_sum, "head", axis=0, tiled=True)
+    result = (middle + narrow_sum.astype(full)).astype(low)
     pre_grad, ab_grad, halo, taps_part, params_part, *moved = backward_chain(
         pre, ab, meta, segrow, edge, edge_meta, taps, params, states, inverse, state_in,
         mixed_grad, ends, adjoints, heads, key, value, sums_up,
     )
-    up_wgrad = far_sums(sums_up, moved[0]) if near else plain_sums(place, pairs_up)
+    got_up = moved
     halo = passed_along(halo, "seq", -1)
     tail = pre_grad[length - 8 :].astype(full) + halo
     pre_grad = lax.dynamic_update_slice(pre_grad, tail.astype(low), (length - 8, 0))
     pairs_in = [(first_in, [pre_grad, ab_grad])]
     sums_in = pair_sums(place, pairs_in) if near else None
-    tokens_grad, mixer_gain_part, *moved = line_call(
+    term, mixer_gain_part, *moved = line_call(
         partial(input_grad_kernel, last, keys, vals), "input_grad", 2, length, width, last,
         [mixer_gain[None, :]], [w_in, w_mix], [pre_grad, gate_pgrad, ab_grad],
-        [tokens, middle_grad],
-        [((length, width), full, "second"), ((8, width), full, "all")],
+        [tokens],
+        [((length, width), low, "second"), ((8, width), full, "all")],
         [pltpu.VMEM((ROWS, width), full)], scatters=[sums_rest, sums_in] if near else [],
     )
-    rest_wgrad = far_sums(sums_rest, moved[0]) if near else plain_sums(place, pairs_rest)
-    in_wgrad = far_sums(sums_in, moved[1]) if near else plain_sums(place, pairs_in)
+    if near:
+        (tokens_grad, query_grad, key_grad, value_grad, alpha_grad, beta_grad, up_grad, lift_grad,
+         down_grad, gate_grad, out_grad) = final_sums(
+            middle_grad, term, sums_in, moved[1], sums_up, got_up[0], sums_rest, moved[0],
+            heads, keys, vals, size,
+        )
+    else:
+        up, rest, into = (plain_sums(place, pairs) for pairs in (pairs_up, pairs_rest, pairs_in))
+        tokens_grad = middle_grad + term.astype(full)
+        query_grad, key_grad, value_grad = into[:, :keys], into[:, keys : 2 * keys], into[:, 2 * keys : wide]
+        alpha_grad, beta_grad = into[:, wide : wide + heads], into[:, wide + heads : wide + 2 * heads]
+        up_grad, lift_grad = up[:, :size], up[:, size:]
+        down_grad, gate_grad, out_grad = (
+            rest[:, :size].T, rest[:, size : size + vals], rest[:, size + vals :].T
+        )
     params_part = jnp.sum(params_part.reshape(2, 8, LANES), axis=1).reshape(1, -1)
     lines = [
         jnp.sum(mixer_gain_part, axis=0, keepdims=True),
@@ -1458,23 +1640,23 @@
         result,
         tokens_grad,
         sums[0],
-        in_wgrad[:, :keys],
-        in_wgrad[:, keys : 2 * keys],
-        in_wgrad[:, 2 * keys : wide],
-        rest_wgrad[:, size : size + vals],
-        in_wgrad[:, wide : wide + heads],
-        in_wgrad[:, wide + heads : wide + 2 * heads],
+        query_grad,
+        key_grad,
+        value_grad,
+        gate_grad,
+        alpha_grad,
+        beta_grad,
         sums[6, LANES : LANES + heads],
         sums[6, :heads],
         taps_grad[:, :keys],
         taps_grad[:, keys : 2 * keys],
         taps_grad[:, 2 * keys :],
         sums[7, :value],
-        rest_wgrad[:, size + vals :].T,
+        out_grad,
         sums[1],
-        up_wgrad[:, :size],
-        up_wgrad[:, size:],
-        rest_wgrad[:, :size].T,
+        up_grad,
+        lift_grad,
+        down_grad,
     )
 
 

time: 841 us -> 787 us (0.936)
  waiting for transfers between devices: 78.8 us -> 19.5 us
  Pallas kernels: 653 us -> 698 us
  other arithmetic: 30.5 us -> 13.9 us
  local copies, waits for them, and re-layouts: 44 us -> 28.3 us
    psum x1 -> x0, waiting for transfers between devices: 37.8 us -> none  [shards(): result = (middle + lax.psum(narrow_part, 'head').astype(full)).astype(low)]
    all_gather x1, waiting for transfers between devices: 27.4 us -> 0.01 us  [shards(): narrow_sum = lax.all_gather(narrow_sum, 'head', axis=0, tiled=True)]
    pallas_call x3, Pallas kernels: 385 us -> 410 us  [line_call(): pl.pallas_call(body, grid=(steps,), in_specs=in_specs, out_specs=out_spec...]
    pallas_call x1 -> x2, Pallas kernels: 55.9 us -> 74.5 us  [the longest x1 56.8 us: input_projection(): pl.pallas_call(partial(input_kernel, wide, gathering), in_specs=[here] +...]
    add x3 -> x0, other arithmetic: 8.61 us -> none  [far_sums(): return sum((got[k] for k in range(3)), start=sums[0].astype(full))]
    unnamed x69 -> x54, local copies, waits for them, and re-layouts: 22.5 us -> 16.6 us
  transfers between devices with their start and end apart: 14 -> 14, of which waited for: 5 -> 5; matrix products, arithmetic and copies ran while one was open for 4% -> 3% of each run, Pallas kernels for 16% -> 41%
where the time goes in v4:
time: 787 us; the launch traced here: 785 us
  Pallas kernels  698 us (89%)
  local copies, waits for them, and re-layouts  28.3 us (4%)
  waiting for transfers between devices  19.5 us (2%)
  between operations  14.7 us (2%)
  other arithmetic  13.9 us (2%)
  starting transfers between devices  11.1 us (1%)
    pallas_call x3, Pallas kernels, line_call(): pl.pallas_call(body, grid=(steps,), in_specs=in_specs, out_specs=out_spec...  410 us
    pallas_call x6, Pallas kernels, weight_call(): pl.pallas_call(partial(weight_kernel, [len(bs) for _, bs in pairs], added...  71.5 us
    pallas_call x1, Pallas kernels, backward_chain(): pl.pallas_call(partial(backward_kernel, heads, key, value, devices, masks...  69.4 us
    pallas_call x1, Pallas kernels, input_projection(): pl.pallas_call(partial(input_kernel, wide, gathering), in_specs=[here] +...  56.8 us
    pallas_call x1, Pallas kernels, forward_chain(): pl.pallas_call(partial(forward_kernel, heads, key, value, gathering), gri...  43.7 us
    pallas_call x1, Pallas kernels, final_sums(): pl.pallas_call(partial(final_kernel, heads, keys, vals, size), grid=(size...  17.8 us
    unnamed x54, local copies, waits for them, and re-layouts  16.6 us
  transfers between devices with their start and end apart: 14, of which 5 were waited for; matrix products, arithmetic and copies ran while one was open for 3% of the time, Pallas kernels for 41%

profile of v4, /device:TPU:0, one launch (start us, length us, event | category | flops | bytes accessed | tf_op | source)
XLA Modules:
  0.0 784.9 jit_solution(12954491695049187312)
XLA Ops:
  7.2 0.8 slice.86
  8.1 2.3 collective-permute-start
  10.4 0.8 reduce-window.9
  13.0 0.7 constant_dynamic-update-slice_fusion.2
  13.8 0.8 copy.112
  14.6 0.8 copy.113
  15.9 0.7 constant_dynamic-update-slice_fusion.1
  16.7 0.7 constant_dynamic-update-slice_fusion.taps_ref
  17.4 0.8 maximum_maximum_fusion.refs_3_
  19.5 56.8 %input_projection.1 = (bf16[1024,2048]{1,0:T(8,128)(2,1)}, bf16[1024,2048]{1,0:T(8,128)(2,1)}, f32[1024,128]{1,0:T(8,128)}, bf16[16,2048]{1,0:T(8,128)(2,1)}, bf...) custom-call(f32[1,2048]{1,0:T(1,128)} %bitcast.73, f32[256,512]{1,0:T(8,128)} %refs_0_.3, ...), custom_call_target="tpu_custom_call" | custom-call | flops 1 | bytes 1 | tf_op jit(solution)/shard_map/input_projection/pallas_call | solution.py:1252
  76.2 0.8 slice.96.edge_ref
  77.1 1.0 copy-done.6
  78.1 1.2 copy-done.8
  79.3 43.7 %chain_forward.1 = (f32[1024,1024]{1,0:T(8,128)}, bf16[1024,512]{1,0:T(8,128)(2,1)S(1)}, bf16[8,4,128,384]{3,2,1,0:T(8,128)(2,1)}, bf16[8,4,128,128]{3,2,1,0:T(8...) custom-call(bf16[1024,2048]{1,0:T(8,128)(2,1)} %get-tuple-element.75.pre_ref.tail_ref, ...), custom_call_target="tpu_custom_call" | custom-call | flops 1 | bytes 1 | tf_op jit(solution)/shard_map/chain_forward/pallas_call | solution.py:354
  123.1 1.0 copy-done.2
  124.0 1.0 copy-done.7
  125.0 0.7 copy-done.9
  125.7 147.6 %mixer_out.1 = (bf16[1024,1024]{1,0:T(8,128)(2,1)}, f32[1024,1024]{1,0:T(8,128)}, f32[1024,1024]{1,0:T(8,128)}, f32[4,128,256]{2,1,0:T(8,128)}, f32[1024,2048]{1...) custom-call(f32[1,256]{1,0:T(1,128)} %bitcast.61, ...), custom_call_target="tpu_custom_call" | custom-call | flops 1 | bytes 1 | tf_op jit(solution)/shard_map/mixer_out/pallas_call | solution.py:982
  273.3 131.1 %ffn.1 = (bf16[1024,1408]{1,0:T(8,128)(2,1)}, bf16[1024,1408]{1,0:T(8,128)(2,1)}, bf16[1024,1408]{1,0:T(8,128)(2,1)}, bf16[1024,2048]{1,0:T(8,128)(2,1)}, f32[10...) custom-call(f32[1,2048]{1,0:T(1,128)} %bitcast.72, bf16[2048,4224]{1,0:T(8,128)(2,1)} %get-tuple-element.86.refs_1_, ...), custom_call_target="tpu_custom_call" | custom-call | flops 1 | bytes 1 | tf_op jit(solution)/shard_map/ffn/pallas_call | solution.py:982
  404.6 11.9 %weight_grads.6 = bf16[4,256,2816]{2,1,0:T(8,128)(2,1)} custom-call(s32[1]{0:T(128)} %bitcast.20.place_ref, bf16[1024,2048]{1,0:T(8,128)(2,1)} %get-tuple-element.87.refs_2_.refs_0_, bf16[1024,1408]{1,0:T(8,128)(2,1)} %get-tuple-element.89.refs_1_, bf16[1024,1408]{1,0:T(8,128)(2,1)} %get-tuple-element.90.refs_2_), custom_call_target="tpu_custom_call" | custom-call | flops 1 | bytes 1 | tf_op jit(solution)/shard_map/weight_grads/pallas_call | solution.py:1312
  416.5 12.7 %gate_back.1 = (bf16[1024,1024]{1,0:T(8,128)(2,1)S(1)}, bf16[1024,1024]{1,0:T(8,128)(2,1)S(1)}, f32[8,256]{1,0:T(8,128)S(1)}, f32[4,128,256]{2,1,0:T(8,128)S(1)}) custom-call(bf16[1024,2048]{1,0:T(8,128)(2,1)} %get-tuple-element.94.dz_ref.refs_2_, f32[1024,1024]{1,0:T(8,128)} %get-tuple-element.96.mixed_ref, f32[1024,1024]{1,0:T(8,128)} %get-tuple-element.97.gate_ref, ...), custom_call_target="tpu_custom_call" | custom-call | flops 1 | bytes 1 | tf_op jit(solution)/shard_map/gate_back/pallas_call | solution.py:429
  429.2 1.3 copy-done
  430.5 1.3 copy-done.5
  431.8 13.5 %weight_grads.8 = bf16[4,256,3456]{2,1,0:T(8,128)(2,1)} custom-call(s32[1]{0:T(128)} %bitcast.20.place_ref, bf16[1024,2048]{1,0:T(8,128)(2,1)} %refs_0_.5, bf16[1024,2048]{1,0:T(8,128)(2,1)} %get-tuple-element.82.refs_5_.refs_1_.refs_0_, bf16[1024,2048]{1,0:T(8,128)(2,1)} %get-tuple-element.94.dz_ref.refs_2_, bf16[1024,1408]{1,0:T(8,128)(2,1)} %get-tuple-element.95.refs_3_, ...), custom_call_target="tpu_custom_call" | custom-call | flops 1 | bytes 1 | tf_op jit(solution)/shard_map/weight_grads/pallas_call | solution.py:1312
  445.8 2.9 collective-permute-start.5
  449.4 6.6 collective-permute-done.5.refs_3_
  456.0 4.8 collective-permute-done.4.refs_2_
  461.9 2.0 copy-done.15
  463.9 12.2 %weight_grads.7.refs_8_.up_own = bf16[4,256,2816]{2,1,0:T(8,128)(2,1)} custom-call(s32[1]{0:T(128)} %bitcast.20.place_ref, bf16[1024,2048]{1,0:T(8,128)(2,1)} %get-tuple-element.87.refs_2_.refs_0_, bf16[1024,1408]{1,0:T(8,128)(2,1)} %get-tuple-element.89.refs_1_, bf16[1024,1408]{1,0:T(8,128)(2,1)} %get-tuple-element.90.refs_2_, bf16[4,256,2816]{2,1,0:T(8,128)(2,1)} %copy-done.15), custom_call_target="tpu_custom_call" | custom-call | flops 1 | bytes 1 | tf_op jit(solution)/shard_map/weight_grads/pallas_call | solution.py:1312
  476.0 5.5 reduce-scatter.2.cloned.1.call-done
  483.0 69.4 %chain_backward.1 = (bf16[1024,2048]{1,0:T(8,128)(2,1)}, bf16[1024,128]{1,0:T(8,128)(2,1)}, f32[8,2048]{1,0:T(8,128)}, f32[32,2048]{1,0:T(8,128)}, f32[16,128]{1,0:T(8,128)}, /*index=5*/bf16[3,256,2816]{2,1,0:T(8,128)(2,1)}) custom-call(bf16[1024,2048]{1,0:T(8,128)(2,1)} %get-tuple-element.75.pre_ref.tail_ref, ...), custom_call_target="tpu_custom_call" | custom-call | flops 1 | bytes 1 | tf_op jit(solution)/shard_map/chain_backward/pallas_call | solution.py:682
  552.5 1.3 collective-permute-start.10
  553.8 2.1 collective-permute-done.10
  555.8 1.4 fusion.refs_1_.refs_5_
  557.2 9.4 %weight_grads.10 = bf16[4,256,2176]{2,1,0:T(8,128)(2,1)} custom-call(s32[1]{0:T(128)} %bitcast.20.place_ref, bf16[1024,2048]{1,0:T(8,128)(2,1)} %get-tuple-element.82.refs_5_.refs_1_.refs_0_, bf16[1024,2048]{1,0:T(8,128)(2,1)} %fusion.refs_1_.refs_5_, bf16[1024,128]{1,0:T(8,128)(2,1)} %get-tuple-element.109.refs_2_.refs_7_), custom_call_target="tpu_custom_call" | custom-call | flops 1 | bytes 1 | tf_op jit(solution)/shard_map/weight_grads/pallas_call | solution.py:1312
  566.6 2.7 collective-permute-start.11
  569.3 14.6 %weight_grads.9.refs_3_.down_own.gate_own.out_own = bf16[4,256,3456]{2,1,0:T(8,128)(2,1)} custom-call(s32[1]{0:T(128)} %bitcast.20.place_ref, bf16[1024,2048]{1,0:T(8,128)(2,1)} %refs_0_.5, bf16[1024,2048]{1,0:T(8,128)(2,1)} %get-tuple-element.82.refs_5_.refs_1_.refs_0_, bf16[1024,2048]{1,0:T(8,128)(2,1)} %get-tuple-element.94.dz_ref.refs_2_, ...), custom_call_target="tpu_custom_call" | custom-call | flops 1 | bytes 1 | tf_op jit(solution)/shard_map/weight_grads/pallas_call | solution.py:1312
  584.1 9.9 %weight_grads.11.refs_4_.in_own = bf16[4,256,2176]{2,1,0:T(8,128)(2,1)} custom-call(s32[1]{0:T(128)} %bitcast.20.place_ref, bf16[1024,2048]{1,0:T(8,128)(2,1)} %get-tuple-element.82.refs_5_.refs_1_.refs_0_, bf16[1024,2048]{1,0:T(8,128)(2,1)} %fusion.refs_1_.refs_5_, bf16[1024,128]{1,0:T(8,128)(2,1)} %get-tuple-element.109.refs_2_.refs_7_, ...), custom_call_target="tpu_custom_call" | custom-call | flops 1 | bytes 1 | tf_op jit(solution)/shard_map/weight_grads/pallas_call | solution.py:1312
  594.0 131.8 %input_grad.1 = (bf16[1024,2048]{1,0:T(8,128)(2,1)}, f32[8,2048]{1,0:T(8,128)}, bf16[3,256,3456]{2,1,0:T(8,128)(2,1)}, bf16[3,256,2176]{2,1,0:T(8,128)(2,1)}) custom-call(f32[1,2048]{1,0:T(1,128)} %bitcast.74, bf16[2048,2176]{1,0:T(8,128)(2,1)} %get-tuple-element.93.refs_1_, bf16[2048,2048]{1,0:T(8,128)(2,1)} %get-tuple-element.79.refs_2_.whole_ref, ...), custom_call_target="tpu_custom_call" | custom-call | flops 1 | bytes 1 | tf_op jit(solution)/shard_map/input_grad/pallas_call | solution.py:982
  725.8 1.9 copy-done.4
  727.8 17.8 %final_sums.1 = (f32[1024,2048]{1,0:T(8,128)}, f32[256,512]{1,0:T(8,128)}, f32[256,512]{1,0:T(8,128)}, f32[256,1024]{1,0:T(8,128)}, f32[256,4]{1,0:T(8,128)S(1)}...) custom-call(f32[1024,2048]{1,0:T(8,128)} %get-tuple-element.92.dmidd, ...), custom_call_target="tpu_custom_call" | custom-call | flops 1 | bytes 1 | tf_op jit(solution)/shard_map/final_sums/pallas_call | solution.py:1380
  746.3 15.2 %small_sums.1 = f32[8,2048]{1,0:T(8,128)} custom-call(f32[8,2048]{1,0:T(8,128)} %concatenate.11.part_ref), custom_call_target="tpu_custom_call" | custom-call | tf_op jit(solution)/shard_map/small_sums/pallas_call | solution.py:1469
  761.5 1.3 slice.111
  762.7 1.4 slice.110
  765.5 1.2 slice_bitcast_fusion.1
  766.7 1.3 fusion.16
  768.0 1.5 fusion.15
  769.5 8.3 %add_convert_fusion = bf16[1024,2048]{1,0:T(8,128)(2,1)} fusion(f32[1024,2048]{1,0:T(8,128)} %get-tuple-element.85.refs_4_, bf16[1024,2048]{1,0:T(8,128)(2,1)} %all-gather.2.cloned.1.call-done), kind=kLoop, calls=%fused_computation | loop fusion | flops 6291456 | bytes 16777216 | tf_op jit(solution)/shard_map/convert_element_type | solution.py:1596
  (98 shorter events, 9.7 us)
Async XLA Ops:
  7.2 474.4 %reduce-scatter.2.cloned.1.call-start = ((), (), s32[]{:S(2)}) async-start(), calls=%async_computation.1 | async-start | bytes 5242880 | tf_op jit(solution)/shard_map/reduce_scatter | solution.py:1584
  8.1 10.8 %collective-permute-start = (bf16[16,2048]{1,0:T(8,128)(2,1)S(1)}, bf16[16,2048]{1,0:T(8,128)(2,1)S(1)}, u32[]{:S(2)}, u32[]{:S(2)}) collective-permute-start(bf16[16,2048]{1,0:T(8,128)(2,1)S(1)} %slice.86), channel_id=1, source_target_pairs={{0,4},{4,8},{8,12},{12,16},{16,20},{20,24},{24,28},{1,5},{5,9},{9,... | collective-permute-start | bytes 196616 | tf_op jit(solution)/shard_map/ppermute | solution.py:1491
  15.8 61.2 %copy-start.1 = (f32[1024,128]{1,0:T(8,128)}, f32[1024,128]{1,0:T(8,128)S(1)}, u32[]{:S(2)}) copy-start(f32[1024,128]{1,0:T(8,128)S(1)} %pad.19.meta_ref) | copy-start | bytes 1572868
  17.4 59.6 %copy-start.12 = (f32[4,2048]{1,0:T(4,128)}, f32[4,2048]{1,0:T(4,128)S(1)}, u32[]{:S(2)}) copy-start(f32[4,2048]{1,0:T(4,128)S(1)} %constant_dynamic-update-slice_fusion.taps_ref) | copy-start | bytes 98308
  18.8 58.2 %copy-start.13 = (f32[8,128]{1,0:T(8,128)}, f32[8,128]{1,0:T(8,128)S(1)}, u32[]{:S(2)}) copy-start(f32[8,128]{1,0:T(8,128)S(1)} %select_maximum_fusion.params_ref) | copy-start | bytes 12292
  18.8 0.6 copy-start.20
  77.0 196.3 %copy-start.10 = (bf16[8,2048]{1,0:T(8,128)(2,1)}, bf16[8,2048]{1,0:T(8,128)(2,1)S(1)}, u32[]{:S(2)}) copy-start(bf16[8,2048]{1,0:T(8,128)(2,1)S(1)} %slice.96.edge_ref) | copy-start | bytes 98308
  77.0 196.3 %copy-start.11 = (f32[8,1024]{1,0:T(8,128)}, f32[8,1024]{1,0:T(8,128)S(1)}, u32[]{:S(2)}) copy-start(f32[8,1024]{1,0:T(8,128)S(1)} %broadcast_in_dim.39.segrow_ref) | copy-start | bytes 98308
  77.0 1.0 copy-start.6
  78.1 1.2 copy-start.8
  123.0 1.0 copy-start.2
  124.0 1.0 copy-start.7
  125.0 0.7 copy-start.9
  404.5 365.0 %all-gather.2.cloned.1.call-start = ((), (), s32[]{:S(2)}) async-start(), calls=%async_computation.2 | async-start | bytes 5242880 | tf_op jit(solution)/shard_map/all_gather | solution.py:1595
  404.5 11.9 %copy-start.3 = (bf16[1024,512]{1,0:T(8,128)(2,1)S(1)}, bf16[1024,512]{1,0:T(8,128)(2,1)}, u32[]{:S(2)}) copy-start(bf16[1024,512]{1,0:T(8,128)(2,1)} %copy-done.2) | copy-start | bytes 3145732
  404.5 11.9 %copy-start.14 = (f32[256]{0:T(256)S(1)}, f32[256]{0:T(256)}, u32[]{:S(2)}) copy-start(f32[256]{0:T(256)} %param.35) | copy-start | bytes 3076
  416.4 44.9 %collective-permute-start.1 = (bf16[4,256,2816]{2,1,0:T(8,128)(2,1)}, bf16[4,256,2816]{2,1,0:T(8,128)(2,1)S(1)}, u32[]{:S(2)}, u32[]{:S(2)}) collective-permute-start(bf16[4,256,2816]{2,1,0:T(8,128)(2,1)} %weight_grads.6), channel_id=1, source_target_pairs={{0,4},{4,0},{8,12},{12,8},{16,20},{20,16},{24,28},{28,24},{1,5},{5... | collective-permute-start | bytes 17301512 | tf_op jit(solution)/shard_map/ppermute | solution.py:770
  429.2 1.3 copy-start
  430.5 1.3 copy-start.5
  445.2 124.1 %collective-permute-start.2 = (bf16[4,256,3456]{2,1,0:T(8,128)(2,1)}, bf16[4,256,3456]{2,1,0:T(8,128)(2,1)}, u32[]{:S(2)}, u32[]{:S(2)}) collective-permute-start(bf16[4,256,3456]{2,1,0:T(8,128)(2,1)} %weight_grads.8), channel_id=1, source_target_pairs={{0,4},{4,0},{8,12},{12,8},{16,20},{20,16},{24,28},{28,24},{1,5},{5... | collective-permute-start | bytes 21233672 | tf_op jit(solution)/shard_map/ppermute | solution.py:770
  445.8 37.2 %copy-start.16 = (bf16[4,128,256]{2,1,0:T(8,128)(2,1)}, bf16[4,128,256]{2,1,0:T(8,128)(2,1)S(1)}, u32[]{:S(2)}) copy-start(bf16[4,128,256]{2,1,0:T(8,128)(2,1)S(1)} %convert_element_type.29) | copy-start | bytes 786436
  445.8 10.2 %collective-permute-start.5 = (bf16[512,256]{1,0:T(8,128)(2,1)S(1)}, bf16[512,256]{1,0:T(8,128)(2,1)S(1)}, u32[]{:S(2)}, u32[]{:S(2)}) collective-permute-start(bf16[512,256]{1,0:T(8,128)(2,1)S(1)} %bitcast.63), channel_id=1, source_target_pairs={{0,24},{4,28},{8,16},{12,20},{16,8},{20,12},{24,0},{28,4},{1,25},{... | collective-permute-start | bytes 786440 | tf_op jit(solution)/shard_map/ppermute | solution.py:770
  448.7 12.1 %collective-permute-start.4 = (bf16[512,256]{1,0:T(8,128)(2,1)S(1)}, bf16[512,256]{1,0:T(8,128)(2,1)S(1)}, u32[]{:S(2)}, u32[]{:S(2)}) collective-permute-start(bf16[512,256]{1,0:T(8,128)(2,1)S(1)} %bitcast.64), channel_id=1, source_target_pairs={{0,16},{4,20},{8,24},{12,28},{16,0},{20,4},{24,8},{28,12},{1,17},{... | collective-permute-start | bytes 786440 | tf_op jit(solution)/shard_map/ppermute | solution.py:770
  448.8 12.5 %collective-permute-start.3 = (bf16[512,256]{1,0:T(8,128)(2,1)S(1)}, bf16[512,256]{1,0:T(8,128)(2,1)}, u32[]{:S(2)}, u32[]{:S(2)}) collective-permute-start(bf16[512,256]{1,0:T(8,128)(2,1)S(1)} %bitcast.65), channel_id=1, source_target_pairs={{0,8},{4,12},{8,0},{12,4},{16,24},{20,28},{24,16},{28,20},{1,9},{5... | collective-permute-start | bytes 786440 | tf_op jit(solution)/shard_map/ppermute | solution.py:770
  456.0 27.0 %copy-start.17 = (bf16[512,256]{1,0:T(8,128)(2,1)}, bf16[512,256]{1,0:T(8,128)(2,1)S(1)}, u32[]{:S(2)}) copy-start(bf16[512,256]{1,0:T(8,128)(2,1)S(1)} %collective-permute-done.5.refs_3_) | copy-start | bytes 786436
  456.0 27.0 %collective-permute-start.6 = (bf16[512,256]{1,0:T(8,128)(2,1)S(1)}, bf16[512,256]{1,0:T(8,128)(2,1)}, u32[]{:S(2)}, u32[]{:S(2)}) collective-permute-start(bf16[512,256]{1,0:T(8,128)(2,1)S(1)} %bitcast.66), channel_id=1, source_target_pairs={{0,4},{4,0},{8,12},{12,8},{16,20},{20,16},{24,28},{28,24},{1,5},{5... | collective-permute-start | bytes 786440 | tf_op jit(solution)/shard_map/ppermute | solution.py:770
  460.8 22.2 %copy-start.18 = (bf16[512,256]{1,0:T(8,128)(2,1)}, bf16[512,256]{1,0:T(8,128)(2,1)S(1)}, u32[]{:S(2)}) copy-start(bf16[512,256]{1,0:T(8,128)(2,1)S(1)} %collective-permute-done.4.refs_2_) | copy-start | bytes 786436
  460.8 22.2 %collective-permute-start.9 = (bf16[512,256]{1,0:T(8,128)(2,1)S(1)}, bf16[512,256]{1,0:T(8,128)(2,1)}, u32[]{:S(2)}, u32[]{:S(2)}) collective-permute-start(bf16[512,256]{1,0:T(8,128)(2,1)S(1)} %collective-permute-done.5.refs_3_), channel_id=1, source_target_pairs={{0,4},{4,0},{8,12},{12,8},{16,20},{20,16},{24,28},{28,24},{1,5},{5... | collective-permute-start | bytes 786440 | tf_op jit(solution)/shard_map/ppermute | solution.py:770
  461.3 21.6 %collective-permute-start.8 = (bf16[512,256]{1,0:T(8,128)(2,1)S(1)}, bf16[512,256]{1,0:T(8,128)(2,1)}, u32[]{:S(2)}, u32[]{:S(2)}) collective-permute-start(bf16[512,256]{1,0:T(8,128)(2,1)S(1)} %collective-permute-done.4.refs_2_), channel_id=1, source_target_pairs={{0,4},{4,0},{8,12},{12,8},{16,20},{20,16},{24,28},{28,24},{1,5},{5... | collective-permute-start | bytes 786440 | tf_op jit(solution)/shard_map/ppermute | solution.py:770
  461.4 2.5 copy-start.15
  461.4 21.6 %collective-permute-start.7 = (bf16[512,256]{1,0:T(8,128)(2,1)}, bf16[512,256]{1,0:T(8,128)(2,1)}, u32[]{:S(2)}, u32[]{:S(2)}) collective-permute-start(bf16[512,256]{1,0:T(8,128)(2,1)} %collective-permute-done.3.refs_1_), channel_id=1, source_target_pairs={{0,4},{4,0},{8,12},{12,8},{16,20},{20,16},{24,28},{28,24},{1,5},{5... | collective-permute-start | bytes 786440 | tf_op jit(solution)/shard_map/ppermute | solution.py:770
  552.5 3.4 collective-permute-start.10
  557.2 12.1 %copy-start.21 = (f32[8,2048]{1,0:T(8,128)S(1)}, f32[8,2048]{1,0:T(8,128)}, u32[]{:S(2)}) copy-start(f32[8,2048]{1,0:T(8,128)} %get-tuple-element.116) | copy-start | bytes 196612
  566.6 17.5 %collective-permute-start.11 = (bf16[4,256,2176]{2,1,0:T(8,128)(2,1)}, bf16[4,256,2176]{2,1,0:T(8,128)(2,1)}, u32[]{:S(2)}, u32[]{:S(2)}) collective-permute-start(bf16[4,256,2176]{2,1,0:T(8,128)(2,1)} %weight_grads.10), channel_id=1, source_target_pairs={{0,4},{4,0},{8,12},{12,8},{16,20},{20,16},{24,28},{28,24},{1,5},{5... | collective-permute-start | bytes 13369352 | tf_op jit(solution)/shard_map/ppermute | solution.py:770
  569.3 14.7 %copy-start.23 = (f32[16,128]{1,0:T(8,128)S(1)}, f32[16,128]{1,0:T(8,128)}, u32[]{:S(2)}) copy-start(f32[16,128]{1,0:T(8,128)} %get-tuple-element.118) | copy-start | bytes 24580
  569.3 14.7 %copy-start.19 = (f32[32,2048]{1,0:T(8,128)S(1)}, f32[32,2048]{1,0:T(8,128)}, u32[]{:S(2)}) copy-start(f32[32,2048]{1,0:T(8,128)} %get-tuple-element.117) | copy-start | bytes 786436
  725.8 1.9 copy-start.4
  727.8 17.8 %copy-start.22 = (f32[8,2048]{1,0:T(8,128)S(1)}, f32[8,2048]{1,0:T(8,128)}, u32[]{:S(2)}) copy-start(f32[8,2048]{1,0:T(8,128)} %get-tuple-element.115) | copy-start | bytes 196612
Sparse Core Ops, SparseCore 0:
  404.6 76.8 reduce-scatter.1
  483.2 81.2 all-gather.1

commit v5 on v4

--- a/solution.py
+++ b/solution.py
@@ -894,9 +894,10 @@
 
 
 def line_call(kernel, name, collective, length, width, last, resident, weights, entering, leaving, outs,
-              scratch, gathers=(), scatters=(), early=None):
+              scratch, gathers=(), scatters=(), early=None, masks=()):
     blocks = length // ROWS
     steps = blocks + AHEAD
+    cuts, weights = [c for _, c in weights], [a for a, _ in weights]
 
     def spec(array, stage):
         if stage == "first":
@@ -919,7 +920,7 @@
     moved += [jax.ShapeDtypeStruct((3,) + a.shape[1:], low) for a in scatters]
     kinds = [Gather] * len(gathers) + [Scatter] * len(scatters)
     whole_first = [pltpu.VMEM(s.shape, low) for s in moved[: len(first_one)]]
-    held = [pltpu.VMEM(a.shape, low) for a in weights] + [pltpu.SemaphoreType.DMA((len(weights),))]
+    held = [pltpu.VMEM(a.shape, low) for a in weights] + [pltpu.SemaphoreType.DMA((sum(len(c) for c in cuts),))]
     held += whole_first + [s for _ in first_one for s in Gather.semaphores]
     held += [s for kind in kinds for s in kind.semaphores]
 
@@ -946,11 +947,28 @@
 
         @pl.when(step == 0)
         def _():
-            greet(union(kinds + [Gather] * len(first_one)), last)
+            greet(sorted({*masks, *union(kinds + [Gather] * len(first_one))}), last)
             for c in [lead] if first_one else carried:
                 c.start()
 
-        load(step, list(zip(heavy, matrices)), sems)
+        waits = []
+        for source, target, parts in zip(heavy, matrices, cuts):
+            for first, count in parts:
+                part = pl.ds(first, count)
+                waits.append(
+                    pltpu.make_async_copy(source.at[:, part], target.at[:, part], sems.at[len(waits)])
+                )
+
+        @pl.when(step == 0)
+        def _():
+            for copy in waits:
+                copy.start()
+
+        def ready(k):
+            @pl.when(step == 0)
+            def _():
+                waits[k].wait()
+
         if first_one:
 
             @pl.when(step == 0)
@@ -970,7 +988,7 @@
                     if isinstance(c, Gather):
                         getattr(c, turn)()
 
-        kernel(matrices, *own_in, *chunks, *own_out, *own_scratch)
+        kernel(ready, matrices, *own_in, *chunks, *own_out, *own_scratch)
 
         @pl.when(step == steps - 1)
         def _():
@@ -994,7 +1012,7 @@
     )(*resident, *weights, *first_one, *gathers, *scatters, *entering, *leaving)
 
 
-def mixer_out_kernel(heads, key, value, last, matrices,
+def mixer_out_kernel(heads, key, value, last, handed, ready, matrices,
                      head_gain_ref, gain_ref,
                      first_ref, local_ref, through_ref, tokens_ref,
                      y_ref, mixed_ref, gate_ref, state_ref, middle_ref, second_ref, *scratch):
@@ -1002,6 +1020,9 @@
     weights, ends = matrices
     vals = heads * value
 
+    if handed is not None:
+        ready(handed)
+
     @pl.when(step == 0)
     def _():
         state_ref[...] = jnp.zeros_like(state_ref)
@@ -1016,6 +1037,7 @@
         lax.fori_loop(0, lax.axis_index("seq"), one, 0)
 
     def gate():
+        ready(0)
         gate_ref[...] = mm(first_ref[...], weights[:, :vals])
 
     def mix():
@@ -1028,6 +1050,7 @@
             y_ref[:, cols] = (o * s3 * head_gain_ref[0:1, :] * (gz * sigmoid(gz))).astype(low)
 
     def project():
+        ready(1)
         return mm_nt(y_ref[...], weights[:, vals:])
 
     def finish(total):
@@ -1039,7 +1062,7 @@
     line_sum(step, last, [gate, mix, project], finish, scratch)
 
 
-def ffn_kernel(last, size, matrices, gain_ref,
+def ffn_kernel(last, size, ready, matrices, gain_ref,
                second_ref, cot_ref, middle_ref, cot_late_ref,
                hidden_ref, dgate_ref, dup_ref, partial_ref, dmiddle_ref, dlow_ref, gain_grad_ref,
                fg, fu, *scratch):
@@ -1052,12 +1075,15 @@
         gain_grad_ref[...] = jnp.zeros_like(gain_grad_ref)
 
     def one():
+        ready(0)
         fg[...] = mm(second_ref[...], weights[:, w_gate])
 
     def two():
+        ready(1)
         fu[...] = mm(second_ref[...], weights[:, w_up])
 
     def three():
+        ready(2)
         g = fg[...]
         hidden = (g * sigmoid(g) * fu[...]).astype(low)
         hidden_ref[...] = hidden
@@ -1088,21 +1114,25 @@
     line_sum(step, last, [one, two, three, four, five], finish, scratch)
 
 
-def input_grad_kernel(last, keys, vals, matrices, gain_ref,
+def input_grad_kernel(last, keys, vals, near, ready, matrices, gain_ref, lines_ref,
                       dpre_ref, dgz_ref, dab_ref, tokens_ref,
-                      term_ref, gain_grad_ref, part, *scratch):
+                      term_ref, gains_ref, part, gain_grad, *scratch):
     step = pl.program_id(0)
     w_in, w_mix = matrices
     wide = 2 * keys + vals
+    if near:
+        (got, sent, came), scratch = scratch[:3], scratch[3:]
 
     @pl.when(step == 0)
     def _():
-        gain_grad_ref[...] = jnp.zeros_like(gain_grad_ref)
+        gain_grad[...] = jnp.zeros_like(gain_grad)
 
     def one():
+        ready(0)
         part[...] = mm_nt(dpre_ref[...], w_in[:, :wide])
 
     def two():
+        ready(1)
         return (
             part[...]
             + mm_nt(dgz_ref[...], w_mix[:, :vals])
@@ -1113,13 +1143,37 @@
         stream = tokens_ref[...].astype(full)
         scale = lax.rsqrt(jnp.mean(stream * stream, axis=-1, keepdims=True) + 1e-06)
         norm = stream * scale
-        gain_grad_ref[...] += jnp.sum((grad * norm).reshape(ROWS // 8, 8, -1), axis=0)
+        gain_grad[...] += jnp.sum((grad * norm).reshape(ROWS // 8, 8, -1), axis=0)
         weighted = grad * gain_ref[0:1, :]
         term_ref[...] = (
             scale * (weighted - norm * jnp.mean(weighted * norm, axis=-1, keepdims=True))
         ).astype(low)
 
     line_sum(step, last, [one, two], finish, scratch)
+
+    @pl.when(step == pl.num_programs(0) - 1)
+    def _():
+        row = lax.broadcasted_iota(jnp.int32, gain_grad.shape, 0)
+        first = jnp.sum(gain_grad[...], axis=0, keepdims=True)
+        own = lines_ref[...] + jnp.where(row == 0, first, 0.0)
+        if not near:
+            gains_ref[...] = own
+            return
+        gain_grad[...] = own
+        me = lax.axis_index("seq")
+
+        def push(mask):
+            return pltpu.make_async_remote_copy(
+                src_ref=gain_grad, dst_ref=got.at[me], send_sem=sent.at[mask], recv_sem=came.at[mask],
+                device_id={"seq": partner(mask)}, device_id_type=MESH,
+            )
+
+        for mask in range(1, NEAR):
+            push(mask).start()
+        got[me] = own
+        for mask in range(1, NEAR):
+            push(mask).wait()
+        gains_ref[...] = sum((got[k] for k in range(1, NEAR)), start=got[0])
 
 
 def input_kernel(wide, gathering, gain_ref, *refs):
@@ -1335,14 +1389,16 @@
     return lax.psum_scatter(grads.reshape(width, -1), "seq", scatter_dimension=0, tiled=True).astype(full)
 
 
-def final_kernel(heads, keys, vals, size, dmiddle_ref, term_ref, in_own, in_got, up_own, up_got, down_own, down_got,
-                 gate_own, gate_got, out_own, out_got,
-                 dtokens_ref, q_ref, k_ref, v_ref, a_ref, b_ref, up_ref, lift_ref, down_ref, gate_ref, out_ref):
+def final_kernel(heads, keys, vals, size, middle_ref, sum_ref, dmiddle_ref, term_ref, in_own, in_got,
+                 up_own, up_got, down_own, down_got, gate_own, gate_got, out_own, out_got,
+                 result_ref, dtokens_ref, q_ref, k_ref, v_ref, a_ref, b_ref, up_ref, lift_ref, down_ref,
+                 gate_ref, out_ref):
     def total(own, got, cols=slice(None)):
         return own[0, :, cols].astype(full) + sum(got[k, :, cols].astype(full) for k in range(3))
 
     @pl.when(pl.program_id(0) < 8)
     def _():
+        result_ref[...] = (middle_ref[...] + sum_ref[...].astype(full)).astype(low)
         dtokens_ref[...] = dmiddle_ref[...] + term_ref[...].astype(full)
         wide = 2 * keys + vals
         q_ref[...] = total(in_own, in_got, slice(0, keys))
@@ -1359,7 +1415,7 @@
     down_ref[...] = total(down_own, down_got).T
 
 
-def final_sums(dmiddle, term, sums_in, got_in, sums_up, got_up, sums_rest, got_rest, heads, keys, vals, size):
+def final_sums(middle, narrow_sum, dmiddle, term, sums_in, got_in, sums_up, got_up, sums_rest, got_rest, heads, keys, vals, size):
     length, width = dmiddle.shape
     rows = sums_in.shape[1]
     eight = lambda n: jnp.minimum(n, 7)
@@ -1370,119 +1426,40 @@
 
     wide_in, wide_up = sums_in.shape[2], sums_up.shape[2]
     at_gate, at_out = size // LANES, (size + vals) // LANES
-    in_specs = [pl.BlockSpec((many, width), lambda n: (eight(n), 0))] * 2
+    tall = pl.BlockSpec((many, width), lambda n: (eight(n), 0))
+    in_specs = [tall] * 4
     in_specs += both(sums_in, (few, wide_in), lambda n: (0, eight(n), 0))
     in_specs += both(sums_up, (few, wide_up), lambda n: (0, eight(n), 0))
     in_specs += both(sums_rest, (rows, LANES), lambda n: (0, 0, n))
     in_specs += both(sums_rest, (rows, LANES), lambda n: (0, 0, at_gate + eight(n)))
     in_specs += both(sums_rest, (rows, LANES), lambda n: (0, 0, at_out + eight(n)))
     byrow = lambda columns: pl.BlockSpec((few, columns), lambda n: (eight(n), 0))
+    outs = [
+        ((length, width), low), ((length, width), full), ((rows, keys), full), ((rows, keys), full),
+        ((rows, vals), full), ((rows, heads), full), ((rows, heads), full), ((rows, size), full),
+        ((rows, size), full), ((size, rows), full), ((rows, vals), full), ((vals, rows), full),
+    ]
     return pl.pallas_call(
         partial(final_kernel, heads, keys, vals, size),
         grid=(size // LANES,),
         in_specs=in_specs,
         out_specs=[
-            pl.BlockSpec((many, width), lambda n: (eight(n), 0)),
+            tall, tall,
             byrow(keys), byrow(keys), byrow(vals), byrow(heads), byrow(heads), byrow(size), byrow(size),
             pl.BlockSpec((LANES, rows), lambda n: (n, 0)),
             pl.BlockSpec((rows, LANES), lambda n: (0, eight(n))),
             pl.BlockSpec((LANES, rows), lambda n: (eight(n), 0)),
         ],
-        out_shape=[
-            jax.ShapeDtypeStruct(shape, full)
-            for shape in (
-                (length, width), (rows, keys), (rows, keys), (rows, vals), (rows, heads), (rows, heads),
-                (rows, size), (rows, size), (size, rows), (rows, vals), (vals, rows),
-            )
-        ],
+        out_shape=[jax.ShapeDtypeStruct(shape, dtype) for shape, dtype in outs],
         compiler_params=pltpu.CompilerParams(vmem_limit_bytes=48 * MIB),
         cost_estimate=FREE,
         name="final_sums",
-    )(dmiddle, term, sums_in, got_in, sums_up, got_up, sums_rest, got_rest, sums_rest, got_rest,
-      sums_rest, got_rest)
-
-
-def small_kernel(count, others, part_ref, out_ref, send, got, got_far, sent, came, sent_far, came_far):
-    me, row = lax.axis_index("seq"), lax.axis_index("head")
-    rows, far = part_ref.shape[0], got_far.shape[2]
-    barrier = pltpu.get_barrier_semaphore()
-
-    def greet(k, carry):
-        pl.semaphore_signal(
-            barrier, inc=1, device_id={"seq": lax.rem(me + k, count)},
-            device_id_type=pl.DeviceIdType.MESH,
-        )
-        return carry
-
-    lax.fori_loop(1, count, greet, 0)
-    for k in range(1, others):
-        pl.semaphore_signal(
-            barrier, inc=1, device_id={"head": lax.rem(row + k, others)},
-            device_id_type=pl.DeviceIdType.MESH,
-        )
-    pl.semaphore_wait(barrier, count + others - 2)
-
-    def along(k):
-        return pltpu.make_async_remote_copy(
-            src_ref=part_ref, dst_ref=got.at[me], send_sem=sent.at[k], recv_sem=came.at[k],
-            device_id={"seq": lax.rem(me + k, count)}, device_id_type=pl.DeviceIdType.MESH,
-        )
-
-    def across(k):
-        return pltpu.make_async_remote_copy(
-            src_ref=send, dst_ref=got_far.at[row], send_sem=sent_far.at[k], recv_sem=came_far.at[k],
-            device_id={"head": lax.rem(row + k, others)}, device_id_type=pl.DeviceIdType.MESH,
-        )
-
-    def start(k, carry):
-        along(k).start()
-        return carry
-
-    def wait(k, carry):
-        along(k).wait()
-        return carry
-
-    lax.fori_loop(1, count, start, 0)
-    got[me] = part_ref[...]
-    lax.fori_loop(1, count, wait, 0)
-
-    def add(k, carry):
-        out_ref[...] += got[k]
-        return carry
-
-    out_ref[...] = got[0]
-    lax.fori_loop(1, count, add, 0)
-    send[...] = out_ref[:, :far]
-    for k in range(1, others):
-        across(k).start()
-    got_far[row] = send[...]
-    for k in range(1, others):
-        across(k).wait()
-    total = got_far[0]
-    for k in range(1, others):
-        total += got_far[k]
-    out_ref[rows - 1 :, :far] = total[rows - 1 :, :]
-
-
-def small_sums(part, far):
-    count, others = lax.axis_size("seq"), lax.axis_size("head")
-    return pl.pallas_call(
-        partial(small_kernel, count, others),
-        in_specs=[pl.BlockSpec(memory_space=pltpu.VMEM)],
-        out_specs=pl.BlockSpec(memory_space=pltpu.VMEM),
-        out_shape=jax.ShapeDtypeStruct(part.shape, full),
-        scratch_shapes=[
-            pltpu.VMEM((part.shape[0], far), full),
-            pltpu.VMEM((count,) + part.shape, full),
-            pltpu.VMEM((others, part.shape[0], far), full),
-            pltpu.SemaphoreType.DMA((count,)),
-            pltpu.SemaphoreType.DMA((count,)),
-            pltpu.SemaphoreType.DMA((others,)),
-            pltpu.SemaphoreType.DMA((others,)),
-        ],
-        compiler_params=pltpu.CompilerParams(collective_id=3, has_side_effects=True),
-        name="small_sums",
-    )(part)
+    )(middle, narrow_sum, dmiddle, term, sums_in, got_in, sums_up, got_up, sums_rest, got_rest, sums_rest,
+      got_rest, sums_rest, got_rest)
+
+
+def small_sums(part):
+    return lax.psum(part, "seq")
 
 
 def passed_along(block, axis, distance):
@@ -1555,14 +1532,14 @@
     )
     end = end.reshape(keys, value + key)
     if near:
-        held, moving = [moved[0]], dict(early=end, gathers=[shard_ffn])
-        (w_mix,) = held
+        w_mix = moved[0]
+        held, moving = [(w_mix, [(0, vals), (vals, vals)])], dict(early=end, gathers=[shard_ffn])
     else:
         w_mix = lax.all_gather(shard_mix, "seq", axis=0, tiled=True)
         ends = lax.all_gather(end, "seq", axis=0, tiled=True)
-        held, moving = [w_mix, ends], {}
+        held, moving = [(w_mix, [(0, vals), (vals, vals)]), (ends, [(0, ends.shape[1])])], {}
     mix_out, mixed, gate_pre, state_in, middle, second_in, *moved = line_call(
-        partial(mixer_out_kernel, heads, key, value, last), "mixer_out", 0, length, width, last,
+        partial(mixer_out_kernel, heads, key, value, last, None if near else 2), "mixer_out", 0, length, width, last,
         [gain, ffn_gain[None, :]], held, [first_in, local, through], [tokens],
         [((length, vals), low, "first"), ((length, vals), full, "first"),
          ((length, vals), full, "first"), ((heads, key, value), full, "all"),
@@ -1575,7 +1552,7 @@
         w_ffn = lax.all_gather(shard_ffn, "seq", axis=0, tiled=True)
     hidden, gate_grad, lift_grad, narrow_part, middle_grad, middle_low, ffn_gain_part = line_call(
         partial(ffn_kernel, last, size), "ffn", 1, length, width, last,
-        [ffn_gain[None, :]], [w_ffn], [second_in, cotangent], [middle, cotangent],
+        [ffn_gain[None, :]], [(w_ffn, [(n * size, size) for n in range(3)])], [second_in, cotangent], [middle, cotangent],
         [((length, size), low, "first")] * 3
         + [((length, width), low, "first"), ((length, width), full, "second"),
            ((length, width), low, "second"), ((8, width), full, "all")],
@@ -1585,15 +1562,20 @@
     gate_pgrad, mixed_grad, head_gain_part, adjoint = gate_back(
         middle_low, w_mix, mixed, gate_pre, gain, through, heads, key, value
     )
+    for mask in (1, 2):
+        head_gain_part += lax.ppermute(
+            head_gain_part, "head", [(i, i ^ mask) for i in range(last + 1)]
+        )
     adjoints = spread(adjoint.astype(low).reshape(keys, value))
     pairs_up = [(second_in, [gate_grad, lift_grad])]
     pairs_rest = [(cotangent, [hidden]), (first_in, [gate_pgrad]), (middle_low, [mix_out])]
     sums_up = pair_sums(place, pairs_up) if near else None
     sums_rest = pair_sums(place, pairs_rest) if near else None
     if near:
-        narrow_sum, sums_up = lax.optimization_barrier((narrow_sum, sums_up))
+        narrow_sum, sums_up, head_gain_part = lax.optimization_barrier(
+            (narrow_sum, sums_up, head_gain_part)
+        )
     narrow_sum = lax.all_gather(narrow_sum, "head", axis=0, tiled=True)
-    result = (middle + narrow_sum.astype(full)).astype(low)
     pre_grad, ab_grad, halo, taps_part, params_part, *moved = backward_chain(
         pre, ab, meta, segrow, edge, edge_meta, taps, params, states, inverse, state_in,
         mixed_grad, ends, adjoints, heads, key, value, sums_up,
@@ -1604,17 +1586,30 @@
     pre_grad = lax.dynamic_update_slice(pre_grad, tail.astype(low), (length - 8, 0))
     pairs_in = [(first_in, [pre_grad, ab_grad])]
     sums_in = pair_sums(place, pairs_in) if near else None
-    term, mixer_gain_part, *moved = line_call(
-        partial(input_grad_kernel, last, keys, vals), "input_grad", 2, length, width, last,
-        [mixer_gain[None, :]], [w_in, w_mix], [pre_grad, gate_pgrad, ab_grad],
-        [tokens],
+    params_part = jnp.sum(params_part.reshape(2, 8, LANES), axis=1).reshape(1, -1)
+    lines = jnp.concatenate(
+        [
+            jnp.zeros((1, width), full),
+            jnp.sum(ffn_gain_part, axis=0, keepdims=True),
+            jnp.sum(taps_part.reshape(4, 8, -1), axis=1),
+            jnp.pad(params_part, ((0, 0), (0, width - params_part.shape[1]))),
+            jnp.pad(jnp.sum(head_gain_part, axis=0)[None], ((0, 0), (0, width - value))),
+        ],
+        axis=0,
+    )
+    term, gains, *moved = line_call(
+        partial(input_grad_kernel, last, keys, vals, near), "input_grad", 2, length, width, last,
+        [mixer_gain[None, :], lines], [(w_in, [(0, w_in.shape[1])]), (w_mix, [(0, vals)])],
+        [pre_grad, gate_pgrad, ab_grad], [tokens],
         [((length, width), low, "second"), ((8, width), full, "all")],
-        [pltpu.VMEM((ROWS, width), full)], scatters=[sums_rest, sums_in] if near else [],
+        [pltpu.VMEM((ROWS, width), full), pltpu.VMEM((8, width), full)]
+        + ([pltpu.VMEM((NEAR, 8, width), full), *[pltpu.SemaphoreType.DMA((NEAR,))] * 2] if near else []),
+        scatters=[sums_rest, sums_in] if near else [], masks=range(1, NEAR) if near else (),
     )
     if near:
-        (tokens_grad, query_grad, key_grad, value_grad, alpha_grad, beta_grad, up_grad, lift_grad,
+        (result, tokens_grad, query_grad, key_grad, value_grad, alpha_grad, beta_grad, up_grad, lift_grad,
          down_grad, gate_grad, out_grad) = final_sums(
-            middle_grad, term, sums_in, moved[1], sums_up, got_up[0], sums_rest, moved[0],
+            middle, narrow_sum, middle_grad, term, sums_in, moved[1], sums_up, got_up[0], sums_rest, moved[0],
             heads, keys, vals, size,
         )
     else:
@@ -1626,15 +1621,8 @@
         down_grad, gate_grad, out_grad = (
             rest[:, :size].T, rest[:, size : size + vals], rest[:, size + vals :].T
         )
-    params_part = jnp.sum(params_part.reshape(2, 8, LANES), axis=1).reshape(1, -1)
-    lines = [
-        jnp.sum(mixer_gain_part, axis=0, keepdims=True),
-        jnp.sum(ffn_gain_part, axis=0, keepdims=True),
-        jnp.sum(taps_part.reshape(4, 8, -1), axis=1),
-        jnp.pad(params_part, ((0, 0), (0, width - params_part.shape[1]))),
-        jnp.pad(jnp.sum(head_gain_part, axis=0)[None], ((0, 0), (0, width - value))),
-    ]
-    sums = small_sums(jnp.concatenate(lines, axis=0), value)
+        result = (middle + narrow_sum.astype(full)).astype(low)
+    sums = gains if near else small_sums(gains)
     taps_grad = sums[2:6]
     return (
         result,

time: 787 us -> 771 us (0.980)
  Pallas kernels: 698 us -> 689 us
  other arithmetic: 13.9 us -> 5.53 us
    pallas_call x1 -> x0, Pallas kernels: 15.2 us -> none  [small_sums(): pl.pallas_call(partial(small_kernel, count, others), in_specs=[pl.BlockSp...]
    ppermute x0 -> x2, waiting for transfers between devices: none -> 8.86 us  [shards(): lax.ppermute(head_gain_part, 'head', [(i, i ^ mask) for i in range(last +...]
    convert_element_type x1 -> x0, other arithmetic: 8.31 us -> none  [shards(): result = (middle + narrow_sum.astype(full)).astype(low)]
    unnamed x54 -> x62, local copies, waits for them, and re-layouts: 16.6 us -> 17.9 us
  transfers between devices with their start and end apart: 14 -> 16, of which waited for: 5 -> 5; matrix products, arithmetic and copies ran while one was open for 3% -> 2% of each run, Pallas kernels for 41% -> 38%
where the time goes in v5:
time: 771 us; the launch traced here: 769 us
  Pallas kernels  689 us (89%)
  local copies, waits for them, and re-layouts  29.6 us (4%)
  waiting for transfers between devices  18.6 us (2%)
  between operations  14.7 us (2%)
  starting transfers between devices  12.2 us (2%)
    pallas_call x3, Pallas kernels, line_call(): pl.pallas_call(body, grid=(steps,), in_specs=in_specs, out_specs=out_spec...  413 us
    pallas_call x6, Pallas kernels, weight_call(): pl.pallas_call(partial(weight_kernel, [len(bs) for _, bs in pairs], added...  71.4 us
    pallas_call x1, Pallas kernels, backward_chain(): pl.pallas_call(partial(backward_kernel, heads, key, value, devices, masks...  69.6 us
    pallas_call x1, Pallas kernels, input_projection(): pl.pallas_call(partial(input_kernel, wide, gathering), in_specs=[here] +...  56.7 us
    pallas_call x1, Pallas kernels, forward_chain(): pl.pallas_call(partial(forward_kernel, heads, key, value, gathering), gri...  43.5 us
    pallas_call x1, Pallas kernels, final_sums(): pl.pallas_call(partial(final_kernel, heads, keys, vals, size), grid=(size...  22.1 us
    unnamed x62, local copies, waits for them, and re-layouts  17.9 us
  transfers between devices with their start and end apart: 16, of which 5 were waited for; matrix products, arithmetic and copies ran while one was open for 2% of the time, Pallas kernels for 38%

profile of v5, /device:TPU:0, one launch (start us, length us, event | category | flops | bytes accessed | tf_op | source)
XLA Modules:
  0.0 769.4 jit_solution(10282167456341563346)
XLA Ops:
  7.2 0.8 slice.86
  8.1 2.3 collective-permute-start
  10.5 0.8 reduce-window.9
  12.8 0.8 copy.112
  13.6 0.8 copy.113
  14.4 0.7 constant_dynamic-update-slice_fusion.2
  16.0 0.7 constant_dynamic-update-slice_fusion.1
  16.7 0.7 constant_dynamic-update-slice_fusion.taps_ref
  17.4 0.8 maximum_maximum_fusion.refs_3_
  19.5 56.7 %input_projection.1 = (bf16[1024,2048]{1,0:T(8,128)(2,1)}, bf16[1024,2048]{1,0:T(8,128)(2,1)}, f32[1024,128]{1,0:T(8,128)}, bf16[16,2048]{1,0:T(8,128)(2,1)}, bf...) custom-call(f32[1,2048]{1,0:T(1,128)} %bitcast.71, f32[256,512]{1,0:T(8,128)} %refs_0_.3, ...), custom_call_target="tpu_custom_call" | custom-call | flops 1 | bytes 1 | tf_op jit(solution)/shard_map/input_projection/pallas_call | solution.py:1306
  76.2 0.8 slice.96.edge_ref
  77.0 1.0 copy-done.6
  78.1 1.2 copy-done.8
  79.3 43.5 %chain_forward.1 = (f32[1024,1024]{1,0:T(8,128)}, bf16[1024,512]{1,0:T(8,128)(2,1)S(1)}, bf16[8,4,128,384]{3,2,1,0:T(8,128)(2,1)}, bf16[8,4,128,128]{3,2,1,0:T(8...) custom-call(bf16[1024,2048]{1,0:T(8,128)(2,1)} %get-tuple-element.77.pre_ref.tail_ref, ...), custom_call_target="tpu_custom_call" | custom-call | flops 1 | bytes 1 | tf_op jit(solution)/shard_map/chain_forward/pallas_call | solution.py:354
  122.9 1.0 copy-done.2
  123.8 1.0 copy-done.7
  124.8 0.7 copy-done.9
  125.5 147.8 %mixer_out.1 = (bf16[1024,1024]{1,0:T(8,128)(2,1)}, f32[1024,1024]{1,0:T(8,128)}, f32[1024,1024]{1,0:T(8,128)}, f32[4,128,256]{2,1,0:T(8,128)}, f32[1024,2048]{1...) custom-call(f32[1,256]{1,0:T(1,128)} %bitcast.60, ...), custom_call_target="tpu_custom_call" | custom-call | flops 1 | bytes 1 | tf_op jit(solution)/shard_map/mixer_out/pallas_call | solution.py:1000
  273.3 127.5 %ffn.1 = (bf16[1024,1408]{1,0:T(8,128)(2,1)}, bf16[1024,1408]{1,0:T(8,128)(2,1)}, bf16[1024,1408]{1,0:T(8,128)(2,1)}, bf16[1024,2048]{1,0:T(8,128)(2,1)}, f32[10...) custom-call(f32[1,2048]{1,0:T(1,128)} %bitcast.70, bf16[2048,4224]{1,0:T(8,128)(2,1)} %get-tuple-element.88.refs_1_, ...), custom_call_target="tpu_custom_call" | custom-call | flops 1 | bytes 1 | tf_op jit(solution)/shard_map/ffn/pallas_call | solution.py:1000
  401.0 11.9 %weight_grads.6 = bf16[4,256,2816]{2,1,0:T(8,128)(2,1)} custom-call(s32[1]{0:T(128)} %bitcast.20.place_ref, bf16[1024,2048]{1,0:T(8,128)(2,1)} %get-tuple-element.89.refs_2_.refs_0_, bf16[1024,1408]{1,0:T(8,128)(2,1)} %get-tuple-element.91.refs_1_, bf16[1024,1408]{1,0:T(8,128)(2,1)} %get-tuple-element.92.refs_2_), custom_call_target="tpu_custom_call" | custom-call | flops 1 | bytes 1 | tf_op jit(solution)/shard_map/weight_grads/pallas_call | solution.py:1366
  412.9 12.7 %gate_back.1 = (bf16[1024,1024]{1,0:T(8,128)(2,1)S(1)}, bf16[1024,1024]{1,0:T(8,128)(2,1)S(1)}, f32[8,256]{1,0:T(8,128)S(1)}, f32[4,128,256]{2,1,0:T(8,128)S(1)}) custom-call(bf16[1024,2048]{1,0:T(8,128)(2,1)} %get-tuple-element.93.dz_ref.refs_2_, f32[1024,1024]{1,0:T(8,128)} %get-tuple-element.94.mixed_ref, f32[1024,1024]{1,0:T(8,128)} %get-tuple-element.95.gate_ref, ...), custom_call_target="tpu_custom_call" | custom-call | flops 1 | bytes 1 | tf_op jit(solution)/shard_map/gate_back/pallas_call | solution.py:429
  425.6 1.3 copy-done
  426.9 1.3 copy-done.5
  428.2 13.5 %weight_grads.8 = bf16[4,256,3456]{2,1,0:T(8,128)(2,1)} custom-call(s32[1]{0:T(128)} %bitcast.20.place_ref, bf16[1024,2048]{1,0:T(8,128)(2,1)} %refs_0_.5, bf16[1024,2048]{1,0:T(8,128)(2,1)} %get-tuple-element.84.refs_5_.refs_1_.refs_0_, bf16[1024,2048]{1,0:T(8,128)(2,1)} %get-tuple-element.93.dz_ref.refs_2_, bf16[1024,1408]{1,0:T(8,128)(2,1)} %get-tuple-element.111.refs_3_, ...), custom_call_target="tpu_custom_call" | custom-call | flops 1 | bytes 1 | tf_op jit(solution)/shard_map/weight_grads/pallas_call | solution.py:1366
  442.2 6.0 collective-permute-done.2
  448.2 2.5 collective-permute-start.6
  451.4 2.8 collective-permute-done.3
  454.3 1.6 collective-permute-start.5
  455.8 2.6 collective-permute-done.6.refs_3_
  458.4 5.1 collective-permute-done.4.refs_1_
  464.0 2.4 copy-done.15
  466.5 12.1 %weight_grads.7.refs_8_.up_own = bf16[4,256,2816]{2,1,0:T(8,128)(2,1)} custom-call(s32[1]{0:T(128)} %bitcast.20.place_ref, bf16[1024,2048]{1,0:T(8,128)(2,1)} %get-tuple-element.89.refs_2_.refs_0_, bf16[1024,1408]{1,0:T(8,128)(2,1)} %get-tuple-element.91.refs_1_, bf16[1024,1408]{1,0:T(8,128)(2,1)} %get-tuple-element.92.refs_2_, bf16[4,256,2816]{2,1,0:T(8,128)(2,1)} %copy-done.15), custom_call_target="tpu_custom_call" | custom-call | flops 1 | bytes 1 | tf_op jit(solution)/shard_map/weight_grads/pallas_call | solution.py:1366
  481.0 69.6 %chain_backward.1 = (bf16[1024,2048]{1,0:T(8,128)(2,1)}, bf16[1024,128]{1,0:T(8,128)(2,1)}, f32[8,2048]{1,0:T(8,128)}, f32[32,2048]{1,0:T(8,128)}, f32[16,128]{1,0:T(8,128)}, /*index=5*/bf16[3,256,2816]{2,1,0:T(8,128)(2,1)}) custom-call(bf16[1024,2048]{1,0:T(8,128)(2,1)} %get-tuple-element.77.pre_ref.tail_ref, ...), custom_call_target="tpu_custom_call" | custom-call | flops 1 | bytes 1 | tf_op jit(solution)/shard_map/chain_backward/pallas_call | solution.py:682
  550.6 1.3 collective-permute-start.12
  551.9 2.1 collective-permute-done.12
  553.9 1.4 fusion.refs_1_.refs_6_
  555.3 9.4 %weight_grads.10 = bf16[4,256,2176]{2,1,0:T(8,128)(2,1)} custom-call(s32[1]{0:T(128)} %bitcast.20.place_ref, bf16[1024,2048]{1,0:T(8,128)(2,1)} %get-tuple-element.84.refs_5_.refs_1_.refs_0_, bf16[1024,2048]{1,0:T(8,128)(2,1)} %fusion.refs_1_.refs_6_, bf16[1024,128]{1,0:T(8,128)(2,1)} %get-tuple-element.116.refs_2_.refs_8_), custom_call_target="tpu_custom_call" | custom-call | flops 1 | bytes 1 | tf_op jit(solution)/shard_map/weight_grads/pallas_call | solution.py:1366
  564.7 2.6 collective-permute-start.13
  567.4 14.6 %weight_grads.9.refs_4_.down_own.gate_own.out_own = bf16[4,256,3456]{2,1,0:T(8,128)(2,1)} custom-call(s32[1]{0:T(128)} %bitcast.20.place_ref, bf16[1024,2048]{1,0:T(8,128)(2,1)} %refs_0_.5, bf16[1024,2048]{1,0:T(8,128)(2,1)} %get-tuple-element.84.refs_5_.refs_1_.refs_0_, bf16[1024,2048]{1,0:T(8,128)(2,1)} %get-tuple-element.93.dz_ref.refs_2_, ...), custom_call_target="tpu_custom_call" | custom-call | flops 1 | bytes 1 | tf_op jit(solution)/shard_map/weight_grads/pallas_call | solution.py:1366
  582.8 9.9 %weight_grads.11.refs_5_.in_own = bf16[4,256,2176]{2,1,0:T(8,128)(2,1)} custom-call(s32[1]{0:T(128)} %bitcast.20.place_ref, bf16[1024,2048]{1,0:T(8,128)(2,1)} %get-tuple-element.84.refs_5_.refs_1_.refs_0_, bf16[1024,2048]{1,0:T(8,128)(2,1)} %fusion.refs_1_.refs_6_, bf16[1024,128]{1,0:T(8,128)(2,1)} %get-tuple-element.116.refs_2_.refs_8_, ...), custom_call_target="tpu_custom_call" | custom-call | flops 1 | bytes 1 | tf_op jit(solution)/shard_map/weight_grads/pallas_call | solution.py:1366
  592.7 137.5 %input_grad.1 = (bf16[1024,2048]{1,0:T(8,128)(2,1)}, f32[8,2048]{1,0:T(8,128)}, bf16[3,256,3456]{2,1,0:T(8,128)(2,1)}, bf16[3,256,2176]{2,1,0:T(8,128)(2,1)}) custom-call(f32[1,2048]{1,0:T(1,128)} %bitcast.72, f32[8,2048]{1,0:T(8,128)} %concatenate.11.refs_1_, bf16[2048,2176]{1,0:T(8,128)(2,1)} %get-tuple-element.110.refs_2_, ...), custom_call_target="tpu_custom_call" | custom-call | flops 1 | bytes 1 | tf_op jit(solution)/shard_map/input_grad/pallas_call | solution.py:1000
  730.2 1.4 slice.110
  731.6 1.3 slice.111
  732.9 1.2 slice_bitcast_fusion.1
  734.1 1.3 fusion.16
  735.4 1.5 fusion.15
  736.9 1.9 copy-done.4
  738.9 22.1 %final_sums.1 = (bf16[1024,2048]{1,0:T(8,128)(2,1)}, f32[1024,2048]{1,0:T(8,128)}, f32[256,512]{1,0:T(8,128)}, f32[256,512]{1,0:T(8,128)}, f32[256,1024]{1,0:T(8...) custom-call(f32[1024,2048]{1,0:T(8,128)} %get-tuple-element.87.refs_, ...), custom_call_target="tpu_custom_call" | custom-call | flops 1 | bytes 1 | tf_op jit(solution)/shard_map/final_sums/pallas_call | solution.py:1442
  (110 shorter events, 10.0 us)
Async XLA Ops:
  7.2 471.4 %reduce-scatter.2.cloned.1.call-start = ((), (), s32[]{:S(2)}) async-start(), calls=%async_computation.1 | async-start | bytes 5242880 | tf_op jit(solution)/shard_map/reduce_scatter | solution.py:1561
  8.1 10.8 %collective-permute-start = (bf16[16,2048]{1,0:T(8,128)(2,1)S(1)}, bf16[16,2048]{1,0:T(8,128)(2,1)S(1)}, u32[]{:S(2)}, u32[]{:S(2)}) collective-permute-start(bf16[16,2048]{1,0:T(8,128)(2,1)S(1)} %slice.86), channel_id=1, source_target_pairs={{0,4},{4,8},{8,12},{12,16},{16,20},{20,24},{24,28},{1,5},{5,9},{9,... | collective-permute-start | bytes 196616 | tf_op jit(solution)/shard_map/ppermute | solution.py:1468
  15.9 61.1 %copy-start.1 = (f32[1024,128]{1,0:T(8,128)}, f32[1024,128]{1,0:T(8,128)S(1)}, u32[]{:S(2)}) copy-start(f32[1024,128]{1,0:T(8,128)S(1)} %pad.19.meta_ref) | copy-start | bytes 1572868
  17.4 59.6 %copy-start.12 = (f32[4,2048]{1,0:T(4,128)}, f32[4,2048]{1,0:T(4,128)S(1)}, u32[]{:S(2)}) copy-start(f32[4,2048]{1,0:T(4,128)S(1)} %constant_dynamic-update-slice_fusion.taps_ref) | copy-start | bytes 98308
  18.8 58.2 %copy-start.13 = (f32[8,128]{1,0:T(8,128)}, f32[8,128]{1,0:T(8,128)S(1)}, u32[]{:S(2)}) copy-start(f32[8,128]{1,0:T(8,128)S(1)} %select_maximum_fusion.params_ref) | copy-start | bytes 12292
  18.9 0.6 copy-start.25
  77.0 196.3 %copy-start.10 = (bf16[8,2048]{1,0:T(8,128)(2,1)}, bf16[8,2048]{1,0:T(8,128)(2,1)S(1)}, u32[]{:S(2)}) copy-start(bf16[8,2048]{1,0:T(8,128)(2,1)S(1)} %slice.96.edge_ref) | copy-start | bytes 98308
  77.0 196.3 %copy-start.11 = (f32[8,1024]{1,0:T(8,128)}, f32[8,1024]{1,0:T(8,128)S(1)}, u32[]{:S(2)}) copy-start(f32[8,1024]{1,0:T(8,128)S(1)} %broadcast_in_dim.39.segrow_ref) | copy-start | bytes 98308
  77.0 1.0 copy-start.6
  78.1 1.2 copy-start.8
  122.8 1.0 copy-start.2
  123.8 1.0 copy-start.7
  124.8 0.7 copy-start.9
  400.9 336.0 %all-gather.2.cloned.1.call-start = ((), (), s32[]{:S(2)}) async-start(), calls=%async_computation.2 | async-start | bytes 5242880 | tf_op jit(solution)/shard_map/all_gather | solution.py:1578
  400.9 11.9 %copy-start.3 = (bf16[1024,512]{1,0:T(8,128)(2,1)S(1)}, bf16[1024,512]{1,0:T(8,128)(2,1)}, u32[]{:S(2)}) copy-start(bf16[1024,512]{1,0:T(8,128)(2,1)} %copy-done.2) | copy-start | bytes 3145732
  401.0 11.9 %copy-start.14 = (f32[256]{0:T(256)S(1)}, f32[256]{0:T(256)}, u32[]{:S(2)}) copy-start(f32[256]{0:T(256)} %param.35) | copy-start | bytes 3076
  412.9 51.1 %collective-permute-start.1 = (bf16[4,256,2816]{2,1,0:T(8,128)(2,1)}, bf16[4,256,2816]{2,1,0:T(8,128)(2,1)S(1)}, u32[]{:S(2)}, u32[]{:S(2)}) collective-permute-start(bf16[4,256,2816]{2,1,0:T(8,128)(2,1)} %weight_grads.6), channel_id=1, source_target_pairs={{0,4},{4,0},{8,12},{12,8},{16,20},{20,16},{24,28},{28,24},{1,5},{5... | collective-permute-start | bytes 17301512 | tf_op jit(solution)/shard_map/ppermute | solution.py:770
  425.5 1.3 copy-start
  426.9 1.3 copy-start.5
  441.7 125.7 %collective-permute-start.11 = (bf16[4,256,3456]{2,1,0:T(8,128)(2,1)}, bf16[4,256,3456]{2,1,0:T(8,128)(2,1)}, u32[]{:S(2)}, u32[]{:S(2)}) collective-permute-start(bf16[4,256,3456]{2,1,0:T(8,128)(2,1)} %weight_grads.8), channel_id=1, source_target_pairs={{0,4},{4,0},{8,12},{12,8},{16,20},{20,16},{24,28},{28,24},{1,5},{5... | collective-permute-start | bytes 21233672 | tf_op jit(solution)/shard_map/ppermute | solution.py:770
  442.2 6.0 collective-permute-start.2
  448.2 6.1 collective-permute-start.3
  448.2 31.9 %copy-start.16 = (bf16[4,128,256]{2,1,0:T(8,128)(2,1)}, bf16[4,128,256]{2,1,0:T(8,128)(2,1)S(1)}, u32[]{:S(2)}) copy-start(bf16[4,128,256]{2,1,0:T(8,128)(2,1)S(1)} %convert_element_type.22) | copy-start | bytes 786436
  448.2 10.1 %collective-permute-start.6 = (bf16[512,256]{1,0:T(8,128)(2,1)S(1)}, bf16[512,256]{1,0:T(8,128)(2,1)S(1)}, u32[]{:S(2)}, u32[]{:S(2)}) collective-permute-start(bf16[512,256]{1,0:T(8,128)(2,1)S(1)} %bitcast.62), channel_id=1, source_target_pairs={{0,24},{4,28},{8,16},{12,20},{16,8},{20,12},{24,0},{28,4},{1,25},{... | collective-permute-start | bytes 786440 | tf_op jit(solution)/shard_map/ppermute | solution.py:770
  450.8 12.7 %collective-permute-start.4 = (bf16[512,256]{1,0:T(8,128)(2,1)S(1)}, bf16[512,256]{1,0:T(8,128)(2,1)S(1)}, u32[]{:S(2)}, u32[]{:S(2)}) collective-permute-start(bf16[512,256]{1,0:T(8,128)(2,1)S(1)} %bitcast.63), channel_id=1, source_target_pairs={{0,8},{4,12},{8,0},{12,4},{16,24},{20,28},{24,16},{28,20},{1,9},{5... | collective-permute-start | bytes 786440 | tf_op jit(solution)/shard_map/ppermute | solution.py:770
  454.3 9.2 %collective-permute-start.5 = (bf16[512,256]{1,0:T(8,128)(2,1)S(1)}, bf16[512,256]{1,0:T(8,128)(2,1)S(1)}, u32[]{:S(2)}, u32[]{:S(2)}) collective-permute-start(bf16[512,256]{1,0:T(8,128)(2,1)S(1)} %bitcast.64), channel_id=1, source_target_pairs={{0,16},{4,20},{8,24},{12,28},{16,0},{20,4},{24,8},{28,12},{1,17},{... | collective-permute-start | bytes 786440 | tf_op jit(solution)/shard_map/ppermute | solution.py:770
  458.4 21.8 %copy-start.17 = (bf16[512,256]{1,0:T(8,128)(2,1)}, bf16[512,256]{1,0:T(8,128)(2,1)S(1)}, u32[]{:S(2)}) copy-start(bf16[512,256]{1,0:T(8,128)(2,1)S(1)} %collective-permute-done.6.refs_3_) | copy-start | bytes 786436
  458.4 21.7 %collective-permute-start.7 = (bf16[512,256]{1,0:T(8,128)(2,1)S(1)}, bf16[512,256]{1,0:T(8,128)(2,1)S(1)}, u32[]{:S(2)}, u32[]{:S(2)}) collective-permute-start(bf16[512,256]{1,0:T(8,128)(2,1)S(1)} %bitcast.65), channel_id=1, source_target_pairs={{0,4},{4,0},{8,12},{12,8},{16,20},{20,16},{24,28},{28,24},{1,5},{5... | collective-permute-start | bytes 786440 | tf_op jit(solution)/shard_map/ppermute | solution.py:770
  463.4 16.7 %copy-start.18 = (bf16[512,256]{1,0:T(8,128)(2,1)}, bf16[512,256]{1,0:T(8,128)(2,1)S(1)}, u32[]{:S(2)}) copy-start(bf16[512,256]{1,0:T(8,128)(2,1)S(1)} %collective-permute-done.4.refs_1_) | copy-start | bytes 786436
  463.4 16.6 %collective-permute-start.10 = (bf16[512,256]{1,0:T(8,128)(2,1)S(1)}, bf16[512,256]{1,0:T(8,128)(2,1)S(1)}, u32[]{:S(2)}, u32[]{:S(2)}) collective-permute-start(bf16[512,256]{1,0:T(8,128)(2,1)S(1)} %collective-permute-done.6.refs_3_), channel_id=1, source_target_pairs={{0,4},{4,0},{8,12},{12,8},{16,20},{20,16},{24,28},{28,24},{1,5},{5... | collective-permute-start | bytes 786440 | tf_op jit(solution)/shard_map/ppermute | solution.py:770
  463.4 16.7 %copy-start.19 = (bf16[512,256]{1,0:T(8,128)(2,1)}, bf16[512,256]{1,0:T(8,128)(2,1)S(1)}, u32[]{:S(2)}) copy-start(bf16[512,256]{1,0:T(8,128)(2,1)S(1)} %collective-permute-done.5.refs_2_) | copy-start | bytes 786436
  463.5 16.6 %collective-permute-start.8 = (bf16[512,256]{1,0:T(8,128)(2,1)S(1)}, bf16[512,256]{1,0:T(8,128)(2,1)S(1)}, u32[]{:S(2)}, u32[]{:S(2)}) collective-permute-start(bf16[512,256]{1,0:T(8,128)(2,1)S(1)} %collective-permute-done.4.refs_1_), channel_id=1, source_target_pairs={{0,4},{4,0},{8,12},{12,8},{16,20},{20,16},{24,28},{28,24},{1,5},{5... | collective-permute-start | bytes 786440 | tf_op jit(solution)/shard_map/ppermute | solution.py:770
  464.0 2.5 copy-start.15
  464.0 16.1 %collective-permute-start.9 = (bf16[512,256]{1,0:T(8,128)(2,1)S(1)}, bf16[512,256]{1,0:T(8,128)(2,1)S(1)}, u32[]{:S(2)}, u32[]{:S(2)}) collective-permute-start(bf16[512,256]{1,0:T(8,128)(2,1)S(1)} %collective-permute-done.5.refs_2_), channel_id=1, source_target_pairs={{0,4},{4,0},{8,12},{12,8},{16,20},{20,16},{24,28},{28,24},{1,5},{5... | collective-permute-start | bytes 786440 | tf_op jit(solution)/shard_map/ppermute | solution.py:770
  480.0 0.7 copy-start.20
  480.1 0.8 copy-start.21
  480.1 0.8 copy-start.22
  480.1 0.9 copy-start.23
  550.6 3.4 collective-permute-start.12
  555.3 12.0 %copy-start.26 = (f32[8,2048]{1,0:T(8,128)S(1)}, f32[8,2048]{1,0:T(8,128)}, u32[]{:S(2)}) copy-start(f32[8,2048]{1,0:T(8,128)} %get-tuple-element.99) | copy-start | bytes 196612
  564.7 18.2 %collective-permute-start.13 = (bf16[4,256,2176]{2,1,0:T(8,128)(2,1)}, bf16[4,256,2176]{2,1,0:T(8,128)(2,1)}, u32[]{:S(2)}, u32[]{:S(2)}) collective-permute-start(bf16[4,256,2176]{2,1,0:T(8,128)(2,1)} %weight_grads.10), channel_id=1, source_target_pairs={{0,4},{4,0},{8,12},{12,8},{16,20},{20,16},{24,28},{28,24},{1,5},{5... | collective-permute-start | bytes 13369352 | tf_op jit(solution)/shard_map/ppermute | solution.py:770
  567.3 14.6 %copy-start.27 = (f32[16,128]{1,0:T(8,128)S(1)}, f32[16,128]{1,0:T(8,128)}, u32[]{:S(2)}) copy-start(f32[16,128]{1,0:T(8,128)} %get-tuple-element.108) | copy-start | bytes 24580
  567.4 14.7 %copy-start.24 = (f32[32,2048]{1,0:T(8,128)S(1)}, f32[32,2048]{1,0:T(8,128)}, u32[]{:S(2)}) copy-start(f32[32,2048]{1,0:T(8,128)} %get-tuple-element.107) | copy-start | bytes 786436
  736.9 1.9 copy-start.4
Sparse Core Ops, SparseCore 0:
  401.0 77.2 reduce-scatter.1
  479.9 81.2 all-gather.1

commit v6 on v5

--- a/solution.py
+++ b/solution.py
@@ -27,12 +27,18 @@
     return sum((1 << i) * ((1 - b) if mask >> i & 1 else b) for i, b in enumerate(bits))
 
 
-def greet(masks, last=None):
+def greet(masks, last=None, all_heads=False):
     barrier = pltpu.get_barrier_semaphore()
     for mask in masks:
         pl.semaphore_signal(barrier, inc=1, device_id={"seq": partner(mask)}, device_id_type=MESH)
     count = len(masks)
-    if last is not None:
+    if all_heads:
+        place = lax.axis_index("head")
+        for k in range(1, last + 1):
+            to = lax.rem(place + k, last + 1)
+            pl.semaphore_signal(barrier, inc=1, device_id={"head": to}, device_id_type=MESH)
+        count += last
+    elif last is not None:
         place = lax.axis_index("head")
         for there, to in ((place > 0, place - 1), (place < last, place + 1)):
 
@@ -465,25 +471,26 @@
 
 
 def backward_kernel(
-    heads, key, value, devices, masks_of, scattering,
+    heads, key, value, devices, scattering,
     pre_ref, tail_ref, ab_ref, meta_ref, segrow_ref, edge_ref, edge_meta_ref, taps_ref, params_ref,
     states_ref, inverse_ref, state_in_ref, do_ref, ends_ref, *refs
 ):
     step = pl.program_id(0)
     steps = pl.num_programs(0)
-    pieces, refs = refs[: len(masks_of)], list(refs[len(masks_of) :])
+    piece, *refs = refs
     parts_ref = refs.pop(0) if scattering else None
     dpre_ref, dab_ref, halo_ref, taps_grad_ref, params_grad_ref = refs[:5]
     refs = refs[5:]
     got_ref = refs.pop(0) if scattering else None
     ext, du, adjoint, adjoints, home, *sems = refs
     if scattering:
-        moving = Scatter(parts_ref, got_ref, *sems)
+        moving = Scatter(parts_ref, got_ref, *sems[:2])
+        lead = Gather(piece, adjoints, *sems[2:])
 
         @pl.when(step == 0)
         def _():
-            greet(Scatter.masks)
-            moving.start()
+            greet(sorted({*Scatter.masks, *Gather.masks}))
+            lead.start()
 
     size = pre_ref.shape[0]
     kfirst, vfirst = heads * key, 2 * heads * key
@@ -492,14 +499,14 @@
     def _():
         adjoint[...] = jnp.zeros_like(adjoint)
         tall = heads * key
-        copies = []
-        for n, (mask, ref) in enumerate(zip(masks_of, pieces)):
-            first = 0 if mask is None else pl.multiple_of(partner(mask) * tall, tall)
-            target = adjoints.at[pl.ds(first, ref.shape[0]), :]
-            copies.append(pltpu.make_async_copy(ref, target, home.at[n]))
-        for copy in copies:
+        if scattering:
+            lead.middle()
+            lead.late()
+            moving.start()
+            lead.end()
+        else:
+            copy = pltpu.make_async_copy(piece, adjoints, home.at[0])
             copy.start()
-        for copy in copies:
             copy.wait()
 
         def one(k, carry):
@@ -672,7 +679,6 @@
     scattering = parts is not None
     moved = [jax.ShapeDtypeStruct((3,) + parts.shape[1:], low)] if scattering else []
     extra = dict(collective_id=6, has_side_effects=True) if scattering else {}
-    masks_of = [mask for mask, _ in adjoints]
     devices = ends.shape[0] // (heads * key)
     length, width = pre.shape
     blocks = length // BLOCK
@@ -680,7 +686,7 @@
     once = dict(pipeline_mode=pl.Buffered(1))
     last = blocks - 1
     return pl.pallas_call(
-        partial(backward_kernel, heads, key, value, devices, masks_of, scattering),
+        partial(backward_kernel, heads, key, value, devices, scattering),
         grid=(blocks,),
         in_specs=[
             pl.BlockSpec((BLOCK, width), lambda n: (last - n, 0)),
@@ -698,7 +704,7 @@
             pl.BlockSpec((BLOCK, heads * value), lambda n: (last - n, 0)),
             pl.BlockSpec(ends.shape, lambda n: (0, 0), **once),
         ]
-        + [pl.BlockSpec(**ANY) for _ in (*adjoints, *moved)],
+        + [pl.BlockSpec(**ANY) for _ in (0, *moved)],
         out_specs=[
             pl.BlockSpec((BLOCK, width), lambda n: (last - n, 0)),
             pl.BlockSpec((BLOCK, LANES), lambda n: (last - n, 0)),
@@ -720,14 +726,14 @@
             pltpu.VMEM((BLOCK + 16, width), full),
             pltpu.VMEM((heads, key, value), full),
             pltpu.VMEM((devices * heads * key, value), low),
-            pltpu.SemaphoreType.DMA((len(adjoints),)),
+            pltpu.SemaphoreType.DMA((1,)),
         ]
-        + (Scatter.semaphores if scattering else []),
+        + (Scatter.semaphores + Gather.semaphores if scattering else []),
         compiler_params=pltpu.CompilerParams(vmem_limit_bytes=56 * MIB, **extra),
         cost_estimate=FREE,
         name="chain_backward",
     )(pre, pre, ab, meta, segrow, edge, edge_meta, taps, params, states, inverse, state_in, do, ends,
-      *[a for _, a in adjoints], *([parts] if scattering else []))
+      adjoints, *([parts] if scattering else []))
 
 
 def segment_tables(doc_lengths, shard, length):
@@ -768,13 +774,6 @@
 
 def exchanged(block, mask):
     return lax.ppermute(block, "seq", [(i, i ^ mask) for i in range(lax.axis_size("seq"))])
-
-
-def spread(shard):
-    if lax.axis_size("seq") != NEAR:
-        return [(None, lax.all_gather(shard, "seq", axis=0, tiled=True))]
-    own = [(0, shard)] + [(mask, exchanged(shard, mask)) for mask in (2, 4, 6)]
-    return own + [(mask + 1, exchanged(a, 1)) for mask, a in own]
 
 
 def line_scratch(length, width):
@@ -947,7 +946,7 @@
 
         @pl.when(step == 0)
         def _():
-            greet(sorted({*masks, *union(kinds + [Gather] * len(first_one))}), last)
+            greet(sorted({*masks, *union(kinds + [Gather] * len(first_one))}), last, bool(masks))
             for c in [lead] if first_one else carried:
                 c.start()
 
@@ -1084,17 +1083,19 @@
 
     def three():
         ready(2)
-        g = fg[...]
-        hidden = (g * sigmoid(g) * fu[...]).astype(low)
+        g, lift = fg[...], fu[...]
+        sig = sigmoid(g)
+        swish = g * sig
+        hidden = (swish * lift).astype(low)
         hidden_ref[...] = hidden
+        fg[...] = lift * (sig * (1.0 + g * (1.0 - sig)))
+        fu[...] = swish
         partial_ref[...] = mm_nt(hidden, weights[:, w_down]).astype(low)
 
     def four():
         dhid = mm(cot_ref[...], weights[:, w_down])
-        g = fg[...]
-        sig = sigmoid(g)
-        dgate_ref[...] = (dhid * fu[...] * (sig * (1.0 + g * (1.0 - sig)))).astype(low)
-        dup_ref[...] = (dhid * (g * sig)).astype(low)
+        dgate_ref[...] = (dhid * fg[...]).astype(low)
+        dup_ref[...] = (dhid * fu[...]).astype(low)
 
     def five():
         return mm_nt(dgate_ref[...], weights[:, w_gate]) + mm_nt(dup_ref[...], weights[:, w_up])
@@ -1114,18 +1115,30 @@
     line_sum(step, last, [one, two, three, four, five], finish, scratch)
 
 
-def input_grad_kernel(last, keys, vals, near, ready, matrices, gain_ref, lines_ref,
+def input_grad_kernel(last, keys, vals, near, ready, matrices, gain_ref, lines_ref, head_ref,
                       dpre_ref, dgz_ref, dab_ref, tokens_ref,
                       term_ref, gains_ref, part, gain_grad, *scratch):
     step = pl.program_id(0)
     w_in, w_mix = matrices
     wide = 2 * keys + vals
     if near:
-        (got, sent, came), scratch = scratch[:3], scratch[3:]
+        (got, sent, came, got_head, sent_head, came_head), scratch = scratch[:6], scratch[6:]
+        place = lax.axis_index("head")
+
+        def across(k):
+            return pltpu.make_async_remote_copy(
+                src_ref=head_ref, dst_ref=got_head.at[place], send_sem=sent_head.at[k],
+                recv_sem=came_head.at[k], device_id={"head": lax.rem(place + k, last + 1)},
+                device_id_type=MESH,
+            )
 
     @pl.when(step == 0)
     def _():
         gain_grad[...] = jnp.zeros_like(gain_grad)
+        if near:
+            for k in range(1, last + 1):
+                across(k).start()
+            got_head[place] = head_ref[...]
 
     def one():
         ready(0)
@@ -1159,7 +1172,11 @@
         if not near:
             gains_ref[...] = own
             return
+        for k in range(1, last + 1):
+            across(k).wait()
+        heads_sum = sum((got_head[k] for k in range(1, last + 1)), start=got_head[0])
         gain_grad[...] = own
+        gain_grad[7:8, : head_ref.shape[1]] = jnp.sum(heads_sum, axis=0, keepdims=True)
         me = lax.axis_index("seq")
 
         def push(mask):
@@ -1170,7 +1187,7 @@
 
         for mask in range(1, NEAR):
             push(mask).start()
-        got[me] = own
+        got[me] = gain_grad[...]
         for mask in range(1, NEAR):
             push(mask).wait()
         gains_ref[...] = sum((got[k] for k in range(1, NEAR)), start=got[0])
@@ -1390,8 +1407,8 @@
 
 
 def final_kernel(heads, keys, vals, size, middle_ref, sum_ref, dmiddle_ref, term_ref, in_own, in_got,
-                 up_own, up_got, down_own, down_got, gate_own, gate_got, out_own, out_got,
-                 result_ref, dtokens_ref, q_ref, k_ref, v_ref, a_ref, b_ref, up_ref, lift_ref, down_ref,
+                 up_own, up_got, down_own, down_got, gate_own, gate_got, out_own, out_got, gains_ref,
+                 tq_ref, tk_ref, tv_ref, result_ref, dtokens_ref, q_ref, k_ref, v_ref, a_ref, b_ref, up_ref, lift_ref, down_ref,
                  gate_ref, out_ref):
     def total(own, got, cols=slice(None)):
         return own[0, :, cols].astype(full) + sum(got[k, :, cols].astype(full) for k in range(3))
@@ -1412,10 +1429,17 @@
         gate_ref[...] = total(gate_own, gate_got)
         out_ref[...] = total(out_own, out_got).T
 
+    @pl.when(pl.program_id(0) == 0)
+    def _():
+        tq_ref[...] = gains_ref[2:6, :keys]
+        tk_ref[...] = gains_ref[2:6, keys : 2 * keys]
+        tv_ref[...] = gains_ref[2:6, 2 * keys :]
+
     down_ref[...] = total(down_own, down_got).T
 
 
-def final_sums(middle, narrow_sum, dmiddle, term, sums_in, got_in, sums_up, got_up, sums_rest, got_rest, heads, keys, vals, size):
+def final_sums(middle, narrow_sum, dmiddle, term, sums_in, got_in, sums_up, got_up, sums_rest, got_rest, gains, heads, keys, vals,
+               size):
     length, width = dmiddle.shape
     rows = sums_in.shape[1]
     eight = lambda n: jnp.minimum(n, 7)
@@ -1433,9 +1457,11 @@
     in_specs += both(sums_rest, (rows, LANES), lambda n: (0, 0, n))
     in_specs += both(sums_rest, (rows, LANES), lambda n: (0, 0, at_gate + eight(n)))
     in_specs += both(sums_rest, (rows, LANES), lambda n: (0, 0, at_out + eight(n)))
+    once = lambda *shape: pl.BlockSpec(shape, lambda n: (0, 0))
+    in_specs += [once(*gains.shape)]
     byrow = lambda columns: pl.BlockSpec((few, columns), lambda n: (eight(n), 0))
     outs = [
-        ((length, width), low), ((length, width), full), ((rows, keys), full), ((rows, keys), full),
+        ((4, keys), full), ((4, keys), full), ((4, vals), full), ((length, width), low), ((length, width), full), ((rows, keys), full), ((rows, keys), full),
         ((rows, vals), full), ((rows, heads), full), ((rows, heads), full), ((rows, size), full),
         ((rows, size), full), ((size, rows), full), ((rows, vals), full), ((vals, rows), full),
     ]
@@ -1444,7 +1470,7 @@
         grid=(size // LANES,),
         in_specs=in_specs,
         out_specs=[
-            tall, tall,
+            once(4, keys), once(4, keys), once(4, vals), tall, tall,
             byrow(keys), byrow(keys), byrow(vals), byrow(heads), byrow(heads), byrow(size), byrow(size),
             pl.BlockSpec((LANES, rows), lambda n: (n, 0)),
             pl.BlockSpec((rows, LANES), lambda n: (0, eight(n))),
@@ -1455,7 +1481,7 @@
         cost_estimate=FREE,
         name="final_sums",
     )(middle, narrow_sum, dmiddle, term, sums_in, got_in, sums_up, got_up, sums_rest, got_rest, sums_rest,
-      got_rest, sums_rest, got_rest)
+      got_rest, sums_rest, got_rest, gains)
 
 
 def small_sums(part):
@@ -1562,25 +1588,23 @@
     gate_pgrad, mixed_grad, head_gain_part, adjoint = gate_back(
         middle_low, w_mix, mixed, gate_pre, gain, through, heads, key, value
     )
-    for mask in (1, 2):
-        head_gain_part += lax.ppermute(
-            head_gain_part, "head", [(i, i ^ mask) for i in range(last + 1)]
-        )
-    adjoints = spread(adjoint.astype(low).reshape(keys, value))
+    if not near:
+        head_gain_part = lax.psum(head_gain_part, "head")
+    adjoint = adjoint.astype(low).reshape(keys, value)
+    if not near:
+        adjoint = lax.all_gather(adjoint, "seq", axis=0, tiled=True)
     pairs_up = [(second_in, [gate_grad, lift_grad])]
     pairs_rest = [(cotangent, [hidden]), (first_in, [gate_pgrad]), (middle_low, [mix_out])]
     sums_up = pair_sums(place, pairs_up) if near else None
     sums_rest = pair_sums(place, pairs_rest) if near else None
-    if near:
-        narrow_sum, sums_up, head_gain_part = lax.optimization_barrier(
-            (narrow_sum, sums_up, head_gain_part)
-        )
-    narrow_sum = lax.all_gather(narrow_sum, "head", axis=0, tiled=True)
     pre_grad, ab_grad, halo, taps_part, params_part, *moved = backward_chain(
         pre, ab, meta, segrow, edge, edge_meta, taps, params, states, inverse, state_in,
-        mixed_grad, ends, adjoints, heads, key, value, sums_up,
+        mixed_grad, ends, adjoint, heads, key, value, sums_up,
     )
     got_up = moved
+    if near:
+        narrow_sum, halo = lax.optimization_barrier((narrow_sum, halo))
+    narrow_sum = lax.all_gather(narrow_sum, "head", axis=0, tiled=True)
     halo = passed_along(halo, "seq", -1)
     tail = pre_grad[length - 8 :].astype(full) + halo
     pre_grad = lax.dynamic_update_slice(pre_grad, tail.astype(low), (length - 8, 0))
@@ -1593,24 +1617,28 @@
             jnp.sum(ffn_gain_part, axis=0, keepdims=True),
             jnp.sum(taps_part.reshape(4, 8, -1), axis=1),
             jnp.pad(params_part, ((0, 0), (0, width - params_part.shape[1]))),
-            jnp.pad(jnp.sum(head_gain_part, axis=0)[None], ((0, 0), (0, width - value))),
+            jnp.zeros((1, width), full)
+            if near
+            else jnp.pad(jnp.sum(head_gain_part, axis=0)[None], ((0, 0), (0, width - value))),
         ],
         axis=0,
     )
     term, gains, *moved = line_call(
         partial(input_grad_kernel, last, keys, vals, near), "input_grad", 2, length, width, last,
-        [mixer_gain[None, :], lines], [(w_in, [(0, w_in.shape[1])]), (w_mix, [(0, vals)])],
+        [mixer_gain[None, :], lines, head_gain_part], [(w_in, [(0, w_in.shape[1])]), (w_mix, [(0, vals)])],
         [pre_grad, gate_pgrad, ab_grad], [tokens],
         [((length, width), low, "second"), ((8, width), full, "all")],
         [pltpu.VMEM((ROWS, width), full), pltpu.VMEM((8, width), full)]
-        + ([pltpu.VMEM((NEAR, 8, width), full), *[pltpu.SemaphoreType.DMA((NEAR,))] * 2] if near else []),
+        + ([pltpu.VMEM((NEAR, 8, width), full), *[pltpu.SemaphoreType.DMA((NEAR,))] * 2] if near else [])
+        + ([pltpu.VMEM((last + 1, 8, value), full), *[pltpu.SemaphoreType.DMA((last + 1,))] * 2] if near else []),
         scatters=[sums_rest, sums_in] if near else [], masks=range(1, NEAR) if near else (),
     )
+    sums = gains if near else small_sums(gains)
     if near:
-        (result, tokens_grad, query_grad, key_grad, value_grad, alpha_grad, beta_grad, up_grad, lift_grad,
+        (tq_grad, tk_grad, tv_grad, result, tokens_grad, query_grad, key_grad, value_grad, alpha_grad, beta_grad, up_grad, lift_grad,
          down_grad, gate_grad, out_grad) = final_sums(
             middle, narrow_sum, middle_grad, term, sums_in, moved[1], sums_up, got_up[0], sums_rest, moved[0],
-            heads, keys, vals, size,
+            gains, heads, keys, vals, size,
         )
     else:
         up, rest, into = (plain_sums(place, pairs) for pairs in (pairs_up, pairs_rest, pairs_in))
@@ -1622,8 +1650,10 @@
             rest[:, :size].T, rest[:, size : size + vals], rest[:, size + vals :].T
         )
         result = (middle + narrow_sum.astype(full)).astype(low)
-    sums = gains if near else small_sums(gains)
-    taps_grad = sums[2:6]
+        taps_grad = sums[2:6]
+        tq_grad, tk_grad, tv_grad = (
+            taps_grad[:, :keys], taps_grad[:, keys : 2 * keys], taps_grad[:, 2 * keys :]
+        )
     return (
         result,
         tokens_grad,
@@ -1636,9 +1666,9 @@
         beta_grad,
         sums[6, LANES : LANES + heads],
         sums[6, :heads],
-        taps_grad[:, :keys],
-        taps_grad[:, keys : 2 * keys],
-        taps_grad[:, 2 * keys :],
+        tq_grad,
+        tk_grad,
+        tv_grad,
         sums[7, :value],
         out_grad,
         sums[1],

time: 771 us -> 770 us (level)
  Pallas kernels: 689 us -> 714 us
  waiting for transfers between devices: 18.6 us -> 2.12 us
    pallas_call x3, Pallas kernels: 413 us -> 426 us  [line_call(): pl.pallas_call(body, grid=(steps,), in_specs=in_specs, out_specs=out_spec...]
    pallas_call x1, Pallas kernels: 69.6 us -> 81.4 us  [backward_chain(): pl.pallas_call(partial(backward_kernel, heads, key, value, devices, scatt...]
    ppermute x2 -> x0, waiting for transfers between devices: 8.86 us -> none  [shards(): lax.ppermute(head_gain_part, 'head', [(i, i ^ mask) for i in range(last +...]
    unnamed x62 -> x48, local copies, waits for them, and re-layouts: 17.9 us -> 16 us
  transfers between devices with their start and end apart: 16 -> 7, of which waited for: 5 -> 1; matrix products, arithmetic and copies ran while one was open for 2% -> 2% of each run, Pallas kernels for 38% -> 41%
where the time goes in v6:
time: 770 us; the launch traced here: 768 us
  Pallas kernels  714 us (93%)
  local copies, waits for them, and re-layouts  25 us (3%)
  between operations  14.6 us (2%)
    pallas_call x3, Pallas kernels, line_call(): pl.pallas_call(body, grid=(steps,), in_specs=in_specs, out_specs=out_spec...  426 us
    pallas_call x1, Pallas kernels, backward_chain(): pl.pallas_call(partial(backward_kernel, heads, key, value, devices, scatt...  81.4 us
    pallas_call x6, Pallas kernels, weight_call(): pl.pallas_call(partial(weight_kernel, [len(bs) for _, bs in pairs], added...  72 us
    pallas_call x1, Pallas kernels, input_projection(): pl.pallas_call(partial(input_kernel, wide, gathering), in_specs=[here] +...  56.8 us
    pallas_call x1, Pallas kernels, forward_chain(): pl.pallas_call(partial(forward_kernel, heads, key, value, gathering), gri...  43.5 us
    pallas_call x1, Pallas kernels, final_sums(): pl.pallas_call(partial(final_kernel, heads, keys, vals, size), grid=(size...  22.2 us
    unnamed x48, local copies, waits for them, and re-layouts  16 us
  transfers between devices with their start and end apart: 7, of which 1 were waited for; matrix products, arithmetic and copies ran while one was open for 2% of the time, Pallas kernels for 41%

profile of v6, /device:TPU:0, one launch (start us, length us, event | category | flops | bytes accessed | tf_op | source)
XLA Modules:
  0.0 767.9 jit_solution(14060377995494057046)
XLA Ops:
  7.2 0.8 slice.73
  8.1 2.3 collective-permute-start
  10.5 0.8 reduce-window.9
  11.3 0.7 bitcast_subtract_fusion
  12.8 0.8 copy.112
  13.6 0.8 copy.113
  14.4 0.7 constant_dynamic-update-slice_fusion.2
  15.1 0.7 negate_bitcast_fusion
  16.0 0.7 constant_dynamic-update-slice_fusion.1
  16.7 0.7 constant_dynamic-update-slice_fusion.taps_ref
  17.4 0.8 maximum_maximum_fusion.refs_3_
  18.2 0.7 select_maximum_fusion.params_ref
  18.9 0.6 copy-done.18
  19.5 56.8 %input_projection.1 = (bf16[1024,2048]{1,0:T(8,128)(2,1)}, bf16[1024,2048]{1,0:T(8,128)(2,1)}, f32[1024,128]{1,0:T(8,128)}, bf16[16,2048]{1,0:T(8,128)(2,1)}, bf...) custom-call(f32[1,2048]{1,0:T(1,128)} %bitcast.64, f32[256,512]{1,0:T(8,128)} %refs_0_.3, ...), custom_call_target="tpu_custom_call" | custom-call | flops 1 | bytes 1 | tf_op jit(solution)/shard_map/input_projection/pallas_call | solution.py:1323
  76.3 0.8 slice.83.edge_ref
  77.1 1.0 copy-done.6
  78.1 1.2 copy-done.8
  79.3 43.5 %chain_forward.1 = (f32[1024,1024]{1,0:T(8,128)}, bf16[1024,512]{1,0:T(8,128)(2,1)S(1)}, bf16[8,4,128,384]{3,2,1,0:T(8,128)(2,1)}, bf16[8,4,128,128]{3,2,1,0:T(8...) custom-call(bf16[1024,2048]{1,0:T(8,128)(2,1)} %get-tuple-element.79.pre_ref.tail_ref, ...), custom_call_target="tpu_custom_call" | custom-call | flops 1 | bytes 1 | tf_op jit(solution)/shard_map/chain_forward/pallas_call | solution.py:360
  122.9 1.0 copy-done.2
  123.9 1.0 copy-done.7
  124.8 0.7 copy-done.9
  125.6 147.7 %mixer_out.1 = (bf16[1024,1024]{1,0:T(8,128)(2,1)}, f32[1024,1024]{1,0:T(8,128)}, f32[1024,1024]{1,0:T(8,128)}, f32[4,128,256]{2,1,0:T(8,128)}, f32[1024,2048]{1...) custom-call(f32[1,256]{1,0:T(1,128)} %bitcast.59, ...), custom_call_target="tpu_custom_call" | custom-call | flops 1 | bytes 1 | tf_op jit(solution)/shard_map/mixer_out/pallas_call | solution.py:999
  273.3 127.6 %ffn.1 = (bf16[1024,1408]{1,0:T(8,128)(2,1)}, bf16[1024,1408]{1,0:T(8,128)(2,1)}, bf16[1024,1408]{1,0:T(8,128)(2,1)}, bf16[1024,2048]{1,0:T(8,128)(2,1)}, f32[10...) custom-call(f32[1,2048]{1,0:T(1,128)} %bitcast.67, bf16[2048,4224]{1,0:T(8,128)(2,1)} %get-tuple-element.90.refs_1_, ...), custom_call_target="tpu_custom_call" | custom-call | flops 1 | bytes 1 | tf_op jit(solution)/shard_map/ffn/pallas_call | solution.py:999
  401.0 11.8 %weight_grads.6 = bf16[4,256,2816]{2,1,0:T(8,128)(2,1)} custom-call(s32[1]{0:T(128)} %bitcast.28.place_ref, bf16[1024,2048]{1,0:T(8,128)(2,1)} %get-tuple-element.91.refs_2_.refs_0_, bf16[1024,1408]{1,0:T(8,128)(2,1)} %get-tuple-element.102.refs_1_, bf16[1024,1408]{1,0:T(8,128)(2,1)} %get-tuple-element.103.refs_2_), custom_call_target="tpu_custom_call" | custom-call | flops 1 | bytes 1 | tf_op jit(solution)/shard_map/weight_grads/pallas_call | solution.py:1383
  412.8 12.6 %gate_back.1 = (bf16[1024,1024]{1,0:T(8,128)(2,1)S(1)}, bf16[1024,1024]{1,0:T(8,128)(2,1)S(1)}, f32[8,256]{1,0:T(8,128)S(1)}, f32[4,128,256]{2,1,0:T(8,128)S(1)}) custom-call(bf16[1024,2048]{1,0:T(8,128)(2,1)} %get-tuple-element.96.dz_ref.refs_2_, f32[1024,1024]{1,0:T(8,128)} %get-tuple-element.97.mixed_ref, f32[1024,1024]{1,0:T(8,128)} %get-tuple-element.98.gate_ref, ...), custom_call_target="tpu_custom_call" | custom-call | flops 1 | bytes 1 | tf_op jit(solution)/shard_map/gate_back/pallas_call | solution.py:435
  425.5 1.3 copy-done
  426.8 1.3 copy-done.5
  428.7 13.5 %weight_grads.8 = bf16[4,256,3456]{2,1,0:T(8,128)(2,1)} custom-call(s32[1]{0:T(128)} %bitcast.28.place_ref, bf16[1024,2048]{1,0:T(8,128)(2,1)} %refs_0_.5, bf16[1024,2048]{1,0:T(8,128)(2,1)} %get-tuple-element.86.refs_5_.refs_1_.refs_0_, bf16[1024,2048]{1,0:T(8,128)(2,1)} %get-tuple-element.96.dz_ref.refs_2_, bf16[1024,1408]{1,0:T(8,128)(2,1)} %get-tuple-element.112.refs_3_, ...), custom_call_target="tpu_custom_call" | custom-call | flops 1 | bytes 1 | tf_op jit(solution)/shard_map/weight_grads/pallas_call | solution.py:1383
  444.1 0.7 convert_element_type.21
  444.8 12.2 %weight_grads.7.refs_1_.up_own = bf16[4,256,2816]{2,1,0:T(8,128)(2,1)} custom-call(s32[1]{0:T(128)} %bitcast.28.place_ref, bf16[1024,2048]{1,0:T(8,128)(2,1)} %get-tuple-element.91.refs_2_.refs_0_, bf16[1024,1408]{1,0:T(8,128)(2,1)} %get-tuple-element.102.refs_1_, bf16[1024,1408]{1,0:T(8,128)(2,1)} %get-tuple-element.103.refs_2_, ...), custom_call_target="tpu_custom_call" | custom-call | flops 1 | bytes 1 | tf_op jit(solution)/shard_map/weight_grads/pallas_call | solution.py:1383
  457.0 81.4 %chain_backward.1 = (bf16[1024,2048]{1,0:T(8,128)(2,1)}, bf16[1024,128]{1,0:T(8,128)(2,1)}, f32[8,2048]{1,0:T(8,128)}, f32[32,2048]{1,0:T(8,128)}, f32[16,128]{1,0:T(8,128)}, /*index=5*/bf16[3,256,2816]{2,1,0:T(8,128)(2,1)}) custom-call(bf16[1024,2048]{1,0:T(8,128)(2,1)} %get-tuple-element.79.pre_ref.tail_ref, ...), custom_call_target="tpu_custom_call" | custom-call | flops 1 | bytes 1 | tf_op jit(solution)/shard_map/chain_backward/pallas_call | solution.py:688
  538.5 1.3 collective-permute-start.3
  539.8 2.1 collective-permute-done.3
  541.9 1.4 fusion.refs_1_.refs_7_
  543.3 9.9 %weight_grads.10 = bf16[4,256,2176]{2,1,0:T(8,128)(2,1)} custom-call(s32[1]{0:T(128)} %bitcast.28.place_ref, bf16[1024,2048]{1,0:T(8,128)(2,1)} %get-tuple-element.86.refs_5_.refs_1_.refs_0_, bf16[1024,2048]{1,0:T(8,128)(2,1)} %fusion.refs_1_.refs_7_, bf16[1024,128]{1,0:T(8,128)(2,1)} %get-tuple-element.117.refs_2_.refs_9_), custom_call_target="tpu_custom_call" | custom-call | flops 1 | bytes 1 | tf_op jit(solution)/shard_map/weight_grads/pallas_call | solution.py:1383
  553.1 1.3 collective-permute-start.4
  554.7 0.7 concatenate.11.refs_1_
  555.3 14.7 %weight_grads.9.refs_5_.down_own.gate_own.out_own = bf16[4,256,3456]{2,1,0:T(8,128)(2,1)} custom-call(s32[1]{0:T(128)} %bitcast.28.place_ref, bf16[1024,2048]{1,0:T(8,128)(2,1)} %refs_0_.5, bf16[1024,2048]{1,0:T(8,128)(2,1)} %get-tuple-element.86.refs_5_.refs_1_.refs_0_, bf16[1024,2048]{1,0:T(8,128)(2,1)} %get-tuple-element.96.dz_ref.refs_2_, ...), custom_call_target="tpu_custom_call" | custom-call | flops 1 | bytes 1 | tf_op jit(solution)/shard_map/weight_grads/pallas_call | solution.py:1383
  570.1 10.0 %weight_grads.11.refs_6_.in_own = bf16[4,256,2176]{2,1,0:T(8,128)(2,1)} custom-call(s32[1]{0:T(128)} %bitcast.28.place_ref, bf16[1024,2048]{1,0:T(8,128)(2,1)} %get-tuple-element.86.refs_5_.refs_1_.refs_0_, bf16[1024,2048]{1,0:T(8,128)(2,1)} %fusion.refs_1_.refs_7_, bf16[1024,128]{1,0:T(8,128)(2,1)} %get-tuple-element.117.refs_2_.refs_9_, ...), custom_call_target="tpu_custom_call" | custom-call | flops 1 | bytes 1 | tf_op jit(solution)/shard_map/weight_grads/pallas_call | solution.py:1383
  580.0 150.5 %input_grad.1 = (bf16[1024,2048]{1,0:T(8,128)(2,1)}, f32[8,2048]{1,0:T(8,128)}, bf16[3,256,3456]{2,1,0:T(8,128)(2,1)}, bf16[3,256,2176]{2,1,0:T(8,128)(2,1)}) custom-call(f32[1,2048]{1,0:T(1,128)} %bitcast.65, f32[8,2048]{1,0:T(8,128)} %concatenate.11.refs_1_, f32[8,256]{1,0:T(8,128)} %copy-done.15, bf16[2048,2176]{1,0:T(8,128)(2,1)} %get-tuple-element.111.refs_3_, ...), custom_call_target="tpu_custom_call" | custom-call | flops 1 | bytes 1 | tf_op jit(solution)/shard_map/input_grad/pallas_call | solution.py:999
  730.5 1.3 slice.95
  731.8 1.2 slice_bitcast_fusion.1
  733.0 1.5 fusion.15
  734.5 1.9 copy-done.4
  736.5 0.8 copy-done.13
  737.3 22.2 %final_sums.1 = (f32[4,512]{1,0:T(4,128)}, f32[4,512]{1,0:T(4,128)}, f32[4,1024]{1,0:T(4,128)}, bf16[1024,2048]{1,0:T(8,128)(2,1)}, f32[1024,2048]{1,0:T(8,128)}...) custom-call(f32[1024,2048]{1,0:T(8,128)} %get-tuple-element.89.refs_, ...), custom_call_target="tpu_custom_call" | custom-call | flops 1 | bytes 1 | tf_op jit(solution)/shard_map/final_sums/pallas_call | solution.py:1468
  759.5 0.7 copy.124
  760.2 0.7 copy.125
  (72 shorter events, 3.8 us)
Async XLA Ops:
  7.2 531.3 %reduce-scatter.2.cloned.1.call-start = ((), (), s32[]{:S(2)}) async-start(), calls=%async_computation.1 | async-start | bytes 5242880 | tf_op jit(solution)/shard_map/reduce_scatter | solution.py:1587
  8.1 10.8 %collective-permute-start = (bf16[16,2048]{1,0:T(8,128)(2,1)S(1)}, bf16[16,2048]{1,0:T(8,128)(2,1)S(1)}, u32[]{:S(2)}, u32[]{:S(2)}) collective-permute-start(bf16[16,2048]{1,0:T(8,128)(2,1)S(1)} %slice.73), channel_id=1, source_target_pairs={{0,4},{4,8},{8,12},{12,16},{16,20},{20,24},{24,28},{1,5},{5,9},{9,... | collective-permute-start | bytes 196616 | tf_op jit(solution)/shard_map/ppermute | solution.py:1494
  15.9 61.2 %copy-start.1 = (f32[1024,128]{1,0:T(8,128)}, f32[1024,128]{1,0:T(8,128)S(1)}, u32[]{:S(2)}) copy-start(f32[1024,128]{1,0:T(8,128)S(1)} %pad.16.meta_ref) | copy-start | bytes 1572868
  17.4 59.6 %copy-start.12 = (f32[4,2048]{1,0:T(4,128)}, f32[4,2048]{1,0:T(4,128)S(1)}, u32[]{:S(2)}) copy-start(f32[4,2048]{1,0:T(4,128)S(1)} %constant_dynamic-update-slice_fusion.taps_ref) | copy-start | bytes 98308
  18.8 58.2 %copy-start.14 = (f32[8,128]{1,0:T(8,128)}, f32[8,128]{1,0:T(8,128)S(1)}, u32[]{:S(2)}) copy-start(f32[8,128]{1,0:T(8,128)S(1)} %select_maximum_fusion.params_ref) | copy-start | bytes 12292
  18.9 0.6 copy-start.18
  77.0 196.2 %copy-start.10 = (bf16[8,2048]{1,0:T(8,128)(2,1)}, bf16[8,2048]{1,0:T(8,128)(2,1)S(1)}, u32[]{:S(2)}) copy-start(bf16[8,2048]{1,0:T(8,128)(2,1)S(1)} %slice.83.edge_ref) | copy-start | bytes 98308
  77.0 196.2 %copy-start.11 = (f32[8,1024]{1,0:T(8,128)}, f32[8,1024]{1,0:T(8,128)S(1)}, u32[]{:S(2)}) copy-start(f32[8,1024]{1,0:T(8,128)S(1)} %broadcast_in_dim.33.segrow_ref) | copy-start | bytes 98308
  77.1 1.0 copy-start.6
  78.1 1.2 copy-start.8
  122.9 1.0 copy-start.2
  123.9 1.0 copy-start.7
  124.8 0.7 copy-start.9
  400.9 333.6 %all-gather.2.cloned.1.call-start = ((), (), s32[]{:S(2)}) async-start(), calls=%async_computation.2 | async-start | bytes 5242880 | tf_op jit(solution)/shard_map/all_gather | solution.py:1607
  401.0 11.9 %copy-start.3 = (bf16[1024,512]{1,0:T(8,128)(2,1)S(1)}, bf16[1024,512]{1,0:T(8,128)(2,1)}, u32[]{:S(2)}) copy-start(bf16[1024,512]{1,0:T(8,128)(2,1)} %copy-done.2) | copy-start | bytes 3145732
  401.0 11.9 %copy-start.16 = (f32[256]{0:T(256)S(1)}, f32[256]{0:T(256)}, u32[]{:S(2)}) copy-start(f32[256]{0:T(256)} %param.35) | copy-start | bytes 3076
  412.8 32.0 %collective-permute-start.1 = (bf16[4,256,2816]{2,1,0:T(8,128)(2,1)}, bf16[4,256,2816]{2,1,0:T(8,128)(2,1)}, u32[]{:S(2)}, u32[]{:S(2)}) collective-permute-start(bf16[4,256,2816]{2,1,0:T(8,128)(2,1)} %weight_grads.6), channel_id=1, source_target_pairs={{0,4},{4,0},{8,12},{12,8},{16,20},{20,16},{24,28},{28,24},{1,5},{5... | collective-permute-start | bytes 17301512 | tf_op jit(solution)/shard_map/ppermute | solution.py:776
  425.5 1.3 copy-start
  426.8 1.3 copy-start.5
  428.1 0.6 copy-start.15
  442.2 113.2 %collective-permute-start.2 = (bf16[4,256,3456]{2,1,0:T(8,128)(2,1)}, bf16[4,256,3456]{2,1,0:T(8,128)(2,1)}, u32[]{:S(2)}, u32[]{:S(2)}) collective-permute-start(bf16[4,256,3456]{2,1,0:T(8,128)(2,1)} %weight_grads.8), channel_id=1, source_target_pairs={{0,4},{4,0},{8,12},{12,8},{16,20},{20,16},{24,28},{28,24},{1,5},{5... | collective-permute-start | bytes 21233672 | tf_op jit(solution)/shard_map/ppermute | solution.py:776
  538.5 3.4 collective-permute-start.3
  543.3 11.2 %copy-start.19 = (f32[8,2048]{1,0:T(8,128)S(1)}, f32[8,2048]{1,0:T(8,128)}, u32[]{:S(2)}) copy-start(f32[8,2048]{1,0:T(8,128)} %get-tuple-element.107) | copy-start | bytes 196612
  543.3 11.3 %copy-start.20 = (f32[16,128]{1,0:T(8,128)S(1)}, f32[16,128]{1,0:T(8,128)}, u32[]{:S(2)}) copy-start(f32[16,128]{1,0:T(8,128)} %get-tuple-element.109) | copy-start | bytes 24580
  543.3 11.3 %copy-start.17 = (f32[32,2048]{1,0:T(8,128)S(1)}, f32[32,2048]{1,0:T(8,128)}, u32[]{:S(2)}) copy-start(f32[32,2048]{1,0:T(8,128)} %get-tuple-element.108) | copy-start | bytes 786436
  553.1 16.9 %collective-permute-start.4 = (bf16[4,256,2176]{2,1,0:T(8,128)(2,1)}, bf16[4,256,2176]{2,1,0:T(8,128)(2,1)}, u32[]{:S(2)}, u32[]{:S(2)}) collective-permute-start(bf16[4,256,2176]{2,1,0:T(8,128)(2,1)} %weight_grads.10), channel_id=1, source_target_pairs={{0,4},{4,0},{8,12},{12,8},{16,20},{20,16},{24,28},{28,24},{1,5},{5... | collective-permute-start | bytes 13369352 | tf_op jit(solution)/shard_map/ppermute | solution.py:776
  734.5 1.9 copy-start.4
  736.5 0.8 copy-start.13
Sparse Core Ops, SparseCore 0:
  401.0 76.8 reduce-scatter.1
  538.6 95.9 all-gather.1

commit v7 on v6

--- a/solution.py
+++ b/solution.py
@@ -116,12 +116,13 @@
     masks = (2, 4, 6)
     semaphores = [pltpu.SemaphoreType.DMA((3,)), pltpu.SemaphoreType.DMA((3,))]
 
-    def __init__(self, parts, got, sent, came):
+    def __init__(self, parts, got, sent, came, first=0):
         self.parts, self.got, self.sent, self.came = parts, got, sent, came
+        self.columns = pl.ds(first, got.shape[2])
 
     def push(self, k):
         return pltpu.make_async_remote_copy(
-            src_ref=self.parts.at[k + 1], dst_ref=self.got.at[k], send_sem=self.sent.at[k],
+            src_ref=self.parts.at[k + 1, :, self.columns], dst_ref=self.got.at[k], send_sem=self.sent.at[k],
             recv_sem=self.came.at[k], device_id={"seq": partner(2 * k + 2)}, device_id_type=MESH,
         )
 
@@ -675,9 +676,9 @@
 
 
 def backward_chain(pre, ab, meta, segrow, edge, edge_meta, taps, params, states, inverse,
-                   state_in, do, ends, adjoints, heads, key, value, parts=None):
+                   state_in, do, ends, adjoints, heads, key, value, parts=None, sent=0):
     scattering = parts is not None
-    moved = [jax.ShapeDtypeStruct((3,) + parts.shape[1:], low)] if scattering else []
+    moved = [jax.ShapeDtypeStruct((3, parts.shape[1], sent), low)] if scattering else []
     extra = dict(collective_id=6, has_side_effects=True) if scattering else {}
     devices = ends.shape[0] // (heads * key)
     length, width = pre.shape
@@ -916,7 +917,8 @@
         for s, (_, _, stage) in zip(shapes, outs)
     ]
     moved = [jax.ShapeDtypeStruct((a.shape[0] * NEAR, a.shape[1]), low) for a in (*first_one, *gathers)]
-    moved += [jax.ShapeDtypeStruct((3,) + a.shape[1:], low) for a in scatters]
+    firsts, scatters = [f for _, f in scatters], [a for a, _ in scatters]
+    moved += [jax.ShapeDtypeStruct((3, a.shape[1], a.shape[2] - f), low) for a, f in zip(scatters, firsts)]
     kinds = [Gather] * len(gathers) + [Scatter] * len(scatters)
     whole_first = [pltpu.VMEM(s.shape, low) for s in moved[: len(first_one)]]
     held = [pltpu.VMEM(a.shape, low) for a in weights] + [pltpu.SemaphoreType.DMA((sum(len(c) for c in cuts),))]
@@ -941,7 +943,11 @@
             lead = Gather(ahead[0], table, *signals)
             back = pltpu.make_async_copy(table, handed[0], signals[2].at[0])
             matrices.append(table)
-        carried = [kind(a, b, *take(len(kind.semaphores))) for kind, a, b in zip(kinds, sources, targets)]
+        begins = [()] * len(gathers) + [(first,) for first in firsts]
+        carried = [
+            kind(a, b, *take(len(kind.semaphores)), *first)
+            for kind, a, b, first in zip(kinds, sources, targets, begins)
+        ]
         step = pl.program_id(0)
 
         @pl.when(step == 0)
@@ -1407,7 +1413,7 @@
 
 
 def final_kernel(heads, keys, vals, size, middle_ref, sum_ref, dmiddle_ref, term_ref, in_own, in_got,
-                 up_own, up_got, down_own, down_got, gate_own, gate_got, out_own, out_got, gains_ref,
+                 up_own, up_got, up_late, down_own, down_got, gate_own, gate_got, out_own, out_got, gains_ref,
                  tq_ref, tk_ref, tv_ref, result_ref, dtokens_ref, q_ref, k_ref, v_ref, a_ref, b_ref, up_ref, lift_ref, down_ref,
                  gate_ref, out_ref):
     def total(own, got, cols=slice(None)):
@@ -1424,8 +1430,11 @@
         small = total(in_own, in_got, slice(wide, wide + LANES))
         a_ref[...] = small[:, :heads]
         b_ref[...] = small[:, heads : 2 * heads]
+        split = up_got.shape[2]
         up_ref[...] = total(up_own, up_got, slice(0, size))
-        lift_ref[...] = total(up_own, up_got, slice(size, 2 * size))
+        lift_ref[:, : split - size] = total(up_own, up_got, slice(size, split))
+        late = sum(up_late[k].astype(full) for k in range(3))
+        lift_ref[:, split - size :] = up_own[0, :, split:].astype(full) + late
         gate_ref[...] = total(gate_own, gate_got)
         out_ref[...] = total(out_own, out_got).T
 
@@ -1438,8 +1447,8 @@
     down_ref[...] = total(down_own, down_got).T
 
 
-def final_sums(middle, narrow_sum, dmiddle, term, sums_in, got_in, sums_up, got_up, sums_rest, got_rest, gains, heads, keys, vals,
-               size):
+def final_sums(middle, narrow_sum, dmiddle, term, sums_in, got_in, sums_up, got_up, got_late, sums_rest, got_rest, gains, heads,
+               keys, vals, size):
     length, width = dmiddle.shape
     rows = sums_in.shape[1]
     eight = lambda n: jnp.minimum(n, 7)
@@ -1448,12 +1457,15 @@
     def both(array, block, index):
         return [pl.BlockSpec((1,) + block, index), pl.BlockSpec((3,) + block, index)]
 
-    wide_in, wide_up = sums_in.shape[2], sums_up.shape[2]
+    wide_in = sums_in.shape[2]
     at_gate, at_out = size // LANES, (size + vals) // LANES
     tall = pl.BlockSpec((many, width), lambda n: (eight(n), 0))
     in_specs = [tall] * 4
     in_specs += both(sums_in, (few, wide_in), lambda n: (0, eight(n), 0))
-    in_specs += both(sums_up, (few, wide_up), lambda n: (0, eight(n), 0))
+    in_specs += [
+        pl.BlockSpec((count, few, a.shape[2]), lambda n: (0, eight(n), 0))
+        for count, a in ((1, sums_up), (3, got_up), (3, got_late))
+    ]
     in_specs += both(sums_rest, (rows, LANES), lambda n: (0, 0, n))
     in_specs += both(sums_rest, (rows, LANES), lambda n: (0, 0, at_gate + eight(n)))
     in_specs += both(sums_rest, (rows, LANES), lambda n: (0, 0, at_out + eight(n)))
@@ -1480,7 +1492,7 @@
         compiler_params=pltpu.CompilerParams(vmem_limit_bytes=48 * MIB),
         cost_estimate=FREE,
         name="final_sums",
-    )(middle, narrow_sum, dmiddle, term, sums_in, got_in, sums_up, got_up, sums_rest, got_rest, sums_rest,
+    )(middle, narrow_sum, dmiddle, term, sums_in, got_in, sums_up, got_up, got_late, sums_rest, got_rest, sums_rest,
       got_rest, sums_rest, got_rest, gains)
 
 
@@ -1593,13 +1605,14 @@
     adjoint = adjoint.astype(low).reshape(keys, value)
     if not near:
         adjoint = lax.all_gather(adjoint, "seq", axis=0, tiled=True)
+    split = 17 * LANES
     pairs_up = [(second_in, [gate_grad, lift_grad])]
     pairs_rest = [(cotangent, [hidden]), (first_in, [gate_pgrad]), (middle_low, [mix_out])]
     sums_up = pair_sums(place, pairs_up) if near else None
     sums_rest = pair_sums(place, pairs_rest) if near else None
     pre_grad, ab_grad, halo, taps_part, params_part, *moved = backward_chain(
         pre, ab, meta, segrow, edge, edge_meta, taps, params, states, inverse, state_in,
-        mixed_grad, ends, adjoint, heads, key, value, sums_up,
+        mixed_grad, ends, adjoint, heads, key, value, sums_up, split,
     )
     got_up = moved
     if near:
@@ -1631,13 +1644,13 @@
         [pltpu.VMEM((ROWS, width), full), pltpu.VMEM((8, width), full)]
         + ([pltpu.VMEM((NEAR, 8, width), full), *[pltpu.SemaphoreType.DMA((NEAR,))] * 2] if near else [])
         + ([pltpu.VMEM((last + 1, 8, value), full), *[pltpu.SemaphoreType.DMA((last + 1,))] * 2] if near else []),
-        scatters=[sums_rest, sums_in] if near else [], masks=range(1, NEAR) if near else (),
+        scatters=[(sums_rest, 0), (sums_in, 0), (sums_up, split)] if near else [], masks=range(1, NEAR) if near else (),
     )
     sums = gains if near else small_sums(gains)
     if near:
         (tq_grad, tk_grad, tv_grad, result, tokens_grad, query_grad, key_grad, value_grad, alpha_grad, beta_grad, up_grad, lift_grad,
          down_grad, gate_grad, out_grad) = final_sums(
-            middle, narrow_sum, middle_grad, term, sums_in, moved[1], sums_up, got_up[0], sums_rest, moved[0],
+            middle, narrow_sum, middle_grad, term, sums_in, moved[1], sums_up, got_up[0], moved[2], sums_rest, moved[0],
             gains, heads, keys, vals, size,
         )
     else:

time: 770 us -> 761 us (0.988)
  Pallas kernels: 714 us -> 703 us
    pallas_call x1, Pallas kernels: 81.4 us -> 69.7 us  [backward_chain(): pl.pallas_call(partial(backward_kernel, heads, key, value, devices, scatt...]
    unnamed x48 -> x50, local copies, waits for them, and re-layouts: 16 us -> 17.3 us
  transfers between devices with their start and end apart: 7 -> 7, of which waited for: 1 -> 1; matrix products, arithmetic and copies ran while one was open for 2% -> 2% of each run, Pallas kernels for 41% -> 40%
where the time goes in v7:
time: 761 us; the launch traced here: 759 us
  Pallas kernels  703 us (92%)
  local copies, waits for them, and re-layouts  26.2 us (3%)
  between operations  14.6 us (2%)
    pallas_call x3, Pallas kernels, line_call(): pl.pallas_call(body, grid=(steps,), in_specs=in_specs, out_specs=out_spec...  426 us
    pallas_call x6, Pallas kernels, weight_call(): pl.pallas_call(partial(weight_kernel, [len(bs) for _, bs in pairs], added...  71.9 us
    pallas_call x1, Pallas kernels, backward_chain(): pl.pallas_call(partial(backward_kernel, heads, key, value, devices, scatt...  69.7 us
    pallas_call x1, Pallas kernels, input_projection(): pl.pallas_call(partial(input_kernel, wide, gathering), in_specs=[here] +...  56.8 us
    pallas_call x1, Pallas kernels, forward_chain(): pl.pallas_call(partial(forward_kernel, heads, key, value, gathering), gri...  43.5 us
    pallas_call x1, Pallas kernels, final_sums(): pl.pallas_call(partial(final_kernel, heads, keys, vals, size), grid=(size...  22 us
    unnamed x50, local copies, waits for them, and re-layouts  17.3 us
  transfers between devices with their start and end apart: 7, of which 1 were waited for; matrix products, arithmetic and copies ran while one was open for 2% of the time, Pallas kernels for 40%

profile of v7, /device:TPU:0, one launch (start us, length us, event | category | flops | bytes accessed | tf_op | source)
XLA Modules:
  0.0 758.7 jit_solution(11404547869445364505)
XLA Ops:
  7.2 0.8 slice.73
  8.1 2.3 collective-permute-start
  10.5 0.8 reduce-window.9
  11.3 0.7 bitcast_subtract_fusion
  12.8 0.8 copy.112
  13.6 0.8 copy.113
  14.4 0.7 constant_dynamic-update-slice_fusion.2
  15.1 0.7 negate_bitcast_fusion
  16.0 0.7 constant_dynamic-update-slice_fusion.1
  16.7 0.7 constant_dynamic-update-slice_fusion.taps_ref
  17.4 0.8 maximum_maximum_fusion.refs_3_
  18.2 0.7 select_maximum_fusion.params_ref
  19.5 56.8 %input_projection.1 = (bf16[1024,2048]{1,0:T(8,128)(2,1)}, bf16[1024,2048]{1,0:T(8,128)(2,1)}, f32[1024,128]{1,0:T(8,128)}, bf16[16,2048]{1,0:T(8,128)(2,1)}, bf...) custom-call(f32[1,2048]{1,0:T(1,128)} %bitcast.66, f32[256,512]{1,0:T(8,128)} %refs_0_.3, ...), custom_call_target="tpu_custom_call" | custom-call | flops 1 | bytes 1 | tf_op jit(solution)/shard_map/input_projection/pallas_call | solution.py:1329
  76.3 0.8 slice.83.edge_ref
  77.1 1.0 copy-done.6
  78.1 1.2 copy-done.8
  79.3 43.5 %chain_forward.1 = (f32[1024,1024]{1,0:T(8,128)}, bf16[1024,512]{1,0:T(8,128)(2,1)S(1)}, bf16[8,4,128,384]{3,2,1,0:T(8,128)(2,1)}, bf16[8,4,128,128]{3,2,1,0:T(8...) custom-call(bf16[1024,2048]{1,0:T(8,128)(2,1)} %get-tuple-element.80.pre_ref.tail_ref, ...), custom_call_target="tpu_custom_call" | custom-call | flops 1 | bytes 1 | tf_op jit(solution)/shard_map/chain_forward/pallas_call | solution.py:361
  122.9 1.0 copy-done.2
  123.8 1.0 copy-done.7
  124.8 0.7 copy-done.10
  125.6 147.5 %mixer_out.1 = (bf16[1024,1024]{1,0:T(8,128)(2,1)}, f32[1024,1024]{1,0:T(8,128)}, f32[1024,1024]{1,0:T(8,128)}, f32[4,128,256]{2,1,0:T(8,128)}, f32[1024,2048]{1...) custom-call(f32[1,256]{1,0:T(1,128)} %bitcast.59, ...), custom_call_target="tpu_custom_call" | custom-call | flops 1 | bytes 1 | tf_op jit(solution)/shard_map/mixer_out/pallas_call | solution.py:1005
  273.1 127.6 %ffn.1 = (bf16[1024,1408]{1,0:T(8,128)(2,1)}, bf16[1024,1408]{1,0:T(8,128)(2,1)}, bf16[1024,1408]{1,0:T(8,128)(2,1)}, bf16[1024,2048]{1,0:T(8,128)(2,1)}, f32[10...) custom-call(f32[1,2048]{1,0:T(1,128)} %bitcast.65, bf16[2048,4224]{1,0:T(8,128)(2,1)} %get-tuple-element.91.refs_1_, ...), custom_call_target="tpu_custom_call" | custom-call | flops 1 | bytes 1 | tf_op jit(solution)/shard_map/ffn/pallas_call | solution.py:1005
  400.8 11.8 %weight_grads.6 = bf16[4,256,2816]{2,1,0:T(8,128)(2,1)} custom-call(s32[1]{0:T(128)} %bitcast.28.place_ref, bf16[1024,2048]{1,0:T(8,128)(2,1)} %get-tuple-element.92.refs_2_.refs_0_, bf16[1024,1408]{1,0:T(8,128)(2,1)} %get-tuple-element.103.refs_1_, bf16[1024,1408]{1,0:T(8,128)(2,1)} %get-tuple-element.104.refs_2_), custom_call_target="tpu_custom_call" | custom-call | flops 1 | bytes 1 | tf_op jit(solution)/shard_map/weight_grads/pallas_call | solution.py:1389
  412.6 12.6 %gate_back.1 = (bf16[1024,1024]{1,0:T(8,128)(2,1)S(1)}, bf16[1024,1024]{1,0:T(8,128)(2,1)S(1)}, f32[8,256]{1,0:T(8,128)S(1)}, f32[4,128,256]{2,1,0:T(8,128)S(1)}) custom-call(bf16[1024,2048]{1,0:T(8,128)(2,1)} %get-tuple-element.97.dz_ref.refs_2_, f32[1024,1024]{1,0:T(8,128)} %get-tuple-element.98.mixed_ref, f32[1024,1024]{1,0:T(8,128)} %get-tuple-element.99.gate_ref, ...), custom_call_target="tpu_custom_call" | custom-call | flops 1 | bytes 1 | tf_op jit(solution)/shard_map/gate_back/pallas_call | solution.py:436
  425.2 1.3 copy-done
  426.6 1.3 copy-done.5
  428.5 13.5 %weight_grads.8 = bf16[4,256,3456]{2,1,0:T(8,128)(2,1)} custom-call(s32[1]{0:T(128)} %bitcast.28.place_ref, bf16[1024,2048]{1,0:T(8,128)(2,1)} %refs_0_.5, bf16[1024,2048]{1,0:T(8,128)(2,1)} %get-tuple-element.87.refs_5_.refs_1_.refs_0_, bf16[1024,2048]{1,0:T(8,128)(2,1)} %get-tuple-element.97.dz_ref.refs_2_, bf16[1024,1408]{1,0:T(8,128)(2,1)} %get-tuple-element.113.refs_3_, ...), custom_call_target="tpu_custom_call" | custom-call | flops 1 | bytes 1 | tf_op jit(solution)/shard_map/weight_grads/pallas_call | solution.py:1389
  443.9 0.7 convert_element_type.21
  444.6 12.2 %weight_grads.7.refs_1_.refs_7_.up_own = bf16[4,256,2816]{2,1,0:T(8,128)(2,1)} custom-call(s32[1]{0:T(128)} %bitcast.28.place_ref, bf16[1024,2048]{1,0:T(8,128)(2,1)} %get-tuple-element.92.refs_2_.refs_0_, bf16[1024,1408]{1,0:T(8,128)(2,1)} %get-tuple-element.103.refs_1_, bf16[1024,1408]{1,0:T(8,128)(2,1)} %get-tuple-element.104.refs_2_, ...), custom_call_target="tpu_custom_call" | custom-call | flops 1 | bytes 1 | tf_op jit(solution)/shard_map/weight_grads/pallas_call | solution.py:1389
  456.8 69.7 %chain_backward.1 = (bf16[1024,2048]{1,0:T(8,128)(2,1)}, bf16[1024,128]{1,0:T(8,128)(2,1)}, f32[8,2048]{1,0:T(8,128)}, f32[32,2048]{1,0:T(8,128)}, f32[16,128]{1,0:T(8,128)}, /*index=5*/bf16[3,256,2176]{2,1,0:T(8,128)(2,1)}) custom-call(bf16[1024,2048]{1,0:T(8,128)(2,1)} %get-tuple-element.80.pre_ref.tail_ref, ...), custom_call_target="tpu_custom_call" | custom-call | flops 1 | bytes 1 | tf_op jit(solution)/shard_map/chain_backward/pallas_call | solution.py:689
  526.5 1.3 collective-permute-start.3
  527.8 2.1 collective-permute-done.3
  529.9 1.4 fusion.refs_1_.refs_8_
  531.3 9.8 %weight_grads.10 = bf16[4,256,2176]{2,1,0:T(8,128)(2,1)} custom-call(s32[1]{0:T(128)} %bitcast.28.place_ref, bf16[1024,2048]{1,0:T(8,128)(2,1)} %get-tuple-element.87.refs_5_.refs_1_.refs_0_, bf16[1024,2048]{1,0:T(8,128)(2,1)} %fusion.refs_1_.refs_8_, bf16[1024,128]{1,0:T(8,128)(2,1)} %get-tuple-element.118.refs_2_.refs_10_), custom_call_target="tpu_custom_call" | custom-call | flops 1 | bytes 1 | tf_op jit(solution)/shard_map/weight_grads/pallas_call | solution.py:1389
  541.1 2.4 collective-permute-start.4
  543.6 0.7 concatenate.11.refs_1_
  544.3 14.7 %weight_grads.9.refs_5_.down_own.gate_own.out_own = bf16[4,256,3456]{2,1,0:T(8,128)(2,1)} custom-call(s32[1]{0:T(128)} %bitcast.28.place_ref, bf16[1024,2048]{1,0:T(8,128)(2,1)} %refs_0_.5, bf16[1024,2048]{1,0:T(8,128)(2,1)} %get-tuple-element.87.refs_5_.refs_1_.refs_0_, bf16[1024,2048]{1,0:T(8,128)(2,1)} %get-tuple-element.97.dz_ref.refs_2_, ...), custom_call_target="tpu_custom_call" | custom-call | flops 1 | bytes 1 | tf_op jit(solution)/shard_map/weight_grads/pallas_call | solution.py:1389
  559.0 10.0 %weight_grads.11.refs_6_.in_own = bf16[4,256,2176]{2,1,0:T(8,128)(2,1)} custom-call(s32[1]{0:T(128)} %bitcast.28.place_ref, bf16[1024,2048]{1,0:T(8,128)(2,1)} %get-tuple-element.87.refs_5_.refs_1_.refs_0_, bf16[1024,2048]{1,0:T(8,128)(2,1)} %fusion.refs_1_.refs_8_, bf16[1024,128]{1,0:T(8,128)(2,1)} %get-tuple-element.118.refs_2_.refs_10_, ...), custom_call_target="tpu_custom_call" | custom-call | flops 1 | bytes 1 | tf_op jit(solution)/shard_map/weight_grads/pallas_call | solution.py:1389
  569.0 151.4 %input_grad.1 = (bf16[1024,2048]{1,0:T(8,128)(2,1)}, f32[8,2048]{1,0:T(8,128)}, bf16[3,256,3456]{2,1,0:T(8,128)(2,1)}, bf16[3,256,2176]{2,1,0:T(8,128)(2,1)}, bf16[3,256,640]{2,1,0:T(8,128)(2,1)}) custom-call(f32[1,2048]{1,0:T(1,128)} %bitcast.67, f32[8,2048]{1,0:T(8,128)} %concatenate.11.refs_1_, f32[8,256]{1,0:T(8,128)} %copy-done.16, ...), custom_call_target="tpu_custom_call" | custom-call | flops 1 | bytes 1 | tf_op jit(solution)/shard_map/input_grad/pallas_call | solution.py:1005
  720.4 1.3 slice.95
  721.7 1.2 slice_bitcast_fusion.1
  722.9 1.5 fusion.15
  724.4 1.9 copy-done.4
  726.3 1.2 copy-done.9
  727.5 0.8 copy-done.14
  728.4 22.0 %final_sums.1 = (f32[4,512]{1,0:T(4,128)}, f32[4,512]{1,0:T(4,128)}, f32[4,1024]{1,0:T(4,128)}, bf16[1024,2048]{1,0:T(8,128)(2,1)}, f32[1024,2048]{1,0:T(8,128)}...) custom-call(f32[1024,2048]{1,0:T(8,128)} %get-tuple-element.90.refs_, ...), custom_call_target="tpu_custom_call" | custom-call | flops 1 | bytes 1 | tf_op jit(solution)/shard_map/final_sums/pallas_call | solution.py:1480
  750.4 0.7 copy.124
  751.0 0.7 copy.125
  (74 shorter events, 4.5 us)
Async XLA Ops:
  7.2 519.3 %reduce-scatter.2.cloned.1.call-start = ((), (), s32[]{:S(2)}) async-start(), calls=%async_computation.1 | async-start | bytes 5242880 | tf_op jit(solution)/shard_map/reduce_scatter | solution.py:1599
  8.1 10.8 %collective-permute-start = (bf16[16,2048]{1,0:T(8,128)(2,1)S(1)}, bf16[16,2048]{1,0:T(8,128)(2,1)S(1)}, u32[]{:S(2)}, u32[]{:S(2)}) collective-permute-start(bf16[16,2048]{1,0:T(8,128)(2,1)S(1)} %slice.73), channel_id=1, source_target_pairs={{0,4},{4,8},{8,12},{12,16},{16,20},{20,24},{24,28},{1,5},{5,9},{9,... | collective-permute-start | bytes 196616 | tf_op jit(solution)/shard_map/ppermute | solution.py:1506
  15.9 61.2 %copy-start.1 = (f32[1024,128]{1,0:T(8,128)}, f32[1024,128]{1,0:T(8,128)S(1)}, u32[]{:S(2)}) copy-start(f32[1024,128]{1,0:T(8,128)S(1)} %pad.16.meta_ref) | copy-start | bytes 1572868
  17.4 59.6 %copy-start.13 = (f32[4,2048]{1,0:T(4,128)}, f32[4,2048]{1,0:T(4,128)S(1)}, u32[]{:S(2)}) copy-start(f32[4,2048]{1,0:T(4,128)S(1)} %constant_dynamic-update-slice_fusion.taps_ref) | copy-start | bytes 98308
  18.8 58.2 %copy-start.15 = (f32[8,128]{1,0:T(8,128)}, f32[8,128]{1,0:T(8,128)S(1)}, u32[]{:S(2)}) copy-start(f32[8,128]{1,0:T(8,128)S(1)} %select_maximum_fusion.params_ref) | copy-start | bytes 12292
  18.9 0.6 copy-start.19
  77.0 196.0 %copy-start.11 = (bf16[8,2048]{1,0:T(8,128)(2,1)}, bf16[8,2048]{1,0:T(8,128)(2,1)S(1)}, u32[]{:S(2)}) copy-start(bf16[8,2048]{1,0:T(8,128)(2,1)S(1)} %slice.83.edge_ref) | copy-start | bytes 98308
  77.0 196.0 %copy-start.12 = (f32[8,1024]{1,0:T(8,128)}, f32[8,1024]{1,0:T(8,128)S(1)}, u32[]{:S(2)}) copy-start(f32[8,1024]{1,0:T(8,128)S(1)} %broadcast_in_dim.33.segrow_ref) | copy-start | bytes 98308
  77.1 1.0 copy-start.6
  78.1 1.2 copy-start.8
  122.9 1.0 copy-start.2
  123.8 1.0 copy-start.7
  124.8 0.7 copy-start.10
  400.7 323.7 %all-gather.2.cloned.1.call-start = ((), (), s32[]{:S(2)}) async-start(), calls=%async_computation.2 | async-start | bytes 5242880 | tf_op jit(solution)/shard_map/all_gather | solution.py:1620
  400.7 11.9 %copy-start.3 = (bf16[1024,512]{1,0:T(8,128)(2,1)S(1)}, bf16[1024,512]{1,0:T(8,128)(2,1)}, u32[]{:S(2)}) copy-start(bf16[1024,512]{1,0:T(8,128)(2,1)} %copy-done.2) | copy-start | bytes 3145732
  400.8 11.9 %copy-start.17 = (f32[256]{0:T(256)S(1)}, f32[256]{0:T(256)}, u32[]{:S(2)}) copy-start(f32[256]{0:T(256)} %param.35) | copy-start | bytes 3076
  412.6 32.0 %collective-permute-start.1 = (bf16[4,256,2816]{2,1,0:T(8,128)(2,1)}, bf16[4,256,2816]{2,1,0:T(8,128)(2,1)}, u32[]{:S(2)}, u32[]{:S(2)}) collective-permute-start(bf16[4,256,2816]{2,1,0:T(8,128)(2,1)} %weight_grads.6), channel_id=1, source_target_pairs={{0,4},{4,0},{8,12},{12,8},{16,20},{20,16},{24,28},{28,24},{1,5},{5... | collective-permute-start | bytes 17301512 | tf_op jit(solution)/shard_map/ppermute | solution.py:777
  425.2 1.3 copy-start
  426.6 1.3 copy-start.5
  427.9 0.6 copy-start.16
  441.9 102.3 %collective-permute-start.2 = (bf16[4,256,3456]{2,1,0:T(8,128)(2,1)}, bf16[4,256,3456]{2,1,0:T(8,128)(2,1)}, u32[]{:S(2)}, u32[]{:S(2)}) collective-permute-start(bf16[4,256,3456]{2,1,0:T(8,128)(2,1)} %weight_grads.8), channel_id=1, source_target_pairs={{0,4},{4,0},{8,12},{12,8},{16,20},{20,16},{24,28},{28,24},{1,5},{5... | collective-permute-start | bytes 21233672 | tf_op jit(solution)/shard_map/ppermute | solution.py:777
  526.5 3.4 collective-permute-start.3
  531.3 12.1 %copy-start.20 = (f32[8,2048]{1,0:T(8,128)S(1)}, f32[8,2048]{1,0:T(8,128)}, u32[]{:S(2)}) copy-start(f32[8,2048]{1,0:T(8,128)} %get-tuple-element.108) | copy-start | bytes 196612
  531.3 12.2 %copy-start.21 = (f32[16,128]{1,0:T(8,128)S(1)}, f32[16,128]{1,0:T(8,128)}, u32[]{:S(2)}) copy-start(f32[16,128]{1,0:T(8,128)} %get-tuple-element.110) | copy-start | bytes 24580
  531.3 12.2 %copy-start.18 = (f32[32,2048]{1,0:T(8,128)S(1)}, f32[32,2048]{1,0:T(8,128)}, u32[]{:S(2)}) copy-start(f32[32,2048]{1,0:T(8,128)} %get-tuple-element.109) | copy-start | bytes 786436
  541.1 17.9 %collective-permute-start.4 = (bf16[4,256,2176]{2,1,0:T(8,128)(2,1)}, bf16[4,256,2176]{2,1,0:T(8,128)(2,1)}, u32[]{:S(2)}, u32[]{:S(2)}) collective-permute-start(bf16[4,256,2176]{2,1,0:T(8,128)(2,1)} %weight_grads.10), channel_id=1, source_target_pairs={{0,4},{4,0},{8,12},{12,8},{16,20},{20,16},{24,28},{28,24},{1,5},{5... | collective-permute-start | bytes 13369352 | tf_op jit(solution)/shard_map/ppermute | solution.py:777
  724.4 1.9 copy-start.4
  726.3 1.2 copy-start.9
  727.5 0.8 copy-start.14
Sparse Core Ops, SparseCore 0:
  400.8 76.8 reduce-scatter.1
  526.7 93.0 all-gather.1

commit v8 on v7

--- a/solution.py
+++ b/solution.py
@@ -1206,19 +1206,24 @@
         small_ref, sources = heavy[3], heavy[4:]
     else:
         (shard_ref, before_hbm, tokens_hbm), refs = refs[:3], refs[3:]
-    first_ref, pre_ref, ab_ref, edge_ref, whole_ref = refs[:5]
+    first_out, pre_ref, ab_ref, edge_ref, whole_ref = refs[:5]
     refs = refs[5:]
     if gathering:
-        (mix_ref, ffn_ref), refs = refs[:2], refs[2:]
-    weights, total, tokens_ref, before, home, *refs = refs
+        (mix_out, ffn_out), refs = refs[:2], refs[2:]
+    weights, total, tokens_ref, before, first_ref, edge_total, home, *refs = refs
     length, width = tokens_ref.shape
     half = width // 4
     back = pltpu.make_async_copy(weights, whole_ref, home.at[0])
+    handing = [pltpu.make_async_copy(first_ref, first_out, home.at[8])]
     here = pltpu.make_async_copy(tokens_hbm, tokens_ref, home.at[1])
     here.start()
     if gathering:
         shard, *buffers = refs[:6]
-        sems = refs[6:]
+        mix_ref, ffn_ref, *sems = refs[6:]
+        handing += [
+            pltpu.make_async_copy(mix_ref, mix_out, home.at[9]),
+            pltpu.make_async_copy(ffn_ref, ffn_out, home.at[10]),
+        ]
         pairs = [(before_hbm, before), *zip(sources, buffers)]
         copies = [pltpu.make_async_copy(a, b, home.at[2 + n]) for n, (a, b) in enumerate(pairs)]
         for copy in copies:
@@ -1250,6 +1255,7 @@
 
     here.wait()
     lax.fori_loop(0, length // rows, norm, 0)
+    handing[0].start()
 
     def add(chip, fresh, done):
         start = pl.multiple_of(chip * half, half)
@@ -1267,6 +1273,11 @@
             return carry
 
         lax.fori_loop(0, length // rows, one, 0)
+
+    def edge_add(chip, fresh):
+        start = pl.multiple_of(chip * half, half)
+        part = mm(before[:, pl.ds(start, half)], weights[pl.ds(start, half), :wide])
+        edge_total[...] = part if fresh else edge_total[...] + part
 
     if gathering:
         moving.local().wait()
@@ -1284,23 +1295,35 @@
         for first in range(0, size, 128):
             cols = slice(2 * size + first, 2 * size + first + 128)
             ffn_ref[:, cols] = down[first : first + 128, :].T.astype(low)
+        for copy in handing[1:]:
+            copy.start()
         moving.middle()
+        before[...] = normed(before[...])
+        edge_add(partner(0) // 2, True)
         moving.traded((5, 6))
         add(partner(2) // 2, False, False)
         moving.late()
         add(partner(4) // 2, False, False)
+        edge_add(partner(2) // 2, False)
+        edge_add(partner(4) // 2, False)
         moving.traded((7,))
         back.start()
         add(partner(6) // 2, False, True)
+        edge_add(partner(6) // 2, False)
     else:
         for copy in copies:
             copy.wait()
         back.start()
         for chip in range(4):
             add(chip, chip == 0, chip == 3)
-    edge_ref[...] = mm(normed(before[...]), weights[:, :wide]).astype(low)
+        before[...] = normed(before[...])
+        for chip in range(4):
+            edge_add(chip, chip == 0)
+    edge_ref[...] = edge_total[...].astype(low)
     if gathering:
         moving.settle()
+    for copy in handing:
+        copy.wait()
     back.wait()
 
 
@@ -1319,7 +1342,7 @@
             jax.ShapeDtypeStruct((rows, 3 * heavy[6].shape[1]), low),
         ]
         more = [pltpu.VMEM((rows, columns), low)] + [pltpu.VMEM(a.shape, full) for a in heavy[4:]]
-        more += Gather.semaphores
+        more += [pltpu.VMEM(s.shape, low) for s in shards_out] + Gather.semaphores
         params = dict(collective_id=4, has_side_effects=True)
     else:
         operands = [*heavy, before, tokens]
@@ -1329,7 +1352,7 @@
     return pl.pallas_call(
         partial(input_kernel, wide, gathering),
         in_specs=[here] + in_specs,
-        out_specs=[here] * 4 + [away] + [here] * len(shards_out),
+        out_specs=[away] + [here] * 3 + [away] * (1 + len(shards_out)),
         out_shape=[
             jax.ShapeDtypeStruct((length, width), low),
             jax.ShapeDtypeStruct((length, wide), low),
@@ -1343,7 +1366,9 @@
             pltpu.VMEM((length, columns), full),
             pltpu.VMEM((length, width), low),
             pltpu.VMEM((16, width), low),
-            pltpu.SemaphoreType.DMA((8,)),
+            pltpu.VMEM((length, width), low),
+            pltpu.VMEM((16, wide), full),
+            pltpu.SemaphoreType.DMA((11,)),
         ]
         + more,
         compiler_params=pltpu.CompilerParams(vmem_limit_bytes=60 * MIB, **params),

time: 761 us -> 758 us (level)
  no operation moved by 1% of the time
where the time goes in v8:
time: 758 us; the launch traced here: 756 us
  Pallas kernels  700 us (92%)
  local copies, waits for them, and re-layouts  26.2 us (3%)
  between operations  14.6 us (2%)
    pallas_call x3, Pallas kernels, line_call(): pl.pallas_call(body, grid=(steps,), in_specs=in_specs, out_specs=out_spec...  426 us
    pallas_call x6, Pallas kernels, weight_call(): pl.pallas_call(partial(weight_kernel, [len(bs) for _, bs in pairs], added...  71.9 us
    pallas_call x1, Pallas kernels, backward_chain(): pl.pallas_call(partial(backward_kernel, heads, key, value, devices, scatt...  69.7 us
    pallas_call x1, Pallas kernels, input_projection(): pl.pallas_call(partial(input_kernel, wide, gathering), in_specs=[here] +...  54.2 us
    pallas_call x1, Pallas kernels, forward_chain(): pl.pallas_call(partial(forward_kernel, heads, key, value, gathering), gri...  43.5 us
    pallas_call x1, Pallas kernels, final_sums(): pl.pallas_call(partial(final_kernel, heads, keys, vals, size), grid=(size...  22 us
    unnamed x50, local copies, waits for them, and re-layouts  17.3 us
  transfers between devices with their start and end apart: 7, of which 1 were waited for; matrix products, arithmetic and copies ran while one was open for 2% of the time, Pallas kernels for 40%

profile of v8, /device:TPU:0, one launch (start us, length us, event | category | flops | bytes accessed | tf_op | source)
XLA Modules:
  0.0 756.2 jit_solution(14432557908409755962)
XLA Ops:
  7.2 0.8 slice.73
  8.1 2.3 collective-permute-start
  10.5 0.8 reduce-window.9
  11.3 0.7 bitcast_subtract_fusion
  12.8 0.8 copy.112
  13.6 0.8 copy.113
  14.4 0.7 constant_dynamic-update-slice_fusion.2
  15.1 0.7 negate_bitcast_fusion
  16.0 0.7 constant_dynamic-update-slice_fusion.1
  16.7 0.7 constant_dynamic-update-slice_fusion.taps_ref
  17.4 0.8 maximum_maximum_fusion.refs_3_
  18.2 0.7 select_maximum_fusion.params_ref
  19.5 54.2 %input_projection.1 = (bf16[1024,2048]{1,0:T(8,128)(2,1)}, bf16[1024,2048]{1,0:T(8,128)(2,1)}, f32[1024,128]{1,0:T(8,128)}, bf16[16,2048]{1,0:T(8,128)(2,1)}, bf...) custom-call(f32[1,2048]{1,0:T(1,128)} %bitcast.66, f32[256,512]{1,0:T(8,128)} %refs_0_.3, ...), custom_call_target="tpu_custom_call" | custom-call | flops 1 | bytes 1 | tf_op jit(solution)/shard_map/input_projection/pallas_call | solution.py:1352
  73.7 0.8 slice.83.edge_ref
  74.5 1.0 copy-done.6
  75.6 1.2 copy-done.8
  76.8 43.5 %chain_forward.1 = (f32[1024,1024]{1,0:T(8,128)}, bf16[1024,512]{1,0:T(8,128)(2,1)S(1)}, bf16[8,4,128,384]{3,2,1,0:T(8,128)(2,1)}, bf16[8,4,128,128]{3,2,1,0:T(8...) custom-call(bf16[1024,2048]{1,0:T(8,128)(2,1)} %get-tuple-element.80.pre_ref.tail_ref, ...), custom_call_target="tpu_custom_call" | custom-call | flops 1 | bytes 1 | tf_op jit(solution)/shard_map/chain_forward/pallas_call | solution.py:361
  120.4 1.0 copy-done.2
  121.3 1.0 copy-done.7
  122.3 0.7 copy-done.10
  123.0 147.5 %mixer_out.1 = (bf16[1024,1024]{1,0:T(8,128)(2,1)}, f32[1024,1024]{1,0:T(8,128)}, f32[1024,1024]{1,0:T(8,128)}, f32[4,128,256]{2,1,0:T(8,128)}, f32[1024,2048]{1...) custom-call(f32[1,256]{1,0:T(1,128)} %bitcast.59, ...), custom_call_target="tpu_custom_call" | custom-call | flops 1 | bytes 1 | tf_op jit(solution)/shard_map/mixer_out/pallas_call | solution.py:1005
  270.6 127.5 %ffn.1 = (bf16[1024,1408]{1,0:T(8,128)(2,1)}, bf16[1024,1408]{1,0:T(8,128)(2,1)}, bf16[1024,1408]{1,0:T(8,128)(2,1)}, bf16[1024,2048]{1,0:T(8,128)(2,1)}, f32[10...) custom-call(f32[1,2048]{1,0:T(1,128)} %bitcast.65, bf16[2048,4224]{1,0:T(8,128)(2,1)} %get-tuple-element.91.refs_1_, ...), custom_call_target="tpu_custom_call" | custom-call | flops 1 | bytes 1 | tf_op jit(solution)/shard_map/ffn/pallas_call | solution.py:1005
  398.2 11.8 %weight_grads.6 = bf16[4,256,2816]{2,1,0:T(8,128)(2,1)} custom-call(s32[1]{0:T(128)} %bitcast.28.place_ref, bf16[1024,2048]{1,0:T(8,128)(2,1)} %get-tuple-element.92.refs_2_.refs_0_, bf16[1024,1408]{1,0:T(8,128)(2,1)} %get-tuple-element.103.refs_1_, bf16[1024,1408]{1,0:T(8,128)(2,1)} %get-tuple-element.104.refs_2_), custom_call_target="tpu_custom_call" | custom-call | flops 1 | bytes 1 | tf_op jit(solution)/shard_map/weight_grads/pallas_call | solution.py:1414
  410.1 12.6 %gate_back.1 = (bf16[1024,1024]{1,0:T(8,128)(2,1)S(1)}, bf16[1024,1024]{1,0:T(8,128)(2,1)S(1)}, f32[8,256]{1,0:T(8,128)S(1)}, f32[4,128,256]{2,1,0:T(8,128)S(1)}) custom-call(bf16[1024,2048]{1,0:T(8,128)(2,1)} %get-tuple-element.97.dz_ref.refs_2_, f32[1024,1024]{1,0:T(8,128)} %get-tuple-element.98.mixed_ref, f32[1024,1024]{1,0:T(8,128)} %get-tuple-element.99.gate_ref, ...), custom_call_target="tpu_custom_call" | custom-call | flops 1 | bytes 1 | tf_op jit(solution)/shard_map/gate_back/pallas_call | solution.py:436
  422.7 1.3 copy-done
  424.0 1.3 copy-done.5
  425.9 13.5 %weight_grads.8 = bf16[4,256,3456]{2,1,0:T(8,128)(2,1)} custom-call(s32[1]{0:T(128)} %bitcast.28.place_ref, bf16[1024,2048]{1,0:T(8,128)(2,1)} %refs_0_.5, bf16[1024,2048]{1,0:T(8,128)(2,1)} %get-tuple-element.87.refs_5_.refs_1_.refs_0_, bf16[1024,2048]{1,0:T(8,128)(2,1)} %get-tuple-element.97.dz_ref.refs_2_, bf16[1024,1408]{1,0:T(8,128)(2,1)} %get-tuple-element.113.refs_3_, ...), custom_call_target="tpu_custom_call" | custom-call | flops 1 | bytes 1 | tf_op jit(solution)/shard_map/weight_grads/pallas_call | solution.py:1414
  441.4 0.7 convert_element_type.21
  442.1 12.2 %weight_grads.7.refs_1_.refs_7_.up_own = bf16[4,256,2816]{2,1,0:T(8,128)(2,1)} custom-call(s32[1]{0:T(128)} %bitcast.28.place_ref, bf16[1024,2048]{1,0:T(8,128)(2,1)} %get-tuple-element.92.refs_2_.refs_0_, bf16[1024,1408]{1,0:T(8,128)(2,1)} %get-tuple-element.103.refs_1_, bf16[1024,1408]{1,0:T(8,128)(2,1)} %get-tuple-element.104.refs_2_, ...), custom_call_target="tpu_custom_call" | custom-call | flops 1 | bytes 1 | tf_op jit(solution)/shard_map/weight_grads/pallas_call | solution.py:1414
  454.2 69.7 %chain_backward.1 = (bf16[1024,2048]{1,0:T(8,128)(2,1)}, bf16[1024,128]{1,0:T(8,128)(2,1)}, f32[8,2048]{1,0:T(8,128)}, f32[32,2048]{1,0:T(8,128)}, f32[16,128]{1,0:T(8,128)}, /*index=5*/bf16[3,256,2176]{2,1,0:T(8,128)(2,1)}) custom-call(bf16[1024,2048]{1,0:T(8,128)(2,1)} %get-tuple-element.80.pre_ref.tail_ref, ...), custom_call_target="tpu_custom_call" | custom-call | flops 1 | bytes 1 | tf_op jit(solution)/shard_map/chain_backward/pallas_call | solution.py:689
  524.0 1.3 collective-permute-start.3
  525.3 2.1 collective-permute-done.3
  527.4 1.4 fusion.refs_1_.refs_8_
  528.7 9.8 %weight_grads.10 = bf16[4,256,2176]{2,1,0:T(8,128)(2,1)} custom-call(s32[1]{0:T(128)} %bitcast.28.place_ref, bf16[1024,2048]{1,0:T(8,128)(2,1)} %get-tuple-element.87.refs_5_.refs_1_.refs_0_, bf16[1024,2048]{1,0:T(8,128)(2,1)} %fusion.refs_1_.refs_8_, bf16[1024,128]{1,0:T(8,128)(2,1)} %get-tuple-element.118.refs_2_.refs_10_), custom_call_target="tpu_custom_call" | custom-call | flops 1 | bytes 1 | tf_op jit(solution)/shard_map/weight_grads/pallas_call | solution.py:1414
  538.5 2.4 collective-permute-start.4
  541.0 0.7 concatenate.11.refs_1_
  541.7 14.7 %weight_grads.9.refs_5_.down_own.gate_own.out_own = bf16[4,256,3456]{2,1,0:T(8,128)(2,1)} custom-call(s32[1]{0:T(128)} %bitcast.28.place_ref, bf16[1024,2048]{1,0:T(8,128)(2,1)} %refs_0_.5, bf16[1024,2048]{1,0:T(8,128)(2,1)} %get-tuple-element.87.refs_5_.refs_1_.refs_0_, bf16[1024,2048]{1,0:T(8,128)(2,1)} %get-tuple-element.97.dz_ref.refs_2_, ...), custom_call_target="tpu_custom_call" | custom-call | flops 1 | bytes 1 | tf_op jit(solution)/shard_map/weight_grads/pallas_call | solution.py:1414
  556.4 10.0 %weight_grads.11.refs_6_.in_own = bf16[4,256,2176]{2,1,0:T(8,128)(2,1)} custom-call(s32[1]{0:T(128)} %bitcast.28.place_ref, bf16[1024,2048]{1,0:T(8,128)(2,1)} %get-tuple-element.87.refs_5_.refs_1_.refs_0_, bf16[1024,2048]{1,0:T(8,128)(2,1)} %fusion.refs_1_.refs_8_, bf16[1024,128]{1,0:T(8,128)(2,1)} %get-tuple-element.118.refs_2_.refs_10_, ...), custom_call_target="tpu_custom_call" | custom-call | flops 1 | bytes 1 | tf_op jit(solution)/shard_map/weight_grads/pallas_call | solution.py:1414
  566.4 151.4 %input_grad.1 = (bf16[1024,2048]{1,0:T(8,128)(2,1)}, f32[8,2048]{1,0:T(8,128)}, bf16[3,256,3456]{2,1,0:T(8,128)(2,1)}, bf16[3,256,2176]{2,1,0:T(8,128)(2,1)}, bf16[3,256,640]{2,1,0:T(8,128)(2,1)}) custom-call(f32[1,2048]{1,0:T(1,128)} %bitcast.67, f32[8,2048]{1,0:T(8,128)} %concatenate.11.refs_1_, f32[8,256]{1,0:T(8,128)} %copy-done.16, ...), custom_call_target="tpu_custom_call" | custom-call | flops 1 | bytes 1 | tf_op jit(solution)/shard_map/input_grad/pallas_call | solution.py:1005
  717.9 1.3 slice.95
  719.1 1.2 slice_bitcast_fusion.1
  720.3 1.5 fusion.15
  721.8 1.9 copy-done.4
  723.8 1.2 copy-done.9
  725.0 0.8 copy-done.14
  725.8 22.0 %final_sums.1 = (f32[4,512]{1,0:T(4,128)}, f32[4,512]{1,0:T(4,128)}, f32[4,1024]{1,0:T(4,128)}, bf16[1024,2048]{1,0:T(8,128)(2,1)}, f32[1024,2048]{1,0:T(8,128)}...) custom-call(f32[1024,2048]{1,0:T(8,128)} %get-tuple-element.90.refs_, ...), custom_call_target="tpu_custom_call" | custom-call | flops 1 | bytes 1 | tf_op jit(solution)/shard_map/final_sums/pallas_call | solution.py:1505
  747.8 0.7 copy.124
  748.5 0.7 copy.125
  (74 shorter events, 4.5 us)
Async XLA Ops:
  7.2 516.8 %reduce-scatter.2.cloned.1.call-start = ((), (), s32[]{:S(2)}) async-start(), calls=%async_computation.1 | async-start | bytes 5242880 | tf_op jit(solution)/shard_map/reduce_scatter | solution.py:1624
  8.1 10.8 %collective-permute-start = (bf16[16,2048]{1,0:T(8,128)(2,1)S(1)}, bf16[16,2048]{1,0:T(8,128)(2,1)S(1)}, u32[]{:S(2)}, u32[]{:S(2)}) collective-permute-start(bf16[16,2048]{1,0:T(8,128)(2,1)S(1)} %slice.73), channel_id=1, source_target_pairs={{0,4},{4,8},{8,12},{12,16},{16,20},{20,24},{24,28},{1,5},{5,9},{9,... | collective-permute-start | bytes 196616 | tf_op jit(solution)/shard_map/ppermute | solution.py:1531
  15.9 58.7 %copy-start.1 = (f32[1024,128]{1,0:T(8,128)}, f32[1024,128]{1,0:T(8,128)S(1)}, u32[]{:S(2)}) copy-start(f32[1024,128]{1,0:T(8,128)S(1)} %pad.16.meta_ref) | copy-start | bytes 1572868
  17.4 57.1 %copy-start.13 = (f32[4,2048]{1,0:T(4,128)}, f32[4,2048]{1,0:T(4,128)S(1)}, u32[]{:S(2)}) copy-start(f32[4,2048]{1,0:T(4,128)S(1)} %constant_dynamic-update-slice_fusion.taps_ref) | copy-start | bytes 98308
  18.8 55.7 %copy-start.15 = (f32[8,128]{1,0:T(8,128)}, f32[8,128]{1,0:T(8,128)S(1)}, u32[]{:S(2)}) copy-start(f32[8,128]{1,0:T(8,128)S(1)} %select_maximum_fusion.params_ref) | copy-start | bytes 12292
  18.9 0.6 copy-start.19
  74.5 196.1 %copy-start.11 = (bf16[8,2048]{1,0:T(8,128)(2,1)}, bf16[8,2048]{1,0:T(8,128)(2,1)S(1)}, u32[]{:S(2)}) copy-start(bf16[8,2048]{1,0:T(8,128)(2,1)S(1)} %slice.83.edge_ref) | copy-start | bytes 98308
  74.5 196.1 %copy-start.12 = (f32[8,1024]{1,0:T(8,128)}, f32[8,1024]{1,0:T(8,128)S(1)}, u32[]{:S(2)}) copy-start(f32[8,1024]{1,0:T(8,128)S(1)} %broadcast_in_dim.33.segrow_ref) | copy-start | bytes 98308
  74.5 1.0 copy-start.6
  75.6 1.2 copy-start.8
  120.3 1.0 copy-start.2
  121.3 1.0 copy-start.7
  122.3 0.7 copy-start.10
  398.1 323.7 %all-gather.2.cloned.1.call-start = ((), (), s32[]{:S(2)}) async-start(), calls=%async_computation.2 | async-start | bytes 5242880 | tf_op jit(solution)/shard_map/all_gather | solution.py:1645
  398.2 11.9 %copy-start.3 = (bf16[1024,512]{1,0:T(8,128)(2,1)S(1)}, bf16[1024,512]{1,0:T(8,128)(2,1)}, u32[]{:S(2)}) copy-start(bf16[1024,512]{1,0:T(8,128)(2,1)} %copy-done.2) | copy-start | bytes 3145732
  398.2 11.9 %copy-start.17 = (f32[256]{0:T(256)S(1)}, f32[256]{0:T(256)}, u32[]{:S(2)}) copy-start(f32[256]{0:T(256)} %param.35) | copy-start | bytes 3076
  410.1 32.0 %collective-permute-start.1 = (bf16[4,256,2816]{2,1,0:T(8,128)(2,1)}, bf16[4,256,2816]{2,1,0:T(8,128)(2,1)}, u32[]{:S(2)}, u32[]{:S(2)}) collective-permute-start(bf16[4,256,2816]{2,1,0:T(8,128)(2,1)} %weight_grads.6), channel_id=1, source_target_pairs={{0,4},{4,0},{8,12},{12,8},{16,20},{20,16},{24,28},{28,24},{1,5},{5... | collective-permute-start | bytes 17301512 | tf_op jit(solution)/shard_map/ppermute | solution.py:777
  422.7 1.3 copy-start
  424.0 1.3 copy-start.5
  425.3 0.6 copy-start.16
  439.4 102.3 %collective-permute-start.2 = (bf16[4,256,3456]{2,1,0:T(8,128)(2,1)}, bf16[4,256,3456]{2,1,0:T(8,128)(2,1)}, u32[]{:S(2)}, u32[]{:S(2)}) collective-permute-start(bf16[4,256,3456]{2,1,0:T(8,128)(2,1)} %weight_grads.8), channel_id=1, source_target_pairs={{0,4},{4,0},{8,12},{12,8},{16,20},{20,16},{24,28},{28,24},{1,5},{5... | collective-permute-start | bytes 21233672 | tf_op jit(solution)/shard_map/ppermute | solution.py:777
  524.0 3.4 collective-permute-start.3
  528.7 12.1 %copy-start.20 = (f32[8,2048]{1,0:T(8,128)S(1)}, f32[8,2048]{1,0:T(8,128)}, u32[]{:S(2)}) copy-start(f32[8,2048]{1,0:T(8,128)} %get-tuple-element.108) | copy-start | bytes 196612
  528.7 12.2 %copy-start.21 = (f32[16,128]{1,0:T(8,128)S(1)}, f32[16,128]{1,0:T(8,128)}, u32[]{:S(2)}) copy-start(f32[16,128]{1,0:T(8,128)} %get-tuple-element.110) | copy-start | bytes 24580
  528.7 12.2 %copy-start.18 = (f32[32,2048]{1,0:T(8,128)S(1)}, f32[32,2048]{1,0:T(8,128)}, u32[]{:S(2)}) copy-start(f32[32,2048]{1,0:T(8,128)} %get-tuple-element.109) | copy-start | bytes 786436
  538.5 17.9 %collective-permute-start.4 = (bf16[4,256,2176]{2,1,0:T(8,128)(2,1)}, bf16[4,256,2176]{2,1,0:T(8,128)(2,1)}, u32[]{:S(2)}, u32[]{:S(2)}) collective-permute-start(bf16[4,256,2176]{2,1,0:T(8,128)(2,1)} %weight_grads.10), channel_id=1, source_target_pairs={{0,4},{4,0},{8,12},{12,8},{16,20},{20,16},{24,28},{28,24},{1,5},{5... | collective-permute-start | bytes 13369352 | tf_op jit(solution)/shard_map/ppermute | solution.py:777
  721.8 1.9 copy-start.4
  723.8 1.2 copy-start.9
  725.0 0.8 copy-start.14
Sparse Core Ops, SparseCore 0:
  398.3 76.8 reduce-scatter.1
  524.1 93.0 all-gather.1
